TPU v7x, 32 devices: a whole 2x2x4 slice. The times are simulated.
32 devices in a mesh: dp: 4 (over x, core), tensor: 8 (over z, y).
Axes of the slice: x: 2, y: 2, z: 4, core: 2. Of those that a mesh axis runs over, the one named last changes fastest.
Arguments:
- tokens: bfloat16 [8192, 2048], P(('dp', 'tensor')), may hold values from -6 to 6
- attn_gain: bfloat16 [2048], replicated, may hold values from 0.099609375 to 1.8984375
- w_query: bfloat16 [2048, 2048], P(None, 'tensor'), may hold values from -0.125 to 0.125
- w_key: bfloat16 [2048, 2048], P(None, 'tensor'), may hold values from -0.125 to 0.125
- w_value: bfloat16 [2048, 2048], P(None, 'tensor'), may hold values from -0.125 to 0.125
- conv_query: bfloat16 [4, 2048], P(None, 'tensor'), may hold values from -3 to 3
- conv_key: bfloat16 [4, 2048], P(None, 'tensor'), may hold values from -3 to 3
- conv_value: bfloat16 [4, 2048], P(None, 'tensor'), may hold values from -3 to 3
- w_beta: bfloat16 [2048, 16], P(None, 'tensor'), may hold values from -0.125 to 0.125
- w_gate_out: bfloat16 [2048, 2048], P(None, 'tensor'), may hold values from -0.125 to 0.125
- head_gain: bfloat16 [128], replicated, may hold values from 0.099609375 to 1.8984375
- w_out: bfloat16 [2048, 2048], P('tensor'), may hold values from -0.25 to 0.25
- ffn_gain: bfloat16 [2048], replicated, may hold values from 0.099609375 to 1.8984375
- w_gate: bfloat16 [2048, 5632], P(None, 'tensor'), may hold values from -0.125 to 0.125
- w_up: bfloat16 [2048, 5632], P(None, 'tensor'), may hold values from -0.125 to 0.125
- w_down: bfloat16 [5632, 2048], P('tensor'), may hold values from -0.15625 to 0.15625
- seq_starts: int32 [4, 2], P('dp'), may hold values from 0 to 1536, as said below
- seq_lengths: int32 [4, 2], P('dp'), may hold values from 512 to 1024, as said below
- cotangent: bfloat16 [8192, 2048], P(('dp', 'tensor')), may hold values from -6 to 6
Outputs:
- output: bfloat16 [8192, 2048], P(('dp', 'tensor'))
- grad_tokens: float32 [8192, 2048], P(('dp', 'tensor'))
- grad_attn_gain: float32 [2048], replicated
- grad_w_query: float32 [2048, 2048], P(None, 'tensor')
- grad_w_key: float32 [2048, 2048], P(None, 'tensor')
- grad_w_value: float32 [2048, 2048], P(None, 'tensor')
- grad_conv_query: float32 [4, 2048], P(None, 'tensor')
- grad_conv_key: float32 [4, 2048], P(None, 'tensor')
- grad_conv_value: float32 [4, 2048], P(None, 'tensor')
- grad_w_beta: float32 [2048, 16], P(None, 'tensor')
- grad_w_gate_out: float32 [2048, 2048], P(None, 'tensor')
- grad_head_gain: float32 [128], replicated
- grad_w_out: float32 [2048, 2048], P('tensor')
- grad_ffn_gain: float32 [2048], replicated
- grad_w_gate: float32 [2048, 5632], P(None, 'tensor')
- grad_w_up: float32 [2048, 5632], P(None, 'tensor')
- grad_w_down: float32 [5632, 2048], P('tensor')
Inputs may be any that keep to these rules, and one draw needn't show every extreme that they name: `seq_lengths`: each shard holds 2 sequences; the first shard's first sequence has 1024 tokens and its last one 2048 // 4. `seq_starts`: the sequences of a shard lie in order within its 2048 slots and do not intersect, the first starting at slot 0; the other slots are padding. The first shard's last sequence ends at its last slot.
All inputs are finite; a program needn't handle non-finite values.
Results may differ from a plain program's by a relative error of at most 0.02.
Values may be sent and summed in bfloat16 or wider, within the bound.
A program may use at most 320 MiB of HBM per device.

v0:
```python
import jax
import jax.numpy as jnp
from jax import lax
from jax.sharding import PartitionSpec as P

STRETCH = 64


highest = lax.Precision.HIGHEST


def round_pass(value):
    return lax.optimization_barrier(value.astype(jnp.bfloat16)).astype(jnp.float32)


def round_keep(value):
    return (round_pass(value), None)


def round_grad(kept, grad):
    return (grad,)


def make_rounding():
    rounder = jax.custom_vjp(round_pass)
    rounder.defvjp(round_keep, round_grad)
    return rounder


def positions(starts, lengths, slot_count):
    places = jnp.arange(slot_count, dtype=jnp.int32)
    begun = (places[:, None] >= starts[None, :]).astype(jnp.int32)
    ended = (places[:, None] >= (starts + lengths)[None, :]).astype(jnp.int32)
    segment = jnp.sum(begun + ended, axis=1)
    live = (segment % 2).astype(jnp.float32)
    return (segment, live)


def short_conv(inputs, taps, segment):
    result = inputs * taps[0]
    for offset in range(1, taps.shape[0]):
        moved = jnp.concatenate(
            [jnp.zeros((offset, inputs.shape[1]), jnp.float32), inputs[:-offset]], 0
        )
        earlier = jnp.concatenate([jnp.full((offset,), -1, jnp.int32), segment[:-offset]], 0)
        result = result + moved * taps[offset] * (earlier == segment).astype(jnp.float32)[:, None]
    return result


def unit_rows(inputs):
    return inputs * lax.rsqrt(jnp.sum(inputs * inputs, axis=-1, keepdims=True) + 1e-06)


def delta_rule(queries, key_rows, values, strength, segment):
    slot_count, head_width = queries.shape
    blocks = slot_count // STRETCH
    query_blocks = (queries * head_width ** (-0.5)).reshape(blocks, STRETCH, head_width)
    key_blocks = key_rows.reshape(blocks, STRETCH, head_width)
    value_blocks = values.reshape(blocks, STRETCH, head_width)
    beta_blocks = strength.reshape(blocks, STRETCH)
    seg_blocks = segment.reshape(blocks, STRETCH)
    same_seg = (seg_blocks[:, :, None] == seg_blocks[:, None, :]).astype(jnp.float32)
    places = jnp.arange(STRETCH)
    strict = (places[:, None] > places[None, :]).astype(jnp.float32)
    inclusive = (places[:, None] >= places[None, :]).astype(jnp.float32)
    key_inner = jnp.einsum("nik,njk->nij", key_blocks, key_blocks, precision=highest)
    system = (
        jnp.eye(STRETCH, dtype=jnp.float32)[None]
        + beta_blocks[:, :, None] * key_inner * same_seg * strict
    )
    weighted = lax.linalg.triangular_solve(
        system, beta_blocks[:, :, None] * key_blocks, left_side=True, lower=True, unit_diagonal=True
    )
    updates = lax.linalg.triangular_solve(
        system,
        beta_blocks[:, :, None] * value_blocks,
        left_side=True,
        lower=True,
        unit_diagonal=True,
    )
    within = (
        jnp.einsum("nik,njk->nij", query_blocks, key_blocks, precision=highest)
        * same_seg
        * inclusive
    )
    earlier_last = jnp.concatenate([jnp.full((1,), -1, jnp.int32), seg_blocks[:-1, STRETCH - 1]], 0)
    continued = (seg_blocks[:, 0] == earlier_last).astype(jnp.float32)
    carried = same_seg[:, :, 0] * continued[:, None]
    ending = same_seg[:, :, STRETCH - 1]
    kept_state = continued * same_seg[:, 0, STRETCH - 1]

    def advance(memory, pieces):
        query_part, key_part, weight_part, update_part, mixing, carry_part, end_part, keep_part = (
            pieces
        )
        change = update_part - carry_part[:, None] * jnp.dot(
            weight_part, memory.T, precision=highest
        )
        result = carry_part[:, None] * jnp.dot(query_part, memory.T, precision=highest) + jnp.dot(
            mixing, change, precision=highest
        )
        memory = keep_part * memory + jnp.dot(
            (end_part[:, None] * change).T, key_part, precision=highest
        )
        return (memory, result)

    start_memory = jnp.zeros((head_width, head_width), jnp.float32)
    last_memory, outputs = lax.scan(
        jax.checkpoint(advance),
        start_memory,
        (query_blocks, key_blocks, weighted, updates, within, carried, ending, kept_state),
    )
    return outputs.reshape(slot_count, head_width)


def mixer_local(
    proj_query,
    proj_key,
    proj_value,
    proj_beta,
    proj_gate,
    taps_query,
    taps_key,
    taps_value,
    gain_head,
    segment,
    live,
    rounder,
):
    slot_count = proj_query.shape[0]
    head_count = proj_beta.shape[1]
    head_width = proj_query.shape[1] // head_count

    def feature(projected, taps):
        return jax.nn.silu(short_conv(projected, taps, segment)).reshape(
            slot_count, head_count, head_width
        )

    queries = rounder(unit_rows(feature(proj_query, taps_query)))
    key_rows = rounder(unit_rows(feature(proj_key, taps_key)))
    values = rounder(feature(proj_value, taps_value))
    strength = jax.nn.sigmoid(proj_beta)
    delta_out = jax.vmap(delta_rule, in_axes=(1, 1, 1, 1, None), out_axes=1)(
        queries, key_rows, values, strength, segment
    )
    head_normed = (
        delta_out
        * lax.rsqrt(jnp.mean(delta_out * delta_out, axis=-1, keepdims=True) + 1e-05)
        * gain_head
    )
    gated = (
        head_normed
        * jax.nn.silu(proj_gate.reshape(slot_count, head_count, head_width))
        * live[:, None, None]
    )
    return gated.reshape(slot_count, head_count * head_width)


def norm_back(inputs, scale, gain, grad_normed):
    weighted_grad = gain * grad_normed
    inner = jnp.mean(weighted_grad * inputs, axis=1, keepdims=True)
    grad_inputs = scale * weighted_grad - inputs * scale * scale * scale * inner
    grad_gain = jnp.sum(grad_normed * inputs * scale, axis=0)
    return (grad_inputs, grad_gain)


def shards(
    tokens,
    attn_gain,
    w_query,
    w_key,
    w_value,
    conv_query,
    conv_key,
    conv_value,
    w_beta,
    w_gate_out,
    head_gain,
    w_out,
    ffn_gain,
    w_gate,
    w_up,
    w_down,
    seq_starts,
    seq_lengths,
    cotangent,
):
    row_count = tokens.shape[0]
    slot_count = row_count * lax.axis_size("tensor")
    segment, live = positions(seq_starts[0], seq_lengths[0], slot_count)
    rounder = make_rounding()
    inputs = tokens.astype(jnp.float32)
    gain_first = attn_gain.astype(jnp.float32)
    scale_first = lax.rsqrt(jnp.mean(inputs * inputs, axis=1, keepdims=True) + 1e-06)
    normed = (inputs * scale_first * gain_first).astype(jnp.bfloat16)
    normed_full = lax.all_gather(normed, "tensor", axis=0, tiled=True)
    mixer_weights = (w_query, w_key, w_value, w_beta, w_gate_out)
    projected = [
        jnp.dot(normed_full, weight, preferred_element_type=jnp.float32) for weight in mixer_weights
    ]

    def mixer_piece(
        proj_query,
        proj_key,
        proj_value,
        proj_beta,
        proj_gate,
        taps_query,
        taps_key,
        taps_value,
        gain_head,
    ):
        return mixer_local(
            proj_query,
            proj_key,
            proj_value,
            proj_beta,
            proj_gate,
            taps_query,
            taps_key,
            taps_value,
            gain_head,
            segment,
            live,
            rounder,
        )

    mixed, mixer_pullback = jax.vjp(
        mixer_piece,
        projected[0],
        projected[1],
        projected[2],
        projected[3],
        projected[4],
        conv_query.astype(jnp.float32),
        conv_key.astype(jnp.float32),
        conv_value.astype(jnp.float32),
        head_gain.astype(jnp.float32),
    )
    mixed_low = mixed.astype(jnp.bfloat16)
    attended = lax.psum_scatter(
        jnp.dot(mixed_low, w_out, preferred_element_type=jnp.float32).astype(jnp.bfloat16),
        "tensor",
        scatter_dimension=0,
        tiled=True,
    ).astype(jnp.float32)
    resid = inputs + attended
    gain_second = ffn_gain.astype(jnp.float32)
    scale_second = lax.rsqrt(jnp.mean(resid * resid, axis=1, keepdims=True) + 1e-06)
    ffn_in = (resid * scale_second * gain_second).astype(jnp.bfloat16)
    ffn_full = lax.all_gather(ffn_in, "tensor", axis=0, tiled=True)
    gate_pre = jnp.dot(ffn_full, w_gate, preferred_element_type=jnp.float32)
    up_pre = jnp.dot(ffn_full, w_up, preferred_element_type=jnp.float32)
    sigmoid_gate = jax.nn.sigmoid(gate_pre)
    silu_gate = gate_pre * sigmoid_gate
    hidden = (silu_gate * up_pre).astype(jnp.bfloat16)
    output = resid + lax.psum_scatter(
        jnp.dot(hidden, w_down, preferred_element_type=jnp.float32).astype(jnp.bfloat16),
        "tensor",
        scatter_dimension=0,
        tiled=True,
    ).astype(jnp.float32)
    grad_full = lax.all_gather(cotangent, "tensor", axis=0, tiled=True)
    grad_hidden = jnp.einsum("sd,fd->sf", grad_full, w_down, preferred_element_type=jnp.float32)
    grad_w_down = jnp.einsum("sf,sd->fd", hidden, grad_full, preferred_element_type=jnp.float32)
    grad_gate = (
        grad_hidden * up_pre * sigmoid_gate * (1.0 + gate_pre * (1.0 - sigmoid_gate))
    ).astype(jnp.bfloat16)
    grad_up = (grad_hidden * silu_gate).astype(jnp.bfloat16)
    grad_w_gate = jnp.einsum("sd,sf->df", ffn_full, grad_gate, preferred_element_type=jnp.float32)
    grad_w_up = jnp.einsum("sd,sf->df", ffn_full, grad_up, preferred_element_type=jnp.float32)
    grad_ffn_in = lax.psum_scatter(
        (
            jnp.einsum("sf,df->sd", grad_gate, w_gate, preferred_element_type=jnp.float32)
            + jnp.einsum("sf,df->sd", grad_up, w_up, preferred_element_type=jnp.float32)
        ).astype(jnp.bfloat16),
        "tensor",
        scatter_dimension=0,
        tiled=True,
    ).astype(jnp.float32)
    grad_through, grad_ffn_gain = norm_back(resid, scale_second, gain_second, grad_ffn_in)
    grad_resid = cotangent.astype(jnp.float32) + grad_through
    grad_attended = lax.all_gather(grad_resid.astype(jnp.bfloat16), "tensor", axis=0, tiled=True)
    grad_mixed = jnp.einsum("sd,hd->sh", grad_attended, w_out, preferred_element_type=jnp.float32)
    grad_w_out = jnp.einsum(
        "sh,sd->hd", mixed_low, grad_attended, preferred_element_type=jnp.float32
    )
    pulled = mixer_pullback(grad_mixed)
    grad_projected = [pulled[index].astype(jnp.bfloat16) for index in range(5)]
    grad_mixer_weights = [
        jnp.einsum("sd,sh->dh", normed_full, grad_part, preferred_element_type=jnp.float32)
        for grad_part in grad_projected
    ]
    summed = jnp.zeros((row_count * lax.axis_size("tensor"), normed.shape[1]), jnp.float32)
    for grad_part, weight in zip(grad_projected, mixer_weights):
        summed = summed + jnp.einsum(
            "sh,dh->sd", grad_part, weight, preferred_element_type=jnp.float32
        )
    grad_normed = lax.psum_scatter(
        summed.astype(jnp.bfloat16), "tensor", scatter_dimension=0, tiled=True
    ).astype(jnp.float32)
    grad_first, grad_attn_gain = norm_back(inputs, scale_first, gain_first, grad_normed)
    grad_tokens = grad_resid + grad_first
    grad_attn_gain, grad_ffn_gain, grad_head_gain = lax.psum(
        (grad_attn_gain, grad_ffn_gain, pulled[8]), ("dp", "tensor")
    )
    mixer_grads = (
        grad_mixer_weights[0],
        grad_mixer_weights[1],
        grad_mixer_weights[2],
        pulled[5],
        pulled[6],
        pulled[7],
        grad_mixer_weights[3],
        grad_mixer_weights[4],
        grad_w_out,
    )
    summed_all = (
        lax.psum(mixer_grads[0].astype(jnp.bfloat16), "dp").astype(jnp.float32),
        lax.psum(mixer_grads[1].astype(jnp.bfloat16), "dp").astype(jnp.float32),
        lax.psum(mixer_grads[2].astype(jnp.bfloat16), "dp").astype(jnp.float32),
        lax.psum(mixer_grads[3].astype(jnp.bfloat16), "dp").astype(jnp.float32),
        lax.psum(mixer_grads[4].astype(jnp.bfloat16), "dp").astype(jnp.float32),
        lax.psum(mixer_grads[5].astype(jnp.bfloat16), "dp").astype(jnp.float32),
        lax.psum(mixer_grads[6].astype(jnp.bfloat16), "dp").astype(jnp.float32),
        lax.psum(mixer_grads[7].astype(jnp.bfloat16), "dp").astype(jnp.float32),
        lax.psum(mixer_grads[8].astype(jnp.bfloat16), "dp").astype(jnp.float32),
        lax.psum(grad_w_gate.astype(jnp.bfloat16), "dp").astype(jnp.float32),
        lax.psum(grad_w_up.astype(jnp.bfloat16), "dp").astype(jnp.float32),
        lax.psum(grad_w_down.astype(jnp.bfloat16), "dp").astype(jnp.float32),
    )
    mixer_grads = summed_all[:9]
    grad_w_gate, grad_w_up, grad_w_down = (summed_all[9], summed_all[10], summed_all[11])
    return (
        output.astype(jnp.bfloat16),
        grad_tokens,
        grad_attn_gain,
        mixer_grads[0],
        mixer_grads[1],
        mixer_grads[2],
        mixer_grads[3],
        mixer_grads[4],
        mixer_grads[5],
        mixer_grads[6],
        mixer_grads[7],
        grad_head_gain,
        mixer_grads[8],
        grad_ffn_gain,
        grad_w_gate,
        grad_w_up,
        grad_w_down,
    )


def solution(mesh):
    placed = (
        P(("dp", "tensor"), None),
        P(),
        P(None, "tensor"),
        P(None, "tensor"),
        P(None, "tensor"),
        P(None, "tensor"),
        P(None, "tensor"),
        P(None, "tensor"),
        P(None, "tensor"),
        P(None, "tensor"),
        P(),
        P("tensor", None),
        P(),
        P(None, "tensor"),
        P(None, "tensor"),
        P("tensor", None),
        P("dp", None),
        P("dp", None),
        P(("dp", "tensor"), None),
    )
    return jax.shard_map(
        shards,
        mesh=mesh,
        in_specs=placed,
        out_specs=(
            P(("dp", "tensor"), None),
            P(("dp", "tensor"), None),
            P(),
            P(None, "tensor"),
            P(None, "tensor"),
            P(None, "tensor"),
            P(None, "tensor"),
            P(None, "tensor"),
            P(None, "tensor"),
            P(None, "tensor"),
            P(None, "tensor"),
            P(),
            P("tensor", None),
            P(),
            P(None, "tensor"),
            P(None, "tensor"),
            P("tensor", None),
        ),
        check_vma=False,
    )
```

profile of v0, /device:TPU:0, one launch (start us, length us, event | category | flops | bytes accessed | tf_op | source)
XLA Modules:
  0.0 2470.4 jit_solution(2814759676212930123)
XLA Ops:
  21.9 118.7 %all-gather.5.cloned.1.call-done = bf16[2048,2048]{1,0:T(8,128)(2,1)} async-done(((bf16[256,2048]{1,0:T(8,128)(2,1)}), bf16[2048,2048]{1,0:T(8,128)(2,1)}) %all-gather.5.cloned.1.call-update) | async-done | bytes 8388624 | tf_op jit(solution)/shard_map/all_gather | solution.py:196
  140.6 5.7 fusion.50
  147.0 7.3 fusion.140
  157.4 6.0 fusion.137
  171.2 6.1 fusion.138
  177.3 6.5 fusion.135
  184.0 6.3 multiply_reduce_fusion.16
  215.5 5.6 copy.314
  224.4 9.4 multiply_bitcast_fusion
  233.7 134.0 %custom-call.14 = f32[2,32,1,64,64]{1,3,4,2,0:T(8,128)} custom-call(f32[2,32,1,64,64]{1,4,3,2,0:T(8,128)} %get-tuple-element.855), custom_call_target="InvertDiagBlocksLowerTriangular" | custom-call | tf_op jit(solution)/shard_map/jvp(vmap())/triangular_solve/custom-call.1 | solution.py:74
  367.7 5.6 copy.318
  389.4 235.3 %while.40 = (s32[]{:T(128)}, f32[2,128,128]{2,1,0:T(8,128)S(1)}, f32[32,2,64,128]{3,2,0,1:T(8,128)}, f32[32,2,128,128]{3,2,1,0:T(8,128)}, f32[32]{0:T(128)S(1)},...) while((s32[]{:T(128)}, f32[2,128,128]{2,1,0:T(8,128)S(1)}, ...), condition=%wide.region_5.7_spmd.clone, body=%wide.region_4.6_spmd.clone.sunk | while | flops 88358912 | bytes 1512373 | solution.py:108
  632.4 7.3 convolution_convert_fusion.1
  640.4 146.7 %reduce-scatter.5.cloned.1.call-done = bf16[256,2048]{1,0:T(8,128)(2,1)} async-done(((bf16[2048,2048]{1,0:T(8,128)(2,1)}), bf16[256,2048]{1,0:T(8,128)(2,1)}) %reduce-scatter.5.cloned.1.call-update) | async-done | bytes 1048592 | tf_op jit(solution)/shard_map/reduce_scatter | solution.py:241
  791.4 123.5 %all-gather.7.cloned.1.call-done = bf16[2048,2048]{1,0:T(8,128)(2,1)} async-done(((bf16[256,2048]{1,0:T(8,128)(2,1)}), bf16[2048,2048]{1,0:T(8,128)(2,1)}) %all-gather.7.cloned.1.call-update) | async-done | bytes 8388624 | tf_op jit(solution)/shard_map/all_gather | solution.py:251
  914.9 11.4 fusion.142
  926.2 8.0 fusion.141
  934.2 106.0 %all-gather.9.cloned.1.call-done = bf16[2048,2048]{1,0:T(8,128)(2,1)} async-done(((bf16[256,2048]{1,0:T(8,128)(2,1)}), bf16[2048,2048]{1,0:T(8,128)(2,1)}) %all-gather.9.cloned.1.call-update) | async-done | bytes 8388624 | tf_op jit(solution)/shard_map/all_gather | solution.py:263
  1040.2 14.7 multiply_convert_fusion
  1054.9 10.7 fusion.143
  1065.6 12.5 add_convert_fusion.1
  1078.2 147.3 %reduce-scatter.9.cloned.1.call-done = bf16[256,2048]{1,0:T(8,128)(2,1)} async-done(((bf16[2048,2048]{1,0:T(8,128)(2,1)}), bf16[256,2048]{1,0:T(8,128)(2,1)}) %reduce-scatter.9.cloned.1.call-update) | async-done | bytes 1048592 | tf_op jit(solution)/shard_map/reduce_scatter | solution.py:272
  1245.1 10.7 convolution_convert_fusion.2
  1255.9 11.0 convolution_convert_fusion.3
  1266.9 7.5 convolution_convert_fusion.4
  1274.4 82.0 %all-gather.11.cloned.1.call-done = bf16[2048,2048]{1,0:T(8,128)(2,1)} async-done(((bf16[256,2048]{1,0:T(8,128)(2,1)}), bf16[2048,2048]{1,0:T(8,128)(2,1)}) %all-gather.11.cloned.1.call-update) | async-done | bytes 8388624 | tf_op jit(solution)/shard_map/all_gather | solution.py:283
  1356.4 7.4 fusion.144
  1382.8 377.5 %while.41 = (s32[]{:T(128)}, f32[2,128,128]{2,1,0:T(8,128)S(1)}, f32[32,2,64,128]{3,2,0,1:T(8,128)}, f32[32,2,64,128]{3,2,0,1:T(8,128)}, f32[32,2,64,128]{3,2,1,...) while((s32[]{:T(128)}, f32[2,128,128]{2,1,0:T(8,128)S(1)}, ...), condition=%wide.region_14.16_spmd.clone, body=%wide.region_13.15_spmd.clone.sunk | while | flops 201637888 | bytes 3902479 | solution.py:108
  1760.4 5.8 fusion.92
  1784.0 5.6 copy.359
  1789.6 5.6 copy.354
  1795.2 8.1 broadcast_multiply_fusion
  1824.4 10.2 fusion.79
  1849.6 8.3 multiply_reduce_fusion.9
  1861.7 6.9 multiply_reduce_fusion.4
  1885.6 7.4 convolution_convert_fusion.5
  1909.0 9.0 fusion.133
  1918.0 8.2 fusion.150
  1926.2 8.2 fusion.151
  1934.4 8.3 fusion.145
  1942.7 26.4 %add_convert_fusion = bf16[2048,2048]{1,0:T(8,128)(2,1)} fusion(f32[2048,2048]{1,0:T(8,128)} %fusion.133, f32[2048,2048]{1,0:T(8,128)} %fusion.151, f32[2048,2048]{1,0:T(8,128)} %fusion.145, f32[2048,2048]{1,0:T(8,128)} %fusion.150, bf16[2048,256]{0,1:T(8,128)(2,1)S(1)} %bitcast.470, bf16[2048,256]{1,0:T(8,128)(2,1)S(1)} %copy-done.58), kind=kOutput, calls=%fused_computation.70 | convolution fusion | flops 2168455168 | bytes 77594624 | tf_op jit(solution)/shard_map/sh,dh->sd/dot_general | solution.py:296
  1969.4 10.9 convolution_convert_fusion
  1985.1 12.4 all-reduce.33
  1999.9 151.3 %all-reduce.37.cloned.1.call-done = (bf16[2048,256]{1,0:T(8,128)(2,1)}, bf16[2048,256]{1,0:T(8,128)(2,1)}, bf16[2048,256]{1,0:T(8,128)(2,1)}, bf16[2048,256]{1,0...) async-done(((bf16[2048,256]{1,0:T(8,128)(2,1)}, bf16[2048,256]{1,0:T(8,128)(2,1)}, ...) | async-done | bytes 13893648 | tf_op jit(solution)/shard_map/psum | solution.py:319
  2171.1 133.0 %reduce-scatter.11.cloned.1.call-done = bf16[256,2048]{1,0:T(8,128)(2,1)} async-done(((bf16[2048,2048]{1,0:T(8,128)(2,1)}), bf16[256,2048]{1,0:T(8,128)(2,1)}) %reduce-scatter.11.cloned.1.call-update) | async-done | bytes 1048592 | tf_op jit(solution)/shard_map/reduce_scatter | solution.py:299
  2306.3 43.1 %all-reduce.32 = (f32[2048]{0:T(1024)}, f32[128]{0:T(128)}, f32[2048]{0:T(1024)}) all-reduce(f32[2048]{0:T(1024)S(1)} %get-tuple-element.718, f32[128]{0:T(128)S(1)} %copy-done.130, f32[2048]{0:T(1024)S(1)} %copy-done.95), channel_id=1, replica_groups=mesh['dp'=4,'tensor'=8] {'dp','tensor'}, use_global_device_ids=true, to_apply=%region_23.27 | all-reduce | flops 4224 | bytes 33792 | tf_op jit(solution)/shard_map/psum | solution.py:304
  2349.5 107.7 %reduce-scatter.7.cloned.1.call-done = bf16[256,2048]{1,0:T(8,128)(2,1)} async-done(((bf16[2048,2048]{1,0:T(8,128)(2,1)}), bf16[256,2048]{1,0:T(8,128)(2,1)}) %reduce-scatter.7.cloned.1.call-update) | async-done | bytes 1048592 | tf_op jit(solution)/shard_map/reduce_scatter | solution.py:257
  2457.2 6.4 fusion.55
  (1215 shorter events, 851.1 us)
Async XLA Ops:
  7.2 1033.0 %copy-start = (bf16[704,2048]{1,0:T(8,128)(2,1)S(1)}, bf16[704,2048]{1,0:T(8,128)(2,1)}, u32[]{:S(2)}) copy-start(bf16[704,2048]{1,0:T(8,128)(2,1)} %param.44) | copy-start | bytes 8650756
  7.2 133.3 %all-gather.5.cloned.1.call-start = ((), (), s32[]{:S(2)}) async-start(), calls=%async_computation.4 | async-start | bytes 9437184 | tf_op jit(solution)/shard_map/all_gather | solution.py:196
  12.8 774.3 %reduce-scatter.5.cloned.1.call-start = ((), (), s32[]{:S(2)}) async-start(), calls=%async_computation.5 | async-start | bytes 9437184 | tf_op jit(solution)/shard_map/reduce_scatter | solution.py:241
  13.2 127.4 %copy-start.93 = (bf16[2048,2]{0,1:T(2,128)(2,1)S(1)}, bf16[2048,2]{0,1:T(2,128)(2,1)}, u32[]{:S(2)}) copy-start(bf16[2048,2]{0,1:T(2,128)(2,1)} %param.37) | copy-start | bytes 24580
  19.5 204.8 %copy-start.69 = (f32[64,64]{1,0:T(8,128)}, f32[64,64]{1,0:T(8,128)S(1)}, u32[]{:S(2)}) copy-start(f32[64,64]{1,0:T(8,128)S(1)} %fusion.110) | copy-start | bytes 49156
  19.5 204.8 %copy-start.73 = (f32[64,64]{1,0:T(8,128)}, f32[64,64]{1,0:T(8,128)S(1)}, u32[]{:S(2)}) copy-start(f32[64,64]{1,0:T(8,128)S(1)} %fusion.109) | copy-start | bytes 49156
  20.0 163.9 %copy-start.102 = (f32[1,256]{1,0:T(1,128)}, f32[1,256]{1,0:T(1,128)S(1)}, u32[]{:S(2)}) copy-start(f32[1,256]{1,0:T(1,128)S(1)} %get-tuple-element.879) | copy-start | bytes 3076
  20.0 163.9 %copy-start.106 = (f32[1,256]{1,0:T(1,128)}, f32[1,256]{1,0:T(1,128)S(1)}, u32[]{:S(2)}) copy-start(f32[1,256]{1,0:T(1,128)S(1)} %get-tuple-element.881) | copy-start | bytes 3076
  20.0 163.9 %copy-start.108 = (f32[1,256]{1,0:T(1,128)}, f32[1,256]{1,0:T(1,128)S(1)}, u32[]{:S(2)}) copy-start(f32[1,256]{1,0:T(1,128)S(1)} %get-tuple-element.880) | copy-start | bytes 3076
  20.0 163.9 %copy-start.120 = (f32[1,256]{1,0:T(1,128)}, f32[1,256]{1,0:T(1,128)S(1)}, u32[]{:S(2)}) copy-start(f32[1,256]{1,0:T(1,128)S(1)} %get-tuple-element.882) | copy-start | bytes 3076
  20.0 163.8 %copy-start.104 = (f32[1,256]{1,0:T(1,128)}, f32[1,256]{1,0:T(1,128)S(1)}, u32[]{:S(2)}) copy-start(f32[1,256]{1,0:T(1,128)S(1)} %get-tuple-element.887) | copy-start | bytes 3076
  20.1 163.8 %copy-start.112 = (f32[1,256]{1,0:T(1,128)}, f32[1,256]{1,0:T(1,128)S(1)}, u32[]{:S(2)}) copy-start(f32[1,256]{1,0:T(1,128)S(1)} %get-tuple-element.889) | copy-start | bytes 3076
  20.1 163.8 %copy-start.114 = (f32[1,256]{1,0:T(1,128)}, f32[1,256]{1,0:T(1,128)S(1)}, u32[]{:S(2)}) copy-start(f32[1,256]{1,0:T(1,128)S(1)} %get-tuple-element.888) | copy-start | bytes 3076
  20.1 163.8 %copy-start.124 = (f32[1,256]{1,0:T(1,128)}, f32[1,256]{1,0:T(1,128)S(1)}, u32[]{:S(2)}) copy-start(f32[1,256]{1,0:T(1,128)S(1)} %get-tuple-element.890) | copy-start | bytes 3076
  20.1 143.4 %copy-start.110 = (f32[1,256]{1,0:T(1,128)}, f32[1,256]{1,0:T(1,128)S(1)}, u32[]{:S(2)}) copy-start(f32[1,256]{1,0:T(1,128)S(1)} %get-tuple-element.883) | copy-start | bytes 3076
  20.1 143.4 %copy-start.116 = (f32[1,256]{1,0:T(1,128)}, f32[1,256]{1,0:T(1,128)S(1)}, u32[]{:S(2)}) copy-start(f32[1,256]{1,0:T(1,128)S(1)} %get-tuple-element.884) | copy-start | bytes 3076
  20.1 143.4 %copy-start.118 = (f32[1,256]{1,0:T(1,128)}, f32[1,256]{1,0:T(1,128)S(1)}, u32[]{:S(2)}) copy-start(f32[1,256]{1,0:T(1,128)S(1)} %get-tuple-element.885) | copy-start | bytes 3076
  20.1 143.4 %copy-start.122 = (f32[1,256]{1,0:T(1,128)}, f32[1,256]{1,0:T(1,128)S(1)}, u32[]{:S(2)}) copy-start(f32[1,256]{1,0:T(1,128)S(1)} %get-tuple-element.886) | copy-start | bytes 3076
  20.2 204.1 %copy-start.91 = (pred[64,64]{1,0:T(8,128)(4,1)}, pred[64,64]{1,0:T(8,128)(4,1)S(1)}, u32[]{:S(2)}) copy-start(pred[64,64]{1,0:T(8,128)(4,1)S(1)} %iota_compare_fusion.1) | copy-start | bytes 12292
  21.0 162.9 %copy-start.85 = (f32[2048]{0:T(1024)}, f32[2048]{0:T(1024)S(1)}, u32[]{:S(2)}) copy-start(f32[2048]{0:T(1024)S(1)} %get-tuple-element.876) | copy-start | bytes 24580
  21.0 162.9 %copy-start.87 = (f32[2048]{0:T(1024)}, f32[2048]{0:T(1024)S(1)}, u32[]{:S(2)}) copy-start(f32[2048]{0:T(1024)S(1)} %get-tuple-element.878) | copy-start | bytes 24580
  21.1 162.9 %copy-start.89 = (f32[2048]{0:T(1024)}, f32[2048]{0:T(1024)S(1)}, u32[]{:S(2)}) copy-start(f32[2048]{0:T(1024)S(1)} %get-tuple-element.877) | copy-start | bytes 24580
  146.9 230.8 %copy-start.56 = (f32[2,32,64]{2,1,0:T(8,128)}, f32[2,32,64]{2,1,0:T(8,128)S(1)}, u32[]{:S(2)}) copy-start(f32[2,32,64]{2,1,0:T(8,128)S(1)} %mul.1002) | copy-start | bytes 49156
  147.0 77.3 %copy-start.67 = (f32[2,32,64]{1,2,0:T(8,128)}, f32[2,32,64]{1,2,0:T(8,128)S(1)}, u32[]{:S(2)}) copy-start(f32[2,32,64]{1,2,0:T(8,128)S(1)} %copy.312) | copy-start | bytes 49156
  639.8 275.1 %all-gather.7.cloned.1.call-start = ((), (), s32[]{:S(2)}) async-start(), calls=%async_computation.6 | async-start | bytes 9437184 | tf_op jit(solution)/shard_map/all_gather | solution.py:251
  640.4 588.5 %copy-start.75 = (f32[2048]{0:T(1024)}, f32[2048]{0:T(1024)S(1)}, u32[]{:S(2)}) copy-start(f32[2048]{0:T(1024)S(1)} %convert_element_type.274) | copy-start | bytes 24580
  789.3 439.6 %copy-start.96 = (f32[256]{0:T(256)}, f32[256]{0:T(256)S(1)}, u32[]{:S(2)}) copy-start(f32[256]{0:T(256)S(1)} %add_rsqrt_fusion.2) | copy-start | bytes 3076
  790.8 249.4 %all-gather.9.cloned.1.call-start = ((), (), s32[]{:S(2)}) async-start(), calls=%async_computation.8 | async-start | bytes 9437184 | tf_op jit(solution)/shard_map/all_gather | solution.py:263
  791.4 434.2 %reduce-scatter.9.cloned.1.call-start = ((), (), s32[]{:S(2)}) async-start(), calls=%async_computation.9 | async-start | bytes 9437184 | tf_op jit(solution)/shard_map/reduce_scatter | solution.py:272
  914.9 11.4 copy-start.132
  914.9 11.4 copy-start.133
  1040.2 14.7 copy-start.134
  1078.2 278.2 %all-gather.11.cloned.1.call-start = ((), (), s32[]{:S(2)}) async-start(), calls=%async_computation.10 | async-start | bytes 9437184 | tf_op jit(solution)/shard_map/all_gather | solution.py:283
  1232.3 918.9 %all-reduce.37.cloned.1.call-start = ((), (), s32[]{:S(2)}) async-start(), calls=%async_computation.12 | async-start | bytes 27787264 | tf_op jit(solution)/shard_map/psum | solution.py:319
  1245.1 21.7 slice-start.2
  1824.4 16.1 copy-start.80
  1824.4 16.1 copy-start.82
  1884.0 16.9 copy-start.49
  1885.6 19.0 copy-start.51
  1908.3 395.8 %reduce-scatter.11.cloned.1.call-start = ((), (), s32[]{:S(2)}) async-start(), calls=%async_computation.11 | async-start | bytes 9437184 | tf_op jit(solution)/shard_map/reduce_scatter | solution.py:299
  1969.1 488.0 %reduce-scatter.7.cloned.1.call-start = ((), (), s32[]{:S(2)}) async-start(), calls=%async_computation.7 | async-start | bytes 9437184 | tf_op jit(solution)/shard_map/reduce_scatter | solution.py:257
  2167.8 136.3 %copy-start.84 = (f32[2048]{0:T(1024)S(1)}, f32[2048]{0:T(1024)}, u32[]{:S(2)}) copy-start(f32[2048]{0:T(1024)} %copy-done.83) | copy-start | bytes 24580
  2167.8 136.3 %copy-start.99 = (f32[256]{0:T(256)S(1)}, f32[256]{0:T(256)}, u32[]{:S(2)}) copy-start(f32[256]{0:T(256)} %copy-done.98) | copy-start | bytes 3076
  2171.1 135.2 %copy-start.95 = (f32[2048]{0:T(1024)S(1)}, f32[2048]{0:T(1024)}, u32[]{:S(2)}) copy-start(f32[2048]{0:T(1024)} %get-tuple-element.716) | copy-start | bytes 24580
  2171.1 135.2 %copy-start.130 = (f32[128]{0:T(128)S(1)}, f32[128]{0:T(128)}, u32[]{:S(2)}) copy-start(f32[128]{0:T(128)} %get-tuple-element.714) | copy-start | bytes 1540
  2171.1 286.1 %copy-start.76 = (f32[2048]{0:T(1024)S(1)}, f32[2048]{0:T(1024)}, u32[]{:S(2)}) copy-start(f32[2048]{0:T(1024)} %copy-done.75) | copy-start | bytes 24580
  2171.1 286.1 %copy-start.97 = (f32[256]{0:T(256)S(1)}, f32[256]{0:T(256)}, u32[]{:S(2)}) copy-start(f32[256]{0:T(256)} %copy-done.96) | copy-start | bytes 3076
  2171.1 286.1 %copy-start.101 = (f32[256]{0:T(256)S(1)}, f32[256]{0:T(256)}, u32[]{:S(2)}) copy-start(f32[256]{0:T(256)} %copy-done.100) | copy-start | bytes 3076
  (107 other events, 451.7 us)
Sparse Core Ops, SparseCore 0:
  12.9 127.6 all-gather.4
  639.9 147.1 reduce-scatter.4
  790.9 123.9 all-gather.6
  917.1 123.1 all-gather.8
  1078.3 147.2 reduce-scatter.8
  1232.4 123.9 all-gather.10
  1908.4 242.8 all-reduce.36
  2154.9 149.1 reduce-scatter.10
  2308.2 148.9 reduce-scatter.6
where the time goes:
time: 2490 us; the launch traced here: 2470 us
  waiting for transfers between devices  1120 us (45%)
  matrix products  695 us (28%)
  local copies, waits for them, and re-layouts  292 us (12%)
  other arithmetic  292 us (12%)
  blocking collectives  55.6 us (2%)
    psum x1, waiting for transfers between devices, shards(): lax.psum(mixer_grads[0].astype(jnp.bfloat16), 'dp').astype(jnp.float32)  151 us
    reduce_scatter x1, waiting for transfers between devices, shards(): lax.psum_scatter((jnp.einsum('sf,df->sd', grad_gate, w_gate, preferred_el...  147 us
    reduce_scatter x1, waiting for transfers between devices, shards(): lax.psum_scatter(jnp.dot(mixed_low, w_out, preferred_element_type=jnp.flo...  147 us
    squeeze x192, local copies, waits for them, and re-layouts, delta_rule(): lax.scan(jax.checkpoint(advance), start_memory, (query_blocks, key_blocks...  141 us
    another operation x4, other arithmetic, delta_rule(): lax.linalg.triangular_solve(system, beta_blocks[:, :, None] * value_block...  134 us
    reduce_scatter x1, waiting for transfers between devices, shards(): lax.psum_scatter(summed.astype(jnp.bfloat16), 'tensor', scatter_dimension...  133 us
    all_gather x1, waiting for transfers between devices, shards(): ffn_full = lax.all_gather(ffn_in, 'tensor', axis=0, tiled=True)  123 us
    all_gather x1, waiting for transfers between devices, shards(): normed_full = lax.all_gather(normed, 'tensor', axis=0, tiled=True)  119 us
  transfers between devices with their start and end apart: 9, of which 9 were waited for; matrix products, arithmetic and copies ran while one was open for 7% of the time, Pallas kernels for 0%

commit v1 on v0

v1 whole, which is shorter than its diff:
```python
import functools
import jax
import jax.numpy as jnp
from jax import lax
from jax.experimental import pallas as pl
from jax.experimental.pallas import tpu as pltpu
from jax.sharding import PartitionSpec as P

CHUNK = 256
F32, BF16 = jnp.float32, jnp.bfloat16


def mm(a, b, contract=(1, 0)):
    return lax.dot_general(
        a.astype(BF16),
        b.astype(BF16),
        (((contract[0],), (contract[1],)), ((), ())),
        preferred_element_type=F32,
    )


def segment_at(places, starts, lengths, seqs):
    segment = jnp.zeros_like(places)
    for s in range(seqs):
        begin = starts[0, s]
        stop = begin + lengths[0, s]
        segment = segment + jnp.where(places >= begin, 1, 0) + jnp.where(places >= stop, 1, 0)
    return jnp.where(places < 0, -1, segment)


def chunk_masks(starts, lengths, seqs, first, size):
    rows = first + lax.broadcasted_iota(jnp.int32, (size, 1), 0)
    columns = first + lax.broadcasted_iota(jnp.int32, (1, size), 1)
    seg_rows = segment_at(rows, starts, lengths, seqs)
    seg_columns = segment_at(columns, starts, lengths, seqs)
    before = segment_at(jnp.full((1, 1), first - 1, jnp.int32), starts, lengths, seqs)
    last = segment_at(jnp.full((1, 1), first + size - 1, jnp.int32), starts, lengths, seqs)
    return rows, seg_rows, seg_columns, before, last


def inverse_unit_lower(lower, size):
    i = lax.broadcasted_iota(jnp.int32, (size, size), 0)
    j = lax.broadcasted_iota(jnp.int32, (size, size), 1)

    def corner(width):
        shift = width.bit_length() - 1
        pair = (i >> (shift + 1)) == (j >> (shift + 1))
        return pair & (((i >> shift) & 1) == 1) & (((j >> shift) & 1) == 0)

    inverse = jnp.where(i == j, 1.0, 0.0) - jnp.where(corner(1), lower, 0.0)
    width = 2
    while width < size:
        low = inverse.astype(BF16)
        if 2 * width == size:
            part = mm(mm(low[width:, width:], lower[width:, :width]), low[:width, :width])
            inverse = jnp.concatenate(
                [
                    inverse[:width],
                    jnp.concatenate([-part, inverse[width:, width:]], axis=1),
                ],
                axis=0,
            )
        else:
            between = jnp.where(corner(width), lower, 0.0)
            inverse = inverse - mm(mm(low, between), low)
        width *= 2
    return inverse


def sigmoid(v):
    return 1.0 / (1.0 + jnp.exp(-v))


def forward_kernel(
    heads, width, seqs,
    starts, lengths, normed, w_query, w_key, w_value, w_gate, w_beta,
    taps_query, taps_key, taps_value, gain,
    mixed, p_query, p_key, p_value, p_gate, p_beta, z_query, z_key, z_value,
    delta_out, change_out, inverse_out, state_out,
    tail_query, tail_key, tail_value, state,
):
    step = pl.program_id(0)
    size = normed.shape[0]
    first = step * size

    @pl.when(step == 0)
    def _():
        for tail in (tail_query, tail_key, tail_value):
            tail[...] = jnp.zeros_like(tail)
        state[...] = jnp.zeros_like(state)

    rows, seg_rows, seg_columns, before, last = chunk_masks(starts, lengths, seqs, first, size)
    same = seg_rows == seg_columns
    i = lax.broadcasted_iota(jnp.int32, (size, size), 0)
    j = lax.broadcasted_iota(jnp.int32, (size, size), 1)
    strict = jnp.where(same & (i > j), 1.0, 0.0)
    inclusive = jnp.where(same & (i >= j), 1.0, 0.0)
    carried = jnp.where(seg_rows == before, 1.0, 0.0)
    ending = jnp.where(seg_rows == last, 1.0, 0.0)
    kept = jnp.where(before == last, 1.0, 0.0)
    live = jnp.where(seg_rows % 2 == 1, 1.0, 0.0)
    joined = [
        jnp.where(segment_at(rows - offset, starts, lengths, seqs) == seg_rows, 1.0, 0.0)
        for offset in range(1, taps_query.shape[0])
    ]
    inputs = normed[...]

    def feature(weight, taps, tail, p_out, z_out):
        projected = jnp.dot(inputs, weight[...], preferred_element_type=F32)
        p_out[...] = projected
        tail[8:, :] = projected
        tap = taps[...].astype(F32)
        result = projected * tap[0:1]
        for offset in range(1, tap.shape[0]):
            result = result + tail[8 - offset : 8 - offset + size, :] * tap[offset : offset + 1] * joined[offset - 1]
        tail[0:8, :] = projected[size - 8 :, :]
        z_out[...] = result
        return result * sigmoid(result)

    u_query = feature(w_query, taps_query, tail_query, p_query, z_query)
    u_key = feature(w_key, taps_key, tail_key, p_key, z_key)
    u_value = feature(w_value, taps_value, tail_value, p_value, z_value)
    gate = jnp.dot(inputs, w_gate[...], preferred_element_type=F32)
    p_gate[...] = gate
    beta_pre = jnp.dot(inputs, w_beta[...], preferred_element_type=F32)
    p_beta[...] = beta_pre
    strength = sigmoid(beta_pre)
    opened = gate * sigmoid(gate)
    scale = width ** (-0.5)
    head_gain = gain[...].astype(F32)
    for h in range(heads):
        cols = slice(h * width, (h + 1) * width)
        uq, uk = u_query[:, cols], u_key[:, cols]
        query = (uq * lax.rsqrt(jnp.sum(uq * uq, axis=1, keepdims=True) + 1e-6)).astype(BF16)
        key = (uk * lax.rsqrt(jnp.sum(uk * uk, axis=1, keepdims=True) + 1e-6)).astype(BF16)
        value = u_value[:, cols].astype(BF16).astype(F32)
        beta = strength[:, h : h + 1]
        memory = state[h]
        low_memory = memory.astype(BF16)
        state_out[0, h] = low_memory
        lower = mm(key, key, (1, 1)) * strict * beta
        inverse = inverse_unit_lower(lower, size).astype(BF16)
        inverse_out[0, h] = inverse
        within = mm(query, key, (1, 1)) * inclusive
        change = mm(inverse, beta * (value - carried * mm(key, low_memory)))
        low_change = change.astype(BF16)
        change_out[:, cols] = low_change
        out = scale * (carried * mm(query, low_memory) + mm(within, low_change))
        state[h] = kept * memory + mm(key, ending * change, (0, 0))
        delta_out[:, cols] = out
        normal = out * lax.rsqrt(jnp.mean(out * out, axis=1, keepdims=True) + 1e-5) * head_gain
        mixed[:, cols] = (normal * opened[:, cols] * live).astype(BF16)


def forward_mixer(normed, w_query, w_key, w_value, w_gate, w_beta, taps_query, taps_key, taps_value, gain, starts, lengths):
    slots, model = normed.shape
    wide = w_query.shape[1]
    width = gain.shape[0]
    heads = wide // width
    seqs = starts.shape[1]
    chunks = slots // CHUNK
    taps = taps_query.shape[0]
    smem = pl.BlockSpec(memory_space=pltpu.SMEM)
    whole = lambda shape: pl.BlockSpec(shape, lambda n: (0,) * len(shape))
    piece = lambda shape: pl.BlockSpec(shape, lambda n: (n,) + (0,) * (len(shape) - 1))
    outs = [
        ((slots, wide), BF16), ((slots, wide), F32), ((slots, wide), F32), ((slots, wide), F32), ((slots, wide), F32),
        ((slots, heads), F32), ((slots, wide), F32), ((slots, wide), F32), ((slots, wide), F32),
        ((slots, wide), F32), ((slots, wide), BF16),
    ]
    return pl.pallas_call(
        functools.partial(forward_kernel, heads, width, seqs),
        name="mixer_forward",
        grid=(chunks,),
        out_shape=[jax.ShapeDtypeStruct(s, d) for s, d in outs]
        + [
            jax.ShapeDtypeStruct((chunks, heads, CHUNK, CHUNK), BF16),
            jax.ShapeDtypeStruct((chunks, heads, width, width), BF16),
        ],
        in_specs=[smem, smem, piece((CHUNK, model))]
        + [whole((model, wide))] * 4
        + [whole((model, heads))]
        + [whole((taps, wide))] * 3
        + [whole((1, width))],
        out_specs=[piece((CHUNK, s[1])) for s, d in outs]
        + [piece((1, heads, CHUNK, CHUNK)), piece((1, heads, width, width))],
        scratch_shapes=[pltpu.VMEM((CHUNK + 8, wide), F32)] * 3 + [pltpu.VMEM((heads, width, width), F32)],
        compiler_params=pltpu.CompilerParams(vmem_limit_bytes=56 << 20),
        cost_estimate=pl.CostEstimate(
            flops=2 * slots * model * wide * 4 + slots * heads * CHUNK * 2 * CHUNK * 20,
            bytes_accessed=slots * model * 2 + 4 * model * wide * 2 + slots * wide * 36,
            transcendentals=slots * wide * 4,
        ),
    )(starts, lengths, normed, w_query, w_key, w_value, w_gate, w_beta, taps_query, taps_key, taps_value, gain.reshape(1, width))


def backward_kernel(
    heads, width, seqs, chunks,
    starts, lengths, normed, grad_attended, mixed, p_query, p_key, p_value, p_gate, p_beta,
    z_query, z_key, z_value, delta_out, change_in, inverse_in, state_in,
    w_query, w_key, w_value, w_gate, w_beta, w_out, taps_query, taps_key, taps_value, gain,
    grad_normed, gw_query, gw_key, gw_value, gw_gate, gw_beta, gw_out,
    gt_query, gt_key, gt_value, g_gain,
    a_query, a_key, a_value, a_gate, a_beta, a_out, head_query, head_key, head_value, flow,
):
    step = pl.program_id(0)
    size = normed.shape[0]
    first = (chunks - 1 - step) * size

    @pl.when(step == 0)
    def _():
        for ref in (a_query, a_key, a_value, a_gate, a_beta, a_out, gt_query, gt_key, gt_value, g_gain, flow):
            ref[...] = jnp.zeros_like(ref)
        for ref in (head_query, head_key, head_value):
            ref[size:, :] = jnp.zeros((8, ref.shape[1]), F32)

    rows, seg_rows, seg_columns, before, last = chunk_masks(starts, lengths, seqs, first, size)
    same = seg_rows == seg_columns
    i = lax.broadcasted_iota(jnp.int32, (size, size), 0)
    j = lax.broadcasted_iota(jnp.int32, (size, size), 1)
    strict = jnp.where(same & (i > j), 1.0, 0.0)
    inclusive = jnp.where(same & (i >= j), 1.0, 0.0)
    carried = jnp.where(seg_rows == before, 1.0, 0.0)
    ending = jnp.where(seg_rows == last, 1.0, 0.0)
    kept = jnp.where(before == last, 1.0, 0.0)
    live = jnp.where(seg_rows % 2 == 1, 1.0, 0.0)
    taps = taps_query.shape[0]
    joined = [
        jnp.where(segment_at(rows + offset, starts, lengths, seqs) == seg_rows, 1.0, 0.0)
        for offset in range(1, taps)
    ]
    inputs = normed[...]
    grad_rows = grad_attended[...]
    grad_mixed = mm(grad_rows, w_out[...], (1, 1))
    a_out[...] += mm(mixed[...], grad_rows, (0, 0))
    strength = sigmoid(p_beta[...])
    scale = width ** (-0.5)
    head_gain = gain[...].astype(F32)

    grads_query, grads_key, grads_value, grads_gate, grads_beta = [], [], [], [], []
    for h in range(heads):
        cols = slice(h * width, (h + 1) * width)
        out = delta_out[:, cols]
        gate = p_gate[:, cols]
        sig_gate = sigmoid(gate)
        silu_gate = gate * sig_gate
        root = lax.rsqrt(jnp.mean(out * out, axis=1, keepdims=True) + 1e-5)
        grad = grad_mixed[:, cols] * live
        unit = out * root
        grads_gate.append(grad * unit * head_gain * (sig_gate * (1.0 + gate * (1.0 - sig_gate))))
        grad_normal = grad * silu_gate
        g_gain[...] += jnp.sum(grad_normal * unit, axis=0, keepdims=True)
        push = grad_normal * head_gain
        grad_out = scale * root * (push - unit * jnp.mean(push * unit, axis=1, keepdims=True))

        zq, zk, zv = z_query[:, cols], z_key[:, cols], z_value[:, cols]
        sq, sk, sv = sigmoid(zq), sigmoid(zk), sigmoid(zv)
        uq, uk = zq * sq, zk * sk
        nq = lax.rsqrt(jnp.sum(uq * uq, axis=1, keepdims=True) + 1e-6)
        nk = lax.rsqrt(jnp.sum(uk * uk, axis=1, keepdims=True) + 1e-6)
        unit_q, unit_k = uq * nq, uk * nk
        query, key = unit_q.astype(BF16), unit_k.astype(BF16)
        beta = strength[:, h : h + 1]
        change = change_in[:, cols]
        inverse = inverse_in[0, h]
        memory = state_in[0, h]
        flowing = flow[h]
        low_flow = flowing.astype(BF16)
        low_out = grad_out.astype(BF16)

        within = mm(query, key, (1, 1)) * inclusive
        grad_within = (mm(low_out, change, (1, 1)) * inclusive).astype(BF16)
        grad_change = mm(within, low_out, (0, 0)) + ending * mm(key, low_flow)
        grad_mid = mm(inverse, grad_change, (0, 0))
        grad_value = beta * grad_mid
        low_value = grad_value.astype(BF16)
        cross = (mm(low_value, change, (1, 1)) * strict).astype(BF16)
        grad_query = carried * mm(low_out, memory, (1, 1)) + mm(grad_within, key)
        grad_key = (
            mm(grad_within, query, (0, 0))
            + ending * mm(change, low_flow, (1, 1))
            - carried * mm(low_value, memory, (1, 1))
            - mm(cross, key)
            - mm(cross, key, (0, 0))
        )
        flow[h] = (
            kept * flowing
            + mm(query, carried * grad_out, (0, 0))
            - mm(key, carried * grad_value, (0, 0))
        )
        grads_beta.append((1.0 - beta) * jnp.sum(grad_mid * change.astype(F32), axis=1, keepdims=True))
        du_q = nq * (grad_query - unit_q * jnp.sum(grad_query * unit_q, axis=1, keepdims=True))
        du_k = nk * (grad_key - unit_k * jnp.sum(grad_key * unit_k, axis=1, keepdims=True))
        grads_query.append(du_q * sq * (1.0 + zq * (1.0 - sq)))
        grads_key.append(du_k * sk * (1.0 + zk * (1.0 - sk)))
        grads_value.append(grad_value * sv * (1.0 + zv * (1.0 - sv)))

    def unconv(parts, taps_ref, head, projected, grad_taps):
        grad = jnp.concatenate(parts, axis=1)
        head[0:size, :] = grad
        tap = taps_ref[...].astype(F32)
        p = projected[...]
        result = grad * tap[0:1]
        grad_taps[0:1, :] += jnp.sum(p * grad, axis=0, keepdims=True)
        for offset in range(1, taps):
            moved = head[offset : offset + size, :] * joined[offset - 1]
            result = result + moved * tap[offset : offset + 1]
            grad_taps[offset : offset + 1, :] += jnp.sum(p * moved, axis=0, keepdims=True)
        head[size:, :] = grad[0:8, :]
        return result.astype(BF16)

    d_query = unconv(grads_query, taps_query, head_query, p_query, gt_query)
    d_key = unconv(grads_key, taps_key, head_key, p_key, gt_key)
    d_value = unconv(grads_value, taps_value, head_value, p_value, gt_value)
    d_gate = jnp.concatenate(grads_gate, axis=1).astype(BF16)
    d_beta = jnp.concatenate(grads_beta, axis=1).astype(BF16)
    grad_normed[...] = (
        mm(d_query, w_query[...], (1, 1))
        + mm(d_key, w_key[...], (1, 1))
        + mm(d_value, w_value[...], (1, 1))
        + mm(d_gate, w_gate[...], (1, 1))
        + mm(d_beta, w_beta[...], (1, 1))
    ).astype(BF16)
    a_query[...] += mm(inputs, d_query, (0, 0))
    a_key[...] += mm(inputs, d_key, (0, 0))
    a_value[...] += mm(inputs, d_value, (0, 0))
    a_gate[...] += mm(inputs, d_gate, (0, 0))
    a_beta[...] += mm(inputs, d_beta, (0, 0))

    @pl.when(step == chunks - 1)
    def _():
        for target, source in (
            (gw_query, a_query), (gw_key, a_key), (gw_value, a_value), (gw_gate, a_gate),
            (gw_beta, a_beta), (gw_out, a_out),
        ):
            target[...] = source[...].astype(target.dtype)


def backward_mixer(normed, grad_attended, saved, w_query, w_key, w_value, w_gate, w_beta, w_out, taps_query, taps_key, taps_value, gain, starts, lengths):
    slots, model = normed.shape
    wide = w_query.shape[1]
    width = gain.shape[0]
    heads = wide // width
    seqs = starts.shape[1]
    chunks = slots // CHUNK
    taps = taps_query.shape[0]
    smem = pl.BlockSpec(memory_space=pltpu.SMEM)
    whole = lambda shape: pl.BlockSpec(shape, lambda n: (0,) * len(shape))
    fixed = lambda shape: pl.BlockSpec(shape, lambda n: (0,) * len(shape), pipeline_mode=pl.Buffered(1))
    piece = lambda shape: pl.BlockSpec(shape, lambda n: (chunks - 1 - n,) + (0,) * (len(shape) - 1))
    rows = lambda a: piece((CHUNK, a.shape[1]))
    outs = (
        [((slots, model), BF16)] + [((model, wide), BF16)] * 4 + [((model, heads), BF16), ((wide, model), BF16)]
        + [((taps, wide), F32)] * 3 + [((1, width), F32)]
    )
    return pl.pallas_call(
        functools.partial(backward_kernel, heads, width, seqs, chunks),
        name="mixer_backward",
        grid=(chunks,),
        out_shape=[jax.ShapeDtypeStruct(s, d) for s, d in outs],
        in_specs=[smem, smem, rows(normed), rows(grad_attended)]
        + [rows(a) for a in saved[:11]]
        + [piece((1, heads, CHUNK, CHUNK)), piece((1, heads, width, width))]
        + [fixed((model, wide))] * 4
        + [fixed((model, heads)), fixed((wide, model))]
        + [fixed((taps, wide))] * 3
        + [fixed((1, width))],
        out_specs=[piece((CHUNK, model))] + [whole(s) for s, d in outs[1:]],
        scratch_shapes=[pltpu.VMEM((model, wide), F32)] * 4
        + [pltpu.VMEM((model, heads), F32), pltpu.VMEM((wide, model), F32)]
        + [pltpu.VMEM((CHUNK + 8, wide), F32)] * 3
        + [pltpu.VMEM((heads, width, width), F32)],
        compiler_params=pltpu.CompilerParams(vmem_limit_bytes=60 << 20),
        cost_estimate=pl.CostEstimate(
            flops=2 * slots * model * wide * 10 + slots * heads * CHUNK * 2 * CHUNK * 8,
            bytes_accessed=slots * model * 6 + 10 * model * wide * 2 + slots * wide * 36,
            transcendentals=slots * wide * 8,
        ),
    )(starts, lengths, normed, grad_attended, *saved, w_query, w_key, w_value, w_gate, w_beta, w_out, taps_query, taps_key, taps_value, gain.reshape(1, width))


def norm_back(inputs, scale, gain, grad_normed):
    weighted_grad = gain * grad_normed
    inner = jnp.mean(weighted_grad * inputs, axis=1, keepdims=True)
    grad_inputs = scale * weighted_grad - inputs * scale * scale * scale * inner
    grad_gain = jnp.sum(grad_normed * inputs * scale, axis=0)
    return (grad_inputs, grad_gain)


def shards(
    tokens,
    attn_gain,
    w_query,
    w_key,
    w_value,
    conv_query,
    conv_key,
    conv_value,
    w_beta,
    w_gate_out,
    head_gain,
    w_out,
    ffn_gain,
    w_gate,
    w_up,
    w_down,
    seq_starts,
    seq_lengths,
    cotangent,
):
    inputs = tokens.astype(jnp.float32)
    gain_first = attn_gain.astype(jnp.float32)
    scale_first = lax.rsqrt(jnp.mean(inputs * inputs, axis=1, keepdims=True) + 1e-06)
    normed = (inputs * scale_first * gain_first).astype(jnp.bfloat16)
    normed_full = lax.all_gather(normed, "tensor", axis=0, tiled=True)
    saved = forward_mixer(
        normed_full, w_query, w_key, w_value, w_gate_out, w_beta,
        conv_query, conv_key, conv_value, head_gain, seq_starts, seq_lengths,
    )
    mixed_low = saved[0]
    attended = lax.psum_scatter(
        jnp.dot(mixed_low, w_out, preferred_element_type=jnp.float32).astype(jnp.bfloat16),
        "tensor",
        scatter_dimension=0,
        tiled=True,
    ).astype(jnp.float32)
    resid = inputs + attended
    gain_second = ffn_gain.astype(jnp.float32)
    scale_second = lax.rsqrt(jnp.mean(resid * resid, axis=1, keepdims=True) + 1e-06)
    ffn_in = (resid * scale_second * gain_second).astype(jnp.bfloat16)
    ffn_full = lax.all_gather(ffn_in, "tensor", axis=0, tiled=True)
    gate_pre = jnp.dot(ffn_full, w_gate, preferred_element_type=jnp.float32)
    up_pre = jnp.dot(ffn_full, w_up, preferred_element_type=jnp.float32)
    sigmoid_gate = jax.nn.sigmoid(gate_pre)
    silu_gate = gate_pre * sigmoid_gate
    hidden = (silu_gate * up_pre).astype(jnp.bfloat16)
    output = resid + lax.psum_scatter(
        jnp.dot(hidden, w_down, preferred_element_type=jnp.float32).astype(jnp.bfloat16),
        "tensor",
        scatter_dimension=0,
        tiled=True,
    ).astype(jnp.float32)
    grad_full = lax.all_gather(cotangent, "tensor", axis=0, tiled=True)
    grad_hidden = jnp.einsum("sd,fd->sf", grad_full, w_down, preferred_element_type=jnp.float32)
    grad_w_down = jnp.einsum("sf,sd->fd", hidden, grad_full, preferred_element_type=jnp.float32)
    grad_gate = (
        grad_hidden * up_pre * sigmoid_gate * (1.0 + gate_pre * (1.0 - sigmoid_gate))
    ).astype(jnp.bfloat16)
    grad_up = (grad_hidden * silu_gate).astype(jnp.bfloat16)
    grad_w_gate = jnp.einsum("sd,sf->df", ffn_full, grad_gate, preferred_element_type=jnp.float32)
    grad_w_up = jnp.einsum("sd,sf->df", ffn_full, grad_up, preferred_element_type=jnp.float32)
    grad_ffn_in = lax.psum_scatter(
        (
            jnp.einsum("sf,df->sd", grad_gate, w_gate, preferred_element_type=jnp.float32)
            + jnp.einsum("sf,df->sd", grad_up, w_up, preferred_element_type=jnp.float32)
        ).astype(jnp.bfloat16),
        "tensor",
        scatter_dimension=0,
        tiled=True,
    ).astype(jnp.float32)
    grad_through, grad_ffn_gain = norm_back(resid, scale_second, gain_second, grad_ffn_in)
    grad_resid = cotangent.astype(jnp.float32) + grad_through
    grad_attended = lax.all_gather(grad_resid.astype(jnp.bfloat16), "tensor", axis=0, tiled=True)
    pulled = backward_mixer(
        normed_full, grad_attended, saved, w_query, w_key, w_value, w_gate_out, w_beta, w_out,
        conv_query, conv_key, conv_value, head_gain, seq_starts, seq_lengths,
    )
    grad_normed = lax.psum_scatter(
        pulled[0], "tensor", scatter_dimension=0, tiled=True
    ).astype(jnp.float32)
    grad_first, grad_attn_gain = norm_back(inputs, scale_first, gain_first, grad_normed)
    grad_tokens = grad_resid + grad_first
    grad_attn_gain, grad_ffn_gain, grad_head_gain = lax.psum(
        (grad_attn_gain, grad_ffn_gain, pulled[10][0]), ("dp", "tensor")
    )
    mixer_grads = (
        pulled[1], pulled[2], pulled[3], pulled[7], pulled[8], pulled[9], pulled[5], pulled[4], pulled[6],
    )
    summed_all = (
        lax.psum(mixer_grads[0].astype(jnp.bfloat16), "dp").astype(jnp.float32),
        lax.psum(mixer_grads[1].astype(jnp.bfloat16), "dp").astype(jnp.float32),
        lax.psum(mixer_grads[2].astype(jnp.bfloat16), "dp").astype(jnp.float32),
        lax.psum(mixer_grads[3].astype(jnp.bfloat16), "dp").astype(jnp.float32),
        lax.psum(mixer_grads[4].astype(jnp.bfloat16), "dp").astype(jnp.float32),
        lax.psum(mixer_grads[5].astype(jnp.bfloat16), "dp").astype(jnp.float32),
        lax.psum(mixer_grads[6].astype(jnp.bfloat16), "dp").astype(jnp.float32),
        lax.psum(mixer_grads[7].astype(jnp.bfloat16), "dp").astype(jnp.float32),
        lax.psum(mixer_grads[8].astype(jnp.bfloat16), "dp").astype(jnp.float32),
        lax.psum(grad_w_gate.astype(jnp.bfloat16), "dp").astype(jnp.float32),
        lax.psum(grad_w_up.astype(jnp.bfloat16), "dp").astype(jnp.float32),
        lax.psum(grad_w_down.astype(jnp.bfloat16), "dp").astype(jnp.float32),
    )
    mixer_grads = summed_all[:9]
    grad_w_gate, grad_w_up, grad_w_down = (summed_all[9], summed_all[10], summed_all[11])
    return (
        output.astype(jnp.bfloat16),
        grad_tokens,
        grad_attn_gain,
        mixer_grads[0],
        mixer_grads[1],
        mixer_grads[2],
        mixer_grads[3],
        mixer_grads[4],
        mixer_grads[5],
        mixer_grads[6],
        mixer_grads[7],
        grad_head_gain,
        mixer_grads[8],
        grad_ffn_gain,
        grad_w_gate,
        grad_w_up,
        grad_w_down,
    )


def solution(mesh):
    placed = (
        P(("dp", "tensor"), None),
        P(),
        P(None, "tensor"),
        P(None, "tensor"),
        P(None, "tensor"),
        P(None, "tensor"),
        P(None, "tensor"),
        P(None, "tensor"),
        P(None, "tensor"),
        P(None, "tensor"),
        P(),
        P("tensor", None),
        P(),
        P(None, "tensor"),
        P(None, "tensor"),
        P("tensor", None),
        P("dp", None),
        P("dp", None),
        P(("dp", "tensor"), None),
    )
    return jax.shard_map(
        shards,
        mesh=mesh,
        in_specs=placed,
        out_specs=(
            P(("dp", "tensor"), None),
            P(("dp", "tensor"), None),
            P(),
            P(None, "tensor"),
            P(None, "tensor"),
            P(None, "tensor"),
            P(None, "tensor"),
            P(None, "tensor"),
            P(None, "tensor"),
            P(None, "tensor"),
            P(None, "tensor"),
            P(),
            P("tensor", None),
            P(),
            P(None, "tensor"),
            P(None, "tensor"),
            P("tensor", None),
        ),
        check_vma=False,
    )
```

time: 2490 us -> 1560 us (0.63)
  matrix products: 695 us -> 104 us
  local copies, waits for them, and re-layouts: 292 us -> 5.37 us
  other arithmetic: 292 us -> 45.2 us
  Pallas kernels: 0 us -> 116 us
  waiting for transfers between devices: 1120 us -> 1200 us
    dot_general x441 -> x0, matrix products: 569 us -> none  [the longest x96 107 us: advance(): jnp.dot(mixing, change, precision=highest)]
    squeeze x193 -> x0, local copies, waits for them, and re-layouts: 141 us -> none  [the longest x192 141 us: delta_rule(): lax.scan(jax.checkpoint(advance), start_memory, (query_blocks, key_blocks...]
    another operation x36 -> x0, other arithmetic: 134 us -> none  [the longest x4 134 us: delta_rule(): lax.linalg.triangular_solve(system, beta_blocks[:, :, None] * value_block...]
    pallas_call x0 -> x2, Pallas kernels: none -> 116 us  [the longest x1 60.3 us: backward_mixer(): pl.pallas_call(functools.partial(backward_kernel, heads, width, seqs, chu...]
    psum x1, waiting for transfers between devices: 151 us -> 208 us  [shards(): lax.psum(mixer_grads[0].astype(jnp.bfloat16), 'dp').astype(jnp.float32)]
    reduce_sum x11 -> x0, other arithmetic: 39.1 us -> none  [the longest x2 15.2 us: short_conv(): moved * taps[offset] * (earlier == segment).astype(jnp.float32)[:, None]]
    dynamic_slice x64 -> x0, local copies, waits for them, and re-layouts: 38.2 us -> none  [delta_rule(): lax.scan(jax.checkpoint(advance), start_memory, (query_blocks, key_blocks...]
    mul x16 -> x0, other arithmetic: 30.4 us -> none  [the longest x9 10.4 us: short_conv(): moved * taps[offset] * (earlier == segment).astype(jnp.float32)[:, None]]
  transfers between devices with their start and end apart: 9 -> 9, of which waited for: 9 -> 9; matrix products, arithmetic and copies ran while one was open for 7% -> 5% of each run, Pallas kernels for 0% -> 0%
where the time goes in v1:
time: 1560 us; the launch traced here: 1550 us
  waiting for transfers between devices  1200 us (77%)
  Pallas kernels  116 us (7%)
  matrix products  104 us (7%)
  blocking collectives  69.4 us (4%)
  other arithmetic  45.2 us (3%)
    psum x1, waiting for transfers between devices, shards(): lax.psum(mixer_grads[0].astype(jnp.bfloat16), 'dp').astype(jnp.float32)  208 us
    reduce_scatter x1, waiting for transfers between devices, shards(): lax.psum_scatter((jnp.einsum('sf,df->sd', grad_gate, w_gate, preferred_el...  147 us
    reduce_scatter x1, waiting for transfers between devices, shards(): lax.psum_scatter(jnp.dot(mixed_low, w_out, preferred_element_type=jnp.flo...  147 us
    reduce_scatter x1, waiting for transfers between devices, shards(): lax.psum_scatter(pulled[0], 'tensor', scatter_dimension=0, tiled=True)  134 us
    all_gather x1, waiting for transfers between devices, shards(): normed_full = lax.all_gather(normed, 'tensor', axis=0, tiled=True)  127 us
    all_gather x1, waiting for transfers between devices, shards(): ffn_full = lax.all_gather(ffn_in, 'tensor', axis=0, tiled=True)  123 us
    reduce_scatter x1, waiting for transfers between devices, shards(): lax.psum_scatter(jnp.dot(hidden, w_down, preferred_element_type=jnp.float...  109 us
    all_gather x1, waiting for transfers between devices, shards(): grad_full = lax.all_gather(cotangent, 'tensor', axis=0, tiled=True)  106 us
  transfers between devices with their start and end apart: 9, of which 9 were waited for; matrix products, arithmetic and copies ran while one was open for 5% of the time, Pallas kernels for 0%

profile of v1, /device:TPU:0, one launch (start us, length us, event | category | flops | bytes accessed | tf_op | source)
XLA Modules:
  0.0 1551.8 jit_solution(4186508286795942128)
XLA Ops:
  7.3 1.7 fusion.16
  8.9 0.7 convert_element_type.109
  9.6 0.6 copy-done.13
  10.2 2.5 fusion.6
  12.8 1.1 copy.36.w_beta
  13.9 126.7 %all-gather.5.cloned.1.call-done.normed = bf16[2048,2048]{1,0:T(8,128)(2,1)} async-done(((bf16[256,2048]{1,0:T(8,128)(2,1)}), bf16[2048,2048]{1,0:T(8,128)(2,1)}) %all-gather.5.cloned.1.call-update) | async-done | bytes 8388624 | tf_op jit(solution)/shard_map/all_gather | solution.py:415
  140.6 56.1 %mixer_forward.1 = (bf16[2048,256]{1,0:T(8,128)(2,1)}, f32[2048,256]{1,0:T(8,128)}, f32[2048,256]{1,0:T(8,128)}, f32[2048,256]{1,0:T(8,128)}, f32[2048,256]{1,0:...) custom-call(s32[1,2]{1,0:T(1,128)} %starts.3, ...), custom_call_target="tpu_custom_call" | custom-call | flops 19327352832 | bytes 31457280 | tf_op jit(solution)/shard_map/mixer_forward/pallas_call | solution.py:171
  196.7 6.9 convolution_convert_fusion.1
  203.6 0.6 copy-done.18
  204.2 146.7 %reduce-scatter.5.cloned.1.call-done = bf16[256,2048]{1,0:T(8,128)(2,1)} async-done(((bf16[2048,2048]{1,0:T(8,128)(2,1)}), bf16[256,2048]{1,0:T(8,128)(2,1)}) %reduce-scatter.5.cloned.1.call-update) | async-done | bytes 1048592 | tf_op jit(solution)/shard_map/reduce_scatter | solution.py:421
  350.9 2.0 multiply_reduce_fusion
  352.9 2.9 multiply_convert_fusion.3
  356.7 123.2 %all-gather.7.cloned.1.call-done = bf16[2048,2048]{1,0:T(8,128)(2,1)} async-done(((bf16[256,2048]{1,0:T(8,128)(2,1)}), bf16[2048,2048]{1,0:T(8,128)(2,1)}) %all-gather.7.cloned.1.call-update) | async-done | bytes 8388624 | tf_op jit(solution)/shard_map/all_gather | solution.py:431
  479.9 11.2 fusion.22
  491.1 8.0 fusion.21
  499.0 106.2 %all-gather.9.cloned.1.call-done = bf16[2048,2048]{1,0:T(8,128)(2,1)} async-done(((bf16[256,2048]{1,0:T(8,128)(2,1)}), bf16[2048,2048]{1,0:T(8,128)(2,1)}) %all-gather.9.cloned.1.call-update) | async-done | bytes 8388624 | tf_op jit(solution)/shard_map/all_gather | solution.py:443
  605.2 14.6 multiply_convert_fusion
  619.9 10.8 fusion.23
  630.7 12.5 add_convert_fusion
  643.3 147.3 %reduce-scatter.9.cloned.1.call-done = bf16[256,2048]{1,0:T(8,128)(2,1)} async-done(((bf16[2048,2048]{1,0:T(8,128)(2,1)}), bf16[256,2048]{1,0:T(8,128)(2,1)}) %reduce-scatter.9.cloned.1.call-update) | async-done | bytes 1048592 | tf_op jit(solution)/shard_map/reduce_scatter | solution.py:452
  790.7 2.7 fusion.15
  793.4 3.3 fusion.20
  796.9 10.8 convolution_convert_fusion.2
  807.7 10.9 convolution_convert_fusion.3
  818.7 7.4 convolution_convert_fusion.4
  826.1 94.8 %all-gather.11.cloned.1.call-done.grad_attended = bf16[2048,2048]{1,0:T(8,128)(2,1)} async-done(((bf16[256,2048]{1,0:T(8,128)(2,1)}), bf16[2048,2048]{1,0:T(8,128)(2,1)}) %all-gather.11.cloned.1.call-update) | async-done | bytes 8388624 | tf_op jit(solution)/shard_map/all_gather | solution.py:463
  920.9 60.3 %mixer_backward.1 = (bf16[2048,2048]{1,0:T(8,128)(2,1)}, bf16[2048,256]{1,0:T(8,128)(2,1)}, bf16[2048,256]{1,0:T(8,128)(2,1)}, bf16[2048,256]{1,0:T(8,128)(2,1)}...) custom-call(s32[1,2]{1,0:T(1,128)} %starts.3, ...), custom_call_target="tpu_custom_call" | custom-call | flops 25769803776 | bytes 54525952 | tf_op jit(solution)/shard_map/mixer_backward/pallas_call | solution.py:356
  981.3 0.7 reduce-scatter.11.cloned.1.call-update
  982.0 10.8 convolution_convert_fusion
  992.9 0.7 copy-done.21
  994.0 27.1 %all-reduce.1 = (bf16[2048,2]{1,0:T(8,128)(2,1)}, bf16[4,256]{1,0:T(4,128)(2,1)S(1)}, bf16[4,256]{1,0:T(4,128)(2,1)S(1)}, bf16[4,256]{1,0:T(4,128)(2,1)S(1)}) all-reduce(bf16[2048,2]{1,0:T(8,128)(2,1)S(1)} %copy-done.12, bf16[4,256]{1,0:T(4,128)(2,1)S(1)} %convert_element_type.129, ...), channel_id=1, replica_groups=mesh['dp'=4,'tensor'=8] {'dp'}, use_global_device_ids=true, to_apply=%region_16.0 | all-reduce | flops 7168 | bytes 28672 | tf_op jit(solution)/shard_map/psum | solution.py:486
  1021.1 1.9 copy.38
  1022.9 0.6 convert_element_type.130
  1023.5 0.6 convert_element_type.132
  1024.7 207.9 %all-reduce.5.cloned.1.call-done = (bf16[2048,256]{1,0:T(8,128)(2,1)}, bf16[2048,256]{1,0:T(8,128)(2,1)}, bf16[2048,256]{1,0:T(8,128)(2,1)}, bf16[2048,256]{1,0:...) async-done(((bf16[2048,256]{1,0:T(8,128)(2,1)}, bf16[2048,256]{1,0:T(8,128)(2,1)}, ...) | async-done | bytes 13893648 | tf_op jit(solution)/shard_map/psum | solution.py:480
  1232.6 2.9 convert_element_type.126
  1235.5 1.5 convert_element_type.127
  1237.0 1.5 convert_element_type.128
  1238.4 1.5 convert_element_type.136
  1239.9 1.6 convert_element_type.137
  1241.5 3.5 convert_element_type.139
  1245.0 3.3 convert_element_type.141
  1248.3 3.3 convert_element_type.143
  1251.6 133.8 %reduce-scatter.11.cloned.1.call-done = bf16[256,2048]{1,0:T(8,128)(2,1)} async-done(((bf16[2048,2048]{1,0:T(8,128)(2,1)}), bf16[256,2048]{1,0:T(8,128)(2,1)}) %reduce-scatter.11.cloned.1.call-update) | async-done | bytes 1048592 | tf_op jit(solution)/shard_map/reduce_scatter | solution.py:468
  1385.5 2.2 fusion.19
  1387.7 42.3 %all-reduce = (f32[2048]{0:T(1024)}, f32[128]{0:T(128)}, f32[2048]{0:T(1024)}) all-reduce(f32[2048]{0:T(1024)S(1)} %get-tuple-element.84, f32[128]{0:T(128)S(1)} %bitcast.22, f32[2048]{0:T(1024)S(1)} %get-tuple-element.82), channel_id=1, replica_groups=mesh['dp'=4,'tensor'=8] {'dp','tensor'}, use_global_device_ids=true, to_apply=%region_9.0 | all-reduce | flops 4224 | bytes 33792 | tf_op jit(solution)/shard_map/psum | solution.py:473
  1430.0 108.6 %reduce-scatter.7.cloned.1.call-done = bf16[256,2048]{1,0:T(8,128)(2,1)} async-done(((bf16[2048,2048]{1,0:T(8,128)(2,1)}), bf16[256,2048]{1,0:T(8,128)(2,1)}) %reduce-scatter.7.cloned.1.call-update) | async-done | bytes 1048592 | tf_op jit(solution)/shard_map/reduce_scatter | solution.py:437
  1538.6 6.4 fusion.10
  (90 shorter events, 2.5 us)
Async XLA Ops:
  7.2 598.1 %copy-start = (bf16[704,2048]{1,0:T(8,128)(2,1)S(1)}, bf16[704,2048]{1,0:T(8,128)(2,1)}, u32[]{:S(2)}) copy-start(bf16[704,2048]{1,0:T(8,128)(2,1)} %param.34) | copy-start | bytes 8650756
  7.2 5.6 copy-start.17
  7.2 133.3 %all-gather.5.cloned.1.call-start = ((), (), s32[]{:S(2)}) async-start(), calls=%async_computation.4 | async-start | bytes 9437184 | tf_op jit(solution)/shard_map/all_gather | solution.py:415
  8.9 0.7 copy-start.15
  9.6 0.6 copy-start.13
  12.8 338.1 %reduce-scatter.5.cloned.1.call-start = ((), (), s32[]{:S(2)}) async-start(), calls=%async_computation.5 | async-start | bytes 9437184 | tf_op jit(solution)/shard_map/reduce_scatter | solution.py:421
  140.6 56.1 %copy-start.11 = (bf16[256,2048]{1,0:T(8,128)(2,1)S(1)}, bf16[256,2048]{1,0:T(8,128)(2,1)}, u32[]{:S(2)}) copy-start(bf16[256,2048]{1,0:T(8,128)(2,1)} %w_out.1) | copy-start | bytes 3145732
  203.5 0.7 copy-start.18
  203.6 276.3 %all-gather.7.cloned.1.call-start = ((), (), s32[]{:S(2)}) async-start(), calls=%async_computation.6 | async-start | bytes 9437184 | tf_op jit(solution)/shard_map/all_gather | solution.py:431
  355.8 249.4 %all-gather.9.cloned.1.call-start = ((), (), s32[]{:S(2)}) async-start(), calls=%async_computation.8 | async-start | bytes 9437184 | tf_op jit(solution)/shard_map/all_gather | solution.py:443
  356.4 434.3 %reduce-scatter.9.cloned.1.call-start = ((), (), s32[]{:S(2)}) async-start(), calls=%async_computation.9 | async-start | bytes 9437184 | tf_op jit(solution)/shard_map/reduce_scatter | solution.py:452
  479.9 11.2 copy-start.23
  479.9 11.2 copy-start.24
  605.2 14.6 copy-start.25
  619.9 10.8 copy-start.27
  619.9 10.8 copy-start.29
  619.9 10.8 copy-start.26
  643.3 277.6 %all-gather.11.cloned.1.call-start = ((), (), s32[]{:S(2)}) async-start(), calls=%async_computation.10 | async-start | bytes 9437184 | tf_op jit(solution)/shard_map/all_gather | solution.py:463
  790.6 2.8 copy-start.1
  790.6 2.8 copy-start.2
  790.6 2.8 copy-start.3
  796.8 435.8 %all-reduce.5.cloned.1.call-start = ((), (), s32[]{:S(2)}) async-start(), calls=%async_computation.12 | async-start | bytes 27787264 | tf_op jit(solution)/shard_map/psum | solution.py:480
  796.9 10.9 copy-start.28
  796.9 21.8 %slice-start = ((s8[8388608]{0:T(1024)(128)(4,1)}), s8[4194304]{0:T(1024)(128)(4,1)S(1)}, s32[]{:S(2)}) async-start(s8[8388608]{0:T(1024)(128)(4,1)} %bitcast.23), calls=%async_computation.13 | async-start | bytes 8388608
  807.7 11.0 slice-start.1
  807.7 11.0 copy-start.30
  981.2 404.2 %reduce-scatter.11.cloned.1.call-start = ((), (), s32[]{:S(2)}) async-start(), calls=%async_computation.11 | async-start | bytes 9437184 | tf_op jit(solution)/shard_map/reduce_scatter | solution.py:468
  982.0 556.6 %reduce-scatter.7.cloned.1.call-start = ((), (), s32[]{:S(2)}) async-start(), calls=%async_computation.7 | async-start | bytes 9437184 | tf_op jit(solution)/shard_map/reduce_scatter | solution.py:437
  992.9 0.7 copy-start.21
  992.9 0.7 copy-start.20
  992.9 0.7 copy-start.19
  992.9 1.1 copy-start.12
  1232.6 2.9 copy-start.10
  1232.6 4.3 copy-start.9
  1235.5 3.0 copy-start.8
  1237.0 3.0 copy-start.7
  1238.4 3.0 copy-start.6
  1241.5 3.5 copy-start.5
  1245.0 3.3 copy-start.4
  1248.3 137.1 %copy-start.14 = (f32[2048]{0:T(1024)S(1)}, f32[2048]{0:T(1024)}, u32[]{:S(2)}) copy-start(f32[2048]{0:T(1024)} %copy-done.13) | copy-start | bytes 24580
  1248.3 137.1 %copy-start.16 = (f32[256]{0:T(256)S(1)}, f32[256]{0:T(256)}, u32[]{:S(2)}) copy-start(f32[256]{0:T(256)} %copy-done.15) | copy-start | bytes 3076
  1248.3 139.3 %copy-start.22 = (f32[1,128]{1,0:T(1,128)S(1)}, f32[1,128]{1,0:T(1,128)}, u32[]{:S(2)}) copy-start(f32[1,128]{1,0:T(1,128)} %get-tuple-element.63) | copy-start | bytes 1540
Sparse Core Ops, SparseCore 0:
  12.9 127.6 all-gather.4
  203.7 147.1 reduce-scatter.4
  355.9 123.9 all-gather.6
  482.1 123.1 all-gather.8
  643.4 147.1 reduce-scatter.8
  796.9 123.9 all-gather.10
  981.4 251.2 all-reduce.4
  1236.2 149.1 reduce-scatter.10
  1389.5 148.9 reduce-scatter.6

commit v2 on v1

--- a/solution.py
+++ b/solution.py
@@ -71,16 +71,22 @@
     return 1.0 / (1.0 + jnp.exp(-v))
 
 
+def normed_rows(tokens, gain):
+    value = tokens[...].astype(F32)
+    unit = value * lax.rsqrt(jnp.mean(value * value, axis=1, keepdims=True) + 1e-6)
+    return unit * gain[...].astype(F32), unit
+
+
 def forward_kernel(
     heads, width, seqs,
-    starts, lengths, normed, w_query, w_key, w_value, w_gate, w_beta,
-    taps_query, taps_key, taps_value, gain,
+    starts, lengths, tokens, w_query, w_key, w_value, w_gate, w_beta,
+    taps_query, taps_key, taps_value, gain, gain_first,
     mixed, p_query, p_key, p_value, p_gate, p_beta, z_query, z_key, z_value,
     delta_out, change_out, inverse_out, state_out,
     tail_query, tail_key, tail_value, state,
 ):
     step = pl.program_id(0)
-    size = normed.shape[0]
+    size = tokens.shape[0]
     first = step * size
 
     @pl.when(step == 0)
@@ -103,7 +109,7 @@
         jnp.where(segment_at(rows - offset, starts, lengths, seqs) == seg_rows, 1.0, 0.0)
         for offset in range(1, taps_query.shape[0])
     ]
-    inputs = normed[...]
+    inputs = normed_rows(tokens, gain_first)[0].astype(BF16)
 
     def feature(weight, taps, tail, p_out, z_out):
         projected = jnp.dot(inputs, weight[...], preferred_element_type=F32)
@@ -152,8 +158,8 @@
         mixed[:, cols] = (normal * opened[:, cols] * live).astype(BF16)
 
 
-def forward_mixer(normed, w_query, w_key, w_value, w_gate, w_beta, taps_query, taps_key, taps_value, gain, starts, lengths):
-    slots, model = normed.shape
+def forward_mixer(tokens, w_query, w_key, w_value, w_gate, w_beta, taps_query, taps_key, taps_value, gain, gain_first, starts, lengths):
+    slots, model = tokens.shape
     wide = w_query.shape[1]
     width = gain.shape[0]
     heads = wide // width
@@ -181,7 +187,7 @@
         + [whole((model, wide))] * 4
         + [whole((model, heads))]
         + [whole((taps, wide))] * 3
-        + [whole((1, width))],
+        + [whole((1, width)), whole((1, model))],
         out_specs=[piece((CHUNK, s[1])) for s, d in outs]
         + [piece((1, heads, CHUNK, CHUNK)), piece((1, heads, width, width))],
         scratch_shapes=[pltpu.VMEM((CHUNK + 8, wide), F32)] * 3 + [pltpu.VMEM((heads, width, width), F32)],
@@ -191,25 +197,25 @@
             bytes_accessed=slots * model * 2 + 4 * model * wide * 2 + slots * wide * 36,
             transcendentals=slots * wide * 4,
         ),
-    )(starts, lengths, normed, w_query, w_key, w_value, w_gate, w_beta, taps_query, taps_key, taps_value, gain.reshape(1, width))
+    )(starts, lengths, tokens, w_query, w_key, w_value, w_gate, w_beta, taps_query, taps_key, taps_value, gain.reshape(1, width), gain_first.reshape(1, model))
 
 
 def backward_kernel(
     heads, width, seqs, chunks,
-    starts, lengths, normed, grad_attended, mixed, p_query, p_key, p_value, p_gate, p_beta,
+    starts, lengths, tokens, grad_attended, mixed, p_query, p_key, p_value, p_gate, p_beta,
     z_query, z_key, z_value, delta_out, change_in, inverse_in, state_in,
-    w_query, w_key, w_value, w_gate, w_beta, w_out, taps_query, taps_key, taps_value, gain,
+    w_query, w_key, w_value, w_gate, w_beta, w_out, taps_query, taps_key, taps_value, gain, gain_first,
     grad_normed, gw_query, gw_key, gw_value, gw_gate, gw_beta, gw_out,
-    gt_query, gt_key, gt_value, g_gain,
-    a_query, a_key, a_value, a_gate, a_beta, a_out, head_query, head_key, head_value, flow,
+    gt_query, gt_key, gt_value, g_gain, g_first,
+    a_query, a_key, a_value, a_gate, a_out, head_query, head_key, head_value, flow,
 ):
     step = pl.program_id(0)
-    size = normed.shape[0]
+    size = tokens.shape[0]
     first = (chunks - 1 - step) * size
 
     @pl.when(step == 0)
     def _():
-        for ref in (a_query, a_key, a_value, a_gate, a_beta, a_out, gt_query, gt_key, gt_value, g_gain, flow):
+        for ref in (a_query, a_key, a_value, a_gate, gw_beta, a_out, gt_query, gt_key, gt_value, g_gain, g_first, flow):
             ref[...] = jnp.zeros_like(ref)
         for ref in (head_query, head_key, head_value):
             ref[size:, :] = jnp.zeros((8, ref.shape[1]), F32)
@@ -229,7 +235,8 @@
         jnp.where(segment_at(rows + offset, starts, lengths, seqs) == seg_rows, 1.0, 0.0)
         for offset in range(1, taps)
     ]
-    inputs = normed[...]
+    normal_rows, unit_rows = normed_rows(tokens, gain_first)
+    inputs = normal_rows.astype(BF16)
     grad_rows = grad_attended[...]
     grad_mixed = mm(grad_rows, w_out[...], (1, 1))
     a_out[...] += mm(mixed[...], grad_rows, (0, 0))
@@ -314,30 +321,32 @@
     d_value = unconv(grads_value, taps_value, head_value, p_value, gt_value)
     d_gate = jnp.concatenate(grads_gate, axis=1).astype(BF16)
     d_beta = jnp.concatenate(grads_beta, axis=1).astype(BF16)
-    grad_normed[...] = (
+    grad_inputs = (
         mm(d_query, w_query[...], (1, 1))
         + mm(d_key, w_key[...], (1, 1))
         + mm(d_value, w_value[...], (1, 1))
         + mm(d_gate, w_gate[...], (1, 1))
         + mm(d_beta, w_beta[...], (1, 1))
-    ).astype(BF16)
+    )
+    grad_normed[...] = grad_inputs.astype(BF16)
+    g_first[...] += jnp.sum(grad_inputs * unit_rows, axis=0, keepdims=True)
     a_query[...] += mm(inputs, d_query, (0, 0))
     a_key[...] += mm(inputs, d_key, (0, 0))
     a_value[...] += mm(inputs, d_value, (0, 0))
     a_gate[...] += mm(inputs, d_gate, (0, 0))
-    a_beta[...] += mm(inputs, d_beta, (0, 0))
+    gw_beta[...] += mm(d_beta, inputs, (0, 0))
 
     @pl.when(step == chunks - 1)
     def _():
         for target, source in (
             (gw_query, a_query), (gw_key, a_key), (gw_value, a_value), (gw_gate, a_gate),
-            (gw_beta, a_beta), (gw_out, a_out),
+            (gw_out, a_out),
         ):
             target[...] = source[...].astype(target.dtype)
 
 
-def backward_mixer(normed, grad_attended, saved, w_query, w_key, w_value, w_gate, w_beta, w_out, taps_query, taps_key, taps_value, gain, starts, lengths):
-    slots, model = normed.shape
+def backward_mixer(tokens, grad_attended, saved, w_query, w_key, w_value, w_gate, w_beta, w_out, taps_query, taps_key, taps_value, gain, gain_first, starts, lengths):
+    slots, model = tokens.shape
     wide = w_query.shape[1]
     width = gain.shape[0]
     heads = wide // width
@@ -350,24 +359,24 @@
     piece = lambda shape: pl.BlockSpec(shape, lambda n: (chunks - 1 - n,) + (0,) * (len(shape) - 1))
     rows = lambda a: piece((CHUNK, a.shape[1]))
     outs = (
-        [((slots, model), BF16)] + [((model, wide), BF16)] * 4 + [((model, heads), BF16), ((wide, model), BF16)]
-        + [((taps, wide), F32)] * 3 + [((1, width), F32)]
+        [((slots, model), BF16)] + [((model, wide), BF16)] * 4 + [((heads, model), F32), ((wide, model), BF16)]
+        + [((taps, wide), F32)] * 3 + [((1, width), F32), ((1, model), F32)]
     )
     return pl.pallas_call(
         functools.partial(backward_kernel, heads, width, seqs, chunks),
         name="mixer_backward",
         grid=(chunks,),
         out_shape=[jax.ShapeDtypeStruct(s, d) for s, d in outs],
-        in_specs=[smem, smem, rows(normed), rows(grad_attended)]
+        in_specs=[smem, smem, rows(tokens), rows(grad_attended)]
         + [rows(a) for a in saved[:11]]
         + [piece((1, heads, CHUNK, CHUNK)), piece((1, heads, width, width))]
         + [fixed((model, wide))] * 4
         + [fixed((model, heads)), fixed((wide, model))]
         + [fixed((taps, wide))] * 3
-        + [fixed((1, width))],
+        + [fixed((1, width)), fixed((1, model))],
         out_specs=[piece((CHUNK, model))] + [whole(s) for s, d in outs[1:]],
         scratch_shapes=[pltpu.VMEM((model, wide), F32)] * 4
-        + [pltpu.VMEM((model, heads), F32), pltpu.VMEM((wide, model), F32)]
+        + [pltpu.VMEM((wide, model), F32)]
         + [pltpu.VMEM((CHUNK + 8, wide), F32)] * 3
         + [pltpu.VMEM((heads, width, width), F32)],
         compiler_params=pltpu.CompilerParams(vmem_limit_bytes=60 << 20),
@@ -376,141 +385,465 @@
             bytes_accessed=slots * model * 6 + 10 * model * wide * 2 + slots * wide * 36,
             transcendentals=slots * wide * 8,
         ),
-    )(starts, lengths, normed, grad_attended, *saved, w_query, w_key, w_value, w_gate, w_beta, w_out, taps_query, taps_key, taps_value, gain.reshape(1, width))
+    )(starts, lengths, tokens, grad_attended, *saved, w_query, w_key, w_value, w_gate, w_beta, w_out, taps_query, taps_key, taps_value, gain.reshape(1, width), gain_first.reshape(1, model))
+
+
+MESH = pl.DeviceIdType.MESH
+SUBS = 2
+
+
+def ring_position(device, count):
+    half, odd = device // 2, device % 2
+    return half + odd * (count - 1 - 2 * half)
+
+
+def ring_device(position, count):
+    back = position // (count // 2)
+    return (1 - back) * 2 * position + back * (2 * (count - 1 - position) + 1)
+
+
+class Ring:
+    def __init__(self, count):
+        self.count = count
+        self.me = lax.axis_index("tensor")
+        self.place = ring_position(self.me, count)
+        self.group = lax.axis_index("dp")
+
+    def at(self, offset):
+        return ring_device((self.place + offset + 2 * self.count) % self.count, self.count)
+
+    def next(self, way):
+        return (self.group, self.at(1 if way == 0 else -1))
+
+    def greet(self):
+        barrier = pltpu.get_barrier_semaphore()
+        for way in (0, 1):
+            pl.semaphore_signal(barrier, inc=1, device_id=self.next(way), device_id_type=MESH)
+        pl.semaphore_wait(barrier, 2)
+
+
+def gather_copy(ring, source, target, sends, recvs, way, sub, step, origin, rows):
+    piece = rows // (2 * SUBS)
+    inside = way * (rows // 2) + sub * piece
+    start = pl.multiple_of(origin * rows + inside, piece)
+    src = target.at[pl.ds(start, piece), :] if source is None else source.at[pl.ds(inside, piece), :]
+    return pltpu.make_async_remote_copy(
+        src_ref=src,
+        dst_ref=target.at[pl.ds(start, piece), :],
+        send_sem=sends.at[way, sub, step],
+        recv_sem=recvs.at[way, sub, step],
+        device_id=ring.next(way),
+        device_id_type=MESH,
+    )
+
+
+def ring_gather(ring, source, target, sends, recvs, local, rows):
+    count = ring.count
+    keep = pltpu.make_async_copy(
+        source, target.at[pl.ds(pl.multiple_of(ring.me * rows, rows), rows), :], local
+    )
+    keep.start()
+    pairs = [(sub, way) for sub in range(SUBS) for way in (0, 1)]
+    for sub, way in pairs:
+        gather_copy(ring, source, target, sends, recvs, way, sub, 0, ring.me, rows).start()
+
+    def origin(way, step):
+        return ring.at(-step if way == 0 else step)
+
+    def forward(step, carry):
+        for sub, way in pairs:
+            gather_copy(
+                ring, None, target, sends, recvs, way, sub, step - 1, origin(way, step), rows
+            ).wait_recv()
+            gather_copy(
+                ring, None, target, sends, recvs, way, sub, step, origin(way, step), rows
+            ).start()
+        return carry
+
+    lax.fori_loop(1, count - 1, forward, 0)
+    for sub, way in pairs:
+        gather_copy(
+            ring, None, target, sends, recvs, way, sub, count - 2, origin(way, count - 1), rows
+        ).wait_recv()
+
+    def drain(step, carry):
+        for sub, way in pairs:
+            gather_copy(ring, None, target, sends, recvs, way, sub, step, ring.me, rows).wait_send()
+        return carry
+
+    lax.fori_loop(0, count - 1, drain, 0)
+    keep.wait()
+
+
+def scatter_copy(ring, slots, sends, recvs, way, sub, step):
+    return pltpu.make_async_remote_copy(
+        src_ref=slots.at[way, sub, step],
+        dst_ref=slots.at[way, sub, step + 1],
+        send_sem=sends.at[way, sub, step],
+        recv_sem=recvs.at[way, sub, step],
+        device_id=ring.next(way),
+        device_id_type=MESH,
+    )
+
+
+def ring_scatter(ring, partial, slots, sends, recvs, rows, finish):
+    count = ring.count
+    piece = rows // (2 * SUBS)
+    pairs = [(sub, way) for sub in range(SUBS) for way in (0, 1)]
+
+    def begin(way, sub, owner):
+        return pl.multiple_of(owner * rows + way * (rows // 2) + sub * piece, piece)
+
+    def owner_at(way, step):
+        return ring.at(-1 - step if way == 0 else 1 + step)
+
+    for sub, way in pairs:
+        slots[way, sub, 0] = partial(begin(way, sub, owner_at(way, 0)), piece).astype(BF16)
+        scatter_copy(ring, slots, sends, recvs, way, sub, 0).start()
+
+    def hop(step, carry):
+        for sub, way in pairs:
+            term = partial(begin(way, sub, owner_at(way, step)), piece)
+            scatter_copy(ring, slots, sends, recvs, way, sub, step - 1).wait_recv()
+            slots[way, sub, step] = (slots[way, sub, step].astype(F32) + term).astype(BF16)
+            scatter_copy(ring, slots, sends, recvs, way, sub, step).start()
+        return carry
+
+    lax.fori_loop(1, count - 1, hop, 0)
+    for sub, way in pairs:
+        term = partial(begin(way, sub, ring.me), piece)
+        scatter_copy(ring, slots, sends, recvs, way, sub, count - 2).wait_recv()
+        finish(way * (rows // 2) + sub * piece, piece, slots[way, sub, count - 1].astype(F32) + term)
+
+    def drain(step, carry):
+        for sub, way in pairs:
+            scatter_copy(ring, slots, sends, recvs, way, sub, step).wait_send()
+        return carry
+
+    lax.fori_loop(0, count - 1, drain, 0)
+
+
+def ring_semaphores(count):
+    return [pltpu.SemaphoreType.DMA((2, SUBS, count - 1))] * 2
+
+
+def ring_slots(count, rows, columns):
+    return pltpu.VMEM((2, SUBS, count, rows // (2 * SUBS), columns), BF16)
+
+
+ANY = pl.BlockSpec(memory_space=pl.ANY)
+VMEM = pl.BlockSpec(memory_space=pltpu.VMEM)
+
+
+def ring_params(number):
+    return pltpu.CompilerParams(
+        collective_id=number, has_side_effects=True, vmem_limit_bytes=56 << 20
+    )
+
+
+def gather_kernel(count, rows, source, target, sends, recvs, local):
+    ring = Ring(count)
+    ring.greet()
+    ring_gather(ring, source, target, sends, recvs, local, rows)
+
+
+def gather_tokens(tokens, count):
+    rows, model = tokens.shape
+    return pl.pallas_call(
+        functools.partial(gather_kernel, count, rows),
+        name="gather_tokens",
+        out_shape=jax.ShapeDtypeStruct((count * rows, model), tokens.dtype),
+        in_specs=[ANY],
+        out_specs=ANY,
+        scratch_shapes=ring_semaphores(count) + [pltpu.SemaphoreType.DMA],
+        compiler_params=ring_params(1),
+        cost_estimate=pl.CostEstimate(flops=0, bytes_accessed=300 << 20, transcendentals=0),
+    )(tokens)
+
+
+def attend_kernel(
+    count, rows, mixed, w_out, tokens, gain, resid, full,
+    slots, low, sends, recvs, sends_two, recvs_two, local,
+):
+    ring = Ring(count)
+    ring.greet()
+
+    def partial(start, size):
+        return mm(mixed[pl.ds(start, size), :], w_out[...])
+
+    def finish(start, size, attended):
+        value = tokens[start : start + size, :].astype(F32) + attended
+        resid[start : start + size, :] = value
+        scale = lax.rsqrt(jnp.mean(value * value, axis=1, keepdims=True) + 1e-6)
+        low[start : start + size, :] = (value * scale * gain[...].astype(F32)).astype(BF16)
+
+    ring_scatter(ring, partial, slots, sends, recvs, rows, finish)
+    ring_gather(ring, low, full, sends_two, recvs_two, local, rows)
+
+
+def attend(mixed, w_out, tokens, gain, count):
+    rows, model = tokens.shape
+    return pl.pallas_call(
+        functools.partial(attend_kernel, count, rows),
+        name="attend",
+        out_shape=[
+            jax.ShapeDtypeStruct((rows, model), F32),
+            jax.ShapeDtypeStruct((count * rows, model), BF16),
+        ],
+        in_specs=[VMEM] * 4,
+        out_specs=[VMEM, ANY],
+        scratch_shapes=[ring_slots(count, rows, model), pltpu.VMEM((rows, model), BF16)]
+        + ring_semaphores(count) * 2
+        + [pltpu.SemaphoreType.DMA],
+        compiler_params=ring_params(2),
+        cost_estimate=pl.CostEstimate(
+            flops=2 * count * rows * model * mixed.shape[1], bytes_accessed=600 << 20, transcendentals=0
+        ),
+    )(mixed, w_out, tokens, gain.reshape(1, model))
 
 
 def norm_back(inputs, scale, gain, grad_normed):
-    weighted_grad = gain * grad_normed
-    inner = jnp.mean(weighted_grad * inputs, axis=1, keepdims=True)
-    grad_inputs = scale * weighted_grad - inputs * scale * scale * scale * inner
-    grad_gain = jnp.sum(grad_normed * inputs * scale, axis=0)
-    return (grad_inputs, grad_gain)
-
-
-def shards(
-    tokens,
-    attn_gain,
-    w_query,
-    w_key,
-    w_value,
-    conv_query,
-    conv_key,
-    conv_value,
-    w_beta,
-    w_gate_out,
-    head_gain,
-    w_out,
-    ffn_gain,
-    w_gate,
-    w_up,
-    w_down,
-    seq_starts,
-    seq_lengths,
-    cotangent,
+    weighted = gain * grad_normed
+    inner = jnp.mean(weighted * inputs, axis=1, keepdims=True)
+    unit = inputs * scale
+    return scale * weighted - unit * (scale * scale * inner), grad_normed * unit
+
+
+def ffn_back_kernel(
+    count, rows, grad_gate, grad_up, w_gate, w_up, resid, cotangent, gain, grad_resid, full, grad_gain,
+    slots, low, sends, recvs, sends_two, recvs_two, local,
 ):
-    inputs = tokens.astype(jnp.float32)
-    gain_first = attn_gain.astype(jnp.float32)
-    scale_first = lax.rsqrt(jnp.mean(inputs * inputs, axis=1, keepdims=True) + 1e-06)
-    normed = (inputs * scale_first * gain_first).astype(jnp.bfloat16)
-    normed_full = lax.all_gather(normed, "tensor", axis=0, tiled=True)
-    saved = forward_mixer(
-        normed_full, w_query, w_key, w_value, w_gate_out, w_beta,
-        conv_query, conv_key, conv_value, head_gain, seq_starts, seq_lengths,
-    )
-    mixed_low = saved[0]
-    attended = lax.psum_scatter(
-        jnp.dot(mixed_low, w_out, preferred_element_type=jnp.float32).astype(jnp.bfloat16),
-        "tensor",
-        scatter_dimension=0,
-        tiled=True,
-    ).astype(jnp.float32)
-    resid = inputs + attended
-    gain_second = ffn_gain.astype(jnp.float32)
-    scale_second = lax.rsqrt(jnp.mean(resid * resid, axis=1, keepdims=True) + 1e-06)
-    ffn_in = (resid * scale_second * gain_second).astype(jnp.bfloat16)
-    ffn_full = lax.all_gather(ffn_in, "tensor", axis=0, tiled=True)
-    gate_pre = jnp.dot(ffn_full, w_gate, preferred_element_type=jnp.float32)
-    up_pre = jnp.dot(ffn_full, w_up, preferred_element_type=jnp.float32)
-    sigmoid_gate = jax.nn.sigmoid(gate_pre)
-    silu_gate = gate_pre * sigmoid_gate
-    hidden = (silu_gate * up_pre).astype(jnp.bfloat16)
-    output = resid + lax.psum_scatter(
-        jnp.dot(hidden, w_down, preferred_element_type=jnp.float32).astype(jnp.bfloat16),
-        "tensor",
-        scatter_dimension=0,
-        tiled=True,
-    ).astype(jnp.float32)
-    grad_full = lax.all_gather(cotangent, "tensor", axis=0, tiled=True)
-    grad_hidden = jnp.einsum("sd,fd->sf", grad_full, w_down, preferred_element_type=jnp.float32)
-    grad_w_down = jnp.einsum("sf,sd->fd", hidden, grad_full, preferred_element_type=jnp.float32)
-    grad_gate = (
-        grad_hidden * up_pre * sigmoid_gate * (1.0 + gate_pre * (1.0 - sigmoid_gate))
-    ).astype(jnp.bfloat16)
-    grad_up = (grad_hidden * silu_gate).astype(jnp.bfloat16)
-    grad_w_gate = jnp.einsum("sd,sf->df", ffn_full, grad_gate, preferred_element_type=jnp.float32)
-    grad_w_up = jnp.einsum("sd,sf->df", ffn_full, grad_up, preferred_element_type=jnp.float32)
-    grad_ffn_in = lax.psum_scatter(
-        (
-            jnp.einsum("sf,df->sd", grad_gate, w_gate, preferred_element_type=jnp.float32)
-            + jnp.einsum("sf,df->sd", grad_up, w_up, preferred_element_type=jnp.float32)
-        ).astype(jnp.bfloat16),
-        "tensor",
-        scatter_dimension=0,
-        tiled=True,
-    ).astype(jnp.float32)
-    grad_through, grad_ffn_gain = norm_back(resid, scale_second, gain_second, grad_ffn_in)
-    grad_resid = cotangent.astype(jnp.float32) + grad_through
-    grad_attended = lax.all_gather(grad_resid.astype(jnp.bfloat16), "tensor", axis=0, tiled=True)
-    pulled = backward_mixer(
-        normed_full, grad_attended, saved, w_query, w_key, w_value, w_gate_out, w_beta, w_out,
-        conv_query, conv_key, conv_value, head_gain, seq_starts, seq_lengths,
-    )
-    grad_normed = lax.psum_scatter(
-        pulled[0], "tensor", scatter_dimension=0, tiled=True
-    ).astype(jnp.float32)
-    grad_first, grad_attn_gain = norm_back(inputs, scale_first, gain_first, grad_normed)
-    grad_tokens = grad_resid + grad_first
-    grad_attn_gain, grad_ffn_gain, grad_head_gain = lax.psum(
-        (grad_attn_gain, grad_ffn_gain, pulled[10][0]), ("dp", "tensor")
-    )
-    mixer_grads = (
-        pulled[1], pulled[2], pulled[3], pulled[7], pulled[8], pulled[9], pulled[5], pulled[4], pulled[6],
-    )
-    summed_all = (
-        lax.psum(mixer_grads[0].astype(jnp.bfloat16), "dp").astype(jnp.float32),
-        lax.psum(mixer_grads[1].astype(jnp.bfloat16), "dp").astype(jnp.float32),
-        lax.psum(mixer_grads[2].astype(jnp.bfloat16), "dp").astype(jnp.float32),
-        lax.psum(mixer_grads[3].astype(jnp.bfloat16), "dp").astype(jnp.float32),
-        lax.psum(mixer_grads[4].astype(jnp.bfloat16), "dp").astype(jnp.float32),
-        lax.psum(mixer_grads[5].astype(jnp.bfloat16), "dp").astype(jnp.float32),
-        lax.psum(mixer_grads[6].astype(jnp.bfloat16), "dp").astype(jnp.float32),
-        lax.psum(mixer_grads[7].astype(jnp.bfloat16), "dp").astype(jnp.float32),
-        lax.psum(mixer_grads[8].astype(jnp.bfloat16), "dp").astype(jnp.float32),
-        lax.psum(grad_w_gate.astype(jnp.bfloat16), "dp").astype(jnp.float32),
-        lax.psum(grad_w_up.astype(jnp.bfloat16), "dp").astype(jnp.float32),
-        lax.psum(grad_w_down.astype(jnp.bfloat16), "dp").astype(jnp.float32),
-    )
-    mixer_grads = summed_all[:9]
-    grad_w_gate, grad_w_up, grad_w_down = (summed_all[9], summed_all[10], summed_all[11])
-    return (
-        output.astype(jnp.bfloat16),
-        grad_tokens,
-        grad_attn_gain,
-        mixer_grads[0],
-        mixer_grads[1],
-        mixer_grads[2],
-        mixer_grads[3],
-        mixer_grads[4],
-        mixer_grads[5],
-        mixer_grads[6],
-        mixer_grads[7],
-        grad_head_gain,
-        mixer_grads[8],
-        grad_ffn_gain,
-        grad_w_gate,
-        grad_w_up,
-        grad_w_down,
-    )
+    ring = Ring(count)
+    ring.greet()
+    grad_gain[...] = jnp.zeros_like(grad_gain)
+
+    def partial(start, size):
+        return mm(grad_gate[pl.ds(start, size), :], w_gate[...], (1, 1)) + mm(
+            grad_up[pl.ds(start, size), :], w_up[...], (1, 1)
+        )
+
+    def finish(start, size, grad):
+        value = resid[start : start + size, :]
+        scale = lax.rsqrt(jnp.mean(value * value, axis=1, keepdims=True) + 1e-6)
+        through, pieces = norm_back(value, scale, gain[...].astype(F32), grad)
+        result = cotangent[start : start + size, :].astype(F32) + through
+        grad_resid[start : start + size, :] = result
+        grad_gain[...] += jnp.sum(pieces, axis=0, keepdims=True)
+        low[start : start + size, :] = result.astype(BF16)
+
+    ring_scatter(ring, partial, slots, sends, recvs, rows, finish)
+    ring_gather(ring, low, full, sends_two, recvs_two, local, rows)
+
+
+def ffn_back(grad_gate, grad_up, w_gate, w_up, resid, cotangent, gain, count):
+    rows, model = resid.shape
+    return pl.pallas_call(
+        functools.partial(ffn_back_kernel, count, rows),
+        name="ffn_back",
+        out_shape=[
+            jax.ShapeDtypeStruct((rows, model), F32),
+            jax.ShapeDtypeStruct((count * rows, model), BF16),
+            jax.ShapeDtypeStruct((1, model), F32),
+        ],
+        in_specs=[VMEM] * 7,
+        out_specs=[VMEM, ANY, VMEM],
+        scratch_shapes=[ring_slots(count, rows, model), pltpu.VMEM((rows, model), BF16)]
+        + ring_semaphores(count) * 2
+        + [pltpu.SemaphoreType.DMA],
+        compiler_params=ring_params(3),
+        cost_estimate=pl.CostEstimate(
+            flops=4 * count * rows * model * grad_up.shape[1], bytes_accessed=600 << 20, transcendentals=0
+        ),
+    )(grad_gate, grad_up, w_gate, w_up, resid, cotangent, gain.reshape(1, model))
+
+
+def last_kernel(
+    count, groups, rows, terms, tokens, grad_resid, gain, small, grad_tokens, total,
+    slots, first_box, second_box, second_own, sends, recvs, first_sends, first_recvs, second_sends, second_recvs,
+):
+    ring = Ring(count)
+    me, group = ring.me, ring.group
+    barrier = pltpu.get_barrier_semaphore()
+    first_peers = [(group, (me + k) % count) for k in range(1, count)]
+    second_peers = [((group + k) % groups, me) for k in range(1, groups)]
+    for peer in first_peers + second_peers:
+        pl.semaphore_signal(barrier, inc=1, device_id=peer, device_id_type=MESH)
+    pl.semaphore_wait(barrier, count + groups - 2)
+
+    def first(k):
+        return pltpu.make_async_remote_copy(
+            src_ref=small.at[0:8], dst_ref=first_box.at[k], send_sem=first_sends.at[k],
+            recv_sem=first_recvs.at[k], device_id=first_peers[k], device_id_type=MESH,
+        )
+
+    def second(k):
+        return pltpu.make_async_remote_copy(
+            src_ref=second_own, dst_ref=second_box.at[k], send_sem=second_sends.at[k],
+            recv_sem=second_recvs.at[k], device_id=second_peers[k], device_id_type=MESH,
+        )
+
+    for k in range(count - 1):
+        first(k).start()
+    for k in range(count - 1):
+        first(k).wait()
+    mine = small[0:8]
+    for k in range(count - 1):
+        mine = mine + first_box[k]
+    second_own[0:8] = mine
+    second_own[8:] = small[8:]
+    for k in range(groups - 1):
+        second(k).start()
+
+    def partial(start, size):
+        return terms[pl.ds(start, size), :].astype(F32)
+
+    def finish(start, size, grad):
+        value = tokens[start : start + size, :].astype(F32)
+        scale = lax.rsqrt(jnp.mean(value * value, axis=1, keepdims=True) + 1e-6)
+        through, pieces = norm_back(value, scale, gain[...].astype(F32), grad)
+        grad_tokens[start : start + size, :] = grad_resid[start : start + size, :] + through
+
+    ring_scatter(ring, partial, slots, sends, recvs, rows, finish)
+    for k in range(groups - 1):
+        second(k).wait()
+    mine = second_own[...]
+    for k in range(groups - 1):
+        mine = mine + second_box[k]
+    total[...] = mine
+
+
+def last_step(terms, tokens, grad_resid, gain, small, count, groups):
+    rows, model = tokens.shape
+    return pl.pallas_call(
+        functools.partial(last_kernel, count, groups, rows),
+        name="last_step",
+        out_shape=[jax.ShapeDtypeStruct((rows, model), F32), jax.ShapeDtypeStruct(small.shape, F32)],
+        in_specs=[VMEM] * 5,
+        out_specs=[VMEM, VMEM],
+        scratch_shapes=[
+            ring_slots(count, rows, model),
+            pltpu.VMEM((count - 1, 8, model), F32),
+            pltpu.VMEM((groups - 1,) + small.shape, F32),
+            pltpu.VMEM(small.shape, F32),
+        ]
+        + ring_semaphores(count)
+        + [pltpu.SemaphoreType.DMA((count - 1,))] * 2
+        + [pltpu.SemaphoreType.DMA((groups - 1,))] * 2,
+        compiler_params=ring_params(4),
+        cost_estimate=pl.CostEstimate(flops=0, bytes_accessed=300 << 20, transcendentals=0),
+    )(terms, tokens, grad_resid, gain.reshape(1, model), small)
+
+
+def swap(value, distance, count):
+    if distance == "core":
+        pairs = [(i, i + 1 - 2 * (i % 2)) for i in range(count)]
+    else:
+        pairs = [(i, (i + 2 * distance) % count) for i in range(count)]
+    return lax.ppermute(value, "dp", pairs)
+
+
+def sum_groups(value, count):
+    rows = value.shape[0] // 2
+    core = lax.axis_index("dp") % 2
+    here = lax.dynamic_slice_in_dim(value, core * rows, rows, 0)
+    away = lax.dynamic_slice_in_dim(value, (1 - core) * rows, rows, 0)
+    here = (here.astype(F32) + swap(away, "core", count).astype(F32)).astype(BF16)
+    total = here.astype(F32)
+    for distance in range(1, count // 2):
+        total = total + swap(here, distance, count).astype(F32)
+    here = total.astype(BF16)
+    other = swap(here, "core", count)
+    lower = jnp.where(core == 0, here, other)
+    upper = jnp.where(core == 0, other, here)
+    return jnp.concatenate([lower, upper], 0).astype(F32)
+
+
+def silu_parts(value):
+    sig = jax.nn.sigmoid(value)
+    return sig, value * sig
+
+
+def make_shards(groups, count):
+    def shards(
+        tokens, attn_gain, w_query, w_key, w_value, conv_query, conv_key, conv_value, w_beta, w_gate_out,
+        head_gain, w_out, ffn_gain, w_gate, w_up, w_down, seq_starts, seq_lengths, cotangent,
+    ):
+        model = tokens.shape[1]
+        tokens_full = gather_tokens(tokens, count)
+        late_cotangent, tokens_full = lax.optimization_barrier((cotangent, tokens_full))
+        grad_full = lax.all_gather(late_cotangent, "tensor", axis=0, tiled=True)
+        saved = forward_mixer(
+            tokens_full, w_query, w_key, w_value, w_gate_out, w_beta,
+            conv_query, conv_key, conv_value, head_gain, attn_gain, seq_starts, seq_lengths,
+        )
+        resid, ffn_full = attend(saved[0], w_out, tokens, ffn_gain, count)
+        gate_pre = jnp.dot(ffn_full, w_gate, preferred_element_type=F32)
+        up_pre = jnp.dot(ffn_full, w_up, preferred_element_type=F32)
+        sig, silu_gate = silu_parts(gate_pre)
+        hidden = (silu_gate * up_pre).astype(BF16)
+        down = jnp.dot(hidden, w_down, preferred_element_type=F32).astype(BF16)
+        grad_hidden = jnp.einsum("sd,fd->sf", grad_full, w_down, preferred_element_type=F32)
+        grad_gate = (grad_hidden * up_pre * sig * (1.0 + gate_pre * (1.0 - sig))).astype(BF16)
+        grad_up = (grad_hidden * silu_gate).astype(BF16)
+        grad_resid, grad_attended, g_second = ffn_back(
+            grad_gate, grad_up, w_gate, w_up, resid, cotangent, ffn_gain, count
+        )
+        gw_down = jnp.einsum("sf,sd->fd", hidden, grad_full, preferred_element_type=F32)
+        gw_gate = jnp.einsum("sd,sf->df", ffn_full, grad_gate, preferred_element_type=F32)
+        gw_up = jnp.einsum("sd,sf->df", ffn_full, grad_up, preferred_element_type=F32)
+        ffn_grads = [sum_groups(g.astype(BF16), groups) for g in (gw_gate, gw_up, gw_down)]
+        output = resid + lax.psum_scatter(
+            down, "tensor", scatter_dimension=0, tiled=True
+        ).astype(F32)
+        pulled = backward_mixer(
+            tokens_full, grad_attended, saved, w_query, w_key, w_value, w_gate_out, w_beta, w_out,
+            conv_query, conv_key, conv_value, head_gain, attn_gain, seq_starts, seq_lengths,
+        )
+        terms, gw_query, gw_key, gw_value, gw_gate_out, gw_beta, gw_out = pulled[:7]
+        gt_query, gt_key, gt_value, g_head, g_first = pulled[7:]
+        wide = gt_query.shape[1]
+        heads = gw_beta.shape[0]
+        taps = gt_query.shape[0]
+        small = jnp.concatenate(
+            [
+                g_first,
+                g_second,
+                jnp.pad(g_head, ((0, 0), (0, model - g_head.shape[1]))),
+                jnp.zeros((5, model), F32),
+                gw_beta,
+                jnp.pad(
+                    jnp.concatenate([gt_query, gt_key, gt_value], 1), ((0, 0), (0, model - 3 * wide))
+                ),
+                jnp.zeros((-(heads + taps) % 8, model), F32),
+            ],
+            0,
+        )
+        grad_tokens, total = last_step(terms, tokens, grad_resid, attn_gain, small, count, groups)
+        mixer_grads = [
+            sum_groups(g, groups) for g in (gw_query, gw_key, gw_value, gw_gate_out, gw_out)
+        ]
+        tap_rows = total[8 + heads : 8 + heads + taps]
+        return (
+            output.astype(BF16),
+            grad_tokens,
+            total[0],
+            mixer_grads[0],
+            mixer_grads[1],
+            mixer_grads[2],
+            tap_rows[:, :wide],
+            tap_rows[:, wide : 2 * wide],
+            tap_rows[:, 2 * wide : 3 * wide],
+            total[8 : 8 + heads].T,
+            mixer_grads[3],
+            total[2, : head_gain.shape[0]],
+            mixer_grads[4],
+            total[1],
+            ffn_grads[0],
+            ffn_grads[1],
+            ffn_grads[2],
+        )
+
+    return shards
 
 
 def solution(mesh):
@@ -536,7 +869,7 @@
         P(("dp", "tensor"), None),
     )
     return jax.shard_map(
-        shards,
+        make_shards(mesh.shape["dp"], mesh.shape["tensor"]),
         mesh=mesh,
         in_specs=placed,
         out_specs=(

time: 1560 us -> 1120 us (0.72)
  waiting for transfers between devices: 1200 us -> 137 us
  Pallas kernels: 116 us -> 806 us
  blocking collectives: 69.4 us -> 0 us
  local copies, waits for them, and re-layouts: 5.37 us -> 31.5 us
  matrix products: 104 us -> 82.1 us
    pallas_call x0 -> x4, Pallas kernels: none -> 687 us  [the longest x1 284 us: ffn_back(): pl.pallas_call(functools.partial(ffn_back_kernel, count, rows), name='ffn...]
    reduce_scatter x4 -> x1, waiting for transfers between devices: 536 us -> 0.01 us  [shards(): lax.psum_scatter(down, 'tensor', scatter_dimension=0, tiled=True)]
    all_gather x4 -> x1, waiting for transfers between devices: 451 us -> 0.01 us  [shards(): grad_full = lax.all_gather(late_cotangent, 'tensor', axis=0, tiled=True)]
    psum x1 -> x0, waiting for transfers between devices: 208 us -> none  [shards(): lax.psum(mixer_grads[0].astype(jnp.bfloat16), 'dp').astype(jnp.float32)]
    ppermute x0 -> x24, waiting for transfers between devices: none -> 137 us  [swap(): return lax.ppermute(value, 'dp', pairs)]
    psum x2 -> x0, blocking collectives: 69.4 us -> none  [the longest x1 42.3 us: shards(): lax.psum((grad_attn_gain, grad_ffn_gain, pulled[10][0]), ('dp', 'tensor'))]
    dot_general x10 -> x7, matrix products: 104 us -> 82.1 us  [the longest x1 19.3 us: shards(): jnp.einsum('sd,sf->df', ffn_full, grad_up, preferred_element_type=F32)]
  transfers between devices with their start and end apart: 9 -> 26, of which waited for: 9 -> 8; matrix products, arithmetic and copies ran while one was open for 5% -> 9% of each run, Pallas kernels for 0% -> 65%
where the time goes in v2:
time: 1120 us; the launch traced here: 1110 us
  Pallas kernels  806 us (72%)
  waiting for transfers between devices  137 us (12%)
  matrix products  82.1 us (7%)
  local copies, waits for them, and re-layouts  31.5 us (3%)
  other arithmetic  31.4 us (3%)
  between operations  14.9 us (1%)
    pallas_call x1, Pallas kernels, ffn_back(): pl.pallas_call(functools.partial(ffn_back_kernel, count, rows), name='ffn...  284 us
    pallas_call x1, Pallas kernels, attend(): pl.pallas_call(functools.partial(attend_kernel, count, rows), name='atten...  214 us
    ppermute x24, waiting for transfers between devices, swap(): return lax.ppermute(value, 'dp', pairs)  137 us
    pallas_call x1, Pallas kernels, last_step(): pl.pallas_call(functools.partial(last_kernel, count, groups, rows), name=...  104 us
    pallas_call x1, Pallas kernels, gather_tokens(): pl.pallas_call(functools.partial(gather_kernel, count, rows), name='gathe...  84.6 us
    pallas_call x1, Pallas kernels, backward_mixer(): pl.pallas_call(functools.partial(backward_kernel, heads, width, seqs, chu...  60.7 us
    pallas_call x1, Pallas kernels, forward_mixer(): pl.pallas_call(functools.partial(forward_kernel, heads, width, seqs), nam...  58 us
  transfers between devices with their start and end apart: 26, of which 8 were waited for; matrix products, arithmetic and copies ran while one was open for 9% of the time, Pallas kernels for 65%

profile of v2, /device:TPU:0, one launch (start us, length us, event | category | flops | bytes accessed | tf_op | source)
XLA Modules:
  0.0 1112.8 jit_solution(6629496000820891354)
XLA Ops:
  7.3 84.6 %gather_tokens.1.tokens = bf16[2048,2048]{1,0:T(8,128)(2,1)} custom-call(bf16[256,2048]{1,0:T(8,128)(2,1)} %tokens.3), custom_call_target="tpu_custom_call" | custom-call | bytes 314572800 | tf_op jit(solution)/shard_map/gather_tokens/pallas_call | solution.py:552
  94.3 4.6 copy.44.w_gate
  98.9 4.7 copy.45.w_up
  103.6 58.0 %mixer_forward.1 = (bf16[2048,256]{1,0:T(8,128)(2,1)}, f32[2048,256]{1,0:T(8,128)}, f32[2048,256]{1,0:T(8,128)}, f32[2048,256]{1,0:T(8,128)}, f32[2048,256]{1,0:...) custom-call(s32[1,2]{1,0:T(1,128)} %starts.3, ...), custom_call_target="tpu_custom_call" | custom-call | flops 19327352832 | bytes 31457280 | tf_op jit(solution)/shard_map/mixer_forward/pallas_call | solution.py:177
  161.6 213.7 %attend.1 = (f32[256,2048]{1,0:T(8,128)}, bf16[2048,2048]{1,0:T(8,128)(2,1)}) custom-call(bf16[2048,256]{1,0:T(8,128)(2,1)} %get-tuple-element.52.mixed, bf16[256,2048]{1,0:T(8,128)(2,1)} %w_out.3, bf16[256,2048]{1,0:T(8,128)(2,1)} %tokens.3, bf16[1,2048]{1,0:T(2,128)(2,1)} %reshape.49.gain), custom_call_target="tpu_custom_call" | custom-call | flops 2147483648 | bytes 629145600 | tf_op jit(solution)/shard_map/attend/pallas_call | solution.py:586
  375.3 10.9 fusion.3
  386.2 8.8 fusion.4
  395.0 15.7 %multiply_convert_fusion = (bf16[2048,704]{1,0:T(8,128)(2,1)}, bf16[2048,704]{1,0:T(8,128)(2,1)}, bf16[2048,704]{1,0:T(8,128)(2,1)S(1)}) fusion(f32[2048,704]{1,0:T(8,128)} %fusion.3, f32[2048,704]{1,0:T(8,128)} %fusion.4, bf16[2048,2048]{1,0:T(8,128)(2,1)} %all-gather.2.cloned.1.call-done, bf16[704,2048]{1,0:T(8,128)(2,1)S(1)} %copy-done), kind=kOutput, calls=%fused_computation.1 | convolution fusion | flops 5927206912 | bytes 31457280 | tf_op jit(solution)/shard_map/sd,fd->sf/dot_general | solution.py:785
  410.7 1.7 copy-done.25
  412.5 8.9 convolution_convert_fusion
  421.3 9.7 convolution_convert_fusion.1
  431.0 1.4 constant_dynamic-slice_fusion
  432.5 19.3 %convolution_convert_fusion.2 = bf16[2048,704]{0,1:T(8,128)(2,1)S(1)} fusion(bf16[2048,2048]{1,0:T(8,128)(2,1)} %get-tuple-element.54, bf16[2048,704]{1,0:T(8,128)(2,1)S(1)} %copy-done.27), kind=kOutput, calls=%fused_computation.7 | convolution fusion | flops 5907021824 | bytes 14155776 | tf_op jit(solution)/shard_map/sd,sf->df/dot_general | solution.py:793
  451.8 1.3 constant_dynamic-slice_fusion.1
  454.3 284.5 %ffn_back.1 = (f32[256,2048]{1,0:T(8,128)}, bf16[2048,2048]{1,0:T(8,128)(2,1)}, f32[1,2048]{1,0:T(1,128)}) custom-call(bf16[2048,704]{1,0:T(8,128)(2,1)} %get-tuple-element.86.grad_gate, bf16[2048,704]{1,0:T(8,128)(2,1)} %get-tuple-element.85.grad_up, bf16[2048,704]{1,0:T(8,128)(2,1)} %copy.44.w_gate, bf16[2048,704]{1,0:T(8,128)(2,1)} %copy.45.w_up, ...), custom_call_target="tpu_custom_call" | custom-call | flops 11811160064 | bytes 629145600 | tf_op jit(solution)/shard_map/ffn_back/pallas_call | solution.py:640
  738.8 60.7 %mixer_backward.1 = (bf16[2048,2048]{1,0:T(8,128)(2,1)}, bf16[2048,256]{1,0:T(8,128)(2,1)}, bf16[2048,256]{1,0:T(8,128)(2,1)}, bf16[2048,256]{1,0:T(8,128)(2,1)}...) custom-call(s32[1,2]{1,0:T(1,128)} %starts.3, ...), custom_call_target="tpu_custom_call" | custom-call | flops 25769803776 | bytes 54525952 | tf_op jit(solution)/shard_map/mixer_backward/pallas_call | solution.py:365
  799.5 1.9 constant_dynamic-slice_fusion.3
  801.5 1.9 constant_dynamic-slice_fusion.4
  803.8 1.9 constant_dynamic-slice_fusion.5
  805.8 1.3 concatenate.31.small
  807.2 104.2 %last_step.1 = (f32[256,2048]{1,0:T(8,128)}, f32[16,2048]{1,0:T(8,128)}) custom-call(bf16[2048,2048]{1,0:T(8,128)(2,1)} %get-tuple-element.69.terms, bf16[256,2048]{1,0:T(8,128)(2,1)} %tokens.3, f32[256,2048]{1,0:T(8,128)} %get-tuple-element.70.grad_resid, bf16[1,2048]{1,0:T(2,128)(2,1)} %reshape.48.gain_first.gain, f32[16,2048]{1,0:T(8,128)} %concatenate.31.small), custom_call_target="tpu_custom_call" | custom-call | bytes 314572800 | tf_op jit(solution)/shard_map/last_step/pallas_call | solution.py:717
  911.5 8.9 convolution_convert_fusion.3
  920.5 1.3 slice_bitcast_fusion.1
  921.9 1.3 fusion.2
  923.2 1.5 fusion.1
  924.7 1.4 slice_bitcast_fusion
  930.5 1.4 collective-permute-start.10
  932.0 12.1 %collective-permute-done.13 = bf16[128,2048]{1,0:T(8,128)(2,1)S(1)} collective-permute-done((bf16[128,2048]{1,0:T(8,128)(2,1)S(1)}, bf16[128,2048]{1,0:T(8,128)(2,1)S(1)}, u32[]{:S(2)}, u32[]{:S(2)}) %collective-permute-start.13) | collective-permute-done | bytes 524320 | tf_op jit(solution)/shard_map/ppermute | solution.py:742
  945.0 10.4 collective-permute-done.10
  956.2 10.4 collective-permute-done.7
  967.4 10.4 collective-permute-done.4
  978.0 10.2 collective-permute-done.1
  988.9 2.0 add_convert_fusion.3
  992.7 1.9 add_convert_fusion.1
  995.4 1.6 maximum_convert_fusion.7
  996.9 1.3 collective-permute-start.19
  998.4 1.5 maximum_convert_fusion.6
  1000.6 1.5 maximum_convert_fusion.5
  1002.2 26.9 %collective-permute-done.22 = bf16[352,2048]{1,0:T(8,128)(2,1)S(1)} collective-permute-done((bf16[352,2048]{1,0:T(8,128)(2,1)S(1)}, bf16[352,2048]{1,0:T(8,128)(2,1)S(1)}, u32[]{:S(2)}, u32[]{:S(2)}) %collective-permute-start.22) | collective-permute-done | bytes 1441824 | tf_op jit(solution)/shard_map/ppermute | solution.py:742
  1029.7 1.5 maximum_convert_fusion.4
  1031.3 28.7 %collective-permute-done.19 = bf16[1024,704]{0,1:T(8,128)(2,1)S(1)} collective-permute-done((bf16[1024,704]{0,1:T(8,128)(2,1)S(1)}, bf16[1024,704]{0,1:T(8,128)(2,1)S(1)}, u32[]{:S(2)}, u32[]{:S(2)}) %collective-permute-start.19) | collective-permute-done | bytes 1441824 | tf_op jit(solution)/shard_map/ppermute | solution.py:742
  1060.7 1.5 maximum_convert_fusion.3
  1062.1 27.8 %collective-permute-done.16 = bf16[1024,704]{0,1:T(8,128)(2,1)S(1)} collective-permute-done((bf16[1024,704]{0,1:T(8,128)(2,1)S(1)}, bf16[1024,704]{0,1:T(8,128)(2,1)S(1)}, u32[]{:S(2)}, u32[]{:S(2)}) %collective-permute-start.16) | collective-permute-done | bytes 1441824 | tf_op jit(solution)/shard_map/ppermute | solution.py:742
  1090.8 3.3 maximum_convert_fusion.2
  1094.3 3.3 maximum_convert_fusion.1
  1097.8 3.3 maximum_convert_fusion
  1101.1 3.3 add_convert_fusion.6
  1104.4 1.3 copy.51
  (131 shorter events, 18.2 us)
Async XLA Ops:
  7.2 387.8 %copy-start = (bf16[704,2048]{1,0:T(8,128)(2,1)S(1)}, bf16[704,2048]{1,0:T(8,128)(2,1)}, u32[]{:S(2)}) copy-start(bf16[704,2048]{1,0:T(8,128)(2,1)} %param.34) | copy-start | bytes 8650756
  7.2 84.8 %copy-start.18 = (bf16[2048]{0:T(1024)(128)(2,1)S(1)}, bf16[2048]{0:T(1024)(128)(2,1)}, u32[]{:S(2)}) copy-start(bf16[2048]{0:T(1024)(128)(2,1)} %param.20) | copy-start | bytes 12292
  7.2 85.4 %copy-start.15 = (bf16[2048,2]{0,1:T(2,128)(2,1)S(1)}, bf16[2048,2]{0,1:T(2,128)(2,1)}, u32[]{:S(2)}) copy-start(bf16[2048,2]{0,1:T(2,128)(2,1)} %param.27) | copy-start | bytes 24580
  7.2 86.4 %copy-start.19 = (bf16[2048]{0:T(1024)(128)(2,1)S(1)}, bf16[2048]{0:T(1024)(128)(2,1)}, u32[]{:S(2)}) copy-start(bf16[2048]{0:T(1024)(128)(2,1)} %param.31) | copy-start | bytes 12292
  7.2 387.8 %all-gather.2.cloned.1.call-start = ((), (), s32[]{:S(2)}) async-start(), calls=%async_computation.2 | async-start | bytes 9437184 | tf_op jit(solution)/shard_map/all_gather | solution.py:774
  91.9 1009.2 %reduce-scatter.2.cloned.1.call-start = ((), (), s32[]{:S(2)}) async-start(), calls=%async_computation.1 | async-start | bytes 9437184 | tf_op jit(solution)/shard_map/reduce_scatter | solution.py:795
  161.6 213.7 %copy-start.2 = (bf16[2048,704]{0,1:T(8,128)(2,1)S(1)}, bf16[2048,704]{0,1:T(8,128)(2,1)}, u32[]{:S(2)}) copy-start(bf16[2048,704]{0,1:T(8,128)(2,1)} %param.32) | copy-start | bytes 8650756
  375.3 10.9 copy-start.3
  375.3 10.9 copy-start.24
  421.3 11.1 %copy-start.27 = (bf16[2048,704]{1,0:T(8,128)(2,1)S(1)}, bf16[2048,704]{1,0:T(8,128)(2,1)}, u32[]{:S(2)}) copy-start(bf16[2048,704]{1,0:T(8,128)(2,1)} %get-tuple-element.85.grad_up) | copy-start | bytes 8650756
  431.0 20.7 %copy-start.4 = (bf16[704,2048]{1,0:T(8,128)(2,1)}, bf16[704,2048]{1,0:T(8,128)(2,1)S(1)}, u32[]{:S(2)}) copy-start(bf16[704,2048]{1,0:T(8,128)(2,1)S(1)} %convolution_convert_fusion.1) | copy-start | bytes 8650756
  432.5 559.1 %collective-permute-start.21 = (bf16[352,2048]{1,0:T(8,128)(2,1)}, bf16[352,2048]{1,0:T(8,128)(2,1)}, u32[]{:S(2)}, u32[]{:S(2)}) collective-permute-start(bf16[352,2048]{1,0:T(8,128)(2,1)} %constant_dynamic-slice_fusion), channel_id=1, source_target_pairs={{0,8},{8,0},{16,24},{24,16},{1,9},{9,1},{17,25},{25,17},{2,10},{10... | collective-permute-start | bytes 4325384 | tf_op jit(solution)/shard_map/ppermute | solution.py:742
  453.8 534.5 %collective-permute-start.18 = (bf16[1024,704]{0,1:T(8,128)(2,1)}, bf16[1024,704]{0,1:T(8,128)(2,1)}, u32[]{:S(2)}, u32[]{:S(2)}) collective-permute-start(bf16[1024,704]{0,1:T(8,128)(2,1)} %constant_dynamic-slice_fusion.1), channel_id=1, source_target_pairs={{0,8},{8,0},{16,24},{24,16},{1,9},{9,1},{17,25},{25,17},{2,10},{10... | collective-permute-start | bytes 4325384 | tf_op jit(solution)/shard_map/ppermute | solution.py:742
  799.5 6.2 copy-start.23
  799.5 6.2 copy-start.20
  799.5 6.2 copy-start.21
  799.5 6.2 copy-start.22
  799.5 6.3 copy-start.14
  799.5 6.3 copy-start.16
  799.5 6.3 copy-start.17
  801.5 124.8 %collective-permute-start.12 = (bf16[128,2048]{1,0:T(8,128)(2,1)}, bf16[128,2048]{1,0:T(8,128)(2,1)}, u32[]{:S(2)}, u32[]{:S(2)}) collective-permute-start(bf16[128,2048]{1,0:T(8,128)(2,1)} %constant_dynamic-slice_fusion.3), channel_id=1, source_target_pairs={{0,8},{8,0},{16,24},{24,16},{1,9},{9,1},{17,25},{25,17},{2,10},{10... | collective-permute-start | bytes 1572872 | tf_op jit(solution)/shard_map/ppermute | solution.py:742
  803.3 124.2 %collective-permute-start.9 = (bf16[1024,256]{1,0:T(8,128)(2,1)}, bf16[1024,256]{1,0:T(8,128)(2,1)}, u32[]{:S(2)}, u32[]{:S(2)}) collective-permute-start(bf16[1024,256]{1,0:T(8,128)(2,1)} %constant_dynamic-slice_fusion.4), channel_id=1, source_target_pairs={{0,8},{8,0},{16,24},{24,16},{1,9},{9,1},{17,25},{25,17},{2,10},{10... | collective-permute-start | bytes 1572872 | tf_op jit(solution)/shard_map/ppermute | solution.py:742
  805.7 123.6 %collective-permute-start.6 = (bf16[1024,256]{1,0:T(8,128)(2,1)}, bf16[1024,256]{1,0:T(8,128)(2,1)S(1)}, u32[]{:S(2)}, u32[]{:S(2)}) collective-permute-start(bf16[1024,256]{1,0:T(8,128)(2,1)} %constant_dynamic-slice_fusion.5), channel_id=1, source_target_pairs={{0,8},{8,0},{16,24},{24,16},{1,9},{9,1},{17,25},{25,17},{2,10},{10... | collective-permute-start | bytes 1572872 | tf_op jit(solution)/shard_map/ppermute | solution.py:742
  807.2 104.3 %copy-start.10 = (bf16[2048,256]{1,0:T(8,128)(2,1)S(1)}, bf16[2048,256]{1,0:T(8,128)(2,1)}, u32[]{:S(2)}) copy-start(bf16[2048,256]{1,0:T(8,128)(2,1)} %get-tuple-element.81) | copy-start | bytes 3145732
  807.2 104.3 %copy-start.26 = (bf16[2048,704]{1,0:T(8,128)(2,1)S(1)}, bf16[2048,704]{1,0:T(8,128)(2,1)}, u32[]{:S(2)}) copy-start(bf16[2048,704]{1,0:T(8,128)(2,1)} %get-tuple-element.86.grad_gate) | copy-start | bytes 8650756
  911.5 14.8 %copy-start.13 = (bf16[256,2048]{1,0:T(8,128)(2,1)S(1)}, bf16[256,2048]{1,0:T(8,128)(2,1)}, u32[]{:S(2)}) copy-start(bf16[256,2048]{1,0:T(8,128)(2,1)} %get-tuple-element.84) | copy-start | bytes 3145732
  920.4 7.7 copy-start.12
  920.4 9.6 copy-start.11
  926.2 3.9 collective-permute-start.3
  927.5 2.9 collective-permute-start
  929.3 14.8 %collective-permute-start.13 = (bf16[128,2048]{1,0:T(8,128)(2,1)S(1)}, bf16[128,2048]{1,0:T(8,128)(2,1)S(1)}, u32[]{:S(2)}, u32[]{:S(2)}) collective-permute-start(bf16[128,2048]{1,0:T(8,128)(2,1)S(1)} %add_convert_fusion.8), channel_id=1, source_target_pairs={{0,16},{8,24},{16,0},{24,8},{1,17},{9,25},{17,1},{25,9},{2,18},{10... | collective-permute-start | bytes 1572872 | tf_op jit(solution)/shard_map/ppermute | solution.py:742
  930.2 60.7 %collective-permute-start.15 = (bf16[1024,704]{0,1:T(8,128)(2,1)S(1)}, bf16[1024,704]{0,1:T(8,128)(2,1)S(1)}, u32[]{:S(2)}, u32[]{:S(2)}) collective-permute-start(bf16[1024,704]{0,1:T(8,128)(2,1)S(1)} %constant_dynamic-slice_fusion.2), channel_id=1, source_target_pairs={{0,8},{8,0},{16,24},{24,16},{1,9},{9,1},{17,25},{25,17},{2,10},{10... | collective-permute-start | bytes 4325384 | tf_op jit(solution)/shard_map/ppermute | solution.py:742
  930.5 24.9 %collective-permute-start.10 = (bf16[1024,256]{1,0:T(8,128)(2,1)S(1)}, bf16[1024,256]{1,0:T(8,128)(2,1)S(1)}, u32[]{:S(2)}, u32[]{:S(2)}) collective-permute-start(bf16[1024,256]{1,0:T(8,128)(2,1)S(1)} %add_convert_fusion.10), channel_id=1, source_target_pairs={{0,16},{8,24},{16,0},{24,8},{1,17},{9,25},{17,1},{25,9},{2,18},{10... | collective-permute-start | bytes 1572872 | tf_op jit(solution)/shard_map/ppermute | solution.py:742
  944.1 22.5 %collective-permute-start.7 = (bf16[1024,256]{1,0:T(8,128)(2,1)S(1)}, bf16[1024,256]{1,0:T(8,128)(2,1)S(1)}, u32[]{:S(2)}, u32[]{:S(2)}) collective-permute-start(bf16[1024,256]{1,0:T(8,128)(2,1)S(1)} %add_convert_fusion.12), channel_id=1, source_target_pairs={{0,16},{8,24},{16,0},{24,8},{1,17},{9,25},{17,1},{25,9},{2,18},{10... | collective-permute-start | bytes 1572872 | tf_op jit(solution)/shard_map/ppermute | solution.py:742
  944.9 43.9 %copy-start.7 = (bf16[2048,704]{0,1:T(8,128)(2,1)S(1)}, bf16[2048,704]{0,1:T(8,128)(2,1)}, u32[]{:S(2)}) copy-start(bf16[2048,704]{0,1:T(8,128)(2,1)} %copy-done.6) | copy-start | bytes 8650756
  955.4 22.5 %collective-permute-start.4 = (bf16[1024,256]{1,0:T(8,128)(2,1)S(1)}, bf16[1024,256]{1,0:T(8,128)(2,1)S(1)}, u32[]{:S(2)}, u32[]{:S(2)}) collective-permute-start(bf16[1024,256]{1,0:T(8,128)(2,1)S(1)} %add_convert_fusion.14), channel_id=1, source_target_pairs={{0,16},{8,24},{16,0},{24,8},{1,17},{9,25},{17,1},{25,9},{2,18},{10... | collective-permute-start | bytes 1572872 | tf_op jit(solution)/shard_map/ppermute | solution.py:742
  966.6 21.5 %collective-permute-start.1 = (bf16[1024,256]{1,0:T(8,128)(2,1)S(1)}, bf16[1024,256]{1,0:T(8,128)(2,1)S(1)}, u32[]{:S(2)}, u32[]{:S(2)}) collective-permute-start(bf16[1024,256]{1,0:T(8,128)(2,1)S(1)} %add_convert_fusion.16), channel_id=1, source_target_pairs={{0,16},{8,24},{16,0},{24,8},{1,17},{9,25},{17,1},{25,9},{2,18},{10... | collective-permute-start | bytes 1572872 | tf_op jit(solution)/shard_map/ppermute | solution.py:742
  977.8 16.7 %collective-permute-start.14 = (bf16[128,2048]{1,0:T(8,128)(2,1)S(1)}, bf16[128,2048]{1,0:T(8,128)(2,1)S(1)}, u32[]{:S(2)}, u32[]{:S(2)}) collective-permute-start(bf16[128,2048]{1,0:T(8,128)(2,1)S(1)} %add_convert_fusion.7), channel_id=1, source_target_pairs={{0,8},{8,0},{16,24},{24,16},{1,9},{9,1},{17,25},{25,17},{2,10},{10... | collective-permute-start | bytes 1572872 | tf_op jit(solution)/shard_map/ppermute | solution.py:742
  988.1 8.8 collective-permute-start.11
  988.3 11.6 %collective-permute-start.8 = (bf16[1024,256]{1,0:T(8,128)(2,1)S(1)}, bf16[1024,256]{1,0:T(8,128)(2,1)S(1)}, u32[]{:S(2)}, u32[]{:S(2)}) collective-permute-start(bf16[1024,256]{1,0:T(8,128)(2,1)S(1)} %add_convert_fusion.11), channel_id=1, source_target_pairs={{0,8},{8,0},{16,24},{24,16},{1,9},{9,1},{17,25},{25,17},{2,10},{10... | collective-permute-start | bytes 1572872 | tf_op jit(solution)/shard_map/ppermute | solution.py:742
  990.9 11.2 %collective-permute-start.5 = (bf16[1024,256]{1,0:T(8,128)(2,1)S(1)}, bf16[1024,256]{1,0:T(8,128)(2,1)S(1)}, u32[]{:S(2)}, u32[]{:S(2)}) collective-permute-start(bf16[1024,256]{1,0:T(8,128)(2,1)S(1)} %add_convert_fusion.13), channel_id=1, source_target_pairs={{0,8},{8,0},{16,24},{24,16},{1,9},{9,1},{17,25},{25,17},{2,10},{10... | collective-permute-start | bytes 1572872 | tf_op jit(solution)/shard_map/ppermute | solution.py:742
  991.6 39.6 %collective-permute-start.2 = (bf16[1024,256]{1,0:T(8,128)(2,1)S(1)}, bf16[1024,256]{1,0:T(8,128)(2,1)S(1)}, u32[]{:S(2)}, u32[]{:S(2)}) collective-permute-start(bf16[1024,256]{1,0:T(8,128)(2,1)S(1)} %add_convert_fusion.15), channel_id=1, source_target_pairs={{0,8},{8,0},{16,24},{24,16},{1,9},{9,1},{17,25},{25,17},{2,10},{10... | collective-permute-start | bytes 1572872 | tf_op jit(solution)/shard_map/ppermute | solution.py:742
  994.6 34.5 %collective-permute-start.22 = (bf16[352,2048]{1,0:T(8,128)(2,1)S(1)}, bf16[352,2048]{1,0:T(8,128)(2,1)S(1)}, u32[]{:S(2)}, u32[]{:S(2)}) collective-permute-start(bf16[352,2048]{1,0:T(8,128)(2,1)S(1)} %add_convert_fusion.1), channel_id=1, source_target_pairs={{0,16},{8,24},{16,0},{24,8},{1,17},{9,25},{17,1},{25,9},{2,18},{10... | collective-permute-start | bytes 4325384 | tf_op jit(solution)/shard_map/ppermute | solution.py:742
  996.9 63.0 %collective-permute-start.19 = (bf16[1024,704]{0,1:T(8,128)(2,1)S(1)}, bf16[1024,704]{0,1:T(8,128)(2,1)S(1)}, u32[]{:S(2)}, u32[]{:S(2)}) collective-permute-start(bf16[1024,704]{0,1:T(8,128)(2,1)S(1)} %add_convert_fusion.3), channel_id=1, source_target_pairs={{0,16},{8,24},{16,0},{24,8},{1,17},{9,25},{17,1},{25,9},{2,18},{10... | collective-permute-start | bytes 4325384 | tf_op jit(solution)/shard_map/ppermute | solution.py:742
  999.9 90.1 %collective-permute-start.16 = (bf16[1024,704]{0,1:T(8,128)(2,1)S(1)}, bf16[1024,704]{0,1:T(8,128)(2,1)S(1)}, u32[]{:S(2)}, u32[]{:S(2)}) collective-permute-start(bf16[1024,704]{0,1:T(8,128)(2,1)S(1)} %add_convert_fusion.5), channel_id=1, source_target_pairs={{0,16},{8,24},{16,0},{24,8},{1,17},{9,25},{17,1},{25,9},{2,18},{10... | collective-permute-start | bytes 4325384 | tf_op jit(solution)/shard_map/ppermute | solution.py:742
  1029.7 61.0 %collective-permute-start.23 = (bf16[352,2048]{1,0:T(8,128)(2,1)S(1)}, bf16[352,2048]{1,0:T(8,128)(2,1)S(1)}, u32[]{:S(2)}, u32[]{:S(2)}) collective-permute-start(bf16[352,2048]{1,0:T(8,128)(2,1)S(1)} %add_convert_fusion), channel_id=1, source_target_pairs={{0,8},{8,0},{16,24},{24,16},{1,9},{9,1},{17,25},{25,17},{2,10},{10... | collective-permute-start | bytes 4325384 | tf_op jit(solution)/shard_map/ppermute | solution.py:742
  1060.6 33.6 %collective-permute-start.20 = (bf16[1024,704]{0,1:T(8,128)(2,1)S(1)}, bf16[1024,704]{0,1:T(8,128)(2,1)S(1)}, u32[]{:S(2)}, u32[]{:S(2)}) collective-permute-start(bf16[1024,704]{0,1:T(8,128)(2,1)S(1)} %add_convert_fusion.2), channel_id=1, source_target_pairs={{0,8},{8,0},{16,24},{24,16},{1,9},{9,1},{17,25},{25,17},{2,10},{10... | collective-permute-start | bytes 4325384 | tf_op jit(solution)/shard_map/ppermute | solution.py:742
  1090.5 7.1 collective-permute-start.17
  (6 other events, 19.2 us)
Sparse Core Ops, SparseCore 0:
  92.0 160.8 all-gather.1
  454.4 253.2 reduce-scatter.1

commit v3 on v1

v3 whole, which is shorter than its diff:
```python
import functools
import jax
import jax.numpy as jnp
from jax import lax
from jax.experimental import pallas as pl
from jax.experimental.pallas import tpu as pltpu
from jax.sharding import PartitionSpec as P

CHUNK = 256
F32, BF16 = jnp.float32, jnp.bfloat16


def mm(a, b, contract=(1, 0)):
    return lax.dot_general(
        a.astype(BF16),
        b.astype(BF16),
        (((contract[0],), (contract[1],)), ((), ())),
        preferred_element_type=F32,
    )


def segment_at(places, starts, lengths, seqs):
    segment = jnp.zeros_like(places)
    for s in range(seqs):
        begin = starts[0, s]
        stop = begin + lengths[0, s]
        segment = segment + jnp.where(places >= begin, 1, 0) + jnp.where(places >= stop, 1, 0)
    return jnp.where(places < 0, -1, segment)


def chunk_masks(starts, lengths, seqs, first, size):
    rows = first + lax.broadcasted_iota(jnp.int32, (size, 1), 0)
    columns = first + lax.broadcasted_iota(jnp.int32, (1, size), 1)
    seg_rows = segment_at(rows, starts, lengths, seqs)
    seg_columns = segment_at(columns, starts, lengths, seqs)
    before = segment_at(jnp.full((1, 1), first - 1, jnp.int32), starts, lengths, seqs)
    last = segment_at(jnp.full((1, 1), first + size - 1, jnp.int32), starts, lengths, seqs)
    return rows, seg_rows, seg_columns, before, last


def inverse_unit_lower(lower, size):
    i = lax.broadcasted_iota(jnp.int32, (size, size), 0)
    j = lax.broadcasted_iota(jnp.int32, (size, size), 1)

    def corner(width):
        shift = width.bit_length() - 1
        pair = (i >> (shift + 1)) == (j >> (shift + 1))
        return pair & (((i >> shift) & 1) == 1) & (((j >> shift) & 1) == 0)

    inverse = jnp.where(i == j, 1.0, 0.0) - jnp.where(corner(1), lower, 0.0)
    width = 2
    while width < size:
        low = inverse.astype(BF16)
        if 2 * width == size:
            part = mm(mm(low[width:, width:], lower[width:, :width]), low[:width, :width])
            inverse = jnp.concatenate(
                [
                    inverse[:width],
                    jnp.concatenate([-part, inverse[width:, width:]], axis=1),
                ],
                axis=0,
            )
        else:
            between = jnp.where(corner(width), lower, 0.0)
            inverse = inverse - mm(mm(low, between), low)
        width *= 2
    return inverse


def sigmoid(v):
    return 1.0 / (1.0 + jnp.exp(-v))


def normed_rows(tokens, gain):
    value = tokens[...].astype(F32)
    unit = value * lax.rsqrt(jnp.mean(value * value, axis=1, keepdims=True) + 1e-6)
    return unit * gain[...].astype(F32), unit


MESH = pl.DeviceIdType.MESH
SUBS = 2


def ring_position(device, count):
    half, odd = device // 2, device % 2
    return half + odd * (count - 1 - 2 * half)


def ring_device(position, count):
    back = position // (count // 2)
    return (1 - back) * 2 * position + back * (2 * (count - 1 - position) + 1)


class Ring:
    def __init__(self, count):
        self.count = count
        self.me = lax.axis_index("tensor")
        self.place = ring_position(self.me, count)
        self.group = lax.axis_index("dp")

    def at(self, offset):
        return ring_device((self.place + offset + 2 * self.count) % self.count, self.count)

    def next(self, way):
        return (self.group, self.at(1 if way == 0 else -1))


def gather_copy(ring, source, target, sends, recvs, way, sub, step, origin, rows):
    piece = rows // (2 * SUBS)
    inside = way * (rows // 2) + sub * piece
    start = pl.multiple_of(origin * rows + inside, piece)
    src = target.at[pl.ds(start, piece), :] if source is None else source.at[pl.ds(inside, piece), :]
    return pltpu.make_async_remote_copy(
        src_ref=src,
        dst_ref=target.at[pl.ds(start, piece), :],
        send_sem=sends.at[way, sub, step],
        recv_sem=recvs.at[way, sub, step],
        device_id=ring.next(way),
        device_id_type=MESH,
    )


PAIRS = [(sub, way) for sub in range(SUBS) for way in (0, 1)]


class Gather:
    def __init__(self, ring, source, target, sends, recvs, local, rows):
        self.ring, self.source, self.target = ring, source, target
        self.sends, self.recvs, self.rows = sends, recvs, rows
        self.keep = pltpu.make_async_copy(
            source, target.at[pl.ds(pl.multiple_of(ring.me * rows, rows), rows), :], local
        )

    def origin(self, way, step):
        return self.ring.at(-step if way == 0 else step)

    def copy(self, way, sub, step, origin, source=None):
        return gather_copy(
            self.ring, source, self.target, self.sends, self.recvs, way, sub, step, origin, self.rows
        )

    def begin(self):
        self.keep.start()
        for sub, way in PAIRS:
            self.copy(way, sub, 0, self.ring.me, self.source).start()

    def arrived(self, step):
        for sub, way in PAIRS:
            self.copy(way, sub, step - 1, self.origin(way, step)).wait_recv()

    def hop(self, step):
        for sub, way in PAIRS:
            self.copy(way, sub, step - 1, self.origin(way, step)).wait_recv()
            self.copy(way, sub, step, self.origin(way, step)).start()

    def end(self):
        def drain(step, carry):
            for sub, way in PAIRS:
                self.copy(way, sub, step, self.ring.me).wait_send()
            return carry

        lax.fori_loop(0, self.ring.count - 1, drain, 0)
        self.keep.wait()


def ring_gather(ring, source, target, sends, recvs, local, rows, between=None):
    gather = Gather(ring, source, target, sends, recvs, local, rows)
    gather.begin()

    def forward(step, carry):
        gather.hop(step)
        if between is not None:
            between(step)
        return carry

    lax.fori_loop(1, ring.count - 1, forward, 0)
    gather.arrived(ring.count - 1)
    if between is not None:
        between(ring.count - 1)
    gather.end()


def scatter_copy(ring, slots, sends, recvs, way, sub, step):
    return pltpu.make_async_remote_copy(
        src_ref=slots.at[way, sub, step],
        dst_ref=slots.at[way, sub, step + 1],
        send_sem=sends.at[way, sub, step],
        recv_sem=recvs.at[way, sub, step],
        device_id=ring.next(way),
        device_id_type=MESH,
    )


class Scatter:
    def __init__(self, ring, partial, slots, sends, recvs, rows, finish):
        self.ring, self.partial, self.slots, self.sends, self.recvs = ring, partial, slots, sends, recvs
        self.half, self.finish = rows // 2, finish
        self.rows, self.piece = rows, rows // (2 * SUBS)

    def terms(self, first, second):
        half = self.half
        return self.partial(
            pl.multiple_of(first * self.rows, half), pl.multiple_of(second * self.rows + half, half)
        )

    def part(self, terms, way, sub):
        start = way * self.half + sub * self.piece
        return terms[start : start + self.piece]

    def copy(self, way, sub, step):
        return scatter_copy(self.ring, self.slots, self.sends, self.recvs, way, sub, step)

    def begin(self):
        terms = self.terms(self.ring.at(-1), self.ring.at(1))
        for sub, way in PAIRS:
            self.slots[way, sub, 0] = self.part(terms, way, sub).astype(BF16)
            self.copy(way, sub, 0).start()

    def hop(self, step):
        terms = self.terms(self.ring.at(-1 - step), self.ring.at(1 + step))
        for sub, way in PAIRS:
            self.copy(way, sub, step - 1).wait_recv()
            self.slots[way, sub, step] = (
                self.slots[way, sub, step].astype(F32) + self.part(terms, way, sub)
            ).astype(BF16)
            self.copy(way, sub, step).start()

    def end(self):
        count = self.ring.count
        terms = self.terms(self.ring.me, self.ring.me)
        for sub, way in PAIRS:
            self.copy(way, sub, count - 2).wait_recv()
            self.finish(
                way * self.half + sub * self.piece,
                self.piece,
                self.slots[way, sub, count - 1].astype(F32) + self.part(terms, way, sub),
            )

        def drain(step, carry):
            for sub, way in PAIRS:
                self.copy(way, sub, step).wait_send()
            return carry

        lax.fori_loop(0, count - 1, drain, 0)


def ring_scatter(ring, partial, slots, sends, recvs, rows, finish, between=None):
    scatter = Scatter(ring, partial, slots, sends, recvs, rows, finish)
    scatter.begin()

    def forward(step, carry):
        scatter.hop(step)
        if between is not None:
            between(step)
        return carry

    lax.fori_loop(1, ring.count - 1, forward, 0)
    scatter.end()


class GroupSum:
    def __init__(self, ring, groups, grads, near, far, targets, near_sems, far_sems, back_sems, keep_sems):
        self.ring, self.groups, self.grads, self.near, self.far, self.targets = ring, groups, grads, near, far, targets
        self.near_sems, self.far_sems, self.back_sems, self.keep_sems = near_sems, far_sems, back_sems, keep_sems
        self.core = ring.group % 2
        self.mate = (ring.group + 1 - 2 * self.core, ring.me)

    def peers(self):
        return [self.mate] + [
            ((self.ring.group + 2 * k) % self.groups, self.ring.me) for k in range(1, self.groups // 2)
        ]

    def half(self, i, core):
        rows = self.near[i].shape[0]
        return pl.ds(pl.multiple_of(core * rows, rows), rows)

    def near_copy(self, i):
        return pltpu.make_async_remote_copy(
            src_ref=self.grads[i].at[self.half(i, 1 - self.core), :], dst_ref=self.near[i],
            send_sem=self.near_sems.at[0, i], recv_sem=self.near_sems.at[1, i],
            device_id=self.mate, device_id_type=MESH,
        )

    def far_copy(self, i, k):
        return pltpu.make_async_remote_copy(
            src_ref=self.near[i], dst_ref=self.far[i].at[k - 1],
            send_sem=self.far_sems.at[0, i, k - 1], recv_sem=self.far_sems.at[1, i, k - 1],
            device_id=((self.ring.group + 2 * k) % self.groups, self.ring.me), device_id_type=MESH,
        )

    def back_copy(self, i):
        return pltpu.make_async_remote_copy(
            src_ref=self.far[i].at[0], dst_ref=self.targets[i].at[self.half(i, self.core), :],
            send_sem=self.back_sems.at[0, i], recv_sem=self.back_sems.at[1, i],
            device_id=self.mate, device_id_type=MESH,
        )

    def keep_copy(self, i):
        return pltpu.make_async_copy(
            self.far[i].at[0], self.targets[i].at[self.half(i, self.core), :], self.keep_sems.at[i]
        )

    def first(self):
        for i in range(len(self.grads)):
            self.near_copy(i).start()

    def second(self):
        for i in range(len(self.grads)):
            self.near_copy(i).wait_recv()
            rows = self.near[i].shape[0]
            block = next(size for size in (64, 32, 16) if rows % size == 0)

            def add(at, carry, i=i, rows=rows, block=block):
                here = pl.ds(pl.multiple_of(at * block, block), block)
                own = pl.ds(pl.multiple_of(self.core * rows + at * block, block), block)
                self.near[i][here, :] = (
                    self.near[i][here, :].astype(F32) + self.grads[i][own, :].astype(F32)
                ).astype(BF16)
                return carry

            lax.fori_loop(0, rows // block, add, 0)
            for k in range(1, self.groups // 2):
                self.far_copy(i, k).start()

    def third(self):
        for i in range(len(self.grads)):
            for k in range(1, self.groups // 2):
                self.far_copy(i, k).wait()
            rows = self.near[i].shape[0]
            block = next(size for size in (64, 32, 16) if rows % size == 0)

            def add(at, carry, i=i, block=block):
                here = pl.ds(pl.multiple_of(at * block, block), block)
                total = self.near[i][here, :].astype(F32)
                for k in range(self.groups // 2 - 1):
                    total = total + self.far[i][k, here, :].astype(F32)
                self.far[i][0, here, :] = total.astype(BF16)
                return carry

            lax.fori_loop(0, rows // block, add, 0)
            self.keep_copy(i).start()
            self.back_copy(i).start()

    def last(self):
        for i in range(len(self.grads)):
            self.near_copy(i).wait_send()
            self.back_copy(i).wait()
            self.keep_copy(i).wait()


def sum_scratch(shapes, groups):
    number = len(shapes)
    return (
        [pltpu.VMEM((rows // 2, columns), BF16) for rows, columns in shapes]
        + [pltpu.VMEM((groups // 2 - 1, rows // 2, columns), BF16) for rows, columns in shapes]
        + [
            pltpu.SemaphoreType.DMA((2, number)),
            pltpu.SemaphoreType.DMA((2, number, groups // 2 - 1)),
            pltpu.SemaphoreType.DMA((2, number)),
            pltpu.SemaphoreType.DMA((number,)),
        ]
    )


def greet(ring, others=()):
    barrier = pltpu.get_barrier_semaphore()
    peers = [ring.next(0), ring.next(1)] + list(others)
    for peer in peers:
        pl.semaphore_signal(barrier, inc=1, device_id=peer, device_id_type=MESH)
    pl.semaphore_wait(barrier, len(peers))


def ring_semaphores(count):
    return [pltpu.SemaphoreType.DMA((2, SUBS, count - 1))] * 2


def ring_slots(count, rows, columns):
    return pltpu.VMEM((2, SUBS, count, rows // (2 * SUBS), columns), BF16)


ANY = pl.BlockSpec(memory_space=pl.ANY)
VMEM = pl.BlockSpec(memory_space=pltpu.VMEM)


def ring_params(number):
    return pltpu.CompilerParams(
        collective_id=number, has_side_effects=True, vmem_limit_bytes=60 << 20
    )


def gather_kernel(count, rows, source, target, sends, recvs, local):
    ring = Ring(count)
    greet(ring)
    ring_gather(ring, source, target, sends, recvs, local, rows)


def gather_tokens(tokens, count):
    rows, model = tokens.shape
    return pl.pallas_call(
        functools.partial(gather_kernel, count, rows),
        name="gather_tokens",
        out_shape=jax.ShapeDtypeStruct((count * rows, model), tokens.dtype),
        in_specs=[ANY],
        out_specs=ANY,
        scratch_shapes=ring_semaphores(count) + [pltpu.SemaphoreType.DMA],
        compiler_params=ring_params(1),
        cost_estimate=pl.CostEstimate(flops=0, bytes_accessed=300 << 20, transcendentals=0),
    )(tokens)


def attend_kernel(
    count, rows, mixed, w_out, tokens, gain, resid, full,
    slots, low, sends, recvs, sends_two, recvs_two, local,
):
    ring = Ring(count)
    greet(ring)

    half = rows // 2

    def partial(first, second):
        return mm(jnp.concatenate([mixed[pl.ds(first, half), :], mixed[pl.ds(second, half), :]], 0), w_out[...])

    def finish(start, size, attended):
        value = tokens[start : start + size, :].astype(F32) + attended
        resid[start : start + size, :] = value
        scale = lax.rsqrt(jnp.mean(value * value, axis=1, keepdims=True) + 1e-6)
        low[start : start + size, :] = (value * scale * gain[...].astype(F32)).astype(BF16)

    ring_scatter(ring, partial, slots, sends, recvs, rows, finish)
    ring_gather(ring, low, full, sends_two, recvs_two, local, rows)


def attend(mixed, w_out, tokens, gain, count):
    rows, model = tokens.shape
    return pl.pallas_call(
        functools.partial(attend_kernel, count, rows),
        name="attend",
        out_shape=[
            jax.ShapeDtypeStruct((rows, model), F32),
            jax.ShapeDtypeStruct((count * rows, model), BF16),
        ],
        in_specs=[VMEM] * 4,
        out_specs=[VMEM, ANY],
        scratch_shapes=[ring_slots(count, rows, model), pltpu.VMEM((rows, model), BF16)]
        + ring_semaphores(count) * 2
        + [pltpu.SemaphoreType.DMA],
        compiler_params=ring_params(2),
        cost_estimate=pl.CostEstimate(
            flops=2 * count * rows * model * mixed.shape[1], bytes_accessed=600 << 20, transcendentals=0
        ),
    )(mixed, w_out, tokens, gain.reshape(1, model))


def norm_back(inputs, scale, gain, grad_normed):
    weighted = gain * grad_normed
    inner = jnp.mean(weighted * inputs, axis=1, keepdims=True)
    unit = inputs * scale
    return scale * weighted - unit * (scale * scale * inner), grad_normed * unit


def ffn_back_kernel(
    count, groups, rows, grad_gate, grad_up, w_gate, w_up, resid, cotangent, gain, gw_one, gw_two, gw_three,
    grad_resid, full, grad_gain, sum_one, sum_two, sum_three,
    slots, low, *rest,
):
    ring = Ring(count)
    sends, recvs, sends_two, recvs_two, local = rest[:5]
    sums = GroupSum(
        ring, groups, (gw_one, gw_two, gw_three), rest[5:8], rest[8:11], (sum_one, sum_two, sum_three), *rest[11:]
    )
    greet(ring, sums.peers())
    sums.first()
    grad_gain[...] = jnp.zeros_like(grad_gain)
    half = rows // 2

    def partial(first, second):
        gates = jnp.concatenate([grad_gate[pl.ds(first, half), :], grad_gate[pl.ds(second, half), :]], 0)
        ups = jnp.concatenate([grad_up[pl.ds(first, half), :], grad_up[pl.ds(second, half), :]], 0)
        return mm(gates, w_gate[...]) + mm(ups, w_up[...])

    def finish(start, size, grad):
        value = resid[start : start + size, :]
        scale = lax.rsqrt(jnp.mean(value * value, axis=1, keepdims=True) + 1e-6)
        through, pieces = norm_back(value, scale, gain[...].astype(F32), grad)
        result = cotangent[start : start + size, :].astype(F32) + through
        grad_resid[start : start + size, :] = result
        grad_gain[...] += jnp.sum(pieces, axis=0, keepdims=True)
        low[start : start + size, :] = result.astype(BF16)

    def between(step):
        @pl.when(step == 2)
        def _():
            sums.second()

    def between_two(step):
        @pl.when(step == count - 2)
        def _():
            sums.third()

    ring_scatter(ring, partial, slots, sends, recvs, rows, finish, between)
    ring_gather(ring, low, full, sends_two, recvs_two, local, rows, between_two)
    sums.last()


def ffn_back(grad_gate, grad_up, w_gate, w_up, resid, cotangent, gain, grads, count, groups):
    rows, model = resid.shape
    return pl.pallas_call(
        functools.partial(ffn_back_kernel, count, groups, rows),
        name="ffn_back",
        out_shape=[
            jax.ShapeDtypeStruct((rows, model), F32),
            jax.ShapeDtypeStruct((count * rows, model), BF16),
            jax.ShapeDtypeStruct((1, model), F32),
        ]
        + [jax.ShapeDtypeStruct(g.shape, BF16) for g in grads],
        in_specs=[VMEM] * 10,
        out_specs=[VMEM, ANY, VMEM] + [ANY] * 3,
        scratch_shapes=[ring_slots(count, rows, model), pltpu.VMEM((rows, model), BF16)]
        + ring_semaphores(count) * 2
        + [pltpu.SemaphoreType.DMA]
        + sum_scratch([g.shape for g in grads], groups),
        compiler_params=ring_params(3),
        cost_estimate=pl.CostEstimate(
            flops=4 * count * rows * model * grad_up.shape[1], bytes_accessed=600 << 20, transcendentals=0
        ),
    )(grad_gate, grad_up, w_gate, w_up, resid, cotangent, gain.reshape(1, model), *grads)


def last_kernel(
    count, groups, rows, terms, tokens, grad_resid, gain, small, *rest,
):
    grads, rest = rest[:5], rest[5:]
    grad_tokens, total = rest[:2]
    targets, rest = rest[2:7], rest[7:]
    slots, first_box, second_box, second_own, sends, recvs = rest[:6]
    first_sends, first_recvs, second_sends, second_recvs = rest[6:10]
    ring = Ring(count)
    sums = GroupSum(ring, groups, grads, rest[10:15], rest[15:20], targets, *rest[20:])
    me, group = ring.me, ring.group
    first_peers = [(group, (me + k) % count) for k in range(1, count)]
    second_peers = [((group + k) % groups, me) for k in range(1, groups)]
    barrier = pltpu.get_barrier_semaphore()
    for peer in first_peers + second_peers:
        pl.semaphore_signal(barrier, inc=1, device_id=peer, device_id_type=MESH)
    pl.semaphore_wait(barrier, count + groups - 2)

    def first(k):
        return pltpu.make_async_remote_copy(
            src_ref=small.at[0:8], dst_ref=first_box.at[k], send_sem=first_sends.at[k],
            recv_sem=first_recvs.at[k], device_id=first_peers[k], device_id_type=MESH,
        )

    def second(k):
        return pltpu.make_async_remote_copy(
            src_ref=second_own, dst_ref=second_box.at[k], send_sem=second_sends.at[k],
            recv_sem=second_recvs.at[k], device_id=second_peers[k], device_id_type=MESH,
        )

    sums.first()
    for k in range(count - 1):
        first(k).start()
    half = rows // 2

    def partial(first, second):
        return jnp.concatenate([terms[pl.ds(first, half), :], terms[pl.ds(second, half), :]], 0).astype(F32)

    def finish(start, size, grad):
        value = tokens[start : start + size, :].astype(F32)
        scale = lax.rsqrt(jnp.mean(value * value, axis=1, keepdims=True) + 1e-6)
        through, pieces = norm_back(value, scale, gain[...].astype(F32), grad)
        grad_tokens[start : start + size, :] = grad_resid[start : start + size, :] + through

    def between(step):
        @pl.when(step == 1)
        def _():
            sums.second()
            for k in range(count - 1):
                first(k).wait()
            mine = small[0:8]
            for k in range(count - 1):
                mine = mine + first_box[k]
            second_own[0:8] = mine
            second_own[8:] = small[8:]
            for k in range(groups - 1):
                second(k).start()

        @pl.when(step == count - 2)
        def _():
            for k in range(groups - 1):
                second(k).wait()
            mine = second_own[...]
            for k in range(groups - 1):
                mine = mine + second_box[k]
            total[...] = mine
            sums.third()

    ring_scatter(ring, partial, slots, sends, recvs, rows, finish, between)
    sums.last()


def last_step(terms, tokens, grad_resid, gain, small, grads, count, groups):
    rows, model = tokens.shape
    return pl.pallas_call(
        functools.partial(last_kernel, count, groups, rows),
        name="last_step",
        out_shape=[jax.ShapeDtypeStruct((rows, model), F32), jax.ShapeDtypeStruct(small.shape, F32)]
        + [jax.ShapeDtypeStruct(g.shape, BF16) for g in grads],
        in_specs=[VMEM] * (5 + len(grads)),
        out_specs=[VMEM, VMEM] + [ANY] * len(grads),
        scratch_shapes=[
            ring_slots(count, rows, model),
            pltpu.VMEM((count - 1, 8, model), F32),
            pltpu.VMEM((groups - 1,) + small.shape, F32),
            pltpu.VMEM(small.shape, F32),
        ]
        + ring_semaphores(count)
        + [pltpu.SemaphoreType.DMA((count - 1,))] * 2
        + [pltpu.SemaphoreType.DMA((groups - 1,))] * 2
        + sum_scratch([g.shape for g in grads], groups),
        compiler_params=ring_params(4),
        cost_estimate=pl.CostEstimate(flops=0, bytes_accessed=300 << 20, transcendentals=0),
    )(terms, tokens, grad_resid, gain.reshape(1, model), small, *grads)


def spread_hops(step, chunks, count, begin, hop, end):
    each = -(-(count - 1) // (chunks - 1))

    @pl.when(step == 0)
    def _():
        begin()

    for place in range(each):
        number = step * each + place

        @pl.when((number > 0) & (number < count - 1))
        def _():
            hop(number)

    @pl.when(step == chunks - 1)
    def _():
        end()


def forward_kernel(
    heads, width, seqs, count, rows_own, chunks,
    starts, lengths, tokens, w_query, w_key, w_value, w_gate, w_beta,
    taps_query, taps_key, taps_value, gain, gain_first, side,
    mixed, p_query, p_key, p_value, p_gate, p_beta, z_query, z_key, z_value,
    delta_out, change_out, inverse_out, state_out, side_full,
    tail_query, tail_key, tail_value, state, sends, recvs, local,
):
    step = pl.program_id(0)
    size = tokens.shape[0]
    first = step * size

    @pl.when(step == 0)
    def _():
        for tail in (tail_query, tail_key, tail_value):
            tail[...] = jnp.zeros_like(tail)
        state[...] = jnp.zeros_like(state)

    ring = Ring(count)
    gather = Gather(ring, side, side_full, sends, recvs, local, rows_own)
    spread_hops(
        step, chunks, count,
        lambda: (greet(ring), gather.begin()),
        gather.hop,
        lambda: (gather.arrived(count - 1), gather.end()),
    )
    rows, seg_rows, seg_columns, before, last = chunk_masks(starts, lengths, seqs, first, size)
    same = seg_rows == seg_columns
    i = lax.broadcasted_iota(jnp.int32, (size, size), 0)
    j = lax.broadcasted_iota(jnp.int32, (size, size), 1)
    strict = jnp.where(same & (i > j), 1.0, 0.0)
    inclusive = jnp.where(same & (i >= j), 1.0, 0.0)
    carried = jnp.where(seg_rows == before, 1.0, 0.0)
    ending = jnp.where(seg_rows == last, 1.0, 0.0)
    kept = jnp.where(before == last, 1.0, 0.0)
    live = jnp.where(seg_rows % 2 == 1, 1.0, 0.0)
    joined = [
        jnp.where(segment_at(rows - offset, starts, lengths, seqs) == seg_rows, 1.0, 0.0)
        for offset in range(1, taps_query.shape[0])
    ]
    inputs = normed_rows(tokens, gain_first)[0].astype(BF16)

    def feature(weight, taps, tail, p_out, z_out):
        projected = jnp.dot(inputs, weight[...], preferred_element_type=F32)
        p_out[...] = projected
        tail[8:, :] = projected
        tap = taps[...].astype(F32)
        result = projected * tap[0:1]
        for offset in range(1, tap.shape[0]):
            result = result + tail[8 - offset : 8 - offset + size, :] * tap[offset : offset + 1] * joined[offset - 1]
        tail[0:8, :] = projected[size - 8 :, :]
        z_out[...] = result
        return result * sigmoid(result)

    u_query = feature(w_query, taps_query, tail_query, p_query, z_query)
    u_key = feature(w_key, taps_key, tail_key, p_key, z_key)
    u_value = feature(w_value, taps_value, tail_value, p_value, z_value)
    gate = jnp.dot(inputs, w_gate[...], preferred_element_type=F32)
    p_gate[...] = gate
    beta_pre = mm(inputs, w_beta[...], (1, 1))
    p_beta[...] = beta_pre
    strength = sigmoid(beta_pre)
    opened = gate * sigmoid(gate)
    scale = width ** (-0.5)
    head_gain = gain[...].astype(F32)
    for h in range(heads):
        cols = slice(h * width, (h + 1) * width)
        uq, uk = u_query[:, cols], u_key[:, cols]
        query = (uq * lax.rsqrt(jnp.sum(uq * uq, axis=1, keepdims=True) + 1e-6)).astype(BF16)
        key = (uk * lax.rsqrt(jnp.sum(uk * uk, axis=1, keepdims=True) + 1e-6)).astype(BF16)
        value = u_value[:, cols].astype(BF16).astype(F32)
        beta = strength[:, h : h + 1]
        memory = state[h]
        low_memory = memory.astype(BF16)
        state_out[0, h] = low_memory
        lower = mm(key, key, (1, 1)) * strict * beta
        inverse = inverse_unit_lower(lower, size).astype(BF16)
        inverse_out[0, h] = inverse
        within = mm(query, key, (1, 1)) * inclusive
        change = mm(inverse, beta * (value - carried * mm(key, low_memory)))
        low_change = change.astype(BF16)
        change_out[:, cols] = low_change
        out = scale * (carried * mm(query, low_memory) + mm(within, low_change))
        state[h] = kept * memory + mm(key, ending * change, (0, 0))
        delta_out[:, cols] = out
        normal = out * lax.rsqrt(jnp.mean(out * out, axis=1, keepdims=True) + 1e-5) * head_gain
        mixed[:, cols] = (normal * opened[:, cols] * live).astype(BF16)


def forward_mixer(tokens, w_query, w_key, w_value, w_gate, w_beta, taps_query, taps_key, taps_value, gain, gain_first, starts, lengths, side, count):
    slots, model = tokens.shape
    wide = w_query.shape[1]
    width = gain.shape[0]
    heads = wide // width
    seqs = starts.shape[1]
    chunks = slots // CHUNK
    taps = taps_query.shape[0]
    smem = pl.BlockSpec(memory_space=pltpu.SMEM)
    whole = lambda shape: pl.BlockSpec(shape, lambda n: (0,) * len(shape))
    piece = lambda shape: pl.BlockSpec(shape, lambda n: (n,) + (0,) * (len(shape) - 1))
    outs = [
        ((slots, wide), BF16), ((slots, wide), F32), ((slots, wide), F32), ((slots, wide), F32), ((slots, wide), F32),
        ((slots, w_beta.shape[0]), F32), ((slots, wide), F32), ((slots, wide), F32), ((slots, wide), F32),
        ((slots, wide), F32), ((slots, wide), BF16),
    ]
    return pl.pallas_call(
        functools.partial(forward_kernel, heads, width, seqs, count, slots // count, chunks),
        name="mixer_forward",
        grid=(chunks,),
        out_shape=[jax.ShapeDtypeStruct(s, d) for s, d in outs]
        + [
            jax.ShapeDtypeStruct((chunks, heads, CHUNK, CHUNK), BF16),
            jax.ShapeDtypeStruct((chunks, heads, width, width), BF16),
            jax.ShapeDtypeStruct((slots, model), BF16),
        ],
        in_specs=[smem, smem, piece((CHUNK, model))]
        + [whole((model, wide))] * 4
        + [whole(w_beta.shape)]
        + [whole((taps, wide))] * 3
        + [whole((1, width)), whole((1, model)), ANY],
        out_specs=[piece((CHUNK, s[1])) for s, d in outs]
        + [piece((1, heads, CHUNK, CHUNK)), piece((1, heads, width, width)), ANY],
        scratch_shapes=[pltpu.VMEM((CHUNK + 8, wide), F32)] * 3
        + [pltpu.VMEM((heads, width, width), F32)]
        + ring_semaphores(count)
        + [pltpu.SemaphoreType.DMA],
        compiler_params=ring_params(5),
        cost_estimate=pl.CostEstimate(
            flops=2 * slots * model * wide * 4 + slots * heads * CHUNK * 2 * CHUNK * 20,
            bytes_accessed=slots * model * 2 + 4 * model * wide * 2 + slots * wide * 36,
            transcendentals=slots * wide * 4,
        ),
    )(starts, lengths, tokens, w_query, w_key, w_value, w_gate, w_beta, taps_query, taps_key, taps_value, gain.reshape(1, width), gain_first.reshape(1, model), side)


def backward_kernel(
    heads, width, seqs, chunks, count, rows_own,
    starts, lengths, tokens, grad_attended, mixed, p_query, p_key, p_value, p_gate, p_beta,
    z_query, z_key, z_value, delta_out, change_in, inverse_in, state_in,
    w_query, w_key, w_value, w_gate, w_beta, w_out, taps_query, taps_key, taps_value, gain, gain_first,
    hidden, w_down, resid, grad_normed, gw_query, gw_key, gw_value, gw_gate, gw_beta, gw_out,
    gt_query, gt_key, gt_value, g_gain, g_first, output,
    a_query, a_key, a_value, a_gate, a_out, head_query, head_key, head_value, flow, slots, sends, recvs,
):
    step = pl.program_id(0)
    size = tokens.shape[0]
    first = (chunks - 1 - step) * size

    @pl.when(step == 0)
    def _():
        for ref in (a_query, a_key, a_value, a_gate, gw_beta, a_out, gt_query, gt_key, gt_value, g_gain, g_first, flow):
            ref[...] = jnp.zeros_like(ref)
        for ref in (head_query, head_key, head_value):
            ref[size:, :] = jnp.zeros((8, ref.shape[1]), F32)

    half = rows_own // 2

    def partial(one, two):
        return mm(jnp.concatenate([hidden[pl.ds(one, half), :], hidden[pl.ds(two, half), :]], 0), w_down[...])

    def finish(start, length, down):
        output[start : start + length, :] = (resid[start : start + length, :] + down).astype(BF16)

    ring = Ring(count)
    scatter = Scatter(ring, partial, slots, sends, recvs, rows_own, finish)
    spread_hops(
        step, chunks, count,
        lambda: (greet(ring), scatter.begin()),
        scatter.hop,
        scatter.end,
    )
    rows, seg_rows, seg_columns, before, last = chunk_masks(starts, lengths, seqs, first, size)
    same = seg_rows == seg_columns
    i = lax.broadcasted_iota(jnp.int32, (size, size), 0)
    j = lax.broadcasted_iota(jnp.int32, (size, size), 1)
    strict = jnp.where(same & (i > j), 1.0, 0.0)
    inclusive = jnp.where(same & (i >= j), 1.0, 0.0)
    carried = jnp.where(seg_rows == before, 1.0, 0.0)
    ending = jnp.where(seg_rows == last, 1.0, 0.0)
    kept = jnp.where(before == last, 1.0, 0.0)
    live = jnp.where(seg_rows % 2 == 1, 1.0, 0.0)
    taps = taps_query.shape[0]
    joined = [
        jnp.where(segment_at(rows + offset, starts, lengths, seqs) == seg_rows, 1.0, 0.0)
        for offset in range(1, taps)
    ]
    normal_rows, unit_rows = normed_rows(tokens, gain_first)
    inputs = normal_rows.astype(BF16)
    grad_rows = grad_attended[...]
    grad_mixed = mm(grad_rows, w_out[...], (1, 1))
    a_out[...] += mm(mixed[...], grad_rows, (0, 0))
    strength = sigmoid(p_beta[...])
    scale = width ** (-0.5)
    head_gain = gain[...].astype(F32)

    grads_query, grads_key, grads_value, grads_gate, grads_beta = [], [], [], [], []
    for h in range(heads):
        cols = slice(h * width, (h + 1) * width)
        out = delta_out[:, cols]
        gate = p_gate[:, cols]
        sig_gate = sigmoid(gate)
        silu_gate = gate * sig_gate
        root = lax.rsqrt(jnp.mean(out * out, axis=1, keepdims=True) + 1e-5)
        grad = grad_mixed[:, cols] * live
        unit = out * root
        grads_gate.append(grad * unit * head_gain * (sig_gate * (1.0 + gate * (1.0 - sig_gate))))
        grad_normal = grad * silu_gate
        g_gain[...] += jnp.sum(grad_normal * unit, axis=0, keepdims=True)
        push = grad_normal * head_gain
        grad_out = scale * root * (push - unit * jnp.mean(push * unit, axis=1, keepdims=True))

        zq, zk, zv = z_query[:, cols], z_key[:, cols], z_value[:, cols]
        sq, sk, sv = sigmoid(zq), sigmoid(zk), sigmoid(zv)
        uq, uk = zq * sq, zk * sk
        nq = lax.rsqrt(jnp.sum(uq * uq, axis=1, keepdims=True) + 1e-6)
        nk = lax.rsqrt(jnp.sum(uk * uk, axis=1, keepdims=True) + 1e-6)
        unit_q, unit_k = uq * nq, uk * nk
        query, key = unit_q.astype(BF16), unit_k.astype(BF16)
        beta = strength[:, h : h + 1]
        change = change_in[:, cols]
        inverse = inverse_in[0, h]
        memory = state_in[0, h]
        flowing = flow[h]
        low_flow = flowing.astype(BF16)
        low_out = grad_out.astype(BF16)

        within = mm(query, key, (1, 1)) * inclusive
        grad_within = (mm(low_out, change, (1, 1)) * inclusive).astype(BF16)
        grad_change = mm(within, low_out, (0, 0)) + ending * mm(key, low_flow)
        grad_mid = mm(inverse, grad_change, (0, 0))
        grad_value = beta * grad_mid
        low_value = grad_value.astype(BF16)
        cross = (mm(low_value, change, (1, 1)) * strict).astype(BF16)
        grad_query = carried * mm(low_out, memory, (1, 1)) + mm(grad_within, key)
        grad_key = (
            mm(grad_within, query, (0, 0))
            + ending * mm(change, low_flow, (1, 1))
            - carried * mm(low_value, memory, (1, 1))
            - mm(cross, key)
            - mm(cross, key, (0, 0))
        )
        flow[h] = (
            kept * flowing
            + mm(query, carried * grad_out, (0, 0))
            - mm(key, carried * grad_value, (0, 0))
        )
        grads_beta.append((1.0 - beta) * jnp.sum(grad_mid * change.astype(F32), axis=1, keepdims=True))
        du_q = nq * (grad_query - unit_q * jnp.sum(grad_query * unit_q, axis=1, keepdims=True))
        du_k = nk * (grad_key - unit_k * jnp.sum(grad_key * unit_k, axis=1, keepdims=True))
        grads_query.append(du_q * sq * (1.0 + zq * (1.0 - sq)))
        grads_key.append(du_k * sk * (1.0 + zk * (1.0 - sk)))
        grads_value.append(grad_value * sv * (1.0 + zv * (1.0 - sv)))

    def unconv(parts, taps_ref, head, projected, grad_taps):
        grad = jnp.concatenate(parts, axis=1)
        head[0:size, :] = grad
        tap = taps_ref[...].astype(F32)
        p = projected[...]
        result = grad * tap[0:1]
        grad_taps[0:1, :] += jnp.sum(p * grad, axis=0, keepdims=True)
        for offset in range(1, taps):
            moved = head[offset : offset + size, :] * joined[offset - 1]
            result = result + moved * tap[offset : offset + 1]
            grad_taps[offset : offset + 1, :] += jnp.sum(p * moved, axis=0, keepdims=True)
        head[size:, :] = grad[0:8, :]
        return result.astype(BF16)

    d_query = unconv(grads_query, taps_query, head_query, p_query, gt_query)
    d_key = unconv(grads_key, taps_key, head_key, p_key, gt_key)
    d_value = unconv(grads_value, taps_value, head_value, p_value, gt_value)
    d_gate = jnp.concatenate(grads_gate, axis=1).astype(BF16)
    spare = [jnp.zeros((size, 1), F32)] * (w_beta.shape[0] - heads)
    d_beta = jnp.concatenate(grads_beta + spare, axis=1).astype(BF16)
    grad_inputs = (
        mm(d_query, w_query[...], (1, 1))
        + mm(d_key, w_key[...], (1, 1))
        + mm(d_value, w_value[...], (1, 1))
        + mm(d_gate, w_gate[...], (1, 1))
        + mm(d_beta, w_beta[...])
    )
    grad_normed[...] = grad_inputs.astype(BF16)
    g_first[...] += jnp.sum(grad_inputs * unit_rows, axis=0, keepdims=True)
    a_query[...] += mm(inputs, d_query, (0, 0))
    a_key[...] += mm(inputs, d_key, (0, 0))
    a_value[...] += mm(inputs, d_value, (0, 0))
    a_gate[...] += mm(inputs, d_gate, (0, 0))
    gw_beta[...] += mm(d_beta, inputs, (0, 0))

    @pl.when(step == chunks - 1)
    def _():
        for target, source in (
            (gw_query, a_query), (gw_key, a_key), (gw_value, a_value), (gw_gate, a_gate),
            (gw_out, a_out),
        ):
            target[...] = source[...].astype(target.dtype)


def backward_mixer(tokens, grad_attended, saved, w_query, w_key, w_value, w_gate, w_beta, w_out, taps_query, taps_key, taps_value, gain, gain_first, starts, lengths, hidden, w_down, resid, count):
    slots, model = tokens.shape
    wide = w_query.shape[1]
    width = gain.shape[0]
    heads = wide // width
    seqs = starts.shape[1]
    chunks = slots // CHUNK
    taps = taps_query.shape[0]
    smem = pl.BlockSpec(memory_space=pltpu.SMEM)
    fixed = lambda shape: pl.BlockSpec(shape, lambda n: (0,) * len(shape), pipeline_mode=pl.Buffered(1))
    piece = lambda shape: pl.BlockSpec(shape, lambda n: (chunks - 1 - n,) + (0,) * (len(shape) - 1))
    rows = lambda a: piece((CHUNK, a.shape[1]))
    outs = (
        [((slots, model), BF16)] + [((model, wide), BF16)] * 4 + [(w_beta.shape, F32), ((wide, model), BF16)]
        + [((taps, wide), F32)] * 3 + [((1, width), F32), ((1, model), F32), (resid.shape, BF16)]
    )
    return pl.pallas_call(
        functools.partial(backward_kernel, heads, width, seqs, chunks, count, slots // count),
        name="mixer_backward",
        grid=(chunks,),
        out_shape=[jax.ShapeDtypeStruct(s, d) for s, d in outs],
        in_specs=[smem, smem, rows(tokens), rows(grad_attended)]
        + [rows(a) for a in saved[:11]]
        + [piece((1, heads, CHUNK, CHUNK)), piece((1, heads, width, width))]
        + [fixed((model, wide))] * 4
        + [fixed(w_beta.shape), fixed((wide, model))]
        + [fixed((taps, wide))] * 3
        + [fixed((1, width)), fixed((1, model)), fixed(hidden.shape), fixed(w_down.shape), fixed(resid.shape)],
        out_specs=[piece((CHUNK, model))] + [fixed(s) for s, d in outs[1:]],
        scratch_shapes=[pltpu.VMEM((model, wide), F32)] * 4
        + [pltpu.VMEM((wide, model), F32)]
        + [pltpu.VMEM((CHUNK + 8, wide), F32)] * 3
        + [pltpu.VMEM((heads, width, width), F32), ring_slots(count, slots // count, model)]
        + ring_semaphores(count),
        compiler_params=ring_params(6),
        cost_estimate=pl.CostEstimate(
            flops=2 * slots * model * wide * 10 + slots * heads * CHUNK * 2 * CHUNK * 8,
            bytes_accessed=slots * model * 6 + 10 * model * wide * 2 + slots * wide * 36,
            transcendentals=slots * wide * 8,
        ),
    )(starts, lengths, tokens, grad_attended, *saved, w_query, w_key, w_value, w_gate, w_beta, w_out, taps_query, taps_key, taps_value, gain.reshape(1, width), gain_first.reshape(1, model), hidden, w_down, resid)


def silu_parts(value):
    sig = jax.nn.sigmoid(value)
    return sig, value * sig


def make_shards(groups, count):
    def shards(
        tokens, attn_gain, w_query, w_key, w_value, conv_query, conv_key, conv_value, w_beta, w_gate_out,
        head_gain, w_out, ffn_gain, w_gate, w_up, w_down, seq_starts, seq_lengths, cotangent,
    ):
        model = tokens.shape[1]
        heads = w_beta.shape[1]
        beta_rows = w_beta.T if heads > 1 else jnp.pad(w_beta.T, ((0, 1), (0, 0)))
        tokens_full = gather_tokens(tokens, count)
        saved = forward_mixer(
            tokens_full, w_query, w_key, w_value, w_gate_out, beta_rows,
            conv_query, conv_key, conv_value, head_gain, attn_gain, seq_starts, seq_lengths, cotangent, count,
        )
        grad_full, saved = saved[-1], saved[:-1]
        resid, ffn_full = attend(saved[0], w_out, tokens, ffn_gain, count)
        gate_pre = jnp.dot(ffn_full, w_gate, preferred_element_type=F32)
        up_pre = jnp.dot(ffn_full, w_up, preferred_element_type=F32)
        sig, silu_gate = silu_parts(gate_pre)
        hidden = (silu_gate * up_pre).astype(BF16)
        grad_hidden = jnp.einsum("sd,fd->sf", grad_full, w_down, preferred_element_type=F32)
        grad_gate = (grad_hidden * up_pre * sig * (1.0 + gate_pre * (1.0 - sig))).astype(BF16)
        grad_up = (grad_hidden * silu_gate).astype(BF16)
        gw_down = jnp.einsum("sf,sd->fd", hidden, grad_full, preferred_element_type=F32)
        gw_gate = jnp.einsum("sd,sf->fd", ffn_full, grad_gate, preferred_element_type=F32)
        gw_up = jnp.einsum("sd,sf->fd", ffn_full, grad_up, preferred_element_type=F32)
        grad_resid, grad_attended, g_second, *ffn_grads = ffn_back(
            grad_gate, grad_up, w_gate.T, w_up.T, resid, cotangent, ffn_gain,
            [g.astype(BF16) for g in (gw_gate, gw_up, gw_down)], count, groups,
        )
        pulled = backward_mixer(
            tokens_full, grad_attended, saved, w_query, w_key, w_value, w_gate_out, beta_rows, w_out,
            conv_query, conv_key, conv_value, head_gain, attn_gain, seq_starts, seq_lengths,
            hidden, w_down, resid, count,
        )
        terms, gw_query, gw_key, gw_value, gw_gate_out, gw_beta, gw_out = pulled[:7]
        gt_query, gt_key, gt_value, g_head, g_first, output = pulled[7:]
        wide = gt_query.shape[1]
        gw_beta = gw_beta[:heads]
        taps = gt_query.shape[0]
        small = jnp.concatenate(
            [
                g_first,
                g_second,
                jnp.pad(g_head, ((0, 0), (0, model - g_head.shape[1]))),
                jnp.zeros((5, model), F32),
                gw_beta,
                jnp.pad(
                    jnp.concatenate([gt_query, gt_key, gt_value], 1), ((0, 0), (0, model - 3 * wide))
                ),
                jnp.zeros((-(heads + taps) % 8, model), F32),
            ],
            0,
        )
        grad_tokens, total, *mixer_grads = last_step(
            terms, tokens, grad_resid, attn_gain, small,
            (gw_query, gw_key, gw_value, gw_gate_out, gw_out), count, groups,
        )
        mixer_grads = [g.astype(F32) for g in mixer_grads]
        tap_rows = total[8 + heads : 8 + heads + taps]
        return (
            output,
            grad_tokens,
            total[0],
            mixer_grads[0],
            mixer_grads[1],
            mixer_grads[2],
            tap_rows[:, :wide],
            tap_rows[:, wide : 2 * wide],
            tap_rows[:, 2 * wide : 3 * wide],
            total[8 : 8 + heads].T,
            mixer_grads[3],
            total[2, : head_gain.shape[0]],
            mixer_grads[4],
            total[1],
            ffn_grads[0].astype(F32).T,
            ffn_grads[1].astype(F32).T,
            ffn_grads[2].astype(F32),
        )

    return shards


def solution(mesh):
    placed = (
        P(("dp", "tensor"), None),
        P(),
        P(None, "tensor"),
        P(None, "tensor"),
        P(None, "tensor"),
        P(None, "tensor"),
        P(None, "tensor"),
        P(None, "tensor"),
        P(None, "tensor"),
        P(None, "tensor"),
        P(),
        P("tensor", None),
        P(),
        P(None, "tensor"),
        P(None, "tensor"),
        P("tensor", None),
        P("dp", None),
        P("dp", None),
        P(("dp", "tensor"), None),
    )
    return jax.shard_map(
        make_shards(mesh.shape["dp"], mesh.shape["tensor"]),
        mesh=mesh,
        in_specs=placed,
        out_specs=(
            P(("dp", "tensor"), None),
            P(("dp", "tensor"), None),
            P(),
            P(None, "tensor"),
            P(None, "tensor"),
            P(None, "tensor"),
            P(None, "tensor"),
            P(None, "tensor"),
            P(None, "tensor"),
            P(None, "tensor"),
            P(None, "tensor"),
            P(),
            P("tensor", None),
            P(),
            P(None, "tensor"),
            P(None, "tensor"),
            P("tensor", None),
        ),
        check_vma=False,
    )
```

time: 1560 us -> 816 us (0.52)
  waiting for transfers between devices: 1200 us -> 0 us
  Pallas kernels: 116 us -> 712 us
  blocking collectives: 69.4 us -> 0 us
  matrix products: 104 us -> 59 us
  other arithmetic: 45.2 us -> 18.7 us
    pallas_call x1 -> x5, Pallas kernels: 56.1 us -> 613 us  [the longest x1 173 us: ffn_back(): pl.pallas_call(functools.partial(ffn_back_kernel, count, groups, rows), n...]
    reduce_scatter x4 -> x0, waiting for transfers between devices: 536 us -> none  [the longest x1 147 us: shards(): lax.psum_scatter((jnp.einsum('sf,df->sd', grad_gate, w_gate, preferred_el...]
    all_gather x4 -> x0, waiting for transfers between devices: 451 us -> none  [the longest x1 127 us: shards(): normed_full = lax.all_gather(normed, 'tensor', axis=0, tiled=True)]
    psum x1 -> x0, waiting for transfers between devices: 208 us -> none  [shards(): lax.psum(mixer_grads[0].astype(jnp.bfloat16), 'dp').astype(jnp.float32)]
    psum x2 -> x0, blocking collectives: 69.4 us -> none  [the longest x1 42.3 us: shards(): lax.psum((grad_attn_gain, grad_ffn_gain, pulled[10][0]), ('dp', 'tensor'))]
    dot_general x10 -> x6, matrix products: 104 us -> 59 us  [the longest x1 13.9 us: shards(): up_pre = jnp.dot(ffn_full, w_up, preferred_element_type=F32)]
    pallas_call x1, Pallas kernels: 60.3 us -> 99.2 us  [backward_mixer(): pl.pallas_call(functools.partial(backward_kernel, heads, width, seqs, chu...]
    convert_element_type x19 -> x6, other arithmetic: 30.2 us -> 12.1 us  [the longest x5 8.78 us: shards(): mixer_grads = [g.astype(F32) for g in mixer_grads]]
  transfers between devices with their start and end apart: 9 -> 0, of which waited for: 9 -> 0; matrix products, arithmetic and copies ran while one was open for 5% -> 0% of each run, Pallas kernels for 0% -> 0%
where the time goes in v3:
time: 816 us; the launch traced here: 805 us
  Pallas kernels  712 us (87%)
  matrix products  59 us (7%)
  other arithmetic  18.7 us (2%)
  local copies, waits for them, and re-layouts  14.3 us (2%)
    pallas_call x1, Pallas kernels, ffn_back(): pl.pallas_call(functools.partial(ffn_back_kernel, count, groups, rows), n...  173 us
    pallas_call x1, Pallas kernels, attend(): pl.pallas_call(functools.partial(attend_kernel, count, rows), name='atten...  163 us
    pallas_call x1, Pallas kernels, last_step(): pl.pallas_call(functools.partial(last_kernel, count, groups, rows), name=...  99.4 us
    pallas_call x1, Pallas kernels, backward_mixer(): pl.pallas_call(functools.partial(backward_kernel, heads, width, seqs, chu...  99.2 us
    pallas_call x1, Pallas kernels, forward_mixer(): pl.pallas_call(functools.partial(forward_kernel, heads, width, seqs, coun...  92.9 us
    pallas_call x1, Pallas kernels, gather_tokens(): pl.pallas_call(functools.partial(gather_kernel, count, rows), name='gathe...  84.6 us

profile of v3, /device:TPU:0, one launch (start us, length us, event | category | flops | bytes accessed | tf_op | source)
XLA Modules:
  0.0 805.3 jit_solution(8444543257931050751)
XLA Ops:
  0.7 0.0 copy-start.10
  0.7 84.6 %gather_tokens.1.tokens = bf16[2048,2048]{1,0:T(8,128)(2,1)} custom-call(bf16[256,2048]{1,0:T(8,128)(2,1)} %tokens.3), custom_call_target="tpu_custom_call" | custom-call | bytes 314572800 | tf_op jit(solution)/shard_map/gather_tokens/pallas_call | solution.py:399
  85.3 0.0 copy-done.10
  85.3 0.6 reshape.48.gain_first.gain
  85.9 92.9 %mixer_forward.1 = (bf16[2048,256]{1,0:T(8,128)(2,1)}, f32[2048,256]{1,0:T(8,128)}, f32[2048,256]{1,0:T(8,128)}, f32[2048,256]{1,0:T(8,128)}, f32[2048,256]{1,0:...) custom-call(s32[1,2]{1,0:T(1,128)} %starts.3, ...), custom_call_target="tpu_custom_call" | custom-call | flops 19327352832 | bytes 31457280 | tf_op jit(solution)/shard_map/mixer_forward/pallas_call | solution.py:749
  178.8 0.0 copy-done.11
  178.8 0.6 reshape.49.gain
  179.4 162.9 %attend.1 = (f32[256,2048]{1,0:T(8,128)}, bf16[2048,2048]{1,0:T(8,128)(2,1)}) custom-call(bf16[2048,256]{1,0:T(8,128)(2,1)} %get-tuple-element.60.mixed, bf16[256,2048]{1,0:T(8,128)(2,1)} %w_out.3, bf16[256,2048]{1,0:T(8,128)(2,1)} %tokens.3, bf16[1,2048]{1,0:T(2,128)(2,1)} %reshape.49.gain), custom_call_target="tpu_custom_call" | custom-call | flops 2147483648 | bytes 629145600 | tf_op jit(solution)/shard_map/attend/pallas_call | solution.py:435
  342.3 0.0 copy-done.12
  342.3 0.0 copy-start.14
  342.3 0.0 copy-start.15
  342.3 0.0 slice-start
  342.3 10.9 %fusion.4 = f32[2048,704]{1,0:T(8,128)} fusion(bf16[2048,2048]{1,0:T(8,128)(2,1)} %get-tuple-element.61, bf16[2048,704]{0,1:T(8,128)(2,1)S(1)} %copy-done.12), kind=kOutput, calls=%fused_computation.18 | convolution fusion | flops 5905580032 | bytes 17039360 | tf_op jit(solution)/shard_map/dot_general | solution.py:1004
  353.3 0.0 copy-done.14
  353.3 0.0 copy-done.15
  353.3 0.0 copy-start.13
  353.3 8.8 %fusion.3 = f32[2048,704]{1,0:T(8,128)} fusion(bf16[2048,2048]{1,0:T(8,128)(2,1)S(1)} %copy-done.15, bf16[704,2048]{1,0:T(8,128)(2,1)S(1)} %copy-done.14), kind=kOutput, calls=%fused_computation.17 | convolution fusion | flops 5905580032 | bytes 17039360 | tf_op jit(solution)/shard_map/sd,fd->sf/dot_general | solution.py:1008
  362.1 0.0 slice-done
  362.1 0.0 slice-done.1
  362.1 0.0 copy-done.13
  362.1 13.9 %multiply_convert_fusion = (bf16[2048,704]{1,0:T(8,128)(2,1)}, bf16[2048,704]{1,0:T(8,128)(2,1)}, bf16[2048,704]{1,0:T(8,128)(2,1)}) fusion(f32[2048,704]{1,0:T(8,128)} %fusion.4, f32[2048,704]{1,0:T(8,128)} %fusion.3, bf16[2048,2048]{1,0:T(8,128)(2,1)S(1)} %bitcast.35, bf16[2048,704]{0,1:T(8,128)(2,1)S(1)} %copy-done.13), kind=kOutput, calls=%fused_computation | convolution fusion | flops 5927206912 | bytes 31457280 | tf_op jit(solution)/shard_map/dot_general | solution.py:1005
  376.0 9.6 %convolution_convert_fusion.2.gw_one = bf16[704,2048]{1,0:T(8,128)(2,1)} fusion(bf16[2048,704]{1,0:T(8,128)(2,1)} %get-tuple-element.102.grad_gate, bf16[2048,2048]{1,0:T(8,128)(2,1)S(1)} %bitcast.35), kind=kOutput, calls=%fused_computation.9 | convolution fusion | flops 5907021824 | bytes 14155776 | tf_op jit(solution)/shard_map/sd,sf->fd/dot_general | solution.py:1012
  385.6 0.0 copy-done.17
  385.6 7.7 convolution_convert_fusion.1.gw_two
  393.3 0.0 slice-done.2
  393.3 0.0 slice-done.3
  393.3 8.1 %convolution_convert_fusion.gw_three = bf16[704,2048]{1,0:T(8,128)(2,1)} fusion(bf16[2048,704]{1,0:T(8,128)(2,1)S(1)} %copy-done.16, bf16[2048,2048]{1,0:T(8,128)(2,1)S(1)} %bitcast.37), kind=kOutput, calls=%fused_computation.7 | convolution fusion | flops 5907021824 | bytes 14155776 | tf_op jit(solution)/shard_map/sf,sd->fd/dot_general | solution.py:1011
  401.4 173.1 %ffn_back.1 = (f32[256,2048]{1,0:T(8,128)}, bf16[2048,2048]{1,0:T(8,128)(2,1)}, f32[1,2048]{1,0:T(1,128)}, bf16[704,2048]{1,0:T(8,128)(2,1)}, bf16[704,2048]{1,0:T(8,128)(2,1)}, /*index=5*/bf16[704,2048]{1,0:T(8,128)(2,1)}) custom-call(bf16[2048,704]{1,0:T(8,128)(2,1)} %get-tuple-element.102.grad_gate, bf16[2048,704]{1,0:T(8,128)(2,1)} %get-tuple-element.103.grad_up, ...), custom_call_target="tpu_custom_call" | custom-call | flops 11811160064 | bytes 629145600 | tf_op jit(solution)/shard_map/ffn_back/pallas_call | solution.py:507
  574.6 99.2 %mixer_backward.1 = (bf16[2048,2048]{1,0:T(8,128)(2,1)}, bf16[2048,256]{1,0:T(8,128)(2,1)}, bf16[2048,256]{1,0:T(8,128)(2,1)}, bf16[2048,256]{1,0:T(8,128)(2,1)}...) custom-call(s32[1,2]{1,0:T(1,128)} %starts.3, ...), custom_call_target="tpu_custom_call" | custom-call | flops 25769803776 | bytes 54525952 | tf_op jit(solution)/shard_map/mixer_backward/pallas_call | solution.py:957
  673.8 0.7 pad.8
  674.4 0.7 select_maximum_fusion
  675.2 2.7 concatenate.7.small
  677.9 99.4 %last_step.1 = (f32[256,2048]{1,0:T(8,128)}, f32[16,2048]{1,0:T(8,128)}, bf16[2048,256]{1,0:T(8,128)(2,1)}, bf16[2048,256]{1,0:T(8,128)(2,1)}, bf16[2048,256]{1,...) custom-call(bf16[2048,2048]{1,0:T(8,128)(2,1)} %get-tuple-element.77.terms, ...), custom_call_target="tpu_custom_call" | custom-call | bytes 314572800 | tf_op jit(solution)/shard_map/last_step/pallas_call | solution.py:603
  777.4 1.6 fusion.1
  779.0 2.8 convert_element_type.48
  781.8 1.5 convert_element_type.49
  783.2 1.5 convert_element_type.50
  784.7 1.3 fusion.2
  786.1 1.4 slice_bitcast_fusion
  787.5 1.5 convert_element_type.51
  789.0 2.0 slice_bitcast_fusion.1
  791.0 1.6 convert_element_type.52
  792.5 5.9 convert_bitcast_fusion
  798.5 3.3 convert_element_type.53
  801.8 0.0 copy-done.8
  801.8 1.0 copy.48
  802.8 1.0 copy-done.3
  803.8 1.3 copy.49
  (30 shorter events, 0.1 us)
Async XLA Ops:
  0.7 84.6 %copy-start.10 = (bf16[2048]{0:T(1024)(128)(2,1)S(1)}, bf16[2048]{0:T(1024)(128)(2,1)}, u32[]{:S(2)}) copy-start(bf16[2048]{0:T(1024)(128)(2,1)} %param.20) | copy-start | bytes 12292
  85.9 92.9 %copy-start.11 = (bf16[2048]{0:T(1024)(128)(2,1)S(1)}, bf16[2048]{0:T(1024)(128)(2,1)}, u32[]{:S(2)}) copy-start(bf16[2048]{0:T(1024)(128)(2,1)} %param.31) | copy-start | bytes 12292
  179.4 162.9 %copy-start.12 = (bf16[2048,704]{0,1:T(8,128)(2,1)S(1)}, bf16[2048,704]{0,1:T(8,128)(2,1)}, u32[]{:S(2)}) copy-start(bf16[2048,704]{0,1:T(8,128)(2,1)} %param.32) | copy-start | bytes 8650756
  342.3 11.0 %copy-start.14 = (bf16[704,2048]{1,0:T(8,128)(2,1)S(1)}, bf16[704,2048]{1,0:T(8,128)(2,1)}, u32[]{:S(2)}) copy-start(bf16[704,2048]{1,0:T(8,128)(2,1)} %w_down.1) | copy-start | bytes 8650756
  342.3 11.0 %copy-start.15 = (bf16[2048,2048]{1,0:T(8,128)(2,1)S(1)}, bf16[2048,2048]{1,0:T(8,128)(2,1)}, u32[]{:S(2)}) copy-start(bf16[2048,2048]{1,0:T(8,128)(2,1)} %get-tuple-element.59) | copy-start | bytes 25165828
  342.3 19.7 %slice-start = ((s8[8388608]{0:T(1024)(128)(4,1)}), s8[4194304]{0:T(1024)(128)(4,1)S(1)}, s32[]{:S(2)}) async-start(s8[8388608]{0:T(1024)(128)(4,1)} %bitcast.34), calls=%async_computation | async-start | bytes 8388608
  353.3 8.8 %slice-start.1 = ((s8[8388608]{0:T(1024)(128)(4,1)}), s8[4194304]{0:T(1024)(128)(4,1)S(1)}, s32[]{:S(2)}) async-start(s8[8388608]{0:T(1024)(128)(4,1)} %bitcast.34), calls=%async_computation.1 | async-start | bytes 8388608
  353.3 8.8 %copy-start.13 = (bf16[2048,704]{0,1:T(8,128)(2,1)S(1)}, bf16[2048,704]{0,1:T(8,128)(2,1)}, u32[]{:S(2)}) copy-start(bf16[2048,704]{0,1:T(8,128)(2,1)} %param.33) | copy-start | bytes 8650756
  376.0 9.6 %copy-start.17 = (bf16[2048,704]{1,0:T(8,128)(2,1)S(1)}, bf16[2048,704]{1,0:T(8,128)(2,1)}, u32[]{:S(2)}) copy-start(bf16[2048,704]{1,0:T(8,128)(2,1)} %get-tuple-element.103.grad_up) | copy-start | bytes 8650756
  376.0 17.3 %slice-start.2 = ((s8[8388608]{0:T(1024)(128)(4,1)}), s8[4194304]{0:T(1024)(128)(4,1)S(1)}, s32[]{:S(2)}) async-start(s8[8388608]{0:T(1024)(128)(4,1)} %bitcast.36), calls=%async_computation.2 | async-start | bytes 8388608
  385.6 7.7 slice-start.3
  385.6 7.7 copy-start.16
  574.6 100.6 %copy-start.9 = (f32[1,2048]{1,0:T(1,128)S(1)}, f32[1,2048]{1,0:T(1,128)}, u32[]{:S(2)}) copy-start(f32[1,2048]{1,0:T(1,128)} %get-tuple-element.80) | copy-start | bytes 24580
  777.4 4.4 copy-start.7
  779.0 4.3 copy-start.6
  781.8 5.7 copy-start.5
  783.2 7.7 copy-start.4
  787.5 5.0 copy-start.1
  787.5 5.0 copy-start.2
  792.5 5.9 copy-start
  798.5 3.3 copy-start.8
  801.8 2.0 copy-start.3

commit v4 on v3

--- a/solution.py
+++ b/solution.py
@@ -127,9 +127,11 @@
     def __init__(self, ring, source, target, sends, recvs, local, rows):
         self.ring, self.source, self.target = ring, source, target
         self.sends, self.recvs, self.rows = sends, recvs, rows
-        self.keep = pltpu.make_async_copy(
-            source, target.at[pl.ds(pl.multiple_of(ring.me * rows, rows), rows), :], local
-        )
+        self.keep = None
+        if source is not None:
+            self.keep = pltpu.make_async_copy(
+                source, target.at[pl.ds(pl.multiple_of(ring.me * rows, rows), rows), :], local
+            )
 
     def origin(self, way, step):
         return self.ring.at(-step if way == 0 else step)
@@ -140,7 +142,8 @@
         )
 
     def begin(self):
-        self.keep.start()
+        if self.keep is not None:
+            self.keep.start()
         for sub, way in PAIRS:
             self.copy(way, sub, 0, self.ring.me, self.source).start()
 
@@ -160,12 +163,15 @@
             return carry
 
         lax.fori_loop(0, self.ring.count - 1, drain, 0)
-        self.keep.wait()
+        if self.keep is not None:
+            self.keep.wait()
 
 
 def ring_gather(ring, source, target, sends, recvs, local, rows, between=None):
     gather = Gather(ring, source, target, sends, recvs, local, rows)
     gather.begin()
+    if between is not None:
+        between(0)
 
     def forward(step, carry):
         gather.hop(step)
@@ -247,6 +253,8 @@
 def ring_scatter(ring, partial, slots, sends, recvs, rows, finish, between=None):
     scatter = Scatter(ring, partial, slots, sends, recvs, rows, finish)
     scatter.begin()
+    if between is not None:
+        between(0)
 
     def forward(step, carry):
         scatter.hop(step)
@@ -255,6 +263,8 @@
         return carry
 
     lax.fori_loop(1, ring.count - 1, forward, 0)
+    if between is not None:
+        between(ring.count - 1)
     scatter.end()
 
 
@@ -300,44 +310,46 @@
             self.far[i].at[0], self.targets[i].at[self.half(i, self.core), :], self.keep_sems.at[i]
         )
 
-    def first(self):
-        for i in range(len(self.grads)):
+    def first(self, chosen):
+        for i in chosen:
             self.near_copy(i).start()
 
-    def second(self):
-        for i in range(len(self.grads)):
+    def each_block(self, i, body):
+        rows = self.near[i].shape[0]
+        block = next(size for size in (64, 32, 16) if rows % size == 0)
+
+        def step(at, carry):
+            start = pl.multiple_of(at * block, block)
+            body(pl.ds(start, block), pl.ds(pl.multiple_of(self.core * rows + start, block), block))
+            return carry
+
+        lax.fori_loop(0, rows // block, step, 0)
+
+    def second(self, chosen):
+        for i in chosen:
             self.near_copy(i).wait_recv()
-            rows = self.near[i].shape[0]
-            block = next(size for size in (64, 32, 16) if rows % size == 0)
-
-            def add(at, carry, i=i, rows=rows, block=block):
-                here = pl.ds(pl.multiple_of(at * block, block), block)
-                own = pl.ds(pl.multiple_of(self.core * rows + at * block, block), block)
+
+            def add(here, own, i=i):
                 self.near[i][here, :] = (
                     self.near[i][here, :].astype(F32) + self.grads[i][own, :].astype(F32)
                 ).astype(BF16)
-                return carry
-
-            lax.fori_loop(0, rows // block, add, 0)
+
+            self.each_block(i, add)
             for k in range(1, self.groups // 2):
                 self.far_copy(i, k).start()
 
-    def third(self):
-        for i in range(len(self.grads)):
+    def third(self, chosen):
+        for i in chosen:
             for k in range(1, self.groups // 2):
                 self.far_copy(i, k).wait()
-            rows = self.near[i].shape[0]
-            block = next(size for size in (64, 32, 16) if rows % size == 0)
-
-            def add(at, carry, i=i, block=block):
-                here = pl.ds(pl.multiple_of(at * block, block), block)
+
+            def add(here, own, i=i):
                 total = self.near[i][here, :].astype(F32)
                 for k in range(self.groups // 2 - 1):
                     total = total + self.far[i][k, here, :].astype(F32)
                 self.far[i][0, here, :] = total.astype(BF16)
-                return carry
-
-            lax.fori_loop(0, rows // block, add, 0)
+
+            self.each_block(i, add)
             self.keep_copy(i).start()
             self.back_copy(i).start()
 
@@ -408,14 +420,27 @@
     )(tokens)
 
 
+def logistic(v):
+    return 1.0 / (1.0 + jnp.exp(-v))
+
+
 def attend_kernel(
-    count, rows, mixed, w_out, tokens, gain, resid, full,
-    slots, low, sends, recvs, sends_two, recvs_two, local,
+    count, rows, mixed, w_out, tokens, gain, w_gate, w_up, w_down, cotangents,
+    resid, full, hidden, grad_gate, grad_up,
+    slots, gathered, grad_hidden, boxes, sends, recvs, sends_two, recvs_two, box_sems, out_sems,
 ):
     ring = Ring(count)
+    half = rows // 2
+
+    def box_copy(block):
+        return pltpu.make_async_copy(
+            cotangents.at[pl.ds(pl.multiple_of(block * rows, rows), rows), :],
+            boxes.at[block % 2],
+            box_sems.at[block % 2],
+        )
+
+    box_copy(0).start()
     greet(ring)
-
-    half = rows // 2
 
     def partial(first, second):
         return mm(jnp.concatenate([mixed[pl.ds(first, half), :], mixed[pl.ds(second, half), :]], 0), w_out[...])
@@ -424,31 +449,89 @@
         value = tokens[start : start + size, :].astype(F32) + attended
         resid[start : start + size, :] = value
         scale = lax.rsqrt(jnp.mean(value * value, axis=1, keepdims=True) + 1e-6)
-        low[start : start + size, :] = (value * scale * gain[...].astype(F32)).astype(BF16)
-
-    ring_scatter(ring, partial, slots, sends, recvs, rows, finish)
-    ring_gather(ring, low, full, sends_two, recvs_two, local, rows)
-
-
-def attend(mixed, w_out, tokens, gain, count):
+        gathered[pl.ds(pl.multiple_of(ring.me * rows + start, size), size), :] = (
+            value * scale * gain[...].astype(F32)
+        ).astype(BF16)
+
+    def hide(block):
+        box_copy(block).wait()
+
+        @pl.when(block + 1 < count)
+        def _():
+            box_copy(block + 1).start()
+
+        grad_hidden[pl.ds(pl.multiple_of(block * rows, rows), rows), :] = mm(
+            boxes[block % 2], w_down[...], (1, 1)
+        )
+
+    ring_scatter(ring, partial, slots, sends, recvs, rows, finish, hide)
+    gather = Gather(ring, None, gathered, sends_two, recvs_two, None, rows)
+
+    def places(step):
+        return [
+            pl.ds(pl.multiple_of(gather.origin(way, step) * rows + way * half, half), half) for way in (0, 1)
+        ]
+
+    def out_copy(way, step):
+        at = places(step)[way]
+        return pltpu.make_async_copy(gathered.at[at, :], full.at[at, :], out_sems.at[way, step])
+
+    def feed(step):
+        one, two = places(step)
+        for way in (0, 1):
+            out_copy(way, step).start()
+        inputs = jnp.concatenate([gathered[one, :], gathered[two, :]], 0)
+        gate = mm(inputs, w_gate[...], (1, 1))
+        up = mm(inputs, w_up[...], (1, 1))
+        grad = jnp.concatenate([grad_hidden[one, :], grad_hidden[two, :]], 0)
+        sig = logistic(gate)
+        opened = gate * sig
+        for target, value in (
+            (hidden, opened * up),
+            (grad_gate, grad * up * sig * (1.0 + gate * (1.0 - sig))),
+            (grad_up, grad * opened),
+        ):
+            low = value.astype(BF16)
+            target[one, :] = low[:half]
+            target[two, :] = low[half:]
+
+    ring_gather(ring, None, gathered, sends_two, recvs_two, None, rows, feed)
+
+    def drain(step, carry):
+        for way in (0, 1):
+            out_copy(way, step).wait()
+        return carry
+
+    lax.fori_loop(0, count, drain, 0)
+
+
+def attend(mixed, w_out, tokens, gain, w_gate, w_up, w_down, cotangents, count):
     rows, model = tokens.shape
+    slots, inner = count * rows, w_down.shape[0]
     return pl.pallas_call(
         functools.partial(attend_kernel, count, rows),
         name="attend",
         out_shape=[
             jax.ShapeDtypeStruct((rows, model), F32),
-            jax.ShapeDtypeStruct((count * rows, model), BF16),
-        ],
-        in_specs=[VMEM] * 4,
-        out_specs=[VMEM, ANY],
-        scratch_shapes=[ring_slots(count, rows, model), pltpu.VMEM((rows, model), BF16)]
+            jax.ShapeDtypeStruct((slots, model), BF16),
+        ]
+        + [jax.ShapeDtypeStruct((slots, inner), BF16)] * 3,
+        in_specs=[VMEM] * 7 + [ANY],
+        out_specs=[VMEM, ANY] + [VMEM] * 3,
+        scratch_shapes=[
+            ring_slots(count, rows, model),
+            pltpu.VMEM((slots, model), BF16),
+            pltpu.VMEM((slots, inner), F32),
+            pltpu.VMEM((2, rows, model), BF16),
+        ]
         + ring_semaphores(count) * 2
-        + [pltpu.SemaphoreType.DMA],
+        + [pltpu.SemaphoreType.DMA((2,)), pltpu.SemaphoreType.DMA((2, count))],
         compiler_params=ring_params(2),
         cost_estimate=pl.CostEstimate(
-            flops=2 * count * rows * model * mixed.shape[1], bytes_accessed=600 << 20, transcendentals=0
+            flops=2 * slots * model * (mixed.shape[1] + 3 * inner), bytes_accessed=600 << 20,
+            transcendentals=slots * inner,
         ),
-    )(mixed, w_out, tokens, gain.reshape(1, model))
+    )(mixed, w_out, tokens, gain.reshape(1, model), w_gate, w_up, w_down, cotangents)
 
 
 def norm_back(inputs, scale, gain, grad_normed):
@@ -458,18 +541,30 @@
     return scale * weighted - unit * (scale * scale * inner), grad_normed * unit
 
 
+JOBS = 8
+
+
 def ffn_back_kernel(
-    count, groups, rows, grad_gate, grad_up, w_gate, w_up, resid, cotangent, gain, gw_one, gw_two, gw_three,
-    grad_resid, full, grad_gain, sum_one, sum_two, sum_three,
-    slots, low, *rest,
+    count, groups, rows, grad_gate, grad_up, hidden, w_gate, w_up, resid, cotangent, gain, inputs, cotangents,
+    grad_resid, full, grad_gain, sum_gate, sum_up, sum_down,
+    slots, low, gw_gate, gw_up, gw_down, boxes, box_sems, *rest,
 ):
     ring = Ring(count)
     sends, recvs, sends_two, recvs_two, local = rest[:5]
     sums = GroupSum(
-        ring, groups, (gw_one, gw_two, gw_three), rest[5:8], rest[8:11], (sum_one, sum_two, sum_three), *rest[11:]
+        ring, groups, (gw_gate, gw_up, gw_down), rest[5:8], rest[8:11], (sum_gate, sum_up, sum_down), *rest[11:]
     )
+    wide = boxes.shape[2]
+
+    def box_copy(job):
+        source = inputs if job < JOBS // 2 else cotangents
+        at = job % (JOBS // 2) * wide
+        return pltpu.make_async_copy(
+            source.at[:, at : at + wide], boxes.at[job % 2], box_sems.at[job % 2]
+        )
+
+    box_copy(0).start()
     greet(ring, sums.peers())
-    sums.first()
     grad_gain[...] = jnp.zeros_like(grad_gain)
     half = rows // 2
 
@@ -487,43 +582,72 @@
         grad_gain[...] += jnp.sum(pieces, axis=0, keepdims=True)
         low[start : start + size, :] = result.astype(BF16)
 
-    def between(step):
-        @pl.when(step == 2)
-        def _():
-            sums.second()
-
-    def between_two(step):
-        @pl.when(step == count - 2)
-        def _():
-            sums.third()
-
-    ring_scatter(ring, partial, slots, sends, recvs, rows, finish, between)
-    ring_gather(ring, low, full, sends_two, recvs_two, local, rows, between_two)
+    def work(job):
+        box_copy(job).wait()
+        if job + 1 < JOBS:
+            box_copy(job + 1).start()
+        at = job % (JOBS // 2) * wide
+        box = boxes[job % 2]
+        if job < JOBS // 2:
+            gw_gate[:, at : at + wide] = mm(grad_gate[...], box, (0, 0)).astype(BF16)
+            gw_up[:, at : at + wide] = mm(grad_up[...], box, (0, 0)).astype(BF16)
+        else:
+            gw_down[:, at : at + wide] = mm(hidden[...], box, (0, 0)).astype(BF16)
+
+    each = JOBS // 4
+    events = {step: [functools.partial(work, step * each + k) for k in range(each)] for step in range(4)}
+    events[1].append(lambda: sums.first((0, 1)))
+    events[3].insert(0, lambda: sums.second((0, 1)))
+    events[3].append(lambda: sums.first((2,)))
+    events[5] = [lambda: sums.second((2,))]
+    events_two = {count - 3: [lambda: sums.third((0, 1))], count - 2: [lambda: sums.third((2,))]}
+
+    def between(table):
+        def run(step):
+            for when, actions in table.items():
+                def act(actions=actions):
+                    for action in actions:
+                        action()
+
+                if isinstance(step, int):
+                    if step == when:
+                        act()
+                else:
+                    pl.when(step == when)(act)
+
+        return run
+
+    ring_scatter(ring, partial, slots, sends, recvs, rows, finish, between(events))
+    ring_gather(ring, low, full, sends_two, recvs_two, local, rows, between(events_two))
     sums.last()
 
 
-def ffn_back(grad_gate, grad_up, w_gate, w_up, resid, cotangent, gain, grads, count, groups):
+def ffn_back(grad_gate, grad_up, hidden, w_gate, w_up, resid, cotangent, gain, inputs, cotangents, count, groups):
     rows, model = resid.shape
+    slots, inner = grad_up.shape
+    shapes = [(inner, model)] * 3
     return pl.pallas_call(
         functools.partial(ffn_back_kernel, count, groups, rows),
         name="ffn_back",
         out_shape=[
             jax.ShapeDtypeStruct((rows, model), F32),
-            jax.ShapeDtypeStruct((count * rows, model), BF16),
+            jax.ShapeDtypeStruct((slots, model), BF16),
             jax.ShapeDtypeStruct((1, model), F32),
         ]
-        + [jax.ShapeDtypeStruct(g.shape, BF16) for g in grads],
-        in_specs=[VMEM] * 10,
+        + [jax.ShapeDtypeStruct(shape, BF16) for shape in shapes],
+        in_specs=[VMEM] * 8 + [ANY] * 2,
         out_specs=[VMEM, ANY, VMEM] + [ANY] * 3,
         scratch_shapes=[ring_slots(count, rows, model), pltpu.VMEM((rows, model), BF16)]
+        + [pltpu.VMEM(shape, BF16) for shape in shapes]
+        + [pltpu.VMEM((2, slots, model // (JOBS // 2)), BF16), pltpu.SemaphoreType.DMA((2,))]
         + ring_semaphores(count) * 2
         + [pltpu.SemaphoreType.DMA]
-        + sum_scratch([g.shape for g in grads], groups),
+        + sum_scratch(shapes, groups),
         compiler_params=ring_params(3),
         cost_estimate=pl.CostEstimate(
-            flops=4 * count * rows * model * grad_up.shape[1], bytes_accessed=600 << 20, transcendentals=0
+            flops=10 * slots * model * inner, bytes_accessed=600 << 20, transcendentals=0
         ),
-    )(grad_gate, grad_up, w_gate, w_up, resid, cotangent, gain.reshape(1, model), *grads)
+    )(grad_gate, grad_up, hidden, w_gate, w_up, resid, cotangent, gain.reshape(1, model), inputs, cotangents)
 
 
 def last_kernel(
@@ -556,7 +680,8 @@
             recv_sem=second_recvs.at[k], device_id=second_peers[k], device_id_type=MESH,
         )
 
-    sums.first()
+    every = range(len(grads))
+    sums.first(every)
     for k in range(count - 1):
         first(k).start()
     half = rows // 2
@@ -571,9 +696,12 @@
         grad_tokens[start : start + size, :] = grad_resid[start : start + size, :] + through
 
     def between(step):
+        if isinstance(step, int):
+            return
+
         @pl.when(step == 1)
         def _():
-            sums.second()
+            sums.second(every)
             for k in range(count - 1):
                 first(k).wait()
             mine = small[0:8]
@@ -592,7 +720,7 @@
             for k in range(groups - 1):
                 mine = mine + second_box[k]
             total[...] = mine
-            sums.third()
+            sums.third(every)
 
     ring_scatter(ring, partial, slots, sends, recvs, rows, finish, between)
     sums.last()
@@ -622,7 +750,7 @@
     )(terms, tokens, grad_resid, gain.reshape(1, model), small, *grads)
 
 
-def spread_hops(step, chunks, count, begin, hop, end):
+def spread_hops(step, chunks, count, begin, hop):
     each = -(-(count - 1) // (chunks - 1))
 
     @pl.when(step == 0)
@@ -635,10 +763,6 @@
         @pl.when((number > 0) & (number < count - 1))
         def _():
             hop(number)
-
-    @pl.when(step == chunks - 1)
-    def _():
-        end()
 
 
 def forward_kernel(
@@ -665,7 +789,6 @@
         step, chunks, count,
         lambda: (greet(ring), gather.begin()),
         gather.hop,
-        lambda: (gather.arrived(count - 1), gather.end()),
     )
     rows, seg_rows, seg_columns, before, last = chunk_masks(starts, lengths, seqs, first, size)
     same = seg_rows == seg_columns
@@ -728,6 +851,11 @@
         delta_out[:, cols] = out
         normal = out * lax.rsqrt(jnp.mean(out * out, axis=1, keepdims=True) + 1e-5) * head_gain
         mixed[:, cols] = (normal * opened[:, cols] * live).astype(BF16)
+
+    @pl.when(step == chunks - 1)
+    def _():
+        gather.arrived(count - 1)
+        gather.end()
 
 
 def forward_mixer(tokens, w_query, w_key, w_value, w_gate, w_beta, taps_query, taps_key, taps_value, gain, gain_first, starts, lengths, side, count):
@@ -810,7 +938,6 @@
         step, chunks, count,
         lambda: (greet(ring), scatter.begin()),
         scatter.hop,
-        scatter.end,
     )
     rows, seg_rows, seg_columns, before, last = chunk_masks(starts, lengths, seqs, first, size)
     same = seg_rows == seg_columns
@@ -936,6 +1063,7 @@
             (gw_out, a_out),
         ):
             target[...] = source[...].astype(target.dtype)
+        scatter.end()
 
 
 def backward_mixer(tokens, grad_attended, saved, w_query, w_key, w_value, w_gate, w_beta, w_out, taps_query, taps_key, taps_value, gain, gain_first, starts, lengths, hidden, w_down, resid, count):
@@ -981,11 +1109,6 @@
     )(starts, lengths, tokens, grad_attended, *saved, w_query, w_key, w_value, w_gate, w_beta, w_out, taps_query, taps_key, taps_value, gain.reshape(1, width), gain_first.reshape(1, model), hidden, w_down, resid)
 
 
-def silu_parts(value):
-    sig = jax.nn.sigmoid(value)
-    return sig, value * sig
-
-
 def make_shards(groups, count):
     def shards(
         tokens, attn_gain, w_query, w_key, w_value, conv_query, conv_key, conv_value, w_beta, w_gate_out,
@@ -1000,20 +1123,12 @@
             conv_query, conv_key, conv_value, head_gain, attn_gain, seq_starts, seq_lengths, cotangent, count,
         )
         grad_full, saved = saved[-1], saved[:-1]
-        resid, ffn_full = attend(saved[0], w_out, tokens, ffn_gain, count)
-        gate_pre = jnp.dot(ffn_full, w_gate, preferred_element_type=F32)
-        up_pre = jnp.dot(ffn_full, w_up, preferred_element_type=F32)
-        sig, silu_gate = silu_parts(gate_pre)
-        hidden = (silu_gate * up_pre).astype(BF16)
-        grad_hidden = jnp.einsum("sd,fd->sf", grad_full, w_down, preferred_element_type=F32)
-        grad_gate = (grad_hidden * up_pre * sig * (1.0 + gate_pre * (1.0 - sig))).astype(BF16)
-        grad_up = (grad_hidden * silu_gate).astype(BF16)
-        gw_down = jnp.einsum("sf,sd->fd", hidden, grad_full, preferred_element_type=F32)
-        gw_gate = jnp.einsum("sd,sf->fd", ffn_full, grad_gate, preferred_element_type=F32)
-        gw_up = jnp.einsum("sd,sf->fd", ffn_full, grad_up, preferred_element_type=F32)
+        resid, ffn_full, hidden, grad_gate, grad_up = attend(
+            saved[0], w_out, tokens, ffn_gain, w_gate.T, w_up.T, w_down, grad_full, count
+        )
         grad_resid, grad_attended, g_second, *ffn_grads = ffn_back(
-            grad_gate, grad_up, w_gate.T, w_up.T, resid, cotangent, ffn_gain,
-            [g.astype(BF16) for g in (gw_gate, gw_up, gw_down)], count, groups,
+            grad_gate, grad_up, hidden, w_gate.T, w_up.T, resid, cotangent, ffn_gain, ffn_full, grad_full,
+            count, groups,
         )
         pulled = backward_mixer(
             tokens_full, grad_attended, saved, w_query, w_key, w_value, w_gate_out, beta_rows, w_out,

time: 816 us -> 760 us (0.931)
  matrix products: 59 us -> 0 us
    dot_general x6 -> x0, matrix products: 59 us -> none  [the longest x1 13.9 us: shards(): up_pre = jnp.dot(ffn_full, w_up, preferred_element_type=F32)]
where the time goes in v4:
time: 760 us; the launch traced here: 750 us
  Pallas kernels  713 us (94%)
  other arithmetic  21.5 us (3%)
  local copies, waits for them, and re-layouts  14.1 us (2%)
    pallas_call x1, Pallas kernels, ffn_back(): pl.pallas_call(functools.partial(ffn_back_kernel, count, groups, rows), n...  172 us
    pallas_call x1, Pallas kernels, attend(): pl.pallas_call(functools.partial(attend_kernel, count, rows), name='atten...  169 us
    pallas_call x1, Pallas kernels, last_step(): pl.pallas_call(functools.partial(last_kernel, count, groups, rows), name=...  99.4 us
    pallas_call x1, Pallas kernels, backward_mixer(): pl.pallas_call(functools.partial(backward_kernel, heads, width, seqs, chu...  97.7 us
    pallas_call x1, Pallas kernels, forward_mixer(): pl.pallas_call(functools.partial(forward_kernel, heads, width, seqs, coun...  91.3 us
    pallas_call x1, Pallas kernels, gather_tokens(): pl.pallas_call(functools.partial(gather_kernel, count, rows), name='gathe...  84.5 us

profile of v4, /device:TPU:0, one launch (start us, length us, event | category | flops | bytes accessed | tf_op | source)
XLA Modules:
  0.0 749.6 jit_solution(15712991442465072296)
XLA Ops:
  0.7 1.3 reshape.48.gain_first.gain
  1.9 84.5 %gather_tokens.1.tokens = bf16[2048,2048]{1,0:T(8,128)(2,1)} custom-call(bf16[256,2048]{1,0:T(8,128)(2,1)} %tokens.3), custom_call_target="tpu_custom_call" | custom-call | bytes 314572800 | tf_op jit(solution)/shard_map/gather_tokens/pallas_call | solution.py:411
  86.5 0.0 copy-start.8
  86.5 91.3 %mixer_forward.1 = (bf16[2048,256]{1,0:T(8,128)(2,1)}, f32[2048,256]{1,0:T(8,128)}, f32[2048,256]{1,0:T(8,128)}, f32[2048,256]{1,0:T(8,128)}, f32[2048,256]{1,0:...) custom-call(s32[1,2]{1,0:T(1,128)} %starts.3, ...), custom_call_target="tpu_custom_call" | custom-call | flops 19327352832 | bytes 31457280 | tf_op jit(solution)/shard_map/mixer_forward/pallas_call | solution.py:877
  177.8 0.0 copy-done.8
  177.8 0.6 reshape.49.gain
  178.4 168.6 %attend.1 = (f32[256,2048]{1,0:T(8,128)}, bf16[2048,2048]{1,0:T(8,128)(2,1)}, bf16[2048,704]{1,0:T(8,128)(2,1)}, bf16[2048,704]{1,0:T(8,128)(2,1)}, bf16[2048,704]{1,0:T(8,128)(2,1)}) custom-call(bf16[2048,256]{1,0:T(8,128)(2,1)} %get-tuple-element.62.mixed, bf16[256,2048]{1,0:T(8,128)(2,1)} %w_out.3, bf16[256,2048]{1,0:T(8,128)(2,1)} %tokens.3, ...), custom_call_target="tpu_custom_call" | custom-call | flops 19864223744 | bytes 629145600 | tf_op jit(solution)/shard_map/attend/pallas_call | solution.py:511
  347.1 171.5 %ffn_back.1 = (f32[256,2048]{1,0:T(8,128)}, bf16[2048,2048]{1,0:T(8,128)(2,1)}, f32[1,2048]{1,0:T(1,128)}, bf16[704,2048]{1,0:T(8,128)(2,1)}, bf16[704,2048]{1,0:T(8,128)(2,1)}, /*index=5*/bf16[704,2048]{1,0:T(8,128)(2,1)}) custom-call(bf16[2048,704]{1,0:T(8,128)(2,1)} %get-tuple-element.64.grad_gate, bf16[2048,704]{1,0:T(8,128)(2,1)} %get-tuple-element.65.grad_up, ...), custom_call_target="tpu_custom_call" | custom-call | flops 29527900160 | bytes 629145600 | tf_op jit(solution)/shard_map/ffn_back/pallas_call | solution.py:629
  518.6 8.7 %convert_bitcast_fusion = (f32[2048,704]{0,1:T(8,128)}, f32[2048,704]{0,1:T(8,128)}) fusion(bf16[704,2048]{1,0:T(8,128)(2,1)} %get-tuple-element.105, bf16[704,2048]{1,0:T(8,128)(2,1)} %get-tuple-element.104), kind=kLoop, calls=%fused_computation | loop fusion | flops 2883584 | bytes 17301504 | tf_op jit(solution)/shard_map/transpose | solution.py:1179
  527.2 0.0 copy-start.7
  527.2 97.7 %mixer_backward.1 = (bf16[2048,2048]{1,0:T(8,128)(2,1)}, bf16[2048,256]{1,0:T(8,128)(2,1)}, bf16[2048,256]{1,0:T(8,128)(2,1)}, bf16[2048,256]{1,0:T(8,128)(2,1)}...) custom-call(s32[1,2]{1,0:T(1,128)} %starts.3, ...), custom_call_target="tpu_custom_call" | custom-call | flops 25769803776 | bytes 54525952 | tf_op jit(solution)/shard_map/mixer_backward/pallas_call | solution.py:1085
  624.9 0.7 select_maximum_fusion
  625.6 0.6 pad.8
  626.3 0.0 copy-done.7
  626.3 2.7 concatenate.7.small
  629.0 99.4 %last_step.1 = (f32[256,2048]{1,0:T(8,128)}, f32[16,2048]{1,0:T(8,128)}, bf16[2048,256]{1,0:T(8,128)(2,1)}, bf16[2048,256]{1,0:T(8,128)(2,1)}, bf16[2048,256]{1,...) custom-call(bf16[2048,2048]{1,0:T(8,128)(2,1)} %get-tuple-element.83.terms, ...), custom_call_target="tpu_custom_call" | custom-call | bytes 314572800 | tf_op jit(solution)/shard_map/last_step/pallas_call | solution.py:731
  728.4 0.0 copy-start.5
  728.4 0.0 copy-start.4
  728.4 2.8 convert_element_type.24
  731.3 0.0 copy-done.5
  731.3 0.0 copy-start.3
  731.3 1.5 convert_element_type.25
  732.8 0.0 copy-done.4
  732.8 0.0 copy-start.2
  732.8 1.5 convert_element_type.26
  734.2 0.0 copy-done.3
  734.2 0.0 copy-start
  734.2 1.5 convert_element_type.27
  735.7 0.0 copy-done.2
  735.7 1.6 convert_element_type.28
  737.3 1.5 fusion
  738.8 1.4 slice_bitcast_fusion
  740.3 1.3 fusion.1
  741.6 1.2 slice_bitcast_fusion.1
  742.8 0.0 copy-done
  742.8 0.0 copy-start.6
  742.8 3.3 convert_element_type.29
  746.1 0.0 copy-done.6
  746.1 0.0 copy-start.1
  746.1 1.0 copy.38
  747.1 1.0 copy-done.1
  748.1 1.3 copy.39
  (2 shorter events, 0.0 us)
Async XLA Ops:
  86.5 91.4 %copy-start.8 = (bf16[2048]{0:T(1024)(128)(2,1)S(1)}, bf16[2048]{0:T(1024)(128)(2,1)}, u32[]{:S(2)}) copy-start(bf16[2048]{0:T(1024)(128)(2,1)} %param.31) | copy-start | bytes 12292
  527.2 99.0 %copy-start.7 = (f32[1,2048]{1,0:T(1,128)S(1)}, f32[1,2048]{1,0:T(1,128)}, u32[]{:S(2)}) copy-start(f32[1,2048]{1,0:T(1,128)} %get-tuple-element.86) | copy-start | bytes 24580
  728.4 2.9 copy-start.5
  728.4 4.3 copy-start.4
  731.3 3.0 copy-start.3
  732.8 3.0 copy-start.2
  734.2 8.5 %copy-start = (bf16[704,2048]{1,0:T(8,128)(2,1)S(1)}, bf16[704,2048]{1,0:T(8,128)(2,1)}, u32[]{:S(2)}) copy-start(bf16[704,2048]{1,0:T(8,128)(2,1)} %get-tuple-element.106) | copy-start | bytes 8650756
  742.8 3.3 copy-start.6
  746.1 2.0 copy-start.1

commit v5 on v4

--- a/solution.py
+++ b/solution.py
@@ -203,10 +203,10 @@
         self.half, self.finish = rows // 2, finish
         self.rows, self.piece = rows, rows // (2 * SUBS)
 
-    def terms(self, first, second):
-        half = self.half
+    def terms(self, step):
+        half, first, second = self.half, self.ring.at(-1 - step), self.ring.at(1 + step)
         return self.partial(
-            pl.multiple_of(first * self.rows, half), pl.multiple_of(second * self.rows + half, half)
+            pl.multiple_of(first * self.rows, half), pl.multiple_of(second * self.rows + half, half), step
         )
 
     def part(self, terms, way, sub):
@@ -217,13 +217,13 @@
         return scatter_copy(self.ring, self.slots, self.sends, self.recvs, way, sub, step)
 
     def begin(self):
-        terms = self.terms(self.ring.at(-1), self.ring.at(1))
+        terms = self.terms(0)
         for sub, way in PAIRS:
             self.slots[way, sub, 0] = self.part(terms, way, sub).astype(BF16)
             self.copy(way, sub, 0).start()
 
     def hop(self, step):
-        terms = self.terms(self.ring.at(-1 - step), self.ring.at(1 + step))
+        terms = self.terms(step)
         for sub, way in PAIRS:
             self.copy(way, sub, step - 1).wait_recv()
             self.slots[way, sub, step] = (
@@ -233,7 +233,7 @@
 
     def end(self):
         count = self.ring.count
-        terms = self.terms(self.ring.me, self.ring.me)
+        terms = self.terms(count - 1)
         for sub, way in PAIRS:
             self.copy(way, sub, count - 2).wait_recv()
             self.finish(
@@ -442,7 +442,7 @@
     box_copy(0).start()
     greet(ring)
 
-    def partial(first, second):
+    def partial(first, second, step):
         return mm(jnp.concatenate([mixed[pl.ds(first, half), :], mixed[pl.ds(second, half), :]], 0), w_out[...])
 
     def finish(start, size, attended):
@@ -568,7 +568,7 @@
     grad_gain[...] = jnp.zeros_like(grad_gain)
     half = rows // 2
 
-    def partial(first, second):
+    def partial(first, second, step):
         gates = jnp.concatenate([grad_gate[pl.ds(first, half), :], grad_gate[pl.ds(second, half), :]], 0)
         ups = jnp.concatenate([grad_up[pl.ds(first, half), :], grad_up[pl.ds(second, half), :]], 0)
         return mm(gates, w_gate[...]) + mm(ups, w_up[...])
@@ -656,10 +656,10 @@
     grads, rest = rest[:5], rest[5:]
     grad_tokens, total = rest[:2]
     targets, rest = rest[2:7], rest[7:]
-    slots, first_box, second_box, second_own, sends, recvs = rest[:6]
-    first_sends, first_recvs, second_sends, second_recvs = rest[6:10]
+    slots, first_box, second_box, second_own, boxes, box_sems, sends, recvs = rest[:8]
+    first_sends, first_recvs, second_sends, second_recvs = rest[8:12]
     ring = Ring(count)
-    sums = GroupSum(ring, groups, grads, rest[10:15], rest[15:20], targets, *rest[20:])
+    sums = GroupSum(ring, groups, grads, rest[12:17], rest[17:22], targets, *rest[22:])
     me, group = ring.me, ring.group
     first_peers = [(group, (me + k) % count) for k in range(1, count)]
     second_peers = [((group + k) % groups, me) for k in range(1, groups)]
@@ -686,8 +686,24 @@
         first(k).start()
     half = rows // 2
 
-    def partial(first, second):
-        return jnp.concatenate([terms[pl.ds(first, half), :], terms[pl.ds(second, half), :]], 0).astype(F32)
+    def box_copy(way, start, slot):
+        return pltpu.make_async_copy(
+            terms.at[pl.ds(start, half), :], boxes.at[slot, way], box_sems.at[slot, way]
+        )
+
+    def fetch(step):
+        for way, owner in ((0, ring.at(-1 - step)), (1, ring.at(1 + step))):
+            box_copy(way, pl.multiple_of(owner * rows + way * half, half), step % 2).start()
+
+    def partial(first, second, step):
+        for way, start in ((0, first), (1, second)):
+            box_copy(way, start, step % 2).wait()
+
+        @pl.when(step + 1 < count)
+        def _():
+            fetch(step + 1)
+
+        return jnp.concatenate([boxes[step % 2, 0], boxes[step % 2, 1]], 0).astype(F32)
 
     def finish(start, size, grad):
         value = tokens[start : start + size, :].astype(F32)
@@ -695,33 +711,35 @@
         through, pieces = norm_back(value, scale, gain[...].astype(F32), grad)
         grad_tokens[start : start + size, :] = grad_resid[start : start + size, :] + through
 
+    def early():
+        sums.second(every)
+        for k in range(count - 1):
+            first(k).wait()
+        mine = small[0:8]
+        for k in range(count - 1):
+            mine = mine + first_box[k]
+        second_own[0:8] = mine
+        second_own[8:] = small[8:]
+        for k in range(groups - 1):
+            second(k).start()
+
+    def late():
+        for k in range(groups - 1):
+            second(k).wait()
+        mine = second_own[...]
+        for k in range(groups - 1):
+            mine = mine + second_box[k]
+        total[...] = mine
+        sums.third(every)
+
     def between(step):
         if isinstance(step, int):
-            return
-
-        @pl.when(step == 1)
-        def _():
-            sums.second(every)
-            for k in range(count - 1):
-                first(k).wait()
-            mine = small[0:8]
-            for k in range(count - 1):
-                mine = mine + first_box[k]
-            second_own[0:8] = mine
-            second_own[8:] = small[8:]
-            for k in range(groups - 1):
-                second(k).start()
-
-        @pl.when(step == count - 2)
-        def _():
-            for k in range(groups - 1):
-                second(k).wait()
-            mine = second_own[...]
-            for k in range(groups - 1):
-                mine = mine + second_box[k]
-            total[...] = mine
-            sums.third(every)
-
+            if step == 0:
+                early()
+        else:
+            pl.when(step == count - 2)(late)
+
+    fetch(0)
     ring_scatter(ring, partial, slots, sends, recvs, rows, finish, between)
     sums.last()
 
@@ -733,13 +751,15 @@
         name="last_step",
         out_shape=[jax.ShapeDtypeStruct((rows, model), F32), jax.ShapeDtypeStruct(small.shape, F32)]
         + [jax.ShapeDtypeStruct(g.shape, BF16) for g in grads],
-        in_specs=[VMEM] * (5 + len(grads)),
+        in_specs=[ANY] + [VMEM] * (4 + len(grads)),
         out_specs=[VMEM, VMEM] + [ANY] * len(grads),
         scratch_shapes=[
             ring_slots(count, rows, model),
             pltpu.VMEM((count - 1, 8, model), F32),
             pltpu.VMEM((groups - 1,) + small.shape, F32),
             pltpu.VMEM(small.shape, F32),
+            pltpu.VMEM((2, 2, rows // 2, model), BF16),
+            pltpu.SemaphoreType.DMA((2, 2)),
         ]
         + ring_semaphores(count)
         + [pltpu.SemaphoreType.DMA((count - 1,))] * 2
@@ -748,6 +768,42 @@
         compiler_params=ring_params(4),
         cost_estimate=pl.CostEstimate(flops=0, bytes_accessed=300 << 20, transcendentals=0),
     )(terms, tokens, grad_resid, gain.reshape(1, model), small, *grads)
+
+
+def results_kernel(heads, taps, wide, width, total, *refs):
+    number = (len(refs) - 7) // 2
+    for source, target in zip(refs[:number], refs[number : 2 * number]):
+        target[...] = source[...].astype(target.dtype)
+    g_first, g_second, g_head, gt_query, gt_key, gt_value, g_beta = refs[2 * number :]
+
+    @pl.when(pl.program_id(0) == 0)
+    def _():
+        g_first[...] = total[0:1, :]
+        g_second[...] = total[1:2, :]
+        g_head[...] = total[2:3, 0:width]
+        row = 8 + heads
+        for place, target in enumerate((gt_query, gt_key, gt_value)):
+            target[...] = total[row : row + taps, place * wide : (place + 1) * wide]
+        g_beta[...] = total[8 : 8 + heads, :]
+
+
+def results(total, arrays, heads, taps, wide, width):
+    model = total.shape[1]
+    steps = next(n for n in (8, 4, 2, 1) if all(a.shape[0] % (8 * n) == 0 for a, _ in arrays))
+    small = [(1, model), (1, model), (1, width)] + [(taps, wide)] * 3 + [(heads, model)]
+    piece = lambda a: pl.BlockSpec((a.shape[0] // steps, a.shape[1]), lambda n: (n, 0))
+    whole = lambda shape: pl.BlockSpec(shape, lambda n: (0, 0))
+    return pl.pallas_call(
+        functools.partial(results_kernel, heads, taps, wide, width),
+        name="results",
+        grid=(steps,),
+        out_shape=[jax.ShapeDtypeStruct(a.shape, kind) for a, kind in arrays]
+        + [jax.ShapeDtypeStruct(shape, F32) for shape in small],
+        in_specs=[whole(total.shape)] + [piece(a) for a, _ in arrays],
+        out_specs=[piece(a) for a, _ in arrays] + [whole(shape) for shape in small],
+        compiler_params=pltpu.CompilerParams(vmem_limit_bytes=56 << 20),
+        cost_estimate=pl.CostEstimate(flops=0, bytes_accessed=48 << 20, transcendentals=0),
+    )(total, *[a for a, _ in arrays])
 
 
 def spread_hops(step, chunks, count, begin, hop):
@@ -904,13 +960,17 @@
     )(starts, lengths, tokens, w_query, w_key, w_value, w_gate, w_beta, taps_query, taps_key, taps_value, gain.reshape(1, width), gain_first.reshape(1, model), side)
 
 
+def small_rows(heads, taps):
+    return -(-(8 + heads + taps) // 8) * 8
+
+
 def backward_kernel(
     heads, width, seqs, chunks, count, rows_own,
     starts, lengths, tokens, grad_attended, mixed, p_query, p_key, p_value, p_gate, p_beta,
     z_query, z_key, z_value, delta_out, change_in, inverse_in, state_in,
     w_query, w_key, w_value, w_gate, w_beta, w_out, taps_query, taps_key, taps_value, gain, gain_first,
-    hidden, w_down, resid, grad_normed, gw_query, gw_key, gw_value, gw_gate, gw_beta, gw_out,
-    gt_query, gt_key, gt_value, g_gain, g_first, output,
+    hidden, w_down, resid, g_second, grad_normed, gw_query, gw_key, gw_value, gw_gate, gw_out,
+    small, output,
     a_query, a_key, a_value, a_gate, a_out, head_query, head_key, head_value, flow, slots, sends, recvs,
 ):
     step = pl.program_id(0)
@@ -919,14 +979,15 @@
 
     @pl.when(step == 0)
     def _():
-        for ref in (a_query, a_key, a_value, a_gate, gw_beta, a_out, gt_query, gt_key, gt_value, g_gain, g_first, flow):
+        for ref in (a_query, a_key, a_value, a_gate, a_out, small, flow):
             ref[...] = jnp.zeros_like(ref)
+        small[1:2, :] = g_second[...]
         for ref in (head_query, head_key, head_value):
             ref[size:, :] = jnp.zeros((8, ref.shape[1]), F32)
 
     half = rows_own // 2
 
-    def partial(one, two):
+    def partial(one, two, number):
         return mm(jnp.concatenate([hidden[pl.ds(one, half), :], hidden[pl.ds(two, half), :]], 0), w_down[...])
 
     def finish(start, length, down):
@@ -975,7 +1036,7 @@
         unit = out * root
         grads_gate.append(grad * unit * head_gain * (sig_gate * (1.0 + gate * (1.0 - sig_gate))))
         grad_normal = grad * silu_gate
-        g_gain[...] += jnp.sum(grad_normal * unit, axis=0, keepdims=True)
+        small[2:3, 0:width] += jnp.sum(grad_normal * unit, axis=0, keepdims=True)
         push = grad_normal * head_gain
         grad_out = scale * root * (push - unit * jnp.mean(push * unit, axis=1, keepdims=True))
 
@@ -1021,23 +1082,28 @@
         grads_key.append(du_k * sk * (1.0 + zk * (1.0 - sk)))
         grads_value.append(grad_value * sv * (1.0 + zv * (1.0 - sv)))
 
-    def unconv(parts, taps_ref, head, projected, grad_taps):
+    tap_row = 8 + heads
+    wide = heads * width
+
+    def unconv(parts, taps_ref, head, projected, place):
+        lanes = slice(place * wide, (place + 1) * wide)
         grad = jnp.concatenate(parts, axis=1)
         head[0:size, :] = grad
         tap = taps_ref[...].astype(F32)
         p = projected[...]
         result = grad * tap[0:1]
-        grad_taps[0:1, :] += jnp.sum(p * grad, axis=0, keepdims=True)
+        small[tap_row : tap_row + 1, lanes] += jnp.sum(p * grad, axis=0, keepdims=True)
         for offset in range(1, taps):
             moved = head[offset : offset + size, :] * joined[offset - 1]
             result = result + moved * tap[offset : offset + 1]
-            grad_taps[offset : offset + 1, :] += jnp.sum(p * moved, axis=0, keepdims=True)
+            row = tap_row + offset
+            small[row : row + 1, lanes] += jnp.sum(p * moved, axis=0, keepdims=True)
         head[size:, :] = grad[0:8, :]
         return result.astype(BF16)
 
-    d_query = unconv(grads_query, taps_query, head_query, p_query, gt_query)
-    d_key = unconv(grads_key, taps_key, head_key, p_key, gt_key)
-    d_value = unconv(grads_value, taps_value, head_value, p_value, gt_value)
+    d_query = unconv(grads_query, taps_query, head_query, p_query, 0)
+    d_key = unconv(grads_key, taps_key, head_key, p_key, 1)
+    d_value = unconv(grads_value, taps_value, head_value, p_value, 2)
     d_gate = jnp.concatenate(grads_gate, axis=1).astype(BF16)
     spare = [jnp.zeros((size, 1), F32)] * (w_beta.shape[0] - heads)
     d_beta = jnp.concatenate(grads_beta + spare, axis=1).astype(BF16)
@@ -1049,12 +1115,12 @@
         + mm(d_beta, w_beta[...])
     )
     grad_normed[...] = grad_inputs.astype(BF16)
-    g_first[...] += jnp.sum(grad_inputs * unit_rows, axis=0, keepdims=True)
+    small[0:1, :] += jnp.sum(grad_inputs * unit_rows, axis=0, keepdims=True)
     a_query[...] += mm(inputs, d_query, (0, 0))
     a_key[...] += mm(inputs, d_key, (0, 0))
     a_value[...] += mm(inputs, d_value, (0, 0))
     a_gate[...] += mm(inputs, d_gate, (0, 0))
-    gw_beta[...] += mm(d_beta, inputs, (0, 0))
+    small[8 : 8 + heads, :] += mm(d_beta, inputs, (0, 0))[:heads]
 
     @pl.when(step == chunks - 1)
     def _():
@@ -1066,7 +1132,7 @@
         scatter.end()
 
 
-def backward_mixer(tokens, grad_attended, saved, w_query, w_key, w_value, w_gate, w_beta, w_out, taps_query, taps_key, taps_value, gain, gain_first, starts, lengths, hidden, w_down, resid, count):
+def backward_mixer(tokens, grad_attended, saved, w_query, w_key, w_value, w_gate, w_beta, w_out, taps_query, taps_key, taps_value, gain, gain_first, starts, lengths, hidden, w_down, resid, g_second, count):
     slots, model = tokens.shape
     wide = w_query.shape[1]
     width = gain.shape[0]
@@ -1079,8 +1145,8 @@
     piece = lambda shape: pl.BlockSpec(shape, lambda n: (chunks - 1 - n,) + (0,) * (len(shape) - 1))
     rows = lambda a: piece((CHUNK, a.shape[1]))
     outs = (
-        [((slots, model), BF16)] + [((model, wide), BF16)] * 4 + [(w_beta.shape, F32), ((wide, model), BF16)]
-        + [((taps, wide), F32)] * 3 + [((1, width), F32), ((1, model), F32), (resid.shape, BF16)]
+        [((slots, model), BF16)] + [((model, wide), BF16)] * 4 + [((wide, model), BF16)]
+        + [((small_rows(heads, taps), model), F32), (resid.shape, BF16)]
     )
     return pl.pallas_call(
         functools.partial(backward_kernel, heads, width, seqs, chunks, count, slots // count),
@@ -1093,7 +1159,7 @@
         + [fixed((model, wide))] * 4
         + [fixed(w_beta.shape), fixed((wide, model))]
         + [fixed((taps, wide))] * 3
-        + [fixed((1, width)), fixed((1, model)), fixed(hidden.shape), fixed(w_down.shape), fixed(resid.shape)],
+        + [fixed((1, width)), fixed((1, model)), fixed(hidden.shape), fixed(w_down.shape), fixed(resid.shape), fixed(g_second.shape)],
         out_specs=[piece((CHUNK, model))] + [fixed(s) for s, d in outs[1:]],
         scratch_shapes=[pltpu.VMEM((model, wide), F32)] * 4
         + [pltpu.VMEM((wide, model), F32)]
@@ -1106,7 +1172,7 @@
             bytes_accessed=slots * model * 6 + 10 * model * wide * 2 + slots * wide * 36,
             transcendentals=slots * wide * 8,
         ),
-    )(starts, lengths, tokens, grad_attended, *saved, w_query, w_key, w_value, w_gate, w_beta, w_out, taps_query, taps_key, taps_value, gain.reshape(1, width), gain_first.reshape(1, model), hidden, w_down, resid)
+    )(starts, lengths, tokens, grad_attended, *saved, w_query, w_key, w_value, w_gate, w_beta, w_out, taps_query, taps_key, taps_value, gain.reshape(1, width), gain_first.reshape(1, model), hidden, w_down, resid, g_second)
 
 
 def make_shards(groups, count):
@@ -1133,51 +1199,38 @@
         pulled = backward_mixer(
             tokens_full, grad_attended, saved, w_query, w_key, w_value, w_gate_out, beta_rows, w_out,
             conv_query, conv_key, conv_value, head_gain, attn_gain, seq_starts, seq_lengths,
-            hidden, w_down, resid, count,
-        )
-        terms, gw_query, gw_key, gw_value, gw_gate_out, gw_beta, gw_out = pulled[:7]
-        gt_query, gt_key, gt_value, g_head, g_first, output = pulled[7:]
-        wide = gt_query.shape[1]
-        gw_beta = gw_beta[:heads]
-        taps = gt_query.shape[0]
-        small = jnp.concatenate(
-            [
-                g_first,
-                g_second,
-                jnp.pad(g_head, ((0, 0), (0, model - g_head.shape[1]))),
-                jnp.zeros((5, model), F32),
-                gw_beta,
-                jnp.pad(
-                    jnp.concatenate([gt_query, gt_key, gt_value], 1), ((0, 0), (0, model - 3 * wide))
-                ),
-                jnp.zeros((-(heads + taps) % 8, model), F32),
-            ],
-            0,
-        )
+            hidden, w_down, resid, g_second, count,
+        )
+        terms, gw_query, gw_key, gw_value, gw_gate_out, gw_out, small, output = pulled
         grad_tokens, total, *mixer_grads = last_step(
             terms, tokens, grad_resid, attn_gain, small,
             (gw_query, gw_key, gw_value, gw_gate_out, gw_out), count, groups,
         )
-        mixer_grads = [g.astype(F32) for g in mixer_grads]
-        tap_rows = total[8 + heads : 8 + heads + taps]
+        taps, wide = conv_query.shape
+        output, grad_tokens, *rest = results(
+            total,
+            [(output, BF16), (grad_tokens, F32)] + [(g, F32) for g in (*mixer_grads, *ffn_grads)],
+            heads, taps, wide, head_gain.shape[0],
+        )
+        grads, (g_first, g_second, g_head, gt_query, gt_key, gt_value, g_beta) = rest[:8], rest[8:]
         return (
             output,
             grad_tokens,
-            total[0],
-            mixer_grads[0],
-            mixer_grads[1],
-            mixer_grads[2],
-            tap_rows[:, :wide],
-            tap_rows[:, wide : 2 * wide],
-            tap_rows[:, 2 * wide : 3 * wide],
-            total[8 : 8 + heads].T,
-            mixer_grads[3],
-            total[2, : head_gain.shape[0]],
-            mixer_grads[4],
-            total[1],
-            ffn_grads[0].astype(F32).T,
-            ffn_grads[1].astype(F32).T,
-            ffn_grads[2].astype(F32),
+            g_first[0],
+            grads[0],
+            grads[1],
+            grads[2],
+            gt_query,
+            gt_key,
+            gt_value,
+            g_beta.T,
+            grads[3],
+            g_head[0],
+            grads[4],
+            g_second[0],
+            grads[5].T,
+            grads[6].T,
+            grads[7],
         )
 
     return shards

time: 760 us -> 742 us (0.976)
  other arithmetic: 21.5 us -> 0 us
  Pallas kernels: 713 us -> 728 us
  local copies, waits for them, and re-layouts: 14.1 us -> 2.58 us
    pallas_call x0 -> x1, Pallas kernels: none -> 17.6 us  [results(): pl.pallas_call(functools.partial(results_kernel, heads, taps, wide, width...]
    convert_element_type x6 -> x0, other arithmetic: 12.1 us -> none  [the longest x5 8.84 us: shards(): mixer_grads = [g.astype(F32) for g in mixer_grads]]
    transpose x1 -> x0, other arithmetic: 8.67 us -> none  [shards(): ffn_grads[1].astype(F32)]
where the time goes in v5:
time: 742 us; the launch traced here: 732 us
  Pallas kernels  728 us (98%)
    pallas_call x1, Pallas kernels, ffn_back(): pl.pallas_call(functools.partial(ffn_back_kernel, count, groups, rows), n...  172 us
    pallas_call x1, Pallas kernels, attend(): pl.pallas_call(functools.partial(attend_kernel, count, rows), name='atten...  169 us
    pallas_call x1, Pallas kernels, backward_mixer(): pl.pallas_call(functools.partial(backward_kernel, heads, width, seqs, chu...  97.9 us
    pallas_call x1, Pallas kernels, last_step(): pl.pallas_call(functools.partial(last_kernel, count, groups, rows), name=...  97.1 us
    pallas_call x1, Pallas kernels, forward_mixer(): pl.pallas_call(functools.partial(forward_kernel, heads, width, seqs, coun...  91.3 us
    pallas_call x1, Pallas kernels, gather_tokens(): pl.pallas_call(functools.partial(gather_kernel, count, rows), name='gathe...  84.5 us
    pallas_call x1, Pallas kernels, results(): pl.pallas_call(functools.partial(results_kernel, heads, taps, wide, width...  17.6 us

profile of v5, /device:TPU:0, one launch (start us, length us, event | category | flops | bytes accessed | tf_op | source)
XLA Modules:
  0.0 732.0 jit_solution(11564904402843048610)
XLA Ops:
  0.7 1.3 reshape.48.gain_first.gain
  1.9 1.3 reshape.49.gain
  3.2 84.5 %gather_tokens.1.tokens = bf16[2048,2048]{1,0:T(8,128)(2,1)} custom-call(bf16[256,2048]{1,0:T(8,128)(2,1)} %tokens.3), custom_call_target="tpu_custom_call" | custom-call | bytes 314572800 | tf_op jit(solution)/shard_map/gather_tokens/pallas_call | solution.py:411
  87.8 91.3 %mixer_forward.1 = (bf16[2048,256]{1,0:T(8,128)(2,1)}, f32[2048,256]{1,0:T(8,128)}, f32[2048,256]{1,0:T(8,128)}, f32[2048,256]{1,0:T(8,128)}, f32[2048,256]{1,0:...) custom-call(s32[1,2]{1,0:T(1,128)} %starts.3, ...), custom_call_target="tpu_custom_call" | custom-call | flops 19327352832 | bytes 31457280 | tf_op jit(solution)/shard_map/mixer_forward/pallas_call | solution.py:933
  179.1 168.5 %attend.1 = (f32[256,2048]{1,0:T(8,128)}, bf16[2048,2048]{1,0:T(8,128)(2,1)}, bf16[2048,704]{1,0:T(8,128)(2,1)}, bf16[2048,704]{1,0:T(8,128)(2,1)}, bf16[2048,704]{1,0:T(8,128)(2,1)}) custom-call(bf16[2048,256]{1,0:T(8,128)(2,1)} %get-tuple-element.74.mixed, bf16[256,2048]{1,0:T(8,128)(2,1)} %w_out.3, bf16[256,2048]{1,0:T(8,128)(2,1)} %tokens.3, ...), custom_call_target="tpu_custom_call" | custom-call | flops 19864223744 | bytes 629145600 | tf_op jit(solution)/shard_map/attend/pallas_call | solution.py:511
  347.7 171.5 %ffn_back.1 = (f32[256,2048]{1,0:T(8,128)}, bf16[2048,2048]{1,0:T(8,128)(2,1)}, f32[1,2048]{1,0:T(1,128)}, bf16[704,2048]{1,0:T(8,128)(2,1)}, bf16[704,2048]{1,0:T(8,128)(2,1)}, /*index=5*/bf16[704,2048]{1,0:T(8,128)(2,1)}) custom-call(bf16[2048,704]{1,0:T(8,128)(2,1)} %get-tuple-element.76.grad_gate, bf16[2048,704]{1,0:T(8,128)(2,1)} %get-tuple-element.77.grad_up, ...), custom_call_target="tpu_custom_call" | custom-call | flops 29527900160 | bytes 629145600 | tf_op jit(solution)/shard_map/ffn_back/pallas_call | solution.py:629
  519.2 97.9 %mixer_backward.1 = (bf16[2048,2048]{1,0:T(8,128)(2,1)}, bf16[2048,256]{1,0:T(8,128)(2,1)}, bf16[2048,256]{1,0:T(8,128)(2,1)}, bf16[2048,256]{1,0:T(8,128)(2,1)}...) custom-call(s32[1,2]{1,0:T(1,128)} %starts.3, ...), custom_call_target="tpu_custom_call" | custom-call | flops 25769803776 | bytes 54525952 | tf_op jit(solution)/shard_map/mixer_backward/pallas_call | solution.py:1151
  617.1 97.1 %last_step.1 = (f32[256,2048]{1,0:T(8,128)}, f32[16,2048]{1,0:T(8,128)}, bf16[2048,256]{1,0:T(8,128)(2,1)}, bf16[2048,256]{1,0:T(8,128)(2,1)}, bf16[2048,256]{1,...) custom-call(bf16[2048,2048]{1,0:T(8,128)(2,1)} %get-tuple-element.95.terms, ...), custom_call_target="tpu_custom_call" | custom-call | bytes 314572800 | tf_op jit(solution)/shard_map/last_step/pallas_call | solution.py:749
  714.2 17.6 %results.1 = (bf16[256,2048]{1,0:T(8,128)(2,1)}, f32[256,2048]{1,0:T(8,128)}, f32[2048,256]{1,0:T(8,128)}, f32[2048,256]{1,0:T(8,128)}, f32[2048,256]{1,0:T(8,12...) custom-call(f32[16,2048]{1,0:T(8,128)} %get-tuple-element.103.total,, ...), custom_call_target="tpu_custom_call" | custom-call | bytes 50331648 | tf_op jit(solution)/shard_map/results/pallas_call | solution.py:796

commit v6 on v5

--- a/solution.py
+++ b/solution.py
@@ -79,6 +79,7 @@
 
 MESH = pl.DeviceIdType.MESH
 SUBS = 2
+PAIRS = [(sub, way) for sub in range(SUBS) for way in (0, 1)]
 
 
 def ring_position(device, count):
@@ -105,84 +106,77 @@
         return (self.group, self.at(1 if way == 0 else -1))
 
 
-def gather_copy(ring, source, target, sends, recvs, way, sub, step, origin, rows):
-    piece = rows // (2 * SUBS)
-    inside = way * (rows // 2) + sub * piece
-    start = pl.multiple_of(origin * rows + inside, piece)
-    src = target.at[pl.ds(start, piece), :] if source is None else source.at[pl.ds(inside, piece), :]
-    return pltpu.make_async_remote_copy(
-        src_ref=src,
-        dst_ref=target.at[pl.ds(start, piece), :],
-        send_sem=sends.at[way, sub, step],
-        recv_sem=recvs.at[way, sub, step],
-        device_id=ring.next(way),
-        device_id_type=MESH,
-    )
-
-
-PAIRS = [(sub, way) for sub in range(SUBS) for way in (0, 1)]
-
-
 class Gather:
-    def __init__(self, ring, source, target, sends, recvs, local, rows):
-        self.ring, self.source, self.target = ring, source, target
-        self.sends, self.recvs, self.rows = sends, recvs, rows
-        self.keep = None
-        if source is not None:
-            self.keep = pltpu.make_async_copy(
-                source, target.at[pl.ds(pl.multiple_of(ring.me * rows, rows), rows), :], local
-            )
+    def __init__(self, ring, own, view, sends, recvs, rows, subs=SUBS):
+        self.ring, self.own, self.view, self.sends, self.recvs, self.rows = ring, own, view, sends, recvs, rows
+        self.piece = rows // (2 * subs)
+        self.pairs = [(sub, way) for sub in range(subs) for way in (0, 1)]
 
     def origin(self, way, step):
         return self.ring.at(-step if way == 0 else step)
 
-    def copy(self, way, sub, step, origin, source=None):
-        return gather_copy(
-            self.ring, source, self.target, self.sends, self.recvs, way, sub, step, origin, self.rows
+    def copy(self, way, sub, step, origin, first=False):
+        inside = way * (self.rows // 2) + sub * self.piece
+        place = self.view(origin, inside, self.piece)
+        return pltpu.make_async_remote_copy(
+            src_ref=self.own(inside, self.piece) if first else place,
+            dst_ref=place,
+            send_sem=self.sends.at[way, sub, step],
+            recv_sem=self.recvs.at[way, sub, step],
+            device_id=self.ring.next(way),
+            device_id_type=MESH,
         )
 
     def begin(self):
-        if self.keep is not None:
-            self.keep.start()
-        for sub, way in PAIRS:
-            self.copy(way, sub, 0, self.ring.me, self.source).start()
+        for sub, way in self.pairs:
+            self.copy(way, sub, 0, self.ring.me, True).start()
 
     def arrived(self, step):
-        for sub, way in PAIRS:
+        for sub, way in self.pairs:
             self.copy(way, sub, step - 1, self.origin(way, step)).wait_recv()
 
     def hop(self, step):
-        for sub, way in PAIRS:
+        for sub, way in self.pairs:
             self.copy(way, sub, step - 1, self.origin(way, step)).wait_recv()
             self.copy(way, sub, step, self.origin(way, step)).start()
 
     def end(self):
         def drain(step, carry):
-            for sub, way in PAIRS:
+            for sub, way in self.pairs:
                 self.copy(way, sub, step, self.ring.me).wait_send()
             return carry
 
         lax.fori_loop(0, self.ring.count - 1, drain, 0)
-        if self.keep is not None:
-            self.keep.wait()
-
-
-def ring_gather(ring, source, target, sends, recvs, local, rows, between=None):
-    gather = Gather(ring, source, target, sends, recvs, local, rows)
-    gather.begin()
-    if between is not None:
-        between(0)
-
-    def forward(step, carry):
-        gather.hop(step)
-        if between is not None:
-            between(step)
+
+
+def row_view(ref, rows):
+    return lambda origin, start, size: ref.at[pl.ds(pl.multiple_of(origin * rows + start, size), size), :]
+
+
+def row_own(ref):
+    return lambda start, size: ref.at[pl.ds(start, size), :]
+
+
+def ring_gather(gather, between):
+    count = gather.ring.count
+
+    def run(step, carry):
+        @pl.when(step == 0)
+        def _():
+            gather.begin()
+
+        @pl.when((step > 0) & (step < count - 1))
+        def _():
+            gather.hop(step)
+
+        @pl.when(step == count - 1)
+        def _():
+            gather.arrived(step)
+
+        between(step)
         return carry
 
-    lax.fori_loop(1, ring.count - 1, forward, 0)
-    gather.arrived(ring.count - 1)
-    if between is not None:
-        between(ring.count - 1)
+    lax.fori_loop(0, count, run, 0)
     gather.end()
 
 
@@ -216,19 +210,20 @@
     def copy(self, way, sub, step):
         return scatter_copy(self.ring, self.slots, self.sends, self.recvs, way, sub, step)
 
-    def begin(self):
-        terms = self.terms(0)
-        for sub, way in PAIRS:
-            self.slots[way, sub, 0] = self.part(terms, way, sub).astype(BF16)
-            self.copy(way, sub, 0).start()
-
     def hop(self, step):
         terms = self.terms(step)
         for sub, way in PAIRS:
-            self.copy(way, sub, step - 1).wait_recv()
-            self.slots[way, sub, step] = (
-                self.slots[way, sub, step].astype(F32) + self.part(terms, way, sub)
-            ).astype(BF16)
+            term = self.part(terms, way, sub)
+
+            @pl.when(step == 0)
+            def _():
+                self.slots[way, sub, 0] = term.astype(BF16)
+
+            @pl.when(step > 0)
+            def _():
+                self.copy(way, sub, step - 1).wait_recv()
+                self.slots[way, sub, step] = (self.slots[way, sub, step].astype(F32) + term).astype(BF16)
+
             self.copy(way, sub, step).start()
 
     def end(self):
@@ -250,21 +245,13 @@
         lax.fori_loop(0, count - 1, drain, 0)
 
 
-def ring_scatter(ring, partial, slots, sends, recvs, rows, finish, between=None):
-    scatter = Scatter(ring, partial, slots, sends, recvs, rows, finish)
-    scatter.begin()
-    if between is not None:
-        between(0)
-
-    def forward(step, carry):
+def ring_scatter(scatter, between):
+    def run(step, carry):
         scatter.hop(step)
-        if between is not None:
-            between(step)
+        between(step)
         return carry
 
-    lax.fori_loop(1, ring.count - 1, forward, 0)
-    if between is not None:
-        between(ring.count - 1)
+    lax.fori_loop(0, scatter.ring.count - 1, run, 0)
     scatter.end()
 
 
@@ -382,8 +369,8 @@
     pl.semaphore_wait(barrier, len(peers))
 
 
-def ring_semaphores(count):
-    return [pltpu.SemaphoreType.DMA((2, SUBS, count - 1))] * 2
+def ring_semaphores(count, subs=SUBS):
+    return [pltpu.SemaphoreType.DMA((2, subs, count - 1))] * 2
 
 
 def ring_slots(count, rows, columns):
@@ -400,102 +387,200 @@
     )
 
 
-def gather_kernel(count, rows, source, target, sends, recvs, local):
+WEIGHT_HOPS = 3
+
+
+def gather_kernel(
+    count, groups, tokens, w_out, tokens_full, w_full,
+    sends, recvs, w_sends, w_recvs, local, far_sems, near_sems,
+):
     ring = Ring(count)
-    greet(ring)
-    ring_gather(ring, source, target, sends, recvs, local, rows)
-
-
-def gather_tokens(tokens, count):
+    rows = tokens.shape[0]
+    group, me = ring.group, ring.me
+    part = w_out.shape[0] // groups
+    across = groups // 2
+    mate = (group + 1 - 2 * (group % 2), me)
+    gather = Gather(ring, row_own(tokens), row_view(tokens_full, rows), sends, recvs, rows)
+    own_part = lambda start, size: w_out.at[pl.ds(pl.multiple_of(group * part + start, size), size), :]
+    weights = Gather(
+        ring, own_part, lambda origin, start, size: w_full.at[origin, group, pl.ds(start, size), :],
+        w_sends, w_recvs, part, 1,
+    )
+    keep = pltpu.make_async_copy(
+        tokens, tokens_full.at[pl.ds(pl.multiple_of(me * rows, rows), rows), :], local.at[0]
+    )
+    keep_part = pltpu.make_async_copy(own_part(0, part), w_full.at[me, group], local.at[1])
+
+    def far(k):
+        return pltpu.make_async_remote_copy(
+            src_ref=w_full.at[:, group], dst_ref=w_full.at[:, group],
+            send_sem=far_sems.at[0, k - 1], recv_sem=far_sems.at[1, k - 1],
+            device_id=((group + 2 * k) % groups, me), device_id_type=MESH,
+        )
+
+    def near(k):
+        held = (group + groups - 2 * k) % groups
+        return pltpu.make_async_remote_copy(
+            src_ref=w_full.at[:, held], dst_ref=w_full.at[:, held],
+            send_sem=near_sems.at[0, k], recv_sem=near_sems.at[1, k],
+            device_id=mate, device_id_type=MESH,
+        )
+
+    greet(ring, [mate] + [((group + 2 * k) % groups, me) for k in range(1, across)])
+    weights.begin()
+    gather.begin()
+    keep.start()
+    keep_part.start()
+    whole_at = -(-(count - 2) // WEIGHT_HOPS) + 1
+
+    def forward(step, carry):
+        for place in range(WEIGHT_HOPS):
+            number = (step - 1) * WEIGHT_HOPS + place + 1
+
+            @pl.when(number < count - 1)
+            def _():
+                weights.hop(number)
+
+        gather.hop(step)
+
+        @pl.when(step == whole_at)
+        def _():
+            weights.arrived(count - 1)
+            keep_part.wait()
+            for k in range(1, across):
+                far(k).start()
+            near(0).start()
+
+        return carry
+
+    lax.fori_loop(1, count - 1, forward, 0)
+    for k in range(1, across):
+        far(k).wait_recv()
+        near(k).start()
+    gather.arrived(count - 1)
+    for k in range(across):
+        near(k).wait()
+    for k in range(1, across):
+        far(k).wait_send()
+    weights.end()
+    gather.end()
+    keep.wait()
+
+
+def gather_tokens(tokens, w_out, count, groups):
     rows, model = tokens.shape
-    return pl.pallas_call(
-        functools.partial(gather_kernel, count, rows),
+    part = w_out.shape[0] // groups
+    full, w_full = pl.pallas_call(
+        functools.partial(gather_kernel, count, groups),
         name="gather_tokens",
-        out_shape=jax.ShapeDtypeStruct((count * rows, model), tokens.dtype),
-        in_specs=[ANY],
-        out_specs=ANY,
-        scratch_shapes=ring_semaphores(count) + [pltpu.SemaphoreType.DMA],
+        out_shape=[
+            jax.ShapeDtypeStruct((count * rows, model), tokens.dtype),
+            jax.ShapeDtypeStruct((count, groups, part, model), w_out.dtype),
+        ],
+        in_specs=[ANY] * 2,
+        out_specs=[ANY] * 2,
+        scratch_shapes=ring_semaphores(count)
+        + ring_semaphores(count, 1)
+        + [
+            pltpu.SemaphoreType.DMA((2,)),
+            pltpu.SemaphoreType.DMA((2, groups // 2 - 1)),
+            pltpu.SemaphoreType.DMA((2, groups // 2)),
+        ],
         compiler_params=ring_params(1),
         cost_estimate=pl.CostEstimate(flops=0, bytes_accessed=300 << 20, transcendentals=0),
-    )(tokens)
-
-
-def logistic(v):
-    return 1.0 / (1.0 + jnp.exp(-v))
+    )(tokens, w_out)
+    return full, w_full.reshape(count * w_out.shape[0], model)
 
 
 def attend_kernel(
-    count, rows, mixed, w_out, tokens, gain, w_gate, w_up, w_down, cotangents,
+    count, mixed, w_out, tokens, gain, w_gate, w_up, w_down, cotangents,
     resid, full, hidden, grad_gate, grad_up,
-    slots, gathered, grad_hidden, boxes, sends, recvs, sends_two, recvs_two, box_sems, out_sems,
+    gathered, gate_box, up_box, down_box, boxes, stages, sends, recvs, weight_sems, box_sems, out_sems, stage_sems,
 ):
     ring = Ring(count)
+    rows = tokens.shape[0]
     half = rows // 2
-
-    def box_copy(block):
+    gather = Gather(
+        ring, lambda start, size: row_view(gathered, rows)(ring.me, start, size), row_view(gathered, rows),
+        sends, recvs, rows,
+    )
+    loads = [
+        pltpu.make_async_copy(source, box, weight_sems.at[k])
+        for k, (source, box) in enumerate(((w_gate, gate_box), (w_up, up_box), (w_down, down_box)))
+    ]
+
+    def place(way, step):
+        return pl.ds(pl.multiple_of(gather.origin(way, step) * rows + way * half, half), half)
+
+    def box_copy(way, step):
         return pltpu.make_async_copy(
-            cotangents.at[pl.ds(pl.multiple_of(block * rows, rows), rows), :],
-            boxes.at[block % 2],
-            box_sems.at[block % 2],
-        )
-
-    box_copy(0).start()
+            cotangents.at[place(way, step), :], boxes.at[step % 2, way], box_sems.at[step % 2, way]
+        )
+
+    def out_copy(way, step):
+        at = place(way, step)
+        return pltpu.make_async_copy(gathered.at[at, :], full.at[at, :], out_sems.at[way, step])
+
+    def stage_copy(k, way, step):
+        target = (hidden, grad_gate, grad_up)[k]
+        return pltpu.make_async_copy(
+            stages.at[step % 2, k, way], target.at[place(way, step), :], stage_sems.at[step % 2, k, way]
+        )
+
+    def settle(step):
+        for k in range(3):
+            for way in (0, 1):
+                stage_copy(k, way, step).wait()
+
+    for way in (0, 1):
+        box_copy(way, 0).start()
+    for load in loads:
+        load.start()
     greet(ring)
-
-    def partial(first, second, step):
-        return mm(jnp.concatenate([mixed[pl.ds(first, half), :], mixed[pl.ds(second, half), :]], 0), w_out[...])
-
-    def finish(start, size, attended):
-        value = tokens[start : start + size, :].astype(F32) + attended
-        resid[start : start + size, :] = value
-        scale = lax.rsqrt(jnp.mean(value * value, axis=1, keepdims=True) + 1e-6)
-        gathered[pl.ds(pl.multiple_of(ring.me * rows + start, size), size), :] = (
-            value * scale * gain[...].astype(F32)
-        ).astype(BF16)
-
-    def hide(block):
-        box_copy(block).wait()
-
-        @pl.when(block + 1 < count)
-        def _():
-            box_copy(block + 1).start()
-
-        grad_hidden[pl.ds(pl.multiple_of(block * rows, rows), rows), :] = mm(
-            boxes[block % 2], w_down[...], (1, 1)
-        )
-
-    ring_scatter(ring, partial, slots, sends, recvs, rows, finish, hide)
-    gather = Gather(ring, None, gathered, sends_two, recvs_two, None, rows)
-
-    def places(step):
-        return [
-            pl.ds(pl.multiple_of(gather.origin(way, step) * rows + way * half, half), half) for way in (0, 1)
-        ]
-
-    def out_copy(way, step):
-        at = places(step)[way]
-        return pltpu.make_async_copy(gathered.at[at, :], full.at[at, :], out_sems.at[way, step])
+    value = tokens[...].astype(F32) + mm(mixed[...], w_out[...])
+    resid[...] = value
+    scale = lax.rsqrt(jnp.mean(value * value, axis=1, keepdims=True) + 1e-6)
+    gathered[pl.ds(pl.multiple_of(ring.me * rows, rows), rows), :] = (
+        value * scale * gain[...].astype(F32)
+    ).astype(BF16)
 
     def feed(step):
-        one, two = places(step)
+        @pl.when(step == 0)
+        def _():
+            for load in loads:
+                load.wait()
+
+        @pl.when(step > 1)
+        def _():
+            settle(step - 2)
+
         for way in (0, 1):
             out_copy(way, step).start()
-        inputs = jnp.concatenate([gathered[one, :], gathered[two, :]], 0)
-        gate = mm(inputs, w_gate[...], (1, 1))
-        up = mm(inputs, w_up[...], (1, 1))
-        grad = jnp.concatenate([grad_hidden[one, :], grad_hidden[two, :]], 0)
-        sig = logistic(gate)
+            box_copy(way, step).wait()
+
+        @pl.when(step + 1 < count)
+        def _():
+            for way in (0, 1):
+                box_copy(way, step + 1).start()
+
+        slot = step % 2
+        inputs = jnp.concatenate([gathered[place(0, step), :], gathered[place(1, step), :]], 0)
+        gate = mm(inputs, gate_box[...], (1, 1))
+        up = mm(inputs, up_box[...], (1, 1))
+        grad = mm(jnp.concatenate([boxes[slot, 0], boxes[slot, 1]], 0), down_box[...], (1, 1))
+        sig = sigmoid(gate)
         opened = gate * sig
-        for target, value in (
-            (hidden, opened * up),
-            (grad_gate, grad * up * sig * (1.0 + gate * (1.0 - sig))),
-            (grad_up, grad * opened),
+        for k, result in enumerate(
+            (opened * up, grad * up * sig * (1.0 + gate * (1.0 - sig)), grad * opened)
         ):
-            low = value.astype(BF16)
-            target[one, :] = low[:half]
-            target[two, :] = low[half:]
-
-    ring_gather(ring, None, gathered, sends_two, recvs_two, None, rows, feed)
+            low = result.astype(BF16)
+            for way in (0, 1):
+                stages[slot, k, way] = low[way * half : way * half + half]
+                stage_copy(k, way, step).start()
+
+    ring_gather(gather, feed)
+    settle(count - 2)
+    settle(count - 1)
 
     def drain(step, carry):
         for way in (0, 1):
@@ -509,26 +594,28 @@
     rows, model = tokens.shape
     slots, inner = count * rows, w_down.shape[0]
     return pl.pallas_call(
-        functools.partial(attend_kernel, count, rows),
+        functools.partial(attend_kernel, count),
         name="attend",
         out_shape=[
             jax.ShapeDtypeStruct((rows, model), F32),
             jax.ShapeDtypeStruct((slots, model), BF16),
         ]
         + [jax.ShapeDtypeStruct((slots, inner), BF16)] * 3,
-        in_specs=[VMEM] * 7 + [ANY],
-        out_specs=[VMEM, ANY] + [VMEM] * 3,
-        scratch_shapes=[
-            ring_slots(count, rows, model),
-            pltpu.VMEM((slots, model), BF16),
-            pltpu.VMEM((slots, inner), F32),
-            pltpu.VMEM((2, rows, model), BF16),
-        ]
-        + ring_semaphores(count) * 2
-        + [pltpu.SemaphoreType.DMA((2,)), pltpu.SemaphoreType.DMA((2, count))],
+        in_specs=[VMEM] * 4 + [ANY] * 4,
+        out_specs=[VMEM] + [ANY] * 4,
+        scratch_shapes=[pltpu.VMEM((slots, model), BF16)]
+        + [pltpu.VMEM((inner, model), BF16)] * 3
+        + [pltpu.VMEM((2, 2, rows // 2, model), BF16), pltpu.VMEM((2, 3, 2, rows // 2, inner), BF16)]
+        + ring_semaphores(count)
+        + [
+            pltpu.SemaphoreType.DMA((3,)),
+            pltpu.SemaphoreType.DMA((2, 2)),
+            pltpu.SemaphoreType.DMA((2, count)),
+            pltpu.SemaphoreType.DMA((2, 3, 2)),
+        ],
         compiler_params=ring_params(2),
         cost_estimate=pl.CostEstimate(
-            flops=2 * slots * model * (mixed.shape[1] + 3 * inner), bytes_accessed=600 << 20,
+            flops=2 * rows * model * model + 6 * slots * model * inner, bytes_accessed=300 << 20,
             transcendentals=slots * inner,
         ),
     )(mixed, w_out, tokens, gain.reshape(1, model), w_gate, w_up, w_down, cotangents)
@@ -556,14 +643,22 @@
     )
     wide = boxes.shape[2]
 
-    def box_copy(job):
-        source = inputs if job < JOBS // 2 else cotangents
-        at = job % (JOBS // 2) * wide
+    def box_copy(job, source):
+        at = pl.multiple_of(job % (JOBS // 2) * wide, wide)
         return pltpu.make_async_copy(
-            source.at[:, at : at + wide], boxes.at[job % 2], box_sems.at[job % 2]
-        )
-
-    box_copy(0).start()
+            source.at[:, pl.ds(at, wide)], boxes.at[job % 2], box_sems.at[job % 2]
+        )
+
+    def fetch(job):
+        @pl.when(job < JOBS // 2)
+        def _():
+            box_copy(job, inputs).start()
+
+        @pl.when(job >= JOBS // 2)
+        def _():
+            box_copy(job, cotangents).start()
+
+    fetch(0)
     greet(ring, sums.peers())
     grad_gain[...] = jnp.zeros_like(grad_gain)
     half = rows // 2
@@ -582,43 +677,64 @@
         grad_gain[...] += jnp.sum(pieces, axis=0, keepdims=True)
         low[start : start + size, :] = result.astype(BF16)
 
-    def work(job):
-        box_copy(job).wait()
-        if job + 1 < JOBS:
-            box_copy(job + 1).start()
-        at = job % (JOBS // 2) * wide
-        box = boxes[job % 2]
-        if job < JOBS // 2:
-            gw_gate[:, at : at + wide] = mm(grad_gate[...], box, (0, 0)).astype(BF16)
-            gw_up[:, at : at + wide] = mm(grad_up[...], box, (0, 0)).astype(BF16)
-        else:
-            gw_down[:, at : at + wide] = mm(hidden[...], box, (0, 0)).astype(BF16)
+    def work(job, carry):
+        box_copy(job, inputs).wait()
+
+        @pl.when(job + 1 < JOBS)
+        def _():
+            fetch(job + 1)
+
+        at = pl.ds(pl.multiple_of(job % (JOBS // 2) * wide, wide), wide)
+
+        @pl.when(job < JOBS // 2)
+        def _():
+            box = boxes[job % 2]
+            gw_gate[:, at] = mm(grad_gate[...], box, (0, 0)).astype(BF16)
+            gw_up[:, at] = mm(grad_up[...], box, (0, 0)).astype(BF16)
+
+        @pl.when(job >= JOBS // 2)
+        def _():
+            gw_down[:, at] = mm(hidden[...], boxes[job % 2], (0, 0)).astype(BF16)
+
+        return carry
 
     each = JOBS // 4
-    events = {step: [functools.partial(work, step * each + k) for k in range(each)] for step in range(4)}
-    events[1].append(lambda: sums.first((0, 1)))
-    events[3].insert(0, lambda: sums.second((0, 1)))
-    events[3].append(lambda: sums.first((2,)))
-    events[5] = [lambda: sums.second((2,))]
-    events_two = {count - 3: [lambda: sums.third((0, 1))], count - 2: [lambda: sums.third((2,))]}
-
-    def between(table):
-        def run(step):
-            for when, actions in table.items():
-                def act(actions=actions):
-                    for action in actions:
-                        action()
-
-                if isinstance(step, int):
-                    if step == when:
-                        act()
-                else:
-                    pl.when(step == when)(act)
-
-        return run
-
-    ring_scatter(ring, partial, slots, sends, recvs, rows, finish, between(events))
-    ring_gather(ring, low, full, sends_two, recvs_two, local, rows, between(events_two))
+
+    def beside_scatter(step):
+        @pl.when(step == 3)
+        def _():
+            sums.second((0, 1))
+
+        @pl.when(step < 4)
+        def _():
+            lax.fori_loop(step * each, step * each + each, work, 0)
+
+        @pl.when(step == 1)
+        def _():
+            sums.first((0, 1))
+
+        @pl.when(step == 3)
+        def _():
+            sums.first((2,))
+
+        @pl.when(step == 5)
+        def _():
+            sums.second((2,))
+
+    def beside_gather(step):
+        @pl.when(step == count - 3)
+        def _():
+            sums.third((0, 1))
+
+        @pl.when(step == count - 2)
+        def _():
+            sums.third((2,))
+
+    ring_scatter(Scatter(ring, partial, slots, sends, recvs, rows, finish), beside_scatter)
+    keep = pltpu.make_async_copy(low, full.at[pl.ds(pl.multiple_of(ring.me * rows, rows), rows), :], local)
+    keep.start()
+    ring_gather(Gather(ring, row_own(low), row_view(full, rows), sends_two, recvs_two, rows), beside_gather)
+    keep.wait()
     sums.last()
 
 
@@ -732,15 +848,12 @@
         total[...] = mine
         sums.third(every)
 
-    def between(step):
-        if isinstance(step, int):
-            if step == 0:
-                early()
-        else:
-            pl.when(step == count - 2)(late)
+    def beside(step):
+        pl.when(step == 0)(early)
+        pl.when(step == count - 2)(late)
 
     fetch(0)
-    ring_scatter(ring, partial, slots, sends, recvs, rows, finish, between)
+    ring_scatter(Scatter(ring, partial, slots, sends, recvs, rows, finish), beside)
     sums.last()
 
 
@@ -806,17 +919,12 @@
     )(total, *[a for a, _ in arrays])
 
 
-def spread_hops(step, chunks, count, begin, hop):
+def spread_hops(step, chunks, count, hop, start=0):
     each = -(-(count - 1) // (chunks - 1))
-
-    @pl.when(step == 0)
-    def _():
-        begin()
-
     for place in range(each):
         number = step * each + place
 
-        @pl.when((number > 0) & (number < count - 1))
+        @pl.when((number >= start) & (number < count - 1))
         def _():
             hop(number)
 
@@ -825,9 +933,9 @@
     heads, width, seqs, count, rows_own, chunks,
     starts, lengths, tokens, w_query, w_key, w_value, w_gate, w_beta,
     taps_query, taps_key, taps_value, gain, gain_first, side,
-    mixed, p_query, p_key, p_value, p_gate, p_beta, z_query, z_key, z_value,
+    mixed_own, mixed, p_query, p_key, p_value, p_gate, p_beta, z_query, z_key, z_value,
     delta_out, change_out, inverse_out, state_out, side_full,
-    tail_query, tail_key, tail_value, state, sends, recvs, local,
+    tail_query, tail_key, tail_value, state, stage, sends, recvs, local, row_sends, row_recvs,
 ):
     step = pl.program_id(0)
     size = tokens.shape[0]
@@ -840,12 +948,41 @@
         state[...] = jnp.zeros_like(state)
 
     ring = Ring(count)
-    gather = Gather(ring, side, side_full, sends, recvs, local, rows_own)
-    spread_hops(
-        step, chunks, count,
-        lambda: (greet(ring), gather.begin()),
-        gather.hop,
+    me, group = ring.me, ring.group
+    wide = heads * width
+    gather = Gather(ring, row_own(side), row_view(side_full, rows_own), sends, recvs, rows_own)
+    keep = pltpu.make_async_copy(
+        side, side_full.at[pl.ds(pl.multiple_of(me * rows_own, rows_own), rows_own), :], local.at[0]
     )
+    own_columns = pl.ds(pl.multiple_of(me * wide, wide), wide)
+
+    def keep_rows():
+        return pltpu.make_async_copy(stage.at[me], mixed_own.at[:, own_columns], local.at[1])
+
+    def row_copy(target):
+        return pltpu.make_async_remote_copy(
+            src_ref=stage.at[target], dst_ref=mixed_own.at[:, own_columns],
+            send_sem=row_sends.at[target], recv_sem=row_recvs.at[me],
+            device_id=(group, target), device_id_type=MESH,
+        )
+
+    def row_arrival(origin):
+        return pltpu.make_async_remote_copy(
+            src_ref=stage.at[me], dst_ref=mixed_own.at[:, own_columns],
+            send_sem=row_sends.at[origin], recv_sem=row_recvs.at[origin],
+            device_id=(group, origin), device_id_type=MESH,
+        )
+
+    @pl.when(step == 0)
+    def _():
+        barrier = pltpu.get_barrier_semaphore()
+        for k in range(1, count):
+            pl.semaphore_signal(barrier, inc=1, device_id=(group, (me + k) % count), device_id_type=MESH)
+        pl.semaphore_wait(barrier, count - 1)
+        gather.begin()
+        keep.start()
+
+    spread_hops(step, chunks, count, gather.hop, 1)
     rows, seg_rows, seg_columns, before, last = chunk_masks(starts, lengths, seqs, first, size)
     same = seg_rows == seg_columns
     i = lax.broadcasted_iota(jnp.int32, (size, size), 0)
@@ -906,12 +1043,31 @@
         state[h] = kept * memory + mm(key, ending * change, (0, 0))
         delta_out[:, cols] = out
         normal = out * lax.rsqrt(jnp.mean(out * out, axis=1, keepdims=True) + 1e-5) * head_gain
-        mixed[:, cols] = (normal * opened[:, cols] * live).astype(BF16)
+        low_mixed = (normal * opened[:, cols] * live).astype(BF16)
+        mixed[:, cols] = low_mixed
+        for place in range(size // rows_own):
+            stage[step * (size // rows_own) + place, :, cols] = low_mixed[place * rows_own : (place + 1) * rows_own]
+
+    for place in range(size // rows_own):
+        target = step * (size // rows_own) + place
+
+        @pl.when(target != me)
+        def _():
+            row_copy(target).start()
+
+        @pl.when(target == me)
+        def _():
+            keep_rows().start()
 
     @pl.when(step == chunks - 1)
     def _():
         gather.arrived(count - 1)
         gather.end()
+        keep.wait()
+        keep_rows().wait()
+        for k in range(1, count):
+            row_copy((me + k) % count).wait_send()
+            row_arrival((me + k) % count).wait_recv()
 
 
 def forward_mixer(tokens, w_query, w_key, w_value, w_gate, w_beta, taps_query, taps_key, taps_value, gain, gain_first, starts, lengths, side, count):
@@ -925,6 +1081,7 @@
     smem = pl.BlockSpec(memory_space=pltpu.SMEM)
     whole = lambda shape: pl.BlockSpec(shape, lambda n: (0,) * len(shape))
     piece = lambda shape: pl.BlockSpec(shape, lambda n: (n,) + (0,) * (len(shape) - 1))
+    own = (slots // count, count * wide)
     outs = [
         ((slots, wide), BF16), ((slots, wide), F32), ((slots, wide), F32), ((slots, wide), F32), ((slots, wide), F32),
         ((slots, w_beta.shape[0]), F32), ((slots, wide), F32), ((slots, wide), F32), ((slots, wide), F32),
@@ -934,7 +1091,8 @@
         functools.partial(forward_kernel, heads, width, seqs, count, slots // count, chunks),
         name="mixer_forward",
         grid=(chunks,),
-        out_shape=[jax.ShapeDtypeStruct(s, d) for s, d in outs]
+        out_shape=[jax.ShapeDtypeStruct(own, BF16)]
+        + [jax.ShapeDtypeStruct(s, d) for s, d in outs]
         + [
             jax.ShapeDtypeStruct((chunks, heads, CHUNK, CHUNK), BF16),
             jax.ShapeDtypeStruct((chunks, heads, width, width), BF16),
@@ -945,12 +1103,14 @@
         + [whole(w_beta.shape)]
         + [whole((taps, wide))] * 3
         + [whole((1, width)), whole((1, model)), ANY],
-        out_specs=[piece((CHUNK, s[1])) for s, d in outs]
+        out_specs=[ANY]
+        + [piece((CHUNK, s[1])) for s, d in outs]
         + [piece((1, heads, CHUNK, CHUNK)), piece((1, heads, width, width)), ANY],
         scratch_shapes=[pltpu.VMEM((CHUNK + 8, wide), F32)] * 3
-        + [pltpu.VMEM((heads, width, width), F32)]
+        + [pltpu.VMEM((heads, width, width), F32), pltpu.VMEM((count, slots // count, wide), BF16)]
         + ring_semaphores(count)
-        + [pltpu.SemaphoreType.DMA],
+        + [pltpu.SemaphoreType.DMA((2,))]
+        + [pltpu.SemaphoreType.DMA((count,))] * 2,
         compiler_params=ring_params(5),
         cost_estimate=pl.CostEstimate(
             flops=2 * slots * model * wide * 4 + slots * heads * CHUNK * 2 * CHUNK * 20,
@@ -995,11 +1155,8 @@
 
     ring = Ring(count)
     scatter = Scatter(ring, partial, slots, sends, recvs, rows_own, finish)
-    spread_hops(
-        step, chunks, count,
-        lambda: (greet(ring), scatter.begin()),
-        scatter.hop,
-    )
+    pl.when(step == 0)(lambda: greet(ring))
+    spread_hops(step, chunks, count, scatter.hop)
     rows, seg_rows, seg_columns, before, last = chunk_masks(starts, lengths, seqs, first, size)
     same = seg_rows == seg_columns
     i = lax.broadcasted_iota(jnp.int32, (size, size), 0)
@@ -1183,14 +1340,14 @@
         model = tokens.shape[1]
         heads = w_beta.shape[1]
         beta_rows = w_beta.T if heads > 1 else jnp.pad(w_beta.T, ((0, 1), (0, 0)))
-        tokens_full = gather_tokens(tokens, count)
-        saved = forward_mixer(
+        tokens_full, w_out_full = gather_tokens(tokens, w_out, count, groups)
+        mixed_own, *saved = forward_mixer(
             tokens_full, w_query, w_key, w_value, w_gate_out, beta_rows,
             conv_query, conv_key, conv_value, head_gain, attn_gain, seq_starts, seq_lengths, cotangent, count,
         )
         grad_full, saved = saved[-1], saved[:-1]
         resid, ffn_full, hidden, grad_gate, grad_up = attend(
-            saved[0], w_out, tokens, ffn_gain, w_gate.T, w_up.T, w_down, grad_full, count
+            mixed_own, w_out_full, tokens, ffn_gain, w_gate.T, w_up.T, w_down, grad_full, count
         )
         grad_resid, grad_attended, g_second, *ffn_grads = ffn_back(
             grad_gate, grad_up, hidden, w_gate.T, w_up.T, resid, cotangent, ffn_gain, ffn_full, grad_full,

time: 742 us -> 724 us (0.976); the launches traced: 732 us -> 722 us
  Pallas kernels: 728 us -> 719 us
    pallas_call x2, Pallas kernels: 253 us -> 219 us  [the longest x1 115 us: gather_tokens(): pl.pallas_call(functools.partial(gather_kernel, count, groups), name='gat...]
    pallas_call x1, Pallas kernels: 91.3 us -> 114 us  [forward_mixer(): pl.pallas_call(functools.partial(forward_kernel, heads, width, seqs, coun...]
where the time goes in v6:
time: 724 us; the launch traced here: 722 us
  Pallas kernels  719 us (99%)
    pallas_call x1, Pallas kernels, ffn_back(): pl.pallas_call(functools.partial(ffn_back_kernel, count, groups, rows), n...  174 us
    pallas_call x1, Pallas kernels, gather_tokens(): pl.pallas_call(functools.partial(gather_kernel, count, groups), name='gat...  115 us
    pallas_call x1, Pallas kernels, forward_mixer(): pl.pallas_call(functools.partial(forward_kernel, heads, width, seqs, coun...  114 us
    pallas_call x1, Pallas kernels, attend(): pl.pallas_call(functools.partial(attend_kernel, count), name='attend', ou...  104 us
    pallas_call x1, Pallas kernels, backward_mixer(): pl.pallas_call(functools.partial(backward_kernel, heads, width, seqs, chu...  98.3 us
    pallas_call x1, Pallas kernels, last_step(): pl.pallas_call(functools.partial(last_kernel, count, groups, rows), name=...  95.2 us
    pallas_call x1, Pallas kernels, results(): pl.pallas_call(functools.partial(results_kernel, heads, taps, wide, width...  17.6 us

profile of v6, /device:TPU:0, one launch (start us, length us, event | category | flops | bytes accessed | tf_op | source)
XLA Modules:
  0.0 722.2 jit_solution(6334088483236772489)
XLA Ops:
  0.7 1.3 reshape.51.gain_first.gain
  1.9 1.3 reshape.53.gain
  3.2 115.2 %gather_tokens.1 = (bf16[2048,2048]{1,0:T(8,128)(2,1)}, bf16[8,4,64,2048]{3,2,1,0:T(8,128)(2,1)}) custom-call(bf16[256,2048]{1,0:T(8,128)(2,1)} %tokens.5, bf16[256,2048]{1,0:T(8,128)(2,1)} %w_out.3), custom_call_target="tpu_custom_call" | custom-call | bytes 314572800 | tf_op jit(solution)/shard_map/gather_tokens/pallas_call | solution.py:473
  118.5 113.9 %mixer_forward.1 = (bf16[256,2048]{1,0:T(8,128)(2,1)}, bf16[2048,256]{1,0:T(8,128)(2,1)}, f32[2048,256]{1,0:T(8,128)}, f32[2048,256]{1,0:T(8,128)}, f32[2048,256...) custom-call(s32[1,2]{1,0:T(1,128)} %starts.3, ...), custom_call_target="tpu_custom_call" | custom-call | flops 19327352832 | bytes 31457280 | tf_op jit(solution)/shard_map/mixer_forward/pallas_call | solution.py:1090
  232.4 104.2 %attend.1 = (f32[256,2048]{1,0:T(8,128)}, bf16[2048,2048]{1,0:T(8,128)(2,1)}, bf16[2048,704]{1,0:T(8,128)(2,1)}, bf16[2048,704]{1,0:T(8,128)(2,1)}, bf16[2048,704]{1,0:T(8,128)(2,1)}) custom-call(bf16[256,2048]{1,0:T(8,128)(2,1)} %get-tuple-element.78.mixed, bf16[2048,2048]{1,0:T(8,128)(2,1)} %bitcast.11, bf16[256,2048]{1,0:T(8,128)(2,1)} %tokens.5, ...), custom_call_target="tpu_custom_call" | custom-call | flops 19864223744 | bytes 314572800 | tf_op jit(solution)/shard_map/attend/pallas_call | solution.py:596
  336.6 174.4 %ffn_back.1 = (f32[256,2048]{1,0:T(8,128)}, bf16[2048,2048]{1,0:T(8,128)(2,1)}, f32[1,2048]{1,0:T(1,128)}, bf16[704,2048]{1,0:T(8,128)(2,1)}, bf16[704,2048]{1,0:T(8,128)(2,1)}, /*index=5*/bf16[704,2048]{1,0:T(8,128)(2,1)}) custom-call(bf16[2048,704]{1,0:T(8,128)(2,1)} %get-tuple-element.81.grad_gate, bf16[2048,704]{1,0:T(8,128)(2,1)} %get-tuple-element.82.grad_up, ...), custom_call_target="tpu_custom_call" | custom-call | flops 29527900160 | bytes 629145600 | tf_op jit(solution)/shard_map/ffn_back/pallas_call | solution.py:745
  510.9 98.3 %mixer_backward.1 = (bf16[2048,2048]{1,0:T(8,128)(2,1)}, bf16[2048,256]{1,0:T(8,128)(2,1)}, bf16[2048,256]{1,0:T(8,128)(2,1)}, bf16[2048,256]{1,0:T(8,128)(2,1)}...) custom-call(s32[1,2]{1,0:T(1,128)} %starts.3, ...), custom_call_target="tpu_custom_call" | custom-call | flops 25769803776 | bytes 54525952 | tf_op jit(solution)/shard_map/mixer_backward/pallas_call | solution.py:1308
  609.2 95.2 %last_step.1 = (f32[256,2048]{1,0:T(8,128)}, f32[16,2048]{1,0:T(8,128)}, bf16[2048,256]{1,0:T(8,128)(2,1)}, bf16[2048,256]{1,0:T(8,128)(2,1)}, bf16[2048,256]{1,...) custom-call(bf16[2048,2048]{1,0:T(8,128)(2,1)} %get-tuple-element.101.terms, ...), custom_call_target="tpu_custom_call" | custom-call | bytes 314572800 | tf_op jit(solution)/shard_map/last_step/pallas_call | solution.py:862
  704.4 17.6 %results.1 = (bf16[256,2048]{1,0:T(8,128)(2,1)}, f32[256,2048]{1,0:T(8,128)}, f32[2048,256]{1,0:T(8,128)}, f32[2048,256]{1,0:T(8,128)}, f32[2048,256]{1,0:T(8,12...) custom-call(f32[16,2048]{1,0:T(8,128)} %get-tuple-element.109.total,, ...), custom_call_target="tpu_custom_call" | custom-call | bytes 50331648 | tf_op jit(solution)/shard_map/results/pallas_call | solution.py:909

commit v7 on v6

--- a/solution.py
+++ b/solution.py
@@ -7,6 +7,7 @@
 from jax.sharding import PartitionSpec as P
 
 CHUNK = 256
+LAGS = 4
 F32, BF16 = jnp.float32, jnp.bfloat16
 
 
@@ -74,7 +75,7 @@
 def normed_rows(tokens, gain):
     value = tokens[...].astype(F32)
     unit = value * lax.rsqrt(jnp.mean(value * value, axis=1, keepdims=True) + 1e-6)
-    return unit * gain[...].astype(F32), unit
+    return unit * gain[...].astype(F32).reshape(1, -1), unit
 
 
 MESH = pl.DeviceIdType.MESH
@@ -157,10 +158,13 @@
     return lambda start, size: ref.at[pl.ds(start, size), :]
 
 
-def ring_gather(gather, between):
+def ring_gather(gather, between, before=None):
     count = gather.ring.count
 
     def run(step, carry):
+        if before is not None:
+            before(step)
+
         @pl.when(step == 0)
         def _():
             gather.begin()
@@ -495,7 +499,7 @@
 def attend_kernel(
     count, mixed, w_out, tokens, gain, w_gate, w_up, w_down, cotangents,
     resid, full, hidden, grad_gate, grad_up,
-    gathered, gate_box, up_box, down_box, boxes, stages, sends, recvs, weight_sems, box_sems, out_sems, stage_sems,
+    gathered, gate_box, up_box, down_box, boxes, ahead, stages, sends, recvs, weight_sems, box_sems, out_sems, stage_sems,
 ):
     ring = Ring(count)
     rows = tokens.shape[0]
@@ -541,14 +545,30 @@
     resid[...] = value
     scale = lax.rsqrt(jnp.mean(value * value, axis=1, keepdims=True) + 1e-6)
     gathered[pl.ds(pl.multiple_of(ring.me * rows, rows), rows), :] = (
-        value * scale * gain[...].astype(F32)
+        value * scale * gain[...].astype(F32).reshape(1, -1)
     ).astype(BF16)
+
+    def hide(step):
+        @pl.when(step == 0)
+        def _():
+            loads[2].wait()
+
+        for way in (0, 1):
+            box_copy(way, step).wait()
+
+        @pl.when(step + 1 < count)
+        def _():
+            for way in (0, 1):
+                box_copy(way, step + 1).start()
+
+        slot = step % 2
+        ahead[...] = mm(jnp.concatenate([boxes[slot, 0], boxes[slot, 1]], 0), down_box[...], (1, 1))
 
     def feed(step):
         @pl.when(step == 0)
         def _():
-            for load in loads:
-                load.wait()
+            loads[0].wait()
+            loads[1].wait()
 
         @pl.when(step > 1)
         def _():
@@ -556,18 +576,11 @@
 
         for way in (0, 1):
             out_copy(way, step).start()
-            box_copy(way, step).wait()
-
-        @pl.when(step + 1 < count)
-        def _():
-            for way in (0, 1):
-                box_copy(way, step + 1).start()
-
         slot = step % 2
         inputs = jnp.concatenate([gathered[place(0, step), :], gathered[place(1, step), :]], 0)
         gate = mm(inputs, gate_box[...], (1, 1))
         up = mm(inputs, up_box[...], (1, 1))
-        grad = mm(jnp.concatenate([boxes[slot, 0], boxes[slot, 1]], 0), down_box[...], (1, 1))
+        grad = ahead[...]
         sig = sigmoid(gate)
         opened = gate * sig
         for k, result in enumerate(
@@ -578,7 +591,14 @@
                 stages[slot, k, way] = low[way * half : way * half + half]
                 stage_copy(k, way, step).start()
 
-    ring_gather(gather, feed)
+    def before(step):
+        pl.when(step > 0)(lambda: hide(step))
+
+    def between(step):
+        pl.when(step == 0)(lambda: hide(step))
+        feed(step)
+
+    ring_gather(gather, between, before)
     settle(count - 2)
     settle(count - 1)
 
@@ -605,7 +625,11 @@
         out_specs=[VMEM] + [ANY] * 4,
         scratch_shapes=[pltpu.VMEM((slots, model), BF16)]
         + [pltpu.VMEM((inner, model), BF16)] * 3
-        + [pltpu.VMEM((2, 2, rows // 2, model), BF16), pltpu.VMEM((2, 3, 2, rows // 2, inner), BF16)]
+        + [
+            pltpu.VMEM((2, 2, rows // 2, model), BF16),
+            pltpu.VMEM((rows, inner), F32),
+            pltpu.VMEM((2, 3, 2, rows // 2, inner), BF16),
+        ]
         + ring_semaphores(count)
         + [
             pltpu.SemaphoreType.DMA((3,)),
@@ -618,7 +642,7 @@
             flops=2 * rows * model * model + 6 * slots * model * inner, bytes_accessed=300 << 20,
             transcendentals=slots * inner,
         ),
-    )(mixed, w_out, tokens, gain.reshape(1, model), w_gate, w_up, w_down, cotangents)
+    )(mixed, w_out, tokens, gain, w_gate, w_up, w_down, cotangents)
 
 
 def norm_back(inputs, scale, gain, grad_normed):
@@ -632,9 +656,9 @@
 
 
 def ffn_back_kernel(
-    count, groups, rows, grad_gate, grad_up, hidden, w_gate, w_up, resid, cotangent, gain, inputs, cotangents,
+    count, groups, rows, grad_gate, grad_up, hidden_in, w_gate, w_up, resid_in, cotangent_in, gain, inputs, cotangents,
     grad_resid, full, grad_gain, sum_gate, sum_up, sum_down,
-    slots, low, gw_gate, gw_up, gw_down, boxes, box_sems, *rest,
+    slots, low, gw_gate, gw_up, gw_down, boxes, box_sems, hidden, resid, cotangent, load_sems, *rest,
 ):
     ring = Ring(count)
     sends, recvs, sends_two, recvs_two, local = rest[:5]
@@ -658,7 +682,13 @@
         def _():
             box_copy(job, cotangents).start()
 
+    loads = [
+        pltpu.make_async_copy(source, target, load_sems.at[k])
+        for k, (source, target) in enumerate(((hidden_in, hidden), (resid_in, resid), (cotangent_in, cotangent)))
+    ]
     fetch(0)
+    for load in loads:
+        load.start()
     greet(ring, sums.peers())
     grad_gain[...] = jnp.zeros_like(grad_gain)
     half = rows // 2
@@ -671,7 +701,7 @@
     def finish(start, size, grad):
         value = resid[start : start + size, :]
         scale = lax.rsqrt(jnp.mean(value * value, axis=1, keepdims=True) + 1e-6)
-        through, pieces = norm_back(value, scale, gain[...].astype(F32), grad)
+        through, pieces = norm_back(value, scale, gain[...].astype(F32).reshape(1, -1), grad)
         result = cotangent[start : start + size, :].astype(F32) + through
         grad_resid[start : start + size, :] = result
         grad_gain[...] += jnp.sum(pieces, axis=0, keepdims=True)
@@ -701,6 +731,11 @@
     each = JOBS // 4
 
     def beside_scatter(step):
+        @pl.when(step == 2)
+        def _():
+            for load in loads:
+                load.wait()
+
         @pl.when(step == 3)
         def _():
             sums.second((0, 1))
@@ -751,11 +786,13 @@
             jax.ShapeDtypeStruct((1, model), F32),
         ]
         + [jax.ShapeDtypeStruct(shape, BF16) for shape in shapes],
-        in_specs=[VMEM] * 8 + [ANY] * 2,
+        in_specs=[VMEM] * 2 + [ANY] + [VMEM] * 2 + [ANY] * 2 + [VMEM] + [ANY] * 2,
         out_specs=[VMEM, ANY, VMEM] + [ANY] * 3,
         scratch_shapes=[ring_slots(count, rows, model), pltpu.VMEM((rows, model), BF16)]
         + [pltpu.VMEM(shape, BF16) for shape in shapes]
         + [pltpu.VMEM((2, slots, model // (JOBS // 2)), BF16), pltpu.SemaphoreType.DMA((2,))]
+        + [pltpu.VMEM((slots, inner), BF16), pltpu.VMEM((rows, model), F32), pltpu.VMEM((rows, model), BF16)]
+        + [pltpu.SemaphoreType.DMA((3,))]
         + ring_semaphores(count) * 2
         + [pltpu.SemaphoreType.DMA]
         + sum_scratch(shapes, groups),
@@ -763,19 +800,23 @@
         cost_estimate=pl.CostEstimate(
             flops=10 * slots * model * inner, bytes_accessed=600 << 20, transcendentals=0
         ),
-    )(grad_gate, grad_up, hidden, w_gate, w_up, resid, cotangent, gain.reshape(1, model), inputs, cotangents)
+    )(grad_gate, grad_up, hidden, w_gate, w_up, resid, cotangent, gain, inputs, cotangents)
 
 
 def last_kernel(
-    count, groups, rows, terms, tokens, grad_resid, gain, small, *rest,
+    count, groups, rows, terms, tokens_in, grad_resid_in, gain, small, *rest,
 ):
     grads, rest = rest[:5], rest[5:]
     grad_tokens, total = rest[:2]
     targets, rest = rest[2:7], rest[7:]
-    slots, first_box, second_box, second_own, boxes, box_sems, sends, recvs = rest[:8]
-    first_sends, first_recvs, second_sends, second_recvs = rest[8:12]
+    slots, first_box, second_box, second_own, boxes, box_sems, tokens, grad_resid, load_sems = rest[:9]
+    sends, recvs, first_sends, first_recvs, second_sends, second_recvs = rest[9:15]
     ring = Ring(count)
-    sums = GroupSum(ring, groups, grads, rest[12:17], rest[17:22], targets, *rest[22:])
+    sums = GroupSum(ring, groups, grads, rest[15:20], rest[20:25], targets, *rest[25:])
+    loads = [
+        pltpu.make_async_copy(tokens_in, tokens, load_sems.at[0]),
+        pltpu.make_async_copy(grad_resid_in, grad_resid, load_sems.at[1]),
+    ]
     me, group = ring.me, ring.group
     first_peers = [(group, (me + k) % count) for k in range(1, count)]
     second_peers = [((group + k) % groups, me) for k in range(1, groups)]
@@ -824,7 +865,7 @@
     def finish(start, size, grad):
         value = tokens[start : start + size, :].astype(F32)
         scale = lax.rsqrt(jnp.mean(value * value, axis=1, keepdims=True) + 1e-6)
-        through, pieces = norm_back(value, scale, gain[...].astype(F32), grad)
+        through, pieces = norm_back(value, scale, gain[...].astype(F32).reshape(1, -1), grad)
         grad_tokens[start : start + size, :] = grad_resid[start : start + size, :] + through
 
     def early():
@@ -846,13 +887,18 @@
         for k in range(groups - 1):
             mine = mine + second_box[k]
         total[...] = mine
-        sums.third(every)
+        for load in loads:
+            load.wait()
 
     def beside(step):
         pl.when(step == 0)(early)
+        for i in every:
+            pl.when(step == count - 1 - len(every) + i)(lambda i=i: sums.third((i,)))
         pl.when(step == count - 2)(late)
 
     fetch(0)
+    for load in loads:
+        load.start()
     ring_scatter(Scatter(ring, partial, slots, sends, recvs, rows, finish), beside)
     sums.last()
 
@@ -864,7 +910,7 @@
         name="last_step",
         out_shape=[jax.ShapeDtypeStruct((rows, model), F32), jax.ShapeDtypeStruct(small.shape, F32)]
         + [jax.ShapeDtypeStruct(g.shape, BF16) for g in grads],
-        in_specs=[ANY] + [VMEM] * (4 + len(grads)),
+        in_specs=[ANY] * 3 + [VMEM] * (2 + len(grads)),
         out_specs=[VMEM, VMEM] + [ANY] * len(grads),
         scratch_shapes=[
             ring_slots(count, rows, model),
@@ -873,6 +919,9 @@
             pltpu.VMEM(small.shape, F32),
             pltpu.VMEM((2, 2, rows // 2, model), BF16),
             pltpu.SemaphoreType.DMA((2, 2)),
+            pltpu.VMEM((rows, model), BF16),
+            pltpu.VMEM((rows, model), F32),
+            pltpu.SemaphoreType.DMA((2,)),
         ]
         + ring_semaphores(count)
         + [pltpu.SemaphoreType.DMA((count - 1,))] * 2
@@ -880,7 +929,7 @@
         + sum_scratch([g.shape for g in grads], groups),
         compiler_params=ring_params(4),
         cost_estimate=pl.CostEstimate(flops=0, bytes_accessed=300 << 20, transcendentals=0),
-    )(terms, tokens, grad_resid, gain.reshape(1, model), small, *grads)
+    )(terms, tokens, grad_resid, gain, small, *grads)
 
 
 def results_kernel(heads, taps, wide, width, total, *refs):
@@ -902,7 +951,7 @@
 
 def results(total, arrays, heads, taps, wide, width):
     model = total.shape[1]
-    steps = next(n for n in (8, 4, 2, 1) if all(a.shape[0] % (8 * n) == 0 for a, _ in arrays))
+    steps = next(n for n in (2, 1) if all(a.shape[0] % (8 * n) == 0 for a, _ in arrays))
     small = [(1, model), (1, model), (1, width)] + [(taps, wide)] * 3 + [(heads, model)]
     piece = lambda a: pl.BlockSpec((a.shape[0] // steps, a.shape[1]), lambda n: (n, 0))
     whole = lambda shape: pl.BlockSpec(shape, lambda n: (0, 0))
@@ -1048,16 +1097,25 @@
         for place in range(size // rows_own):
             stage[step * (size // rows_own) + place, :, cols] = low_mixed[place * rows_own : (place + 1) * rows_own]
 
-    for place in range(size // rows_own):
-        target = step * (size // rows_own) + place
-
-        @pl.when(target != me)
-        def _():
-            row_copy(target).start()
-
-        @pl.when(target == me)
-        def _():
-            keep_rows().start()
+    each = size // rows_own
+
+    def send(chunk, due):
+        for place in range(each):
+            target = chunk * each + place
+
+            @pl.when((chunk >= 0) & (target != me) & due((me + target) % LAGS))
+            def _():
+                row_copy(target).start()
+
+    for lag in range(LAGS):
+        send(step - lag, lambda own_lag, lag=lag: own_lag == lag)
+    for place in range(each):
+        pl.when(step * each + place == me)(lambda: keep_rows().start())
+
+    @pl.when(step == chunks - 1)
+    def _():
+        for back in range(LAGS - 1):
+            send(step - back, lambda own_lag, back=back: own_lag > back)
 
     @pl.when(step == chunks - 1)
     def _():
@@ -1102,7 +1160,7 @@
         + [whole((model, wide))] * 4
         + [whole(w_beta.shape)]
         + [whole((taps, wide))] * 3
-        + [whole((1, width)), whole((1, model)), ANY],
+        + [whole((1, width)), VMEM, ANY],
         out_specs=[ANY]
         + [piece((CHUNK, s[1])) for s, d in outs]
         + [piece((1, heads, CHUNK, CHUNK)), piece((1, heads, width, width)), ANY],
@@ -1117,7 +1175,7 @@
             bytes_accessed=slots * model * 2 + 4 * model * wide * 2 + slots * wide * 36,
             transcendentals=slots * wide * 4,
         ),
-    )(starts, lengths, tokens, w_query, w_key, w_value, w_gate, w_beta, taps_query, taps_key, taps_value, gain.reshape(1, width), gain_first.reshape(1, model), side)
+    )(starts, lengths, tokens, w_query, w_key, w_value, w_gate, w_beta, taps_query, taps_key, taps_value, gain.reshape(1, width), gain_first, side)
 
 
 def small_rows(heads, taps):
@@ -1128,10 +1186,11 @@
     heads, width, seqs, chunks, count, rows_own,
     starts, lengths, tokens, grad_attended, mixed, p_query, p_key, p_value, p_gate, p_beta,
     z_query, z_key, z_value, delta_out, change_in, inverse_in, state_in,
-    w_query, w_key, w_value, w_gate, w_beta, w_out, taps_query, taps_key, taps_value, gain, gain_first,
-    hidden, w_down, resid, g_second, grad_normed, gw_query, gw_key, gw_value, gw_gate, gw_out,
+    w_query_in, w_key_in, w_value_in, w_gate_in, w_beta, w_out, taps_query, taps_key, taps_value, gain, gain_first,
+    hidden, w_down, resid_in, g_second, grad_normed, gw_query, gw_key, gw_value, gw_gate, gw_out,
     small, output,
-    a_query, a_key, a_value, a_gate, a_out, head_query, head_key, head_value, flow, slots, sends, recvs,
+    a_query, a_key, a_value, a_gate, a_out, head_query, head_key, head_value, flow,
+    w_query, w_key, w_value, w_gate, resid, load_sems, slots, sends, recvs,
 ):
     step = pl.program_id(0)
     size = tokens.shape[0]
@@ -1155,7 +1214,19 @@
 
     ring = Ring(count)
     scatter = Scatter(ring, partial, slots, sends, recvs, rows_own, finish)
-    pl.when(step == 0)(lambda: greet(ring))
+    loads = [
+        pltpu.make_async_copy(source, target, load_sems.at[k])
+        for k, (source, target) in enumerate(
+            ((w_query_in, w_query), (w_key_in, w_key), (w_value_in, w_value), (w_gate_in, w_gate), (resid_in, resid))
+        )
+    ]
+
+    @pl.when(step == 0)
+    def _():
+        for load in loads:
+            load.start()
+        greet(ring)
+
     spread_hops(step, chunks, count, scatter.hop)
     rows, seg_rows, seg_columns, before, last = chunk_masks(starts, lengths, seqs, first, size)
     same = seg_rows == seg_columns
@@ -1264,6 +1335,12 @@
     d_gate = jnp.concatenate(grads_gate, axis=1).astype(BF16)
     spare = [jnp.zeros((size, 1), F32)] * (w_beta.shape[0] - heads)
     d_beta = jnp.concatenate(grads_beta + spare, axis=1).astype(BF16)
+
+    @pl.when(step == 0)
+    def _():
+        for load in loads:
+            load.wait()
+
     grad_inputs = (
         mm(d_query, w_query[...], (1, 1))
         + mm(d_key, w_key[...], (1, 1))
@@ -1313,15 +1390,17 @@
         in_specs=[smem, smem, rows(tokens), rows(grad_attended)]
         + [rows(a) for a in saved[:11]]
         + [piece((1, heads, CHUNK, CHUNK)), piece((1, heads, width, width))]
-        + [fixed((model, wide))] * 4
+        + [ANY] * 4
         + [fixed(w_beta.shape), fixed((wide, model))]
         + [fixed((taps, wide))] * 3
-        + [fixed((1, width)), fixed((1, model)), fixed(hidden.shape), fixed(w_down.shape), fixed(resid.shape), fixed(g_second.shape)],
+        + [fixed((1, width)), VMEM, fixed(hidden.shape), fixed(w_down.shape), ANY, fixed(g_second.shape)],
         out_specs=[piece((CHUNK, model))] + [fixed(s) for s, d in outs[1:]],
         scratch_shapes=[pltpu.VMEM((model, wide), F32)] * 4
         + [pltpu.VMEM((wide, model), F32)]
         + [pltpu.VMEM((CHUNK + 8, wide), F32)] * 3
-        + [pltpu.VMEM((heads, width, width), F32), ring_slots(count, slots // count, model)]
+        + [pltpu.VMEM((heads, width, width), F32)]
+        + [pltpu.VMEM((model, wide), BF16)] * 4
+        + [pltpu.VMEM(resid.shape, F32), pltpu.SemaphoreType.DMA((5,)), ring_slots(count, slots // count, model)]
         + ring_semaphores(count),
         compiler_params=ring_params(6),
         cost_estimate=pl.CostEstimate(
@@ -1329,7 +1408,7 @@
             bytes_accessed=slots * model * 6 + 10 * model * wide * 2 + slots * wide * 36,
             transcendentals=slots * wide * 8,
         ),
-    )(starts, lengths, tokens, grad_attended, *saved, w_query, w_key, w_value, w_gate, w_beta, w_out, taps_query, taps_key, taps_value, gain.reshape(1, width), gain_first.reshape(1, model), hidden, w_down, resid, g_second)
+    )(starts, lengths, tokens, grad_attended, *saved, w_query, w_key, w_value, w_gate, w_beta, w_out, taps_query, taps_key, taps_value, gain.reshape(1, width), gain_first, hidden, w_down, resid, g_second)
 
 
 def make_shards(groups, count):

time: 724 us -> 716 us (0.989)
  no operation moved by 1% of the time
where the time goes in v7:
time: 716 us; the launch traced here: 715 us
  Pallas kernels  714 us (100%)
    pallas_call x1, Pallas kernels, ffn_back(): pl.pallas_call(functools.partial(ffn_back_kernel, count, groups, rows), n...  173 us
    pallas_call x1, Pallas kernels, gather_tokens(): pl.pallas_call(functools.partial(gather_kernel, count, groups), name='gat...  115 us
    pallas_call x1, Pallas kernels, forward_mixer(): pl.pallas_call(functools.partial(forward_kernel, heads, width, seqs, coun...  113 us
    pallas_call x1, Pallas kernels, attend(): pl.pallas_call(functools.partial(attend_kernel, count), name='attend', ou...  105 us
    pallas_call x1, Pallas kernels, backward_mixer(): pl.pallas_call(functools.partial(backward_kernel, heads, width, seqs, chu...  97.3 us
    pallas_call x1, Pallas kernels, last_step(): pl.pallas_call(functools.partial(last_kernel, count, groups, rows), name=...  94.7 us
    pallas_call x1, Pallas kernels, results(): pl.pallas_call(functools.partial(results_kernel, heads, taps, wide, width...  15.8 us

profile of v7, /device:TPU:0, one launch (start us, length us, event | category | flops | bytes accessed | tf_op | source)
XLA Modules:
  0.0 714.5 jit_solution(1067196932442683858)
XLA Ops:
  0.7 115.3 %gather_tokens.1 = (bf16[2048,2048]{1,0:T(8,128)(2,1)}, bf16[8,4,64,2048]{3,2,1,0:T(8,128)(2,1)}) custom-call(bf16[256,2048]{1,0:T(8,128)(2,1)} %tokens_in.1, bf16[256,2048]{1,0:T(8,128)(2,1)} %w_out.3), custom_call_target="tpu_custom_call" | custom-call | bytes 314572800 | tf_op jit(solution)/shard_map/gather_tokens/pallas_call | solution.py:477
  115.9 112.7 %mixer_forward.1 = (bf16[256,2048]{1,0:T(8,128)(2,1)}, bf16[2048,256]{1,0:T(8,128)(2,1)}, f32[2048,256]{1,0:T(8,128)}, f32[2048,256]{1,0:T(8,128)}, f32[2048,256...) custom-call(s32[1,2]{1,0:T(1,128)} %starts.3, ...), custom_call_target="tpu_custom_call" | custom-call | flops 19327352832 | bytes 31457280 | tf_op jit(solution)/shard_map/mixer_forward/pallas_call | solution.py:1148
  228.7 105.1 %attend.1 = (f32[256,2048]{1,0:T(8,128)}, bf16[2048,2048]{1,0:T(8,128)(2,1)}, bf16[2048,704]{1,0:T(8,128)(2,1)}, bf16[2048,704]{1,0:T(8,128)(2,1)}, bf16[2048,704]{1,0:T(8,128)(2,1)}) custom-call(bf16[256,2048]{1,0:T(8,128)(2,1)} %get-tuple-element.78.mixed, bf16[2048,2048]{1,0:T(8,128)(2,1)} %bitcast.11, bf16[256,2048]{1,0:T(8,128)(2,1)} %tokens_in.1, ...), custom_call_target="tpu_custom_call" | custom-call | flops 19864223744 | bytes 314572800 | tf_op jit(solution)/shard_map/attend/pallas_call | solution.py:616
  333.8 172.8 %ffn_back.1 = (f32[256,2048]{1,0:T(8,128)}, bf16[2048,2048]{1,0:T(8,128)(2,1)}, f32[1,2048]{1,0:T(1,128)}, bf16[704,2048]{1,0:T(8,128)(2,1)}, bf16[704,2048]{1,0:T(8,128)(2,1)}, /*index=5*/bf16[704,2048]{1,0:T(8,128)(2,1)}) custom-call(bf16[2048,704]{1,0:T(8,128)(2,1)} %get-tuple-element.81.grad_gate, bf16[2048,704]{1,0:T(8,128)(2,1)} %get-tuple-element.82.grad_up, ...), custom_call_target="tpu_custom_call" | custom-call | flops 29527900160 | bytes 629145600 | tf_op jit(solution)/shard_map/ffn_back/pallas_call | solution.py:780
  506.6 97.3 %mixer_backward.1 = (bf16[2048,2048]{1,0:T(8,128)(2,1)}, bf16[2048,256]{1,0:T(8,128)(2,1)}, bf16[2048,256]{1,0:T(8,128)(2,1)}, bf16[2048,256]{1,0:T(8,128)(2,1)}...) custom-call(s32[1,2]{1,0:T(1,128)} %starts.3, ...), custom_call_target="tpu_custom_call" | custom-call | flops 25769803776 | bytes 54525952 | tf_op jit(solution)/shard_map/mixer_backward/pallas_call | solution.py:1385
  603.8 94.7 %last_step.1 = (f32[256,2048]{1,0:T(8,128)}, f32[16,2048]{1,0:T(8,128)}, bf16[2048,256]{1,0:T(8,128)(2,1)}, bf16[2048,256]{1,0:T(8,128)(2,1)}, bf16[2048,256]{1,...) custom-call(bf16[2048,2048]{1,0:T(8,128)(2,1)} %get-tuple-element.101.terms, ...), custom_call_target="tpu_custom_call" | custom-call | bytes 314572800 | tf_op jit(solution)/shard_map/last_step/pallas_call | solution.py:908
  698.5 15.8 %results.1 = (bf16[256,2048]{1,0:T(8,128)(2,1)}, f32[256,2048]{1,0:T(8,128)}, f32[2048,256]{1,0:T(8,128)}, f32[2048,256]{1,0:T(8,128)}, f32[2048,256]{1,0:T(8,12...) custom-call(f32[16,2048]{1,0:T(8,128)} %get-tuple-element.109.total,, ...), custom_call_target="tpu_custom_call" | custom-call | bytes 50331648 | tf_op jit(solution)/shard_map/results/pallas_call | solution.py:958

commit v8 on v7

--- a/solution.py
+++ b/solution.py
@@ -7,7 +7,6 @@
 from jax.sharding import PartitionSpec as P
 
 CHUNK = 256
-LAGS = 4
 F32, BF16 = jnp.float32, jnp.bfloat16
 
 
@@ -158,13 +157,10 @@
     return lambda start, size: ref.at[pl.ds(start, size), :]
 
 
-def ring_gather(gather, between, before=None):
+def ring_gather(gather, between):
     count = gather.ring.count
 
     def run(step, carry):
-        if before is not None:
-            before(step)
-
         @pl.when(step == 0)
         def _():
             gather.begin()
@@ -497,33 +493,47 @@
 
 
 def attend_kernel(
-    count, mixed, w_out, tokens, gain, w_gate, w_up, w_down, cotangents,
-    resid, full, hidden, grad_gate, grad_up,
-    gathered, gate_box, up_box, down_box, boxes, ahead, stages, sends, recvs, weight_sems, box_sems, out_sems, stage_sems,
+    count, mixed, w_out, tokens, gain, w_gate, w_up, w_down, cotangent,
+    resid, full, hidden, grad_gate, grad_up, cotangents,
+    gathered, out_box, gate_box, up_box, down_box, mixed_boxes, token_boxes, normed, gates, stages,
+    sends, recvs, weight_sems, keep_sem, mixed_sems, token_sems, out_sems, normed_sems, stage_sems,
 ):
     ring = Ring(count)
-    rows = tokens.shape[0]
+    rows = cotangent.shape[0]
     half = rows // 2
-    gather = Gather(
-        ring, lambda start, size: row_view(gathered, rows)(ring.me, start, size), row_view(gathered, rows),
-        sends, recvs, rows,
+    gather = Gather(ring, row_own(cotangent), row_view(gathered, rows), sends, recvs, rows)
+    keep = pltpu.make_async_copy(
+        cotangent, gathered.at[pl.ds(pl.multiple_of(ring.me * rows, rows), rows), :], keep_sem
     )
     loads = [
         pltpu.make_async_copy(source, box, weight_sems.at[k])
-        for k, (source, box) in enumerate(((w_gate, gate_box), (w_up, up_box), (w_down, down_box)))
+        for k, (source, box) in enumerate(
+            ((w_out, out_box), (w_gate, gate_box), (w_up, up_box), (w_down, down_box))
+        )
     ]
 
     def place(way, step):
         return pl.ds(pl.multiple_of(gather.origin(way, step) * rows + way * half, half), half)
 
-    def box_copy(way, step):
+    def mixed_copy(way, step):
         return pltpu.make_async_copy(
-            cotangents.at[place(way, step), :], boxes.at[step % 2, way], box_sems.at[step % 2, way]
+            mixed.at[:, place(way, step), :], mixed_boxes.at[step % 2, way], mixed_sems.at[step % 2, way]
+        )
+
+    def token_copy(way, step):
+        return pltpu.make_async_copy(
+            tokens.at[place(way, step), :], token_boxes.at[step % 2, way], token_sems.at[step % 2, way]
         )
 
     def out_copy(way, step):
         at = place(way, step)
-        return pltpu.make_async_copy(gathered.at[at, :], full.at[at, :], out_sems.at[way, step])
+        return pltpu.make_async_copy(gathered.at[at, :], cotangents.at[at, :], out_sems.at[way, step])
+
+    def normed_copy(way, step):
+        return pltpu.make_async_copy(
+            normed.at[step % 2, pl.ds(way * half, half), :], full.at[place(way, step), :],
+            normed_sems.at[step % 2, way],
+        )
 
     def stage_copy(k, way, step):
         target = (hidden, grad_gate, grad_up)[k]
@@ -532,73 +542,103 @@
         )
 
     def settle(step):
-        for k in range(3):
-            for way in (0, 1):
+        for way in (0, 1):
+            normed_copy(way, step).wait()
+            for k in range(3):
                 stage_copy(k, way, step).wait()
 
-    for way in (0, 1):
-        box_copy(way, 0).start()
+    def fetch(step):
+        for way in (0, 1):
+            mixed_copy(way, step).start()
+            token_copy(way, step).start()
+
+    def put(k, step, value):
+        low = value.astype(BF16)
+        for way in (0, 1):
+            stages[step % 2, k, way] = low[way * half : way * half + half]
+            stage_copy(k, way, step).start()
+
+    def prepare(step):
+        @pl.when(step > 1)
+        def _():
+            settle(step - 2)
+
+        slot = step % 2
+        for way in (0, 1):
+            mixed_copy(way, step).wait()
+            token_copy(way, step).wait()
+
+        @pl.when(step + 1 < count)
+        def _():
+            fetch(step + 1)
+
+        heads = jnp.concatenate(
+            [
+                jnp.concatenate([mixed_boxes[slot, way, j] for j in range(count)], 1)
+                for way in (0, 1)
+            ],
+            0,
+        )
+        value = jnp.concatenate([token_boxes[slot, 0], token_boxes[slot, 1]], 0).astype(F32)
+        value = value + mm(heads, out_box[...])
+
+        @pl.when(step == 0)
+        def _():
+            resid[...] = value
+
+        scale = lax.rsqrt(jnp.mean(value * value, axis=1, keepdims=True) + 1e-6)
+        normed[slot] = (value * scale * gain[...].astype(F32).reshape(1, -1)).astype(BF16)
+        for way in (0, 1):
+            normed_copy(way, step).start()
+        inputs = normed[slot]
+        gate = mm(inputs, gate_box[...], (1, 1))
+        up = mm(inputs, up_box[...], (1, 1))
+        sig = sigmoid(gate)
+        opened = gate * sig
+        put(0, step, opened * up)
+        gates[0] = up * sig * (1.0 + gate * (1.0 - sig))
+        gates[1] = opened
+
+    def feed(step):
+        for way in (0, 1):
+            out_copy(way, step).start()
+        grad = mm(
+            jnp.concatenate([gathered[place(0, step), :], gathered[place(1, step), :]], 0), down_box[...], (1, 1)
+        )
+        put(1, step, grad * gates[0])
+        put(2, step, grad * gates[1])
+
+    def run(step, carry):
+        @pl.when(step == 0)
+        def _():
+            gather.begin()
+            for load in loads:
+                load.wait()
+
+        prepare(step)
+
+        @pl.when(step == 0)
+        def _():
+            keep.wait()
+
+        @pl.when((step > 0) & (step < count - 1))
+        def _():
+            gather.hop(step)
+
+        @pl.when(step == count - 1)
+        def _():
+            gather.arrived(step)
+
+        feed(step)
+        return carry
+
+    keep.start()
+    fetch(0)
     for load in loads:
         load.start()
     greet(ring)
-    value = tokens[...].astype(F32) + mm(mixed[...], w_out[...])
-    resid[...] = value
-    scale = lax.rsqrt(jnp.mean(value * value, axis=1, keepdims=True) + 1e-6)
-    gathered[pl.ds(pl.multiple_of(ring.me * rows, rows), rows), :] = (
-        value * scale * gain[...].astype(F32).reshape(1, -1)
-    ).astype(BF16)
-
-    def hide(step):
-        @pl.when(step == 0)
-        def _():
-            loads[2].wait()
-
-        for way in (0, 1):
-            box_copy(way, step).wait()
-
-        @pl.when(step + 1 < count)
-        def _():
-            for way in (0, 1):
-                box_copy(way, step + 1).start()
-
-        slot = step % 2
-        ahead[...] = mm(jnp.concatenate([boxes[slot, 0], boxes[slot, 1]], 0), down_box[...], (1, 1))
-
-    def feed(step):
-        @pl.when(step == 0)
-        def _():
-            loads[0].wait()
-            loads[1].wait()
-
-        @pl.when(step > 1)
-        def _():
-            settle(step - 2)
-
-        for way in (0, 1):
-            out_copy(way, step).start()
-        slot = step % 2
-        inputs = jnp.concatenate([gathered[place(0, step), :], gathered[place(1, step), :]], 0)
-        gate = mm(inputs, gate_box[...], (1, 1))
-        up = mm(inputs, up_box[...], (1, 1))
-        grad = ahead[...]
-        sig = sigmoid(gate)
-        opened = gate * sig
-        for k, result in enumerate(
-            (opened * up, grad * up * sig * (1.0 + gate * (1.0 - sig)), grad * opened)
-        ):
-            low = result.astype(BF16)
-            for way in (0, 1):
-                stages[slot, k, way] = low[way * half : way * half + half]
-                stage_copy(k, way, step).start()
-
-    def before(step):
-        pl.when(step > 0)(lambda: hide(step))
-
-    def between(step):
-        pl.when(step == 0)(lambda: hide(step))
-        feed(step)
-
-    ring_gather(gather, between, before)
+    lax.fori_loop(0, count, run, 0)
+    gather.end()
     settle(count - 2)
     settle(count - 1)
 
@@ -610,9 +650,10 @@
     lax.fori_loop(0, count, drain, 0)
 
 
-def attend(mixed, w_out, tokens, gain, w_gate, w_up, w_down, cotangents, count):
-    rows, model = tokens.shape
+def attend(mixed, w_out, tokens, gain, w_gate, w_up, w_down, cotangent, count):
+    rows, model = cotangent.shape
     slots, inner = count * rows, w_down.shape[0]
+    wide = mixed.shape[2]
     return pl.pallas_call(
         functools.partial(attend_kernel, count),
         name="attend",
@@ -620,29 +661,35 @@
             jax.ShapeDtypeStruct((rows, model), F32),
             jax.ShapeDtypeStruct((slots, model), BF16),
         ]
-        + [jax.ShapeDtypeStruct((slots, inner), BF16)] * 3,
-        in_specs=[VMEM] * 4 + [ANY] * 4,
-        out_specs=[VMEM] + [ANY] * 4,
-        scratch_shapes=[pltpu.VMEM((slots, model), BF16)]
+        + [jax.ShapeDtypeStruct((slots, inner), BF16)] * 3
+        + [jax.ShapeDtypeStruct((slots, model), BF16)],
+        in_specs=[ANY] * 3 + [VMEM] + [ANY] * 4,
+        out_specs=[VMEM] + [ANY] * 5,
+        scratch_shapes=[pltpu.VMEM((slots, model), BF16), pltpu.VMEM(w_out.shape, BF16)]
         + [pltpu.VMEM((inner, model), BF16)] * 3
         + [
+            pltpu.VMEM((2, 2, count, rows // 2, wide), BF16),
             pltpu.VMEM((2, 2, rows // 2, model), BF16),
-            pltpu.VMEM((rows, inner), F32),
+            pltpu.VMEM((2, rows, model), BF16),
+            pltpu.VMEM((2, rows, inner), F32),
             pltpu.VMEM((2, 3, 2, rows // 2, inner), BF16),
         ]
         + ring_semaphores(count)
         + [
-            pltpu.SemaphoreType.DMA((3,)),
+            pltpu.SemaphoreType.DMA((4,)),
+            pltpu.SemaphoreType.DMA,
+            pltpu.SemaphoreType.DMA((2, 2)),
             pltpu.SemaphoreType.DMA((2, 2)),
             pltpu.SemaphoreType.DMA((2, count)),
+            pltpu.SemaphoreType.DMA((2, 2)),
             pltpu.SemaphoreType.DMA((2, 3, 2)),
         ],
         compiler_params=ring_params(2),
         cost_estimate=pl.CostEstimate(
-            flops=2 * rows * model * model + 6 * slots * model * inner, bytes_accessed=300 << 20,
+            flops=2 * slots * model * model + 6 * slots * model * inner, bytes_accessed=300 << 20,
             transcendentals=slots * inner,
         ),
-    )(mixed, w_out, tokens, gain, w_gate, w_up, w_down, cotangents)
+    )(mixed, w_out, tokens, gain, w_gate, w_up, w_down, cotangent)
 
 
 def norm_back(inputs, scale, gain, grad_normed):
@@ -979,12 +1026,12 @@
 
 
 def forward_kernel(
-    heads, width, seqs, count, rows_own, chunks,
+    heads, width, seqs, count, chunks,
     starts, lengths, tokens, w_query, w_key, w_value, w_gate, w_beta,
-    taps_query, taps_key, taps_value, gain, gain_first, side,
-    mixed_own, mixed, p_query, p_key, p_value, p_gate, p_beta, z_query, z_key, z_value,
-    delta_out, change_out, inverse_out, state_out, side_full,
-    tail_query, tail_key, tail_value, state, stage, sends, recvs, local, row_sends, row_recvs,
+    taps_query, taps_key, taps_value, gain, gain_first,
+    mixed_full, mixed, p_query, p_key, p_value, p_gate, p_beta, z_query, z_key, z_value,
+    delta_out, change_out, inverse_out, state_out,
+    tail_query, tail_key, tail_value, state, stage, sends, recvs, keeps,
 ):
     step = pl.program_id(0)
     size = tokens.shape[0]
@@ -997,41 +1044,32 @@
         state[...] = jnp.zeros_like(state)
 
     ring = Ring(count)
-    me, group = ring.me, ring.group
-    wide = heads * width
-    gather = Gather(ring, row_own(side), row_view(side_full, rows_own), sends, recvs, rows_own)
-    keep = pltpu.make_async_copy(
-        side, side_full.at[pl.ds(pl.multiple_of(me * rows_own, rows_own), rows_own), :], local.at[0]
-    )
-    own_columns = pl.ds(pl.multiple_of(me * wide, wide), wide)
-
-    def keep_rows():
-        return pltpu.make_async_copy(stage.at[me], mixed_own.at[:, own_columns], local.at[1])
-
-    def row_copy(target):
-        return pltpu.make_async_remote_copy(
-            src_ref=stage.at[target], dst_ref=mixed_own.at[:, own_columns],
-            send_sem=row_sends.at[target], recv_sem=row_recvs.at[me],
-            device_id=(group, target), device_id_type=MESH,
-        )
-
-    def row_arrival(origin):
-        return pltpu.make_async_remote_copy(
-            src_ref=stage.at[me], dst_ref=mixed_own.at[:, own_columns],
-            send_sem=row_sends.at[origin], recv_sem=row_recvs.at[origin],
-            device_id=(group, origin), device_id_type=MESH,
-        )
-
-    @pl.when(step == 0)
-    def _():
-        barrier = pltpu.get_barrier_semaphore()
-        for k in range(1, count):
-            pl.semaphore_signal(barrier, inc=1, device_id=(group, (me + k) % count), device_id_type=MESH)
-        pl.semaphore_wait(barrier, count - 1)
-        gather.begin()
-        keep.start()
-
-    spread_hops(step, chunks, count, gather.hop, 1)
+
+    def chunk_gather(chunk):
+        return Gather(
+            ring,
+            lambda start, length: stage.at[chunk, pl.ds(start, length), :],
+            lambda origin, start, length: mixed_full.at[
+                origin, pl.ds(pl.multiple_of(chunk * size + start, length), length), :
+            ],
+            sends.at[chunk], recvs.at[chunk], size, 1,
+        )
+
+    def keep(chunk):
+        return pltpu.make_async_copy(
+            stage.at[chunk],
+            mixed_full.at[ring.me, pl.ds(pl.multiple_of(chunk * size, size), size), :],
+            keeps.at[chunk],
+        )
+
+    def turn(late):
+        for age in range(1, count // 2 + 1):
+            number = 2 * age - 1 + late
+            if number < count - 1:
+                pl.when(step >= age)(lambda age=age, number=number: chunk_gather(step - age).hop(number))
+
+    pl.when(step == 0)(lambda: greet(ring))
+    turn(0)
     rows, seg_rows, seg_columns, before, last = chunk_masks(starts, lengths, seqs, first, size)
     same = seg_rows == seg_columns
     i = lax.broadcasted_iota(jnp.int32, (size, size), 0)
@@ -1072,6 +1110,8 @@
     scale = width ** (-0.5)
     head_gain = gain[...].astype(F32)
     for h in range(heads):
+        if h == heads // 2:
+            turn(1)
         cols = slice(h * width, (h + 1) * width)
         uq, uk = u_query[:, cols], u_key[:, cols]
         query = (uq * lax.rsqrt(jnp.sum(uq * uq, axis=1, keepdims=True) + 1e-6)).astype(BF16)
@@ -1094,41 +1134,32 @@
         normal = out * lax.rsqrt(jnp.mean(out * out, axis=1, keepdims=True) + 1e-5) * head_gain
         low_mixed = (normal * opened[:, cols] * live).astype(BF16)
         mixed[:, cols] = low_mixed
-        for place in range(size // rows_own):
-            stage[step * (size // rows_own) + place, :, cols] = low_mixed[place * rows_own : (place + 1) * rows_own]
-
-    each = size // rows_own
-
-    def send(chunk, due):
-        for place in range(each):
-            target = chunk * each + place
-
-            @pl.when((chunk >= 0) & (target != me) & due((me + target) % LAGS))
-            def _():
-                row_copy(target).start()
-
-    for lag in range(LAGS):
-        send(step - lag, lambda own_lag, lag=lag: own_lag == lag)
-    for place in range(each):
-        pl.when(step * each + place == me)(lambda: keep_rows().start())
+        stage[step, :, cols] = low_mixed
+
+    chunk_gather(step).begin()
+    keep(step).start()
 
     @pl.when(step == chunks - 1)
     def _():
-        for back in range(LAGS - 1):
-            send(step - back, lambda own_lag, back=back: own_lag > back)
-
-    @pl.when(step == chunks - 1)
-    def _():
-        gather.arrived(count - 1)
-        gather.end()
-        keep.wait()
-        keep_rows().wait()
-        for k in range(1, count):
-            row_copy((me + k) % count).wait_send()
-            row_arrival((me + k) % count).wait_recv()
-
-
-def forward_mixer(tokens, w_query, w_key, w_value, w_gate, w_beta, taps_query, taps_key, taps_value, gain, gain_first, starts, lengths, side, count):
+        def finish(number, carry):
+            for age in range(min(chunks, count // 2)):
+                pl.when(2 * age + number < count - 1)(
+                    lambda age=age: chunk_gather(chunks - 1 - age).hop(2 * age + number)
+                )
+            return carry
+
+        lax.fori_loop(1, count - 1, finish, 0)
+
+        def settle(chunk, carry):
+            chunk_gather(chunk).arrived(count - 1)
+            chunk_gather(chunk).end()
+            keep(chunk).wait()
+            return carry
+
+        lax.fori_loop(0, chunks, settle, 0)
+
+
+def forward_mixer(tokens, w_query, w_key, w_value, w_gate, w_beta, taps_query, taps_key, taps_value, gain, gain_first, starts, lengths, count):
     slots, model = tokens.shape
     wide = w_query.shape[1]
     width = gain.shape[0]
@@ -1139,43 +1170,40 @@
     smem = pl.BlockSpec(memory_space=pltpu.SMEM)
     whole = lambda shape: pl.BlockSpec(shape, lambda n: (0,) * len(shape))
     piece = lambda shape: pl.BlockSpec(shape, lambda n: (n,) + (0,) * (len(shape) - 1))
-    own = (slots // count, count * wide)
     outs = [
         ((slots, wide), BF16), ((slots, wide), F32), ((slots, wide), F32), ((slots, wide), F32), ((slots, wide), F32),
         ((slots, w_beta.shape[0]), F32), ((slots, wide), F32), ((slots, wide), F32), ((slots, wide), F32),
         ((slots, wide), F32), ((slots, wide), BF16),
     ]
     return pl.pallas_call(
-        functools.partial(forward_kernel, heads, width, seqs, count, slots // count, chunks),
+        functools.partial(forward_kernel, heads, width, seqs, count, chunks),
         name="mixer_forward",
         grid=(chunks,),
-        out_shape=[jax.ShapeDtypeStruct(own, BF16)]
+        out_shape=[jax.ShapeDtypeStruct((count, slots, wide), BF16)]
         + [jax.ShapeDtypeStruct(s, d) for s, d in outs]
         + [
             jax.ShapeDtypeStruct((chunks, heads, CHUNK, CHUNK), BF16),
             jax.ShapeDtypeStruct((chunks, heads, width, width), BF16),
-            jax.ShapeDtypeStruct((slots, model), BF16),
         ],
         in_specs=[smem, smem, piece((CHUNK, model))]
         + [whole((model, wide))] * 4
         + [whole(w_beta.shape)]
         + [whole((taps, wide))] * 3
-        + [whole((1, width)), VMEM, ANY],
+        + [whole((1, width)), VMEM],
         out_specs=[ANY]
         + [piece((CHUNK, s[1])) for s, d in outs]
-        + [piece((1, heads, CHUNK, CHUNK)), piece((1, heads, width, width)), ANY],
+        + [piece((1, heads, CHUNK, CHUNK)), piece((1, heads, width, width))],
         scratch_shapes=[pltpu.VMEM((CHUNK + 8, wide), F32)] * 3
-        + [pltpu.VMEM((heads, width, width), F32), pltpu.VMEM((count, slots // count, wide), BF16)]
-        + ring_semaphores(count)
-        + [pltpu.SemaphoreType.DMA((2,))]
-        + [pltpu.SemaphoreType.DMA((count,))] * 2,
+        + [pltpu.VMEM((heads, width, width), F32), pltpu.VMEM((chunks, CHUNK, wide), BF16)]
+        + [pltpu.SemaphoreType.DMA((chunks, 2, 1, count - 1))] * 2
+        + [pltpu.SemaphoreType.DMA((chunks,))],
         compiler_params=ring_params(5),
         cost_estimate=pl.CostEstimate(
             flops=2 * slots * model * wide * 4 + slots * heads * CHUNK * 2 * CHUNK * 20,
             bytes_accessed=slots * model * 2 + 4 * model * wide * 2 + slots * wide * 36,
             transcendentals=slots * wide * 4,
         ),
-    )(starts, lengths, tokens, w_query, w_key, w_value, w_gate, w_beta, taps_query, taps_key, taps_value, gain.reshape(1, width), gain_first, side)
+    )(starts, lengths, tokens, w_query, w_key, w_value, w_gate, w_beta, taps_query, taps_key, taps_value, gain.reshape(1, width), gain_first)
 
 
 def small_rows(heads, taps):
@@ -1420,13 +1448,12 @@
         heads = w_beta.shape[1]
         beta_rows = w_beta.T if heads > 1 else jnp.pad(w_beta.T, ((0, 1), (0, 0)))
         tokens_full, w_out_full = gather_tokens(tokens, w_out, count, groups)
-        mixed_own, *saved = forward_mixer(
+        mixed_full, *saved = forward_mixer(
             tokens_full, w_query, w_key, w_value, w_gate_out, beta_rows,
-            conv_query, conv_key, conv_value, head_gain, attn_gain, seq_starts, seq_lengths, cotangent, count,
-        )
-        grad_full, saved = saved[-1], saved[:-1]
-        resid, ffn_full, hidden, grad_gate, grad_up = attend(
-            mixed_own, w_out_full, tokens, ffn_gain, w_gate.T, w_up.T, w_down, grad_full, count
+            conv_query, conv_key, conv_value, head_gain, attn_gain, seq_starts, seq_lengths, count,
+        )
+        resid, ffn_full, hidden, grad_gate, grad_up, grad_full = attend(
+            mixed_full, w_out_full, tokens_full, ffn_gain, w_gate.T, w_up.T, w_down, cotangent, count
         )
         grad_resid, grad_attended, g_second, *ffn_grads = ffn_back(
             grad_gate, grad_up, hidden, w_gate.T, w_up.T, resid, cotangent, ffn_gain, ffn_full, grad_full,

time: 716 us -> 709 us (level)
  Pallas kernels: 714 us -> 706 us
    pallas_call x1, Pallas kernels: 105 us -> 87.9 us  [attend(): pl.pallas_call(functools.partial(attend_kernel, count), name='attend', ou...]
    pallas_call x1, Pallas kernels: 94.7 us -> 103 us  [last_step(): pl.pallas_call(functools.partial(last_kernel, count, groups, rows), name=...]
where the time goes in v8:
time: 709 us; the launch traced here: 707 us
  Pallas kernels  706 us (100%)
    pallas_call x1, Pallas kernels, ffn_back(): pl.pallas_call(functools.partial(ffn_back_kernel, count, groups, rows), n...  169 us
    pallas_call x1, Pallas kernels, forward_mixer(): pl.pallas_call(functools.partial(forward_kernel, heads, width, seqs, coun...  120 us
    pallas_call x1, Pallas kernels, gather_tokens(): pl.pallas_call(functools.partial(gather_kernel, count, groups), name='gat...  115 us
    pallas_call x1, Pallas kernels, last_step(): pl.pallas_call(functools.partial(last_kernel, count, groups, rows), name=...  103 us
    pallas_call x1, Pallas kernels, backward_mixer(): pl.pallas_call(functools.partial(backward_kernel, heads, width, seqs, chu...  95.9 us
    pallas_call x1, Pallas kernels, attend(): pl.pallas_call(functools.partial(attend_kernel, count), name='attend', ou...  87.9 us
    pallas_call x1, Pallas kernels, results(): pl.pallas_call(functools.partial(results_kernel, heads, taps, wide, width...  15.8 us

profile of v8, /device:TPU:0, one launch (start us, length us, event | category | flops | bytes accessed | tf_op | source)
XLA Modules:
  0.0 707.2 jit_solution(13607344023322948692)
XLA Ops:
  0.7 115.3 %gather_tokens.1 = (bf16[2048,2048]{1,0:T(8,128)(2,1)}, bf16[8,4,64,2048]{3,2,1,0:T(8,128)(2,1)}) custom-call(bf16[256,2048]{1,0:T(8,128)(2,1)} %tokens_in.1, bf16[256,2048]{1,0:T(8,128)(2,1)} %w_out.3), custom_call_target="tpu_custom_call" | custom-call | bytes 314572800 | tf_op jit(solution)/shard_map/gather_tokens/pallas_call | solution.py:473
  115.9 119.8 %mixer_forward.1 = (bf16[8,2048,256]{2,1,0:T(8,128)(2,1)}, bf16[2048,256]{1,0:T(8,128)(2,1)}, f32[2048,256]{1,0:T(8,128)}, f32[2048,256]{1,0:T(8,128)}, f32[2048...) custom-call(s32[1,2]{1,0:T(1,128)} %starts.3, ...), custom_call_target="tpu_custom_call" | custom-call | flops 19327352832 | bytes 31457280 | tf_op jit(solution)/shard_map/mixer_forward/pallas_call | solution.py:1178
  235.8 87.9 %attend.1 = (f32[256,2048]{1,0:T(8,128)}, bf16[2048,2048]{1,0:T(8,128)(2,1)}, bf16[2048,704]{1,0:T(8,128)(2,1)}, bf16[2048,704]{1,0:T(8,128)(2,1)}, bf16[2048,70...) custom-call(bf16[8,2048,256]{2,1,0:T(8,128)(2,1)} %get-tuple-element.78.mixed, bf16[2048,2048]{1,0:T(8,128)(2,1)} %bitcast.11, ...), custom_call_target="tpu_custom_call" | custom-call | flops 34896609280 | bytes 314572800 | tf_op jit(solution)/shard_map/attend/pallas_call | solution.py:657
  323.6 168.9 %ffn_back.1 = (f32[256,2048]{1,0:T(8,128)}, bf16[2048,2048]{1,0:T(8,128)(2,1)}, f32[1,2048]{1,0:T(1,128)}, bf16[704,2048]{1,0:T(8,128)(2,1)}, bf16[704,2048]{1,0:T(8,128)(2,1)}, /*index=5*/bf16[704,2048]{1,0:T(8,128)(2,1)}) custom-call(bf16[2048,704]{1,0:T(8,128)(2,1)} %get-tuple-element.80.grad_gate, bf16[2048,704]{1,0:T(8,128)(2,1)} %get-tuple-element.81.grad_up, ...), custom_call_target="tpu_custom_call" | custom-call | flops 29527900160 | bytes 629145600 | tf_op jit(solution)/shard_map/ffn_back/pallas_call | solution.py:827
  492.6 95.9 %mixer_backward.1 = (bf16[2048,2048]{1,0:T(8,128)(2,1)}, bf16[2048,256]{1,0:T(8,128)(2,1)}, bf16[2048,256]{1,0:T(8,128)(2,1)}, bf16[2048,256]{1,0:T(8,128)(2,1)}...) custom-call(s32[1,2]{1,0:T(1,128)} %starts.3, ...), custom_call_target="tpu_custom_call" | custom-call | flops 25769803776 | bytes 54525952 | tf_op jit(solution)/shard_map/mixer_backward/pallas_call | solution.py:1413
  588.5 102.7 %last_step.1 = (f32[256,2048]{1,0:T(8,128)}, f32[16,2048]{1,0:T(8,128)}, bf16[2048,256]{1,0:T(8,128)(2,1)}, bf16[2048,256]{1,0:T(8,128)(2,1)}, bf16[2048,256]{1,...) custom-call(bf16[2048,2048]{1,0:T(8,128)(2,1)} %get-tuple-element.101.terms, ...), custom_call_target="tpu_custom_call" | custom-call | bytes 314572800 | tf_op jit(solution)/shard_map/last_step/pallas_call | solution.py:955
  691.1 15.8 %results.1 = (bf16[256,2048]{1,0:T(8,128)(2,1)}, f32[256,2048]{1,0:T(8,128)}, f32[2048,256]{1,0:T(8,128)}, f32[2048,256]{1,0:T(8,128)}, f32[2048,256]{1,0:T(8,12...) custom-call(f32[16,2048]{1,0:T(8,128)} %get-tuple-element.109.total,, ...), custom_call_target="tpu_custom_call" | custom-call | bytes 50331648 | tf_op jit(solution)/shard_map/results/pallas_call | solution.py:1005

commit v9 on v8

--- a/solution.py
+++ b/solution.py
@@ -387,109 +387,90 @@
     )
 
 
-WEIGHT_HOPS = 3
-
-
-def gather_kernel(
-    count, groups, tokens, w_out, tokens_full, w_full,
-    sends, recvs, w_sends, w_recvs, local, far_sems, near_sems,
-):
+class WholeWeight:
+    def __init__(self, ring, groups, weight, full, sends, recvs, keep_sem, far_sems, near_sems):
+        self.ring, self.groups, self.full, self.far_sems, self.near_sems = ring, groups, full, far_sems, near_sems
+        part = weight.shape[0] // groups
+        group = ring.group
+        own = lambda start, size: weight.at[pl.ds(pl.multiple_of(group * part + start, size), size), :]
+        self.gather = Gather(
+            ring, own, lambda origin, start, size: full.at[origin, group, pl.ds(start, size), :],
+            sends, recvs, part, 1,
+        )
+        self.keep = pltpu.make_async_copy(own(0, part), full.at[ring.me, group], keep_sem)
+        self.mate = (group + 1 - 2 * (group % 2), ring.me)
+        self.across = groups // 2
+
+    def peer(self, k):
+        return ((self.ring.group + 2 * k) % self.groups, self.ring.me)
+
+    def peers(self):
+        return [self.mate] + [self.peer(k) for k in range(1, self.across)]
+
+    def far(self, k):
+        part = self.full.at[:, self.ring.group]
+        return pltpu.make_async_remote_copy(
+            src_ref=part, dst_ref=part, send_sem=self.far_sems.at[0, k - 1], recv_sem=self.far_sems.at[1, k - 1],
+            device_id=self.peer(k), device_id_type=MESH,
+        )
+
+    def near(self, k):
+        part = self.full.at[:, (self.ring.group + self.groups - 2 * k) % self.groups]
+        return pltpu.make_async_remote_copy(
+            src_ref=part, dst_ref=part, send_sem=self.near_sems.at[0, k], recv_sem=self.near_sems.at[1, k],
+            device_id=self.mate, device_id_type=MESH,
+        )
+
+    def begin(self):
+        self.gather.begin()
+        self.keep.start()
+
+    def exchange(self):
+        self.gather.arrived(self.ring.count - 1)
+        self.keep.wait()
+        for k in range(1, self.across):
+            self.far(k).start()
+        self.near(0).start()
+
+    def back(self):
+        for k in range(1, self.across):
+            self.far(k).wait_recv()
+            self.near(k).start()
+
+    def end(self):
+        for k in range(self.across):
+            self.near(k).wait()
+        for k in range(1, self.across):
+            self.far(k).wait_send()
+        self.gather.end()
+
+
+def gather_kernel(count, tokens, tokens_full, sends, recvs, local):
     ring = Ring(count)
     rows = tokens.shape[0]
-    group, me = ring.group, ring.me
-    part = w_out.shape[0] // groups
-    across = groups // 2
-    mate = (group + 1 - 2 * (group % 2), me)
-    gather = Gather(ring, row_own(tokens), row_view(tokens_full, rows), sends, recvs, rows)
-    own_part = lambda start, size: w_out.at[pl.ds(pl.multiple_of(group * part + start, size), size), :]
-    weights = Gather(
-        ring, own_part, lambda origin, start, size: w_full.at[origin, group, pl.ds(start, size), :],
-        w_sends, w_recvs, part, 1,
+    greet(ring)
+    keep = pltpu.make_async_copy(
+        tokens, tokens_full.at[pl.ds(pl.multiple_of(ring.me * rows, rows), rows), :], local
     )
-    keep = pltpu.make_async_copy(
-        tokens, tokens_full.at[pl.ds(pl.multiple_of(me * rows, rows), rows), :], local.at[0]
+    keep.start()
+    ring_gather(
+        Gather(ring, row_own(tokens), row_view(tokens_full, rows), sends, recvs, rows), lambda step: None
     )
-    keep_part = pltpu.make_async_copy(own_part(0, part), w_full.at[me, group], local.at[1])
-
-    def far(k):
-        return pltpu.make_async_remote_copy(
-            src_ref=w_full.at[:, group], dst_ref=w_full.at[:, group],
-            send_sem=far_sems.at[0, k - 1], recv_sem=far_sems.at[1, k - 1],
-            device_id=((group + 2 * k) % groups, me), device_id_type=MESH,
-        )
-
-    def near(k):
-        held = (group + groups - 2 * k) % groups
-        return pltpu.make_async_remote_copy(
-            src_ref=w_full.at[:, held], dst_ref=w_full.at[:, held],
-            send_sem=near_sems.at[0, k], recv_sem=near_sems.at[1, k],
-            device_id=mate, device_id_type=MESH,
-        )
-
-    greet(ring, [mate] + [((group + 2 * k) % groups, me) for k in range(1, across)])
-    weights.begin()
-    gather.begin()
-    keep.start()
-    keep_part.start()
-    whole_at = -(-(count - 2) // WEIGHT_HOPS) + 1
-
-    def forward(step, carry):
-        for place in range(WEIGHT_HOPS):
-            number = (step - 1) * WEIGHT_HOPS + place + 1
-
-            @pl.when(number < count - 1)
-            def _():
-                weights.hop(number)
-
-        gather.hop(step)
-
-        @pl.when(step == whole_at)
-        def _():
-            weights.arrived(count - 1)
-            keep_part.wait()
-            for k in range(1, across):
-                far(k).start()
-            near(0).start()
-
-        return carry
-
-    lax.fori_loop(1, count - 1, forward, 0)
-    for k in range(1, across):
-        far(k).wait_recv()
-        near(k).start()
-    gather.arrived(count - 1)
-    for k in range(across):
-        near(k).wait()
-    for k in range(1, across):
-        far(k).wait_send()
-    weights.end()
-    gather.end()
     keep.wait()
 
 
-def gather_tokens(tokens, w_out, count, groups):
+def gather_tokens(tokens, count):
     rows, model = tokens.shape
-    part = w_out.shape[0] // groups
-    full, w_full = pl.pallas_call(
-        functools.partial(gather_kernel, count, groups),
+    return pl.pallas_call(
+        functools.partial(gather_kernel, count),
         name="gather_tokens",
-        out_shape=[
-            jax.ShapeDtypeStruct((count * rows, model), tokens.dtype),
-            jax.ShapeDtypeStruct((count, groups, part, model), w_out.dtype),
-        ],
-        in_specs=[ANY] * 2,
-        out_specs=[ANY] * 2,
-        scratch_shapes=ring_semaphores(count)
-        + ring_semaphores(count, 1)
-        + [
-            pltpu.SemaphoreType.DMA((2,)),
-            pltpu.SemaphoreType.DMA((2, groups // 2 - 1)),
-            pltpu.SemaphoreType.DMA((2, groups // 2)),
-        ],
+        out_shape=jax.ShapeDtypeStruct((count * rows, model), tokens.dtype),
+        in_specs=[ANY],
+        out_specs=ANY,
+        scratch_shapes=ring_semaphores(count) + [pltpu.SemaphoreType.DMA],
         compiler_params=ring_params(1),
         cost_estimate=pl.CostEstimate(flops=0, bytes_accessed=300 << 20, transcendentals=0),
-    )(tokens, w_out)
-    return full, w_full.reshape(count * w_out.shape[0], model)
+    )(tokens)
 
 
 def attend_kernel(
@@ -1025,13 +1006,47 @@
             hop(number)
 
 
+def plan_hops(chunks, hops, latency=1.4, segment=2.5):
+    now, link, due, done, table = 0.0, 0.0, {}, {}, []
+
+    def send(chunk):
+        nonlocal link
+        link = max(now, link) + 1.0
+        done[chunk] = done.get(chunk, -1) + 1
+        due[chunk] = link + latency
+
+    def waiting():
+        return [chunk for chunk in done if done[chunk] < hops - 1]
+
+    for step in range(chunks):
+        for half in range(2):
+            ready, moves = True, []
+            while ready:
+                ready = sorted((due[chunk], chunk) for chunk in waiting() if due[chunk] <= now)
+                if ready:
+                    send(ready[0][1])
+                    moves.append((ready[0][1], done[ready[0][1]]))
+            table.append(moves)
+            now += segment
+        send(step)
+    rest = []
+    while waiting():
+        now, chunk = max((now, 0), min((due[chunk], chunk) for chunk in waiting()))[0], min(
+            (due[chunk], chunk) for chunk in waiting()
+        )[1]
+        send(chunk)
+        rest.append((chunk, done[chunk]))
+    return table, rest
+
+
 def forward_kernel(
-    heads, width, seqs, count, chunks,
+    heads, width, seqs, count, groups, chunks,
     starts, lengths, tokens, w_query, w_key, w_value, w_gate, w_beta,
-    taps_query, taps_key, taps_value, gain, gain_first,
-    mixed_full, mixed, p_query, p_key, p_value, p_gate, p_beta, z_query, z_key, z_value,
+    taps_query, taps_key, taps_value, gain, gain_first, w_out,
+    mixed_full, w_full, mixed, p_query, p_key, p_value, p_gate, p_beta, z_query, z_key, z_value,
     delta_out, change_out, inverse_out, state_out,
     tail_query, tail_key, tail_value, state, stage, sends, recvs, keeps,
+    w_sends, w_recvs, w_keep, w_far, w_near,
 ):
     step = pl.program_id(0)
     size = tokens.shape[0]
@@ -1062,13 +1077,30 @@
             keeps.at[chunk],
         )
 
+    weight = WholeWeight(ring, groups, w_out, w_full, w_sends, w_recvs, w_keep, w_far, w_near)
+    table, rest = plan_hops(chunks, count - 1)
+
     def turn(late):
-        for age in range(1, count // 2 + 1):
-            number = 2 * age - 1 + late
-            if number < count - 1:
-                pl.when(step >= age)(lambda age=age, number=number: chunk_gather(step - age).hop(number))
-
-    pl.when(step == 0)(lambda: greet(ring))
+        number = 2 * step + late
+
+        @pl.when((number > 0) & (number < count - 1))
+        def _():
+            weight.gather.hop(number)
+
+        if late == (count - 1) % 2:
+            pl.when(number == count - 1)(weight.exchange)
+        for place, moves in enumerate(table[late::2]):
+            if moves:
+                @pl.when(step == place)
+                def _():
+                    for chunk, hop in moves:
+                        chunk_gather(chunk).hop(hop)
+
+    @pl.when(step == 0)
+    def _():
+        greet(ring, weight.peers())
+        weight.begin()
+
     turn(0)
     rows, seg_rows, seg_columns, before, last = chunk_masks(starts, lengths, seqs, first, size)
     same = seg_rows == seg_columns
@@ -1141,14 +1173,10 @@
 
     @pl.when(step == chunks - 1)
     def _():
-        def finish(number, carry):
-            for age in range(min(chunks, count // 2)):
-                pl.when(2 * age + number < count - 1)(
-                    lambda age=age: chunk_gather(chunks - 1 - age).hop(2 * age + number)
-                )
-            return carry
-
-        lax.fori_loop(1, count - 1, finish, 0)
+        for place, (chunk, hop) in enumerate(rest):
+            if place == len(rest) // 2:
+                weight.back()
+            chunk_gather(chunk).hop(hop)
 
         def settle(chunk, carry):
             chunk_gather(chunk).arrived(count - 1)
@@ -1157,9 +1185,10 @@
             return carry
 
         lax.fori_loop(0, chunks, settle, 0)
-
-
-def forward_mixer(tokens, w_query, w_key, w_value, w_gate, w_beta, taps_query, taps_key, taps_value, gain, gain_first, starts, lengths, count):
+        weight.end()
+
+
+def forward_mixer(tokens, w_query, w_key, w_value, w_gate, w_beta, taps_query, taps_key, taps_value, gain, gain_first, starts, lengths, w_out, count, groups):
     slots, model = tokens.shape
     wide = w_query.shape[1]
     width = gain.shape[0]
@@ -1167,6 +1196,7 @@
     seqs = starts.shape[1]
     chunks = slots // CHUNK
     taps = taps_query.shape[0]
+    part = w_out.shape[0] // groups
     smem = pl.BlockSpec(memory_space=pltpu.SMEM)
     whole = lambda shape: pl.BlockSpec(shape, lambda n: (0,) * len(shape))
     piece = lambda shape: pl.BlockSpec(shape, lambda n: (n,) + (0,) * (len(shape) - 1))
@@ -1176,10 +1206,13 @@
         ((slots, wide), F32), ((slots, wide), BF16),
     ]
     return pl.pallas_call(
-        functools.partial(forward_kernel, heads, width, seqs, count, chunks),
+        functools.partial(forward_kernel, heads, width, seqs, count, groups, chunks),
         name="mixer_forward",
         grid=(chunks,),
-        out_shape=[jax.ShapeDtypeStruct((count, slots, wide), BF16)]
+        out_shape=[
+            jax.ShapeDtypeStruct((count, slots, wide), BF16),
+            jax.ShapeDtypeStruct((count, groups, part, model), BF16),
+        ]
         + [jax.ShapeDtypeStruct(s, d) for s, d in outs]
         + [
             jax.ShapeDtypeStruct((chunks, heads, CHUNK, CHUNK), BF16),
@@ -1189,21 +1222,27 @@
         + [whole((model, wide))] * 4
         + [whole(w_beta.shape)]
         + [whole((taps, wide))] * 3
-        + [whole((1, width)), VMEM],
-        out_specs=[ANY]
+        + [whole((1, width)), VMEM, ANY],
+        out_specs=[ANY, ANY]
         + [piece((CHUNK, s[1])) for s, d in outs]
         + [piece((1, heads, CHUNK, CHUNK)), piece((1, heads, width, width))],
         scratch_shapes=[pltpu.VMEM((CHUNK + 8, wide), F32)] * 3
         + [pltpu.VMEM((heads, width, width), F32), pltpu.VMEM((chunks, CHUNK, wide), BF16)]
         + [pltpu.SemaphoreType.DMA((chunks, 2, 1, count - 1))] * 2
-        + [pltpu.SemaphoreType.DMA((chunks,))],
+        + [pltpu.SemaphoreType.DMA((chunks,))]
+        + ring_semaphores(count, 1)
+        + [
+            pltpu.SemaphoreType.DMA,
+            pltpu.SemaphoreType.DMA((2, groups // 2 - 1)),
+            pltpu.SemaphoreType.DMA((2, groups // 2)),
+        ],
         compiler_params=ring_params(5),
         cost_estimate=pl.CostEstimate(
             flops=2 * slots * model * wide * 4 + slots * heads * CHUNK * 2 * CHUNK * 20,
             bytes_accessed=slots * model * 2 + 4 * model * wide * 2 + slots * wide * 36,
             transcendentals=slots * wide * 4,
         ),
-    )(starts, lengths, tokens, w_query, w_key, w_value, w_gate, w_beta, taps_query, taps_key, taps_value, gain.reshape(1, width), gain_first)
+    )(starts, lengths, tokens, w_query, w_key, w_value, w_gate, w_beta, taps_query, taps_key, taps_value, gain.reshape(1, width), gain_first, w_out)
 
 
 def small_rows(heads, taps):
@@ -1447,11 +1486,12 @@
         model = tokens.shape[1]
         heads = w_beta.shape[1]
         beta_rows = w_beta.T if heads > 1 else jnp.pad(w_beta.T, ((0, 1), (0, 0)))
-        tokens_full, w_out_full = gather_tokens(tokens, w_out, count, groups)
-        mixed_full, *saved = forward_mixer(
+        tokens_full = gather_tokens(tokens, count)
+        mixed_full, w_out_full, *saved = forward_mixer(
             tokens_full, w_query, w_key, w_value, w_gate_out, beta_rows,
-            conv_query, conv_key, conv_value, head_gain, attn_gain, seq_starts, seq_lengths, count,
-        )
+            conv_query, conv_key, conv_value, head_gain, attn_gain, seq_starts, seq_lengths, w_out, count, groups,
+        )
+        w_out_full = w_out_full.reshape(-1, tokens.shape[1])
         resid, ffn_full, hidden, grad_gate, grad_up, grad_full = attend(
             mixed_full, w_out_full, tokens_full, ffn_gain, w_gate.T, w_up.T, w_down, cotangent, count
         )

time: 709 us -> 679 us (0.958)
  Pallas kernels: 706 us -> 671 us
    pallas_call x1, Pallas kernels: 115 us -> 84.6 us  [gather_tokens(): pl.pallas_call(functools.partial(gather_kernel, count), name='gather_toke...]
where the time goes in v9:
time: 679 us; the launch traced here: 672 us
  Pallas kernels  671 us (99%)
    pallas_call x1, Pallas kernels, ffn_back(): pl.pallas_call(functools.partial(ffn_back_kernel, count, groups, rows), n...  170 us
    pallas_call x1, Pallas kernels, forward_mixer(): pl.pallas_call(functools.partial(forward_kernel, heads, width, seqs, coun...  121 us
    pallas_call x1, Pallas kernels, backward_mixer(): pl.pallas_call(functools.partial(backward_kernel, heads, width, seqs, chu...  97.3 us
    pallas_call x1, Pallas kernels, last_step(): pl.pallas_call(functools.partial(last_kernel, count, groups, rows), name=...  96.6 us
    pallas_call x1, Pallas kernels, attend(): pl.pallas_call(functools.partial(attend_kernel, count), name='attend', ou...  86 us
    pallas_call x1, Pallas kernels, gather_tokens(): pl.pallas_call(functools.partial(gather_kernel, count), name='gather_toke...  84.6 us
    pallas_call x1, Pallas kernels, results(): pl.pallas_call(functools.partial(results_kernel, heads, taps, wide, width...  15.8 us

profile of v9, /device:TPU:0, one launch (start us, length us, event | category | flops | bytes accessed | tf_op | source)
XLA Modules:
  0.0 671.9 jit_solution(2205218773233984103)
XLA Ops:
  0.7 84.6 %gather_tokens.1.tokens = bf16[2048,2048]{1,0:T(8,128)(2,1)} custom-call(bf16[256,2048]{1,0:T(8,128)(2,1)} %tokens_in.1), custom_call_target="tpu_custom_call" | custom-call | bytes 314572800 | tf_op jit(solution)/shard_map/gather_tokens/pallas_call | solution.py:464
  85.3 120.6 %mixer_forward.1 = (bf16[8,2048,256]{2,1,0:T(8,128)(2,1)}, bf16[8,4,64,2048]{3,2,1,0:T(8,128)(2,1)}, bf16[2048,256]{1,0:T(8,128)(2,1)}, f32[2048,256]{1,0:T(8,12...) custom-call(s32[1,2]{1,0:T(1,128)} %starts.3, ...), custom_call_target="tpu_custom_call" | custom-call | flops 19327352832 | bytes 31457280 | tf_op jit(solution)/shard_map/mixer_forward/pallas_call | solution.py:1208
  205.8 86.0 %attend.1 = (f32[256,2048]{1,0:T(8,128)}, bf16[2048,2048]{1,0:T(8,128)(2,1)}, bf16[2048,704]{1,0:T(8,128)(2,1)}, bf16[2048,704]{1,0:T(8,128)(2,1)}, bf16[2048,70...) custom-call(bf16[8,2048,256]{2,1,0:T(8,128)(2,1)} %get-tuple-element.76.mixed, bf16[2048,2048]{1,0:T(8,128)(2,1)} %bitcast.25, ...), custom_call_target="tpu_custom_call" | custom-call | flops 34896609280 | bytes 314572800 | tf_op jit(solution)/shard_map/attend/pallas_call | solution.py:638
  291.8 170.1 %ffn_back.1 = (f32[256,2048]{1,0:T(8,128)}, bf16[2048,2048]{1,0:T(8,128)(2,1)}, f32[1,2048]{1,0:T(1,128)}, bf16[704,2048]{1,0:T(8,128)(2,1)}, bf16[704,2048]{1,0:T(8,128)(2,1)}, /*index=5*/bf16[704,2048]{1,0:T(8,128)(2,1)}) custom-call(bf16[2048,704]{1,0:T(8,128)(2,1)} %get-tuple-element.78.grad_gate, bf16[2048,704]{1,0:T(8,128)(2,1)} %get-tuple-element.79.grad_up, ...), custom_call_target="tpu_custom_call" | custom-call | flops 29527900160 | bytes 629145600 | tf_op jit(solution)/shard_map/ffn_back/pallas_call | solution.py:808
  461.9 97.3 %mixer_backward.1 = (bf16[2048,2048]{1,0:T(8,128)(2,1)}, bf16[2048,256]{1,0:T(8,128)(2,1)}, bf16[2048,256]{1,0:T(8,128)(2,1)}, bf16[2048,256]{1,0:T(8,128)(2,1)}...) custom-call(s32[1,2]{1,0:T(1,128)} %starts.3, ...), custom_call_target="tpu_custom_call" | custom-call | flops 25769803776 | bytes 54525952 | tf_op jit(solution)/shard_map/mixer_backward/pallas_call | solution.py:1452
  559.3 96.6 %last_step.1 = (f32[256,2048]{1,0:T(8,128)}, f32[16,2048]{1,0:T(8,128)}, bf16[2048,256]{1,0:T(8,128)(2,1)}, bf16[2048,256]{1,0:T(8,128)(2,1)}, bf16[2048,256]{1,...) custom-call(bf16[2048,2048]{1,0:T(8,128)(2,1)} %get-tuple-element.99.terms, ...), custom_call_target="tpu_custom_call" | custom-call | bytes 314572800 | tf_op jit(solution)/shard_map/last_step/pallas_call | solution.py:936
  655.8 15.8 %results.1 = (bf16[256,2048]{1,0:T(8,128)(2,1)}, f32[256,2048]{1,0:T(8,128)}, f32[2048,256]{1,0:T(8,128)}, f32[2048,256]{1,0:T(8,128)}, f32[2048,256]{1,0:T(8,12...) custom-call(f32[16,2048]{1,0:T(8,128)} %get-tuple-element.107.total,, ...), custom_call_target="tpu_custom_call" | custom-call | bytes 50331648 | tf_op jit(solution)/shard_map/results/pallas_call | solution.py:986

commit v10 on v9

--- a/solution.py
+++ b/solution.py
@@ -157,13 +157,12 @@
     return lambda start, size: ref.at[pl.ds(start, size), :]
 
 
-def ring_gather(gather, between):
+def ring_gather(gather, between, begun=False):
     count = gather.ring.count
 
     def run(step, carry):
-        @pl.when(step == 0)
-        def _():
-            gather.begin()
+        if not begun:
+            pl.when(step == 0)(gather.begin)
 
         @pl.when((step > 0) & (step < count - 1))
         def _():
@@ -192,7 +191,8 @@
 
 
 class Scatter:
-    def __init__(self, ring, partial, slots, sends, recvs, rows, finish):
+    def __init__(self, ring, partial, slots, sends, recvs, rows, finish, after=None):
+        self.after = after
         self.ring, self.partial, self.slots, self.sends, self.recvs = ring, partial, slots, sends, recvs
         self.half, self.finish = rows // 2, finish
         self.rows, self.piece = rows, rows // (2 * SUBS)
@@ -236,6 +236,8 @@
                 self.piece,
                 self.slots[way, sub, count - 1].astype(F32) + self.part(terms, way, sub),
             )
+            if self.after is not None:
+                self.after(way, sub)
 
         def drain(step, carry):
             for sub, way in PAIRS:
@@ -407,10 +409,12 @@
     def peers(self):
         return [self.mate] + [self.peer(k) for k in range(1, self.across)]
 
-    def far(self, k):
-        part = self.full.at[:, self.ring.group]
+    def far(self, k, way, step):
+        gather = self.gather
+        part = self.full.at[gather.origin(way, step), self.ring.group, pl.ds(way * gather.piece, gather.piece), :]
         return pltpu.make_async_remote_copy(
-            src_ref=part, dst_ref=part, send_sem=self.far_sems.at[0, k - 1], recv_sem=self.far_sems.at[1, k - 1],
+            src_ref=part, dst_ref=part,
+            send_sem=self.far_sems.at[0, k - 1, way, step], recv_sem=self.far_sems.at[1, k - 1, way, step],
             device_id=self.peer(k), device_id_type=MESH,
         )
 
@@ -421,27 +425,44 @@
             device_id=self.mate, device_id_type=MESH,
         )
 
+    def pass_on(self, step):
+        for k in range(1, self.across):
+            for way in (0, 1):
+                self.far(k, way, step).start()
+
     def begin(self):
         self.gather.begin()
         self.keep.start()
 
+    def hop(self, step):
+        self.gather.hop(step)
+        self.pass_on(step)
+
     def exchange(self):
         self.gather.arrived(self.ring.count - 1)
+        self.pass_on(self.ring.count - 1)
         self.keep.wait()
+        self.pass_on(0)
+        self.near(0).start()
+
+    def every_far(self, body):
+        def run(step, carry):
+            for k in range(1, self.across):
+                for way in (0, 1):
+                    body(self.far(k, way, step))
+            return carry
+
+        lax.fori_loop(0, self.ring.count, run, 0)
+
+    def back(self):
+        self.every_far(lambda copy: copy.wait_recv())
         for k in range(1, self.across):
-            self.far(k).start()
-        self.near(0).start()
-
-    def back(self):
-        for k in range(1, self.across):
-            self.far(k).wait_recv()
             self.near(k).start()
 
     def end(self):
         for k in range(self.across):
             self.near(k).wait()
-        for k in range(1, self.across):
-            self.far(k).wait_send()
+        self.every_far(lambda copy: copy.wait_send())
         self.gather.end()
 
 
@@ -793,10 +814,12 @@
         def _():
             sums.third((2,))
 
-    ring_scatter(Scatter(ring, partial, slots, sends, recvs, rows, finish), beside_scatter)
+    gather = Gather(ring, row_own(low), row_view(full, rows), sends_two, recvs_two, rows)
+    start = lambda way, sub: gather.copy(way, sub, 0, ring.me, True).start()
+    ring_scatter(Scatter(ring, partial, slots, sends, recvs, rows, finish, start), beside_scatter)
     keep = pltpu.make_async_copy(low, full.at[pl.ds(pl.multiple_of(ring.me * rows, rows), rows), :], local)
     keep.start()
-    ring_gather(Gather(ring, row_own(low), row_view(full, rows), sends_two, recvs_two, rows), beside_gather)
+    ring_gather(gather, beside_gather, True)
     keep.wait()
     sums.last()
 
@@ -1006,39 +1029,6 @@
             hop(number)
 
 
-def plan_hops(chunks, hops, latency=1.4, segment=2.5):
-    now, link, due, done, table = 0.0, 0.0, {}, {}, []
-
-    def send(chunk):
-        nonlocal link
-        link = max(now, link) + 1.0
-        done[chunk] = done.get(chunk, -1) + 1
-        due[chunk] = link + latency
-
-    def waiting():
-        return [chunk for chunk in done if done[chunk] < hops - 1]
-
-    for step in range(chunks):
-        for half in range(2):
-            ready, moves = True, []
-            while ready:
-                ready = sorted((due[chunk], chunk) for chunk in waiting() if due[chunk] <= now)
-                if ready:
-                    send(ready[0][1])
-                    moves.append((ready[0][1], done[ready[0][1]]))
-            table.append(moves)
-            now += segment
-        send(step)
-    rest = []
-    while waiting():
-        now, chunk = max((now, 0), min((due[chunk], chunk) for chunk in waiting()))[0], min(
-            (due[chunk], chunk) for chunk in waiting()
-        )[1]
-        send(chunk)
-        rest.append((chunk, done[chunk]))
-    return table, rest
-
-
 def forward_kernel(
     heads, width, seqs, count, groups, chunks,
     starts, lengths, tokens, w_query, w_key, w_value, w_gate, w_beta,
@@ -1078,30 +1068,24 @@
         )
 
     weight = WholeWeight(ring, groups, w_out, w_full, w_sends, w_recvs, w_keep, w_far, w_near)
-    table, rest = plan_hops(chunks, count - 1)
-
-    def turn(late):
-        number = 2 * step + late
-
-        @pl.when((number > 0) & (number < count - 1))
-        def _():
-            weight.gather.hop(number)
-
-        if late == (count - 1) % 2:
+    each = -(-(count - 1) // (chunks - 1))
+
+    def weight_hops():
+        for place in range(each):
+            number = step * each + place
+            pl.when((number > 0) & (number < count - 1))(lambda: weight.hop(number))
             pl.when(number == count - 1)(weight.exchange)
-        for place, moves in enumerate(table[late::2]):
-            if moves:
-                @pl.when(step == place)
-                def _():
-                    for chunk, hop in moves:
-                        chunk_gather(chunk).hop(hop)
+
+    def chunk_hops():
+        for age in range(1, min(count - 1, chunks)):
+            pl.when(step >= age)(lambda age=age: chunk_gather(step - age).hop(age))
 
     @pl.when(step == 0)
     def _():
         greet(ring, weight.peers())
         weight.begin()
 
-    turn(0)
+    weight_hops()
     rows, seg_rows, seg_columns, before, last = chunk_masks(starts, lengths, seqs, first, size)
     same = seg_rows == seg_columns
     i = lax.broadcasted_iota(jnp.int32, (size, size), 0)
@@ -1143,7 +1127,7 @@
     head_gain = gain[...].astype(F32)
     for h in range(heads):
         if h == heads // 2:
-            turn(1)
+            chunk_hops()
         cols = slice(h * width, (h + 1) * width)
         uq, uk = u_query[:, cols], u_key[:, cols]
         query = (uq * lax.rsqrt(jnp.sum(uq * uq, axis=1, keepdims=True) + 1e-6)).astype(BF16)
@@ -1173,10 +1157,15 @@
 
     @pl.when(step == chunks - 1)
     def _():
-        for place, (chunk, hop) in enumerate(rest):
-            if place == len(rest) // 2:
-                weight.back()
-            chunk_gather(chunk).hop(hop)
+        def finish(number, carry):
+            pl.when(number == (count - 1) // 2)(weight.back)
+            for age in range(min(count - 1, chunks) - 1, -1, -1):
+                pl.when(age + number < count - 1)(
+                    lambda age=age: chunk_gather(chunks - 1 - age).hop(age + number)
+                )
+            return carry
+
+        lax.fori_loop(1, count - 1, finish, 0)
 
         def settle(chunk, carry):
             chunk_gather(chunk).arrived(count - 1)
@@ -1233,7 +1222,7 @@
         + ring_semaphores(count, 1)
         + [
             pltpu.SemaphoreType.DMA,
-            pltpu.SemaphoreType.DMA((2, groups // 2 - 1)),
+            pltpu.SemaphoreType.DMA((2, groups // 2 - 1, 2, count)),
             pltpu.SemaphoreType.DMA((2, groups // 2)),
         ],
         compiler_params=ring_params(5),

time: 679 us -> 677 us (level)
  no operation moved by 1% of the time
where the time goes in v10:
time: 677 us; the launch traced here: 675 us
  Pallas kernels  674 us (100%)
    pallas_call x1, Pallas kernels, ffn_back(): pl.pallas_call(functools.partial(ffn_back_kernel, count, groups, rows), n...  169 us
    pallas_call x1, Pallas kernels, forward_mixer(): pl.pallas_call(functools.partial(forward_kernel, heads, width, seqs, coun...  123 us
    pallas_call x1, Pallas kernels, backward_mixer(): pl.pallas_call(functools.partial(backward_kernel, heads, width, seqs, chu...  97.3 us
    pallas_call x1, Pallas kernels, last_step(): pl.pallas_call(functools.partial(last_kernel, count, groups, rows), name=...  96 us
    pallas_call x1, Pallas kernels, attend(): pl.pallas_call(functools.partial(attend_kernel, count), name='attend', ou...  88.3 us
    pallas_call x1, Pallas kernels, gather_tokens(): pl.pallas_call(functools.partial(gather_kernel, count), name='gather_toke...  84.6 us
    pallas_call x1, Pallas kernels, results(): pl.pallas_call(functools.partial(results_kernel, heads, taps, wide, width...  15.8 us

profile of v10, /device:TPU:0, one launch (start us, length us, event | category | flops | bytes accessed | tf_op | source)
XLA Modules:
  0.0 675.4 jit_solution(5209547633147240863)
XLA Ops:
  0.7 84.6 %gather_tokens.1.tokens = bf16[2048,2048]{1,0:T(8,128)(2,1)} custom-call(bf16[256,2048]{1,0:T(8,128)(2,1)} %tokens_in.1), custom_call_target="tpu_custom_call" | custom-call | bytes 314572800 | tf_op jit(solution)/shard_map/gather_tokens/pallas_call | solution.py:485
  85.3 123.1 %mixer_forward.1 = (bf16[8,2048,256]{2,1,0:T(8,128)(2,1)}, bf16[8,4,64,2048]{3,2,1,0:T(8,128)(2,1)}, bf16[2048,256]{1,0:T(8,128)(2,1)}, f32[2048,256]{1,0:T(8,12...) custom-call(s32[1,2]{1,0:T(1,128)} %starts.3, ...), custom_call_target="tpu_custom_call" | custom-call | flops 19327352832 | bytes 31457280 | tf_op jit(solution)/shard_map/mixer_forward/pallas_call | solution.py:1197
  208.4 88.3 %attend.1 = (f32[256,2048]{1,0:T(8,128)}, bf16[2048,2048]{1,0:T(8,128)(2,1)}, bf16[2048,704]{1,0:T(8,128)(2,1)}, bf16[2048,704]{1,0:T(8,128)(2,1)}, bf16[2048,70...) custom-call(bf16[8,2048,256]{2,1,0:T(8,128)(2,1)} %get-tuple-element.76.mixed, bf16[2048,2048]{1,0:T(8,128)(2,1)} %bitcast.25, ...), custom_call_target="tpu_custom_call" | custom-call | flops 34896609280 | bytes 314572800 | tf_op jit(solution)/shard_map/attend/pallas_call | solution.py:659
  296.7 169.3 %ffn_back.1 = (f32[256,2048]{1,0:T(8,128)}, bf16[2048,2048]{1,0:T(8,128)(2,1)}, f32[1,2048]{1,0:T(1,128)}, bf16[704,2048]{1,0:T(8,128)(2,1)}, bf16[704,2048]{1,0:T(8,128)(2,1)}, /*index=5*/bf16[704,2048]{1,0:T(8,128)(2,1)}) custom-call(bf16[2048,704]{1,0:T(8,128)(2,1)} %get-tuple-element.78.grad_gate, bf16[2048,704]{1,0:T(8,128)(2,1)} %get-tuple-element.79.grad_up, ...), custom_call_target="tpu_custom_call" | custom-call | flops 29527900160 | bytes 629145600 | tf_op jit(solution)/shard_map/ffn_back/pallas_call | solution.py:831
  466.0 97.3 %mixer_backward.1 = (bf16[2048,2048]{1,0:T(8,128)(2,1)}, bf16[2048,256]{1,0:T(8,128)(2,1)}, bf16[2048,256]{1,0:T(8,128)(2,1)}, bf16[2048,256]{1,0:T(8,128)(2,1)}...) custom-call(s32[1,2]{1,0:T(1,128)} %starts.3, ...), custom_call_target="tpu_custom_call" | custom-call | flops 25769803776 | bytes 54525952 | tf_op jit(solution)/shard_map/mixer_backward/pallas_call | solution.py:1441
  563.4 96.0 %last_step.1 = (f32[256,2048]{1,0:T(8,128)}, f32[16,2048]{1,0:T(8,128)}, bf16[2048,256]{1,0:T(8,128)(2,1)}, bf16[2048,256]{1,0:T(8,128)(2,1)}, bf16[2048,256]{1,...) custom-call(bf16[2048,2048]{1,0:T(8,128)(2,1)} %get-tuple-element.99.terms, ...), custom_call_target="tpu_custom_call" | custom-call | bytes 314572800 | tf_op jit(solution)/shard_map/last_step/pallas_call | solution.py:959
  659.4 15.8 %results.1 = (bf16[256,2048]{1,0:T(8,128)(2,1)}, f32[256,2048]{1,0:T(8,128)}, f32[2048,256]{1,0:T(8,128)}, f32[2048,256]{1,0:T(8,128)}, f32[2048,256]{1,0:T(8,12...) custom-call(f32[16,2048]{1,0:T(8,128)} %get-tuple-element.107.total,, ...), custom_call_target="tpu_custom_call" | custom-call | bytes 50331648 | tf_op jit(solution)/shard_map/results/pallas_call | solution.py:1009

commit v11 on v10

--- a/solution.py
+++ b/solution.py
@@ -211,7 +211,9 @@
         return scatter_copy(self.ring, self.slots, self.sends, self.recvs, way, sub, step)
 
     def hop(self, step):
-        terms = self.terms(step)
+        self.pass_on(step, self.terms(step))
+
+    def pass_on(self, step, terms):
         for sub, way in PAIRS:
             term = self.part(terms, way, sub)
 
@@ -227,8 +229,11 @@
             self.copy(way, sub, step).start()
 
     def end(self):
+        self.take(self.terms(self.ring.count - 1))
+        self.drain()
+
+    def take(self, terms):
         count = self.ring.count
-        terms = self.terms(count - 1)
         for sub, way in PAIRS:
             self.copy(way, sub, count - 2).wait_recv()
             self.finish(
@@ -239,22 +244,27 @@
             if self.after is not None:
                 self.after(way, sub)
 
-        def drain(step, carry):
+    def drain(self):
+        def run(step, carry):
             for sub, way in PAIRS:
                 self.copy(way, sub, step).wait_send()
             return carry
 
-        lax.fori_loop(0, count - 1, drain, 0)
+        lax.fori_loop(0, self.ring.count - 1, run, 0)
 
 
 def ring_scatter(scatter, between):
+    count = scatter.ring.count
+
     def run(step, carry):
-        scatter.hop(step)
+        terms = scatter.terms(step)
+        pl.when(step < count - 1)(lambda: scatter.pass_on(step, terms))
+        pl.when(step == count - 1)(lambda: scatter.take(terms))
         between(step)
         return carry
 
-    lax.fori_loop(0, scatter.ring.count - 1, run, 0)
-    scatter.end()
+    lax.fori_loop(0, count, run, 0)
+    scatter.drain()
 
 
 class GroupSum:
@@ -1029,6 +1039,29 @@
             hop(number)
 
 
+def plan_hops(chunks, hops, latency=0.8, segment=2.5):
+    now, link, due, done, table = 0.0, 0.0, {}, {}, []
+
+    def send(chunk):
+        nonlocal link
+        link = max(now, link) + 1.0
+        done[chunk] = done.get(chunk, -1) + 1
+        due[chunk] = link + latency
+
+    for step in range(chunks):
+        for half in range(2):
+            ready, moves = True, []
+            while ready:
+                ready = sorted((due[c], c) for c in due if due[c] <= now and done[c] < hops - 1)
+                if ready:
+                    send(ready[0][1])
+                    moves.append((ready[0][1], done[ready[0][1]]))
+            table.append(moves)
+            now += segment
+        send(step)
+    return table, [done[chunk] for chunk in range(chunks)]
+
+
 def forward_kernel(
     heads, width, seqs, count, groups, chunks,
     starts, lengths, tokens, w_query, w_key, w_value, w_gate, w_beta,
@@ -1070,15 +1103,21 @@
     weight = WholeWeight(ring, groups, w_out, w_full, w_sends, w_recvs, w_keep, w_far, w_near)
     each = -(-(count - 1) // (chunks - 1))
 
-    def weight_hops():
+    def weight_hops(late=0):
         for place in range(each):
-            number = step * each + place
+            number = (2 * step + late) * each + place
             pl.when((number > 0) & (number < count - 1))(lambda: weight.hop(number))
             pl.when(number == count - 1)(weight.exchange)
 
-    def chunk_hops():
-        for age in range(1, min(count - 1, chunks)):
-            pl.when(step >= age)(lambda age=age: chunk_gather(step - age).hop(age))
+    table, done = plan_hops(chunks, count - 1)
+
+    def chunk_hops(half):
+        for place, moves in enumerate(table[half::2]):
+            if moves:
+                @pl.when(step == place)
+                def _():
+                    for chunk, hop in moves:
+                        chunk_gather(chunk).hop(hop)
 
     @pl.when(step == 0)
     def _():
@@ -1086,6 +1125,7 @@
         weight.begin()
 
     weight_hops()
+    chunk_hops(0)
     rows, seg_rows, seg_columns, before, last = chunk_masks(starts, lengths, seqs, first, size)
     same = seg_rows == seg_columns
     i = lax.broadcasted_iota(jnp.int32, (size, size), 0)
@@ -1127,7 +1167,8 @@
     head_gain = gain[...].astype(F32)
     for h in range(heads):
         if h == heads // 2:
-            chunk_hops()
+            weight_hops(1)
+            chunk_hops(1)
         cols = slice(h * width, (h + 1) * width)
         uq, uk = u_query[:, cols], u_key[:, cols]
         query = (uq * lax.rsqrt(jnp.sum(uq * uq, axis=1, keepdims=True) + 1e-6)).astype(BF16)
@@ -1159,10 +1200,11 @@
     def _():
         def finish(number, carry):
             pl.when(number == (count - 1) // 2)(weight.back)
-            for age in range(min(count - 1, chunks) - 1, -1, -1):
-                pl.when(age + number < count - 1)(
-                    lambda age=age: chunk_gather(chunks - 1 - age).hop(age + number)
-                )
+            for chunk in range(chunks):
+                if done[chunk] < count - 2:
+                    pl.when(done[chunk] + number < count - 1)(
+                        lambda chunk=chunk: chunk_gather(chunk).hop(done[chunk] + number)
+                    )
             return carry
 
         lax.fori_loop(1, count - 1, finish, 0)

time: 677 us -> 672 us (level)
  no operation moved by 1% of the time
where the time goes in v11:
time: 672 us; the launch traced here: 670 us
  Pallas kernels  670 us (100%)
    pallas_call x1, Pallas kernels, ffn_back(): pl.pallas_call(functools.partial(ffn_back_kernel, count, groups, rows), n...  169 us
    pallas_call x1, Pallas kernels, forward_mixer(): pl.pallas_call(functools.partial(forward_kernel, heads, width, seqs, coun...  120 us
    pallas_call x1, Pallas kernels, backward_mixer(): pl.pallas_call(functools.partial(backward_kernel, heads, width, seqs, chu...  97.1 us
    pallas_call x1, Pallas kernels, last_step(): pl.pallas_call(functools.partial(last_kernel, count, groups, rows), name=...  96.1 us
    pallas_call x1, Pallas kernels, attend(): pl.pallas_call(functools.partial(attend_kernel, count), name='attend', ou...  86.3 us
    pallas_call x1, Pallas kernels, gather_tokens(): pl.pallas_call(functools.partial(gather_kernel, count), name='gather_toke...  84.6 us
    pallas_call x1, Pallas kernels, results(): pl.pallas_call(functools.partial(results_kernel, heads, taps, wide, width...  15.8 us

profile of v11, /device:TPU:0, one launch (start us, length us, event | category | flops | bytes accessed | tf_op | source)
XLA Modules:
  0.0 670.4 jit_solution(16589683083678661801)
XLA Ops:
  0.7 84.6 %gather_tokens.1.tokens = bf16[2048,2048]{1,0:T(8,128)(2,1)} custom-call(bf16[256,2048]{1,0:T(8,128)(2,1)} %tokens_in.1), custom_call_target="tpu_custom_call" | custom-call | bytes 314572800 | tf_op jit(solution)/shard_map/gather_tokens/pallas_call | solution.py:495
  85.3 120.4 %mixer_forward.1 = (bf16[8,2048,256]{2,1,0:T(8,128)(2,1)}, bf16[8,4,64,2048]{3,2,1,0:T(8,128)(2,1)}, bf16[2048,256]{1,0:T(8,128)(2,1)}, f32[2048,256]{1,0:T(8,12...) custom-call(s32[1,2]{1,0:T(1,128)} %starts.3, ...), custom_call_target="tpu_custom_call" | custom-call | flops 19327352832 | bytes 31457280 | tf_op jit(solution)/shard_map/mixer_forward/pallas_call | solution.py:1239
  205.7 86.3 %attend.1 = (f32[256,2048]{1,0:T(8,128)}, bf16[2048,2048]{1,0:T(8,128)(2,1)}, bf16[2048,704]{1,0:T(8,128)(2,1)}, bf16[2048,704]{1,0:T(8,128)(2,1)}, bf16[2048,70...) custom-call(bf16[8,2048,256]{2,1,0:T(8,128)(2,1)} %get-tuple-element.76.mixed, bf16[2048,2048]{1,0:T(8,128)(2,1)} %bitcast.25, ...), custom_call_target="tpu_custom_call" | custom-call | flops 34896609280 | bytes 314572800 | tf_op jit(solution)/shard_map/attend/pallas_call | solution.py:669
  292.0 169.2 %ffn_back.1 = (f32[256,2048]{1,0:T(8,128)}, bf16[2048,2048]{1,0:T(8,128)(2,1)}, f32[1,2048]{1,0:T(1,128)}, bf16[704,2048]{1,0:T(8,128)(2,1)}, bf16[704,2048]{1,0:T(8,128)(2,1)}, /*index=5*/bf16[704,2048]{1,0:T(8,128)(2,1)}) custom-call(bf16[2048,704]{1,0:T(8,128)(2,1)} %get-tuple-element.78.grad_gate, bf16[2048,704]{1,0:T(8,128)(2,1)} %get-tuple-element.79.grad_up, ...), custom_call_target="tpu_custom_call" | custom-call | flops 29527900160 | bytes 629145600 | tf_op jit(solution)/shard_map/ffn_back/pallas_call | solution.py:841
  461.2 97.1 %mixer_backward.1 = (bf16[2048,2048]{1,0:T(8,128)(2,1)}, bf16[2048,256]{1,0:T(8,128)(2,1)}, bf16[2048,256]{1,0:T(8,128)(2,1)}, bf16[2048,256]{1,0:T(8,128)(2,1)}...) custom-call(s32[1,2]{1,0:T(1,128)} %starts.3, ...), custom_call_target="tpu_custom_call" | custom-call | flops 25769803776 | bytes 54525952 | tf_op jit(solution)/shard_map/mixer_backward/pallas_call | solution.py:1483
  558.3 96.1 %last_step.1 = (f32[256,2048]{1,0:T(8,128)}, f32[16,2048]{1,0:T(8,128)}, bf16[2048,256]{1,0:T(8,128)(2,1)}, bf16[2048,256]{1,0:T(8,128)(2,1)}, bf16[2048,256]{1,...) custom-call(bf16[2048,2048]{1,0:T(8,128)(2,1)} %get-tuple-element.99.terms, ...), custom_call_target="tpu_custom_call" | custom-call | bytes 314572800 | tf_op jit(solution)/shard_map/last_step/pallas_call | solution.py:969
  654.4 15.8 %results.1 = (bf16[256,2048]{1,0:T(8,128)(2,1)}, f32[256,2048]{1,0:T(8,128)}, f32[2048,256]{1,0:T(8,128)}, f32[2048,256]{1,0:T(8,128)}, f32[2048,256]{1,0:T(8,12...) custom-call(f32[16,2048]{1,0:T(8,128)} %get-tuple-element.107.total,, ...), custom_call_target="tpu_custom_call" | custom-call | bytes 50331648 | tf_op jit(solution)/shard_map/results/pallas_call | solution.py:1019

commit v12 on v11

--- a/solution.py
+++ b/solution.py
@@ -870,10 +870,10 @@
     grads, rest = rest[:5], rest[5:]
     grad_tokens, total = rest[:2]
     targets, rest = rest[2:7], rest[7:]
-    slots, first_box, second_box, second_own, boxes, box_sems, tokens, grad_resid, load_sems = rest[:9]
-    sends, recvs, first_sends, first_recvs, second_sends, second_recvs = rest[9:15]
+    slots, first_box, slice_own, spread, second_box, second_own, boxes, box_sems, tokens, grad_resid, load_sems = rest[:11]
+    sends, recvs, first_sends, first_recvs, spread_sends, spread_recvs, second_sends, second_recvs = rest[11:19]
     ring = Ring(count)
-    sums = GroupSum(ring, groups, grads, rest[15:20], rest[20:25], targets, *rest[25:])
+    sums = GroupSum(ring, groups, grads, rest[19:24], rest[24:29], targets, *rest[29:])
     loads = [
         pltpu.make_async_copy(tokens_in, tokens, load_sems.at[0]),
         pltpu.make_async_copy(grad_resid_in, grad_resid, load_sems.at[1]),
@@ -886,10 +886,22 @@
         pl.semaphore_signal(barrier, inc=1, device_id=peer, device_id_type=MESH)
     pl.semaphore_wait(barrier, count + groups - 2)
 
+    lanes = small.shape[1] // count
+
+    def lanes_of(device):
+        return pl.ds(pl.multiple_of(device * lanes, lanes), lanes)
+
     def first(k):
+        peer = first_peers[k]
         return pltpu.make_async_remote_copy(
-            src_ref=small.at[0:8], dst_ref=first_box.at[k], send_sem=first_sends.at[k],
-            recv_sem=first_recvs.at[k], device_id=first_peers[k], device_id_type=MESH,
+            src_ref=small.at[0:8, lanes_of(peer[1])], dst_ref=first_box.at[k], send_sem=first_sends.at[k],
+            recv_sem=first_recvs.at[k], device_id=peer, device_id_type=MESH,
+        )
+
+    def share(k):
+        return pltpu.make_async_remote_copy(
+            src_ref=slice_own, dst_ref=spread.at[:, lanes_of(me)], send_sem=spread_sends.at[k],
+            recv_sem=spread_recvs.at[k], device_id=first_peers[k], device_id_type=MESH,
         )
 
     def second(k):
@@ -933,10 +945,18 @@
         sums.second(every)
         for k in range(count - 1):
             first(k).wait()
-        mine = small[0:8]
+        mine = small[0:8, lanes_of(me)]
         for k in range(count - 1):
             mine = mine + first_box[k]
-        second_own[0:8] = mine
+        slice_own[...] = mine
+        spread[:, lanes_of(me)] = mine
+        for k in range(count - 1):
+            share(k).start()
+
+    def soon():
+        for k in range(count - 1):
+            share(k).wait()
+        second_own[0:8] = spread[...]
         second_own[8:] = small[8:]
         for k in range(groups - 1):
             second(k).start()
@@ -953,6 +973,7 @@
 
     def beside(step):
         pl.when(step == 0)(early)
+        pl.when(step == 1)(soon)
         for i in every:
             pl.when(step == count - 1 - len(every) + i)(lambda i=i: sums.third((i,)))
         pl.when(step == count - 2)(late)
@@ -975,7 +996,9 @@
         out_specs=[VMEM, VMEM] + [ANY] * len(grads),
         scratch_shapes=[
             ring_slots(count, rows, model),
-            pltpu.VMEM((count - 1, 8, model), F32),
+            pltpu.VMEM((count - 1, 8, model // count), F32),
+            pltpu.VMEM((8, model // count), F32),
+            pltpu.VMEM((8, model), F32),
             pltpu.VMEM((groups - 1,) + small.shape, F32),
             pltpu.VMEM(small.shape, F32),
             pltpu.VMEM((2, 2, rows // 2, model), BF16),
@@ -985,7 +1008,7 @@
             pltpu.SemaphoreType.DMA((2,)),
         ]
         + ring_semaphores(count)
-        + [pltpu.SemaphoreType.DMA((count - 1,))] * 2
+        + [pltpu.SemaphoreType.DMA((count - 1,))] * 4
         + [pltpu.SemaphoreType.DMA((groups - 1,))] * 2
         + sum_scratch([g.shape for g in grads], groups),
         compiler_params=ring_params(4),

time: 672 us -> 666 us (level)
  no operation moved by 1% of the time
where the time goes in v12:
time: 666 us
  Pallas kernels  665 us (100%)
    pallas_call x1, Pallas kernels, ffn_back(): pl.pallas_call(functools.partial(ffn_back_kernel, count, groups, rows), n...  169 us
    pallas_call x1, Pallas kernels, forward_mixer(): pl.pallas_call(functools.partial(forward_kernel, heads, width, seqs, coun...  120 us
    pallas_call x1, Pallas kernels, backward_mixer(): pl.pallas_call(functools.partial(backward_kernel, heads, width, seqs, chu...  97.1 us
    pallas_call x1, Pallas kernels, last_step(): pl.pallas_call(functools.partial(last_kernel, count, groups, rows), name=...  91.2 us
    pallas_call x1, Pallas kernels, attend(): pl.pallas_call(functools.partial(attend_kernel, count), name='attend', ou...  86.3 us
    pallas_call x1, Pallas kernels, gather_tokens(): pl.pallas_call(functools.partial(gather_kernel, count), name='gather_toke...  84.6 us
    pallas_call x1, Pallas kernels, results(): pl.pallas_call(functools.partial(results_kernel, heads, taps, wide, width...  15.8 us

profile of v12, /device:TPU:0, one launch (start us, length us, event | category | flops | bytes accessed | tf_op | source)
XLA Modules:
  0.0 665.6 jit_solution(13979460254363804256)
XLA Ops:
  0.7 84.6 %gather_tokens.1.tokens = bf16[2048,2048]{1,0:T(8,128)(2,1)} custom-call(bf16[256,2048]{1,0:T(8,128)(2,1)} %tokens_in.1), custom_call_target="tpu_custom_call" | custom-call | bytes 314572800 | tf_op jit(solution)/shard_map/gather_tokens/pallas_call | solution.py:495
  85.3 120.4 %mixer_forward.1 = (bf16[8,2048,256]{2,1,0:T(8,128)(2,1)}, bf16[8,4,64,2048]{3,2,1,0:T(8,128)(2,1)}, bf16[2048,256]{1,0:T(8,128)(2,1)}, f32[2048,256]{1,0:T(8,12...) custom-call(s32[1,2]{1,0:T(1,128)} %starts.3, ...), custom_call_target="tpu_custom_call" | custom-call | flops 19327352832 | bytes 31457280 | tf_op jit(solution)/shard_map/mixer_forward/pallas_call | solution.py:1262
  205.7 86.3 %attend.1 = (f32[256,2048]{1,0:T(8,128)}, bf16[2048,2048]{1,0:T(8,128)(2,1)}, bf16[2048,704]{1,0:T(8,128)(2,1)}, bf16[2048,704]{1,0:T(8,128)(2,1)}, bf16[2048,70...) custom-call(bf16[8,2048,256]{2,1,0:T(8,128)(2,1)} %get-tuple-element.76.mixed, bf16[2048,2048]{1,0:T(8,128)(2,1)} %bitcast.25, ...), custom_call_target="tpu_custom_call" | custom-call | flops 34896609280 | bytes 314572800 | tf_op jit(solution)/shard_map/attend/pallas_call | solution.py:669
  292.0 169.2 %ffn_back.1 = (f32[256,2048]{1,0:T(8,128)}, bf16[2048,2048]{1,0:T(8,128)(2,1)}, f32[1,2048]{1,0:T(1,128)}, bf16[704,2048]{1,0:T(8,128)(2,1)}, bf16[704,2048]{1,0:T(8,128)(2,1)}, /*index=5*/bf16[704,2048]{1,0:T(8,128)(2,1)}) custom-call(bf16[2048,704]{1,0:T(8,128)(2,1)} %get-tuple-element.78.grad_gate, bf16[2048,704]{1,0:T(8,128)(2,1)} %get-tuple-element.79.grad_up, ...), custom_call_target="tpu_custom_call" | custom-call | flops 29527900160 | bytes 629145600 | tf_op jit(solution)/shard_map/ffn_back/pallas_call | solution.py:841
  461.2 97.1 %mixer_backward.1 = (bf16[2048,2048]{1,0:T(8,128)(2,1)}, bf16[2048,256]{1,0:T(8,128)(2,1)}, bf16[2048,256]{1,0:T(8,128)(2,1)}, bf16[2048,256]{1,0:T(8,128)(2,1)}...) custom-call(s32[1,2]{1,0:T(1,128)} %starts.3, ...), custom_call_target="tpu_custom_call" | custom-call | flops 25769803776 | bytes 54525952 | tf_op jit(solution)/shard_map/mixer_backward/pallas_call | solution.py:1506
  558.3 91.2 %last_step.1 = (f32[256,2048]{1,0:T(8,128)}, f32[16,2048]{1,0:T(8,128)}, bf16[2048,256]{1,0:T(8,128)(2,1)}, bf16[2048,256]{1,0:T(8,128)(2,1)}, bf16[2048,256]{1,...) custom-call(bf16[2048,2048]{1,0:T(8,128)(2,1)} %get-tuple-element.99.terms, ...), custom_call_target="tpu_custom_call" | custom-call | bytes 314572800 | tf_op jit(solution)/shard_map/last_step/pallas_call | solution.py:990
  649.6 15.8 %results.1 = (bf16[256,2048]{1,0:T(8,128)(2,1)}, f32[256,2048]{1,0:T(8,128)}, f32[2048,256]{1,0:T(8,128)}, f32[2048,256]{1,0:T(8,128)}, f32[2048,256]{1,0:T(8,12...) custom-call(f32[16,2048]{1,0:T(8,128)} %get-tuple-element.107.total,, ...), custom_call_target="tpu_custom_call" | custom-call | bytes 50331648 | tf_op jit(solution)/shard_map/results/pallas_call | solution.py:1042

commit v13 on v12

--- a/solution.py
+++ b/solution.py
@@ -715,9 +715,9 @@
 
 
 def ffn_back_kernel(
-    count, groups, rows, grad_gate, grad_up, hidden_in, w_gate, w_up, resid_in, cotangent_in, gain, inputs, cotangents,
+    count, groups, rows, grad_gate_in, grad_up_in, hidden_in, w_gate_in, w_up_in, resid_in, cotangent_in, gain, inputs, cotangents,
     grad_resid, full, grad_gain, sum_gate, sum_up, sum_down,
-    slots, low, gw_gate, gw_up, gw_down, boxes, box_sems, hidden, resid, cotangent, load_sems, *rest,
+    slots, low, gw_gate, gw_up, gw_down, boxes, box_sems, hidden, resid, cotangent, grad_gate, grad_up, w_gate, w_up, load_sems, *rest,
 ):
     ring = Ring(count)
     sends, recvs, sends_two, recvs_two, local = rest[:5]
@@ -743,12 +743,21 @@
 
     loads = [
         pltpu.make_async_copy(source, target, load_sems.at[k])
-        for k, (source, target) in enumerate(((hidden_in, hidden), (resid_in, resid), (cotangent_in, cotangent)))
+        for k, (source, target) in enumerate(
+            (
+                (w_gate_in, w_gate), (w_up_in, w_up), (grad_gate_in, grad_gate), (grad_up_in, grad_up),
+                (hidden_in, hidden), (resid_in, resid), (cotangent_in, cotangent),
+            )
+        )
     ]
+    for load in loads[:4]:
+        load.start()
     fetch(0)
-    for load in loads:
+    for load in loads[4:]:
         load.start()
     greet(ring, sums.peers())
+    for load in loads[:4]:
+        load.wait()
     grad_gain[...] = jnp.zeros_like(grad_gain)
     half = rows // 2
 
@@ -792,7 +801,7 @@
     def beside_scatter(step):
         @pl.when(step == 2)
         def _():
-            for load in loads:
+            for load in loads[4:]:
                 load.wait()
 
         @pl.when(step == 3)
@@ -847,13 +856,15 @@
             jax.ShapeDtypeStruct((1, model), F32),
         ]
         + [jax.ShapeDtypeStruct(shape, BF16) for shape in shapes],
-        in_specs=[VMEM] * 2 + [ANY] + [VMEM] * 2 + [ANY] * 2 + [VMEM] + [ANY] * 2,
+        in_specs=[ANY] * 7 + [VMEM] + [ANY] * 2,
         out_specs=[VMEM, ANY, VMEM] + [ANY] * 3,
         scratch_shapes=[ring_slots(count, rows, model), pltpu.VMEM((rows, model), BF16)]
         + [pltpu.VMEM(shape, BF16) for shape in shapes]
         + [pltpu.VMEM((2, slots, model // (JOBS // 2)), BF16), pltpu.SemaphoreType.DMA((2,))]
         + [pltpu.VMEM((slots, inner), BF16), pltpu.VMEM((rows, model), F32), pltpu.VMEM((rows, model), BF16)]
-        + [pltpu.SemaphoreType.DMA((3,))]
+        + [pltpu.VMEM((slots, inner), BF16)] * 2
+        + [pltpu.VMEM((inner, model), BF16)] * 2
+        + [pltpu.SemaphoreType.DMA((7,))]
         + ring_semaphores(count) * 2
         + [pltpu.SemaphoreType.DMA]
         + sum_scratch(shapes, groups),
@@ -867,17 +878,24 @@
 def last_kernel(
     count, groups, rows, terms, tokens_in, grad_resid_in, gain, small, *rest,
 ):
-    grads, rest = rest[:5], rest[5:]
+    grads_in, rest = rest[:5], rest[5:]
     grad_tokens, total = rest[:2]
     targets, rest = rest[2:7], rest[7:]
     slots, first_box, slice_own, spread, second_box, second_own, boxes, box_sems, tokens, grad_resid, load_sems = rest[:11]
     sends, recvs, first_sends, first_recvs, spread_sends, spread_recvs, second_sends, second_recvs = rest[11:19]
     ring = Ring(count)
-    sums = GroupSum(ring, groups, grads, rest[19:24], rest[24:29], targets, *rest[29:])
+    grads, grad_sems = rest[33:38], rest[38]
+    sums = GroupSum(ring, groups, grads, rest[19:24], rest[24:29], targets, *rest[29:33])
     loads = [
         pltpu.make_async_copy(tokens_in, tokens, load_sems.at[0]),
         pltpu.make_async_copy(grad_resid_in, grad_resid, load_sems.at[1]),
     ]
+    fills = [
+        pltpu.make_async_copy(source, target, grad_sems.at[k])
+        for k, (source, target) in enumerate(zip(grads_in, grads))
+    ]
+    for fill in fills:
+        fill.start()
     me, group = ring.me, ring.group
     first_peers = [(group, (me + k) % count) for k in range(1, count)]
     second_peers = [((group + k) % groups, me) for k in range(1, groups)]
@@ -911,6 +929,8 @@
         )
 
     every = range(len(grads))
+    for fill in fills:
+        fill.wait()
     sums.first(every)
     for k in range(count - 1):
         first(k).start()
@@ -992,7 +1012,7 @@
         name="last_step",
         out_shape=[jax.ShapeDtypeStruct((rows, model), F32), jax.ShapeDtypeStruct(small.shape, F32)]
         + [jax.ShapeDtypeStruct(g.shape, BF16) for g in grads],
-        in_specs=[ANY] * 3 + [VMEM] * (2 + len(grads)),
+        in_specs=[ANY] * 3 + [VMEM] * 2 + [ANY] * len(grads),
         out_specs=[VMEM, VMEM] + [ANY] * len(grads),
         scratch_shapes=[
             ring_slots(count, rows, model),
@@ -1010,7 +1030,9 @@
         + ring_semaphores(count)
         + [pltpu.SemaphoreType.DMA((count - 1,))] * 4
         + [pltpu.SemaphoreType.DMA((groups - 1,))] * 2
-        + sum_scratch([g.shape for g in grads], groups),
+        + sum_scratch([g.shape for g in grads], groups)
+        + [pltpu.VMEM(g.shape, BF16) for g in grads]
+        + [pltpu.SemaphoreType.DMA((len(grads),))],
         compiler_params=ring_params(4),
         cost_estimate=pl.CostEstimate(flops=0, bytes_accessed=300 << 20, transcendentals=0),
     )(terms, tokens, grad_resid, gain, small, *grads)
@@ -1087,12 +1109,12 @@
 
 def forward_kernel(
     heads, width, seqs, count, groups, chunks,
-    starts, lengths, tokens, w_query, w_key, w_value, w_gate, w_beta,
+    starts, lengths, tokens, w_query_in, w_key_in, w_value_in, w_gate_in, w_beta,
     taps_query, taps_key, taps_value, gain, gain_first, w_out,
     mixed_full, w_full, mixed, p_query, p_key, p_value, p_gate, p_beta, z_query, z_key, z_value,
     delta_out, change_out, inverse_out, state_out,
     tail_query, tail_key, tail_value, state, stage, sends, recvs, keeps,
-    w_sends, w_recvs, w_keep, w_far, w_near,
+    w_sends, w_recvs, w_keep, w_far, w_near, w_query, w_key, w_value, w_gate, load_sems,
 ):
     step = pl.program_id(0)
     size = tokens.shape[0]
@@ -1144,8 +1166,18 @@
 
     @pl.when(step == 0)
     def _():
+        loads = [
+            pltpu.make_async_copy(source, target, load_sems.at[k])
+            for k, (source, target) in enumerate(
+                ((w_query_in, w_query), (w_key_in, w_key), (w_value_in, w_value), (w_gate_in, w_gate))
+            )
+        ]
+        for load in loads:
+            load.start()
         greet(ring, weight.peers())
         weight.begin()
+        for load in loads:
+            load.wait()
 
     weight_hops()
     chunk_hops(0)
@@ -1273,7 +1305,7 @@
             jax.ShapeDtypeStruct((chunks, heads, width, width), BF16),
         ],
         in_specs=[smem, smem, piece((CHUNK, model))]
-        + [whole((model, wide))] * 4
+        + [ANY] * 4
         + [whole(w_beta.shape)]
         + [whole((taps, wide))] * 3
         + [whole((1, width)), VMEM, ANY],
@@ -1289,7 +1321,9 @@
             pltpu.SemaphoreType.DMA,
             pltpu.SemaphoreType.DMA((2, groups // 2 - 1, 2, count)),
             pltpu.SemaphoreType.DMA((2, groups // 2)),
-        ],
+        ]
+        + [pltpu.VMEM((model, wide), BF16)] * 4
+        + [pltpu.SemaphoreType.DMA((4,))],
         compiler_params=ring_params(5),
         cost_estimate=pl.CostEstimate(
             flops=2 * slots * model * wide * 4 + slots * heads * CHUNK * 2 * CHUNK * 20,
@@ -1307,11 +1341,11 @@
     heads, width, seqs, chunks, count, rows_own,
     starts, lengths, tokens, grad_attended, mixed, p_query, p_key, p_value, p_gate, p_beta,
     z_query, z_key, z_value, delta_out, change_in, inverse_in, state_in,
-    w_query_in, w_key_in, w_value_in, w_gate_in, w_beta, w_out, taps_query, taps_key, taps_value, gain, gain_first,
-    hidden, w_down, resid_in, g_second, grad_normed, gw_query, gw_key, gw_value, gw_gate, gw_out,
+    w_query_in, w_key_in, w_value_in, w_gate_in, w_beta, w_out_in, taps_query, taps_key, taps_value, gain, gain_first,
+    hidden_in, w_down_in, resid_in, g_second, grad_normed, gw_query, gw_key, gw_value, gw_gate, gw_out,
     small, output,
     a_query, a_key, a_value, a_gate, a_out, head_query, head_key, head_value, flow,
-    w_query, w_key, w_value, w_gate, resid, load_sems, slots, sends, recvs,
+    w_query, w_key, w_value, w_gate, resid, w_out, hidden, w_down, load_sems, slots, sends, recvs,
 ):
     step = pl.program_id(0)
     size = tokens.shape[0]
@@ -1338,17 +1372,25 @@
     loads = [
         pltpu.make_async_copy(source, target, load_sems.at[k])
         for k, (source, target) in enumerate(
-            ((w_query_in, w_query), (w_key_in, w_key), (w_value_in, w_value), (w_gate_in, w_gate), (resid_in, resid))
+            ((w_query_in, w_query), (w_key_in, w_key), (w_value_in, w_value), (w_gate_in, w_gate), (resid_in, resid),
+             (w_out_in, w_out), (hidden_in, hidden), (w_down_in, w_down))
         )
     ]
 
     @pl.when(step == 0)
     def _():
-        for load in loads:
+        for load in reversed(loads):
             load.start()
         greet(ring)
+        for load in loads[6:]:
+            load.wait()
 
     spread_hops(step, chunks, count, scatter.hop)
+
+    @pl.when(step == 0)
+    def _():
+        loads[5].wait()
+
     rows, seg_rows, seg_columns, before, last = chunk_masks(starts, lengths, seqs, first, size)
     same = seg_rows == seg_columns
     i = lax.broadcasted_iota(jnp.int32, (size, size), 0)
@@ -1459,7 +1501,7 @@
 
     @pl.when(step == 0)
     def _():
-        for load in loads:
+        for load in loads[:5]:
             load.wait()
 
     grad_inputs = (
@@ -1512,16 +1554,18 @@
         + [rows(a) for a in saved[:11]]
         + [piece((1, heads, CHUNK, CHUNK)), piece((1, heads, width, width))]
         + [ANY] * 4
-        + [fixed(w_beta.shape), fixed((wide, model))]
+        + [fixed(w_beta.shape), ANY]
         + [fixed((taps, wide))] * 3
-        + [fixed((1, width)), VMEM, fixed(hidden.shape), fixed(w_down.shape), ANY, fixed(g_second.shape)],
+        + [fixed((1, width)), VMEM, ANY, ANY, ANY, fixed(g_second.shape)],
         out_specs=[piece((CHUNK, model))] + [fixed(s) for s, d in outs[1:]],
         scratch_shapes=[pltpu.VMEM((model, wide), F32)] * 4
         + [pltpu.VMEM((wide, model), F32)]
         + [pltpu.VMEM((CHUNK + 8, wide), F32)] * 3
         + [pltpu.VMEM((heads, width, width), F32)]
         + [pltpu.VMEM((model, wide), BF16)] * 4
-        + [pltpu.VMEM(resid.shape, F32), pltpu.SemaphoreType.DMA((5,)), ring_slots(count, slots // count, model)]
+        + [pltpu.VMEM(resid.shape, F32)]
+        + [pltpu.VMEM(a.shape, BF16) for a in (w_out, hidden, w_down)]
+        + [pltpu.SemaphoreType.DMA((8,)), ring_slots(count, slots // count, model)]
         + ring_semaphores(count),
         compiler_params=ring_params(6),
         cost_estimate=pl.CostEstimate(

time: 666 us -> 659 us (0.989)
  Pallas kernels: 665 us -> 658 us
where the time goes in v13:
time: 659 us
  Pallas kernels  658 us (100%)
    pallas_call x1, Pallas kernels, ffn_back(): pl.pallas_call(functools.partial(ffn_back_kernel, count, groups, rows), n...  165 us
    pallas_call x1, Pallas kernels, forward_mixer(): pl.pallas_call(functools.partial(forward_kernel, heads, width, seqs, coun...  120 us
    pallas_call x1, Pallas kernels, backward_mixer(): pl.pallas_call(functools.partial(backward_kernel, heads, width, seqs, chu...  96.5 us
    pallas_call x1, Pallas kernels, last_step(): pl.pallas_call(functools.partial(last_kernel, count, groups, rows), name=...  89.7 us
    pallas_call x1, Pallas kernels, attend(): pl.pallas_call(functools.partial(attend_kernel, count), name='attend', ou...  86.7 us
    pallas_call x1, Pallas kernels, gather_tokens(): pl.pallas_call(functools.partial(gather_kernel, count), name='gather_toke...  84.6 us
    pallas_call x1, Pallas kernels, results(): pl.pallas_call(functools.partial(results_kernel, heads, taps, wide, width...  15.8 us

profile of v13, /device:TPU:0, one launch (start us, length us, event | category | flops | bytes accessed | tf_op | source)
XLA Modules:
  0.0 658.8 jit_solution(17217266287160132102)
XLA Ops:
  0.7 84.6 %gather_tokens.1.tokens = bf16[2048,2048]{1,0:T(8,128)(2,1)} custom-call(bf16[256,2048]{1,0:T(8,128)(2,1)} %tokens_in.1), custom_call_target="tpu_custom_call" | custom-call | bytes 314572800 | tf_op jit(solution)/shard_map/gather_tokens/pallas_call | solution.py:495
  85.3 119.6 %mixer_forward.1 = (bf16[8,2048,256]{2,1,0:T(8,128)(2,1)}, bf16[8,4,64,2048]{3,2,1,0:T(8,128)(2,1)}, bf16[2048,256]{1,0:T(8,128)(2,1)}, f32[2048,256]{1,0:T(8,12...) custom-call(s32[1,2]{1,0:T(1,128)} %starts.3, ...), custom_call_target="tpu_custom_call" | custom-call | flops 19327352832 | bytes 31457280 | tf_op jit(solution)/shard_map/mixer_forward/pallas_call | solution.py:1294
  204.8 86.7 %attend.1 = (f32[256,2048]{1,0:T(8,128)}, bf16[2048,2048]{1,0:T(8,128)(2,1)}, bf16[2048,704]{1,0:T(8,128)(2,1)}, bf16[2048,704]{1,0:T(8,128)(2,1)}, bf16[2048,70...) custom-call(bf16[8,2048,256]{2,1,0:T(8,128)(2,1)} %get-tuple-element.76.mixed, bf16[2048,2048]{1,0:T(8,128)(2,1)} %bitcast.25, ...), custom_call_target="tpu_custom_call" | custom-call | flops 34896609280 | bytes 314572800 | tf_op jit(solution)/shard_map/attend/pallas_call | solution.py:669
  291.5 165.1 %ffn_back.1 = (f32[256,2048]{1,0:T(8,128)}, bf16[2048,2048]{1,0:T(8,128)(2,1)}, f32[1,2048]{1,0:T(1,128)}, bf16[704,2048]{1,0:T(8,128)(2,1)}, bf16[704,2048]{1,0:T(8,128)(2,1)}, /*index=5*/bf16[704,2048]{1,0:T(8,128)(2,1)}) custom-call(bf16[2048,704]{1,0:T(8,128)(2,1)} %get-tuple-element.78.grad_gate_in, bf16[2048,704]{1,0:T(8,128)(2,1)} %get-tuple-element.79.grad_up_in, ...), custom_call_target="tpu_custom_call" | custom-call | flops 29527900160 | bytes 629145600 | tf_op jit(solution)/shard_map/ffn_back/pallas_call | solution.py:850
  456.6 96.5 %mixer_backward.1 = (bf16[2048,2048]{1,0:T(8,128)(2,1)}, bf16[2048,256]{1,0:T(8,128)(2,1)}, bf16[2048,256]{1,0:T(8,128)(2,1)}, bf16[2048,256]{1,0:T(8,128)(2,1)}...) custom-call(s32[1,2]{1,0:T(1,128)} %starts.3, ...), custom_call_target="tpu_custom_call" | custom-call | flops 25769803776 | bytes 54525952 | tf_op jit(solution)/shard_map/mixer_backward/pallas_call | solution.py:1548
  553.0 89.7 %last_step.1 = (f32[256,2048]{1,0:T(8,128)}, f32[16,2048]{1,0:T(8,128)}, bf16[2048,256]{1,0:T(8,128)(2,1)}, bf16[2048,256]{1,0:T(8,128)(2,1)}, bf16[2048,256]{1,...) custom-call(bf16[2048,2048]{1,0:T(8,128)(2,1)} %get-tuple-element.99.terms, ...), custom_call_target="tpu_custom_call" | custom-call | bytes 314572800 | tf_op jit(solution)/shard_map/last_step/pallas_call | solution.py:1010
  642.8 15.8 %results.1 = (bf16[256,2048]{1,0:T(8,128)(2,1)}, f32[256,2048]{1,0:T(8,128)}, f32[2048,256]{1,0:T(8,128)}, f32[2048,256]{1,0:T(8,128)}, f32[2048,256]{1,0:T(8,12...) custom-call(f32[16,2048]{1,0:T(8,128)} %get-tuple-element.107.total,, ...), custom_call_target="tpu_custom_call" | custom-call | bytes 50331648 | tf_op jit(solution)/shard_map/results/pallas_call | solution.py:1064

commit v14 on v13

--- a/solution.py
+++ b/solution.py
@@ -894,8 +894,22 @@
         pltpu.make_async_copy(source, target, grad_sems.at[k])
         for k, (source, target) in enumerate(zip(grads_in, grads))
     ]
+    half = rows // 2
+
+    def box_copy(way, start, slot):
+        return pltpu.make_async_copy(
+            terms.at[pl.ds(start, half), :], boxes.at[slot, way], box_sems.at[slot, way]
+        )
+
+    def fetch(step):
+        for way, owner in ((0, ring.at(-1 - step)), (1, ring.at(1 + step))):
+            box_copy(way, pl.multiple_of(owner * rows + way * half, half), step % 2).start()
+
+    fetch(0)
     for fill in fills:
         fill.start()
+    for load in loads:
+        load.start()
     me, group = ring.me, ring.group
     first_peers = [(group, (me + k) % count) for k in range(1, count)]
     second_peers = [((group + k) % groups, me) for k in range(1, groups)]
@@ -934,17 +948,6 @@
     sums.first(every)
     for k in range(count - 1):
         first(k).start()
-    half = rows // 2
-
-    def box_copy(way, start, slot):
-        return pltpu.make_async_copy(
-            terms.at[pl.ds(start, half), :], boxes.at[slot, way], box_sems.at[slot, way]
-        )
-
-    def fetch(step):
-        for way, owner in ((0, ring.at(-1 - step)), (1, ring.at(1 + step))):
-            box_copy(way, pl.multiple_of(owner * rows + way * half, half), step % 2).start()
-
     def partial(first, second, step):
         for way, start in ((0, first), (1, second)):
             box_copy(way, start, step % 2).wait()
@@ -998,9 +1001,6 @@
             pl.when(step == count - 1 - len(every) + i)(lambda i=i: sums.third((i,)))
         pl.when(step == count - 2)(late)
 
-    fetch(0)
-    for load in loads:
-        load.start()
     ring_scatter(Scatter(ring, partial, slots, sends, recvs, rows, finish), beside)
     sums.last()
 

time: 659 us -> 658 us (level)
  no operation moved by 1% of the time
where the time goes in v14:
time: 658 us
  Pallas kernels  657 us (100%)
    pallas_call x1, Pallas kernels, ffn_back(): pl.pallas_call(functools.partial(ffn_back_kernel, count, groups, rows), n...  165 us
    pallas_call x1, Pallas kernels, forward_mixer(): pl.pallas_call(functools.partial(forward_kernel, heads, width, seqs, coun...  120 us
    pallas_call x1, Pallas kernels, backward_mixer(): pl.pallas_call(functools.partial(backward_kernel, heads, width, seqs, chu...  96.5 us
    pallas_call x1, Pallas kernels, last_step(): pl.pallas_call(functools.partial(last_kernel, count, groups, rows), name=...  88.5 us
    pallas_call x1, Pallas kernels, attend(): pl.pallas_call(functools.partial(attend_kernel, count), name='attend', ou...  86.7 us
    pallas_call x1, Pallas kernels, gather_tokens(): pl.pallas_call(functools.partial(gather_kernel, count), name='gather_toke...  84.6 us
    pallas_call x1, Pallas kernels, results(): pl.pallas_call(functools.partial(results_kernel, heads, taps, wide, width...  15.8 us

profile of v14, /device:TPU:0, one launch (start us, length us, event | category | flops | bytes accessed | tf_op | source)
XLA Modules:
  0.0 657.6 jit_solution(17195722918267516210)
XLA Ops:
  0.7 84.6 %gather_tokens.1.tokens = bf16[2048,2048]{1,0:T(8,128)(2,1)} custom-call(bf16[256,2048]{1,0:T(8,128)(2,1)} %tokens_in.1), custom_call_target="tpu_custom_call" | custom-call | bytes 314572800 | tf_op jit(solution)/shard_map/gather_tokens/pallas_call | solution.py:495
  85.3 119.6 %mixer_forward.1 = (bf16[8,2048,256]{2,1,0:T(8,128)(2,1)}, bf16[8,4,64,2048]{3,2,1,0:T(8,128)(2,1)}, bf16[2048,256]{1,0:T(8,128)(2,1)}, f32[2048,256]{1,0:T(8,12...) custom-call(s32[1,2]{1,0:T(1,128)} %starts.3, ...), custom_call_target="tpu_custom_call" | custom-call | flops 19327352832 | bytes 31457280 | tf_op jit(solution)/shard_map/mixer_forward/pallas_call | solution.py:1294
  204.8 86.7 %attend.1 = (f32[256,2048]{1,0:T(8,128)}, bf16[2048,2048]{1,0:T(8,128)(2,1)}, bf16[2048,704]{1,0:T(8,128)(2,1)}, bf16[2048,704]{1,0:T(8,128)(2,1)}, bf16[2048,70...) custom-call(bf16[8,2048,256]{2,1,0:T(8,128)(2,1)} %get-tuple-element.76.mixed, bf16[2048,2048]{1,0:T(8,128)(2,1)} %bitcast.25, ...), custom_call_target="tpu_custom_call" | custom-call | flops 34896609280 | bytes 314572800 | tf_op jit(solution)/shard_map/attend/pallas_call | solution.py:669
  291.5 165.1 %ffn_back.1 = (f32[256,2048]{1,0:T(8,128)}, bf16[2048,2048]{1,0:T(8,128)(2,1)}, f32[1,2048]{1,0:T(1,128)}, bf16[704,2048]{1,0:T(8,128)(2,1)}, bf16[704,2048]{1,0:T(8,128)(2,1)}, /*index=5*/bf16[704,2048]{1,0:T(8,128)(2,1)}) custom-call(bf16[2048,704]{1,0:T(8,128)(2,1)} %get-tuple-element.78.grad_gate_in, bf16[2048,704]{1,0:T(8,128)(2,1)} %get-tuple-element.79.grad_up_in, ...), custom_call_target="tpu_custom_call" | custom-call | flops 29527900160 | bytes 629145600 | tf_op jit(solution)/shard_map/ffn_back/pallas_call | solution.py:850
  456.6 96.5 %mixer_backward.1 = (bf16[2048,2048]{1,0:T(8,128)(2,1)}, bf16[2048,256]{1,0:T(8,128)(2,1)}, bf16[2048,256]{1,0:T(8,128)(2,1)}, bf16[2048,256]{1,0:T(8,128)(2,1)}...) custom-call(s32[1,2]{1,0:T(1,128)} %starts.3, ...), custom_call_target="tpu_custom_call" | custom-call | flops 25769803776 | bytes 54525952 | tf_op jit(solution)/shard_map/mixer_backward/pallas_call | solution.py:1548
  553.0 88.5 %last_step.1 = (f32[256,2048]{1,0:T(8,128)}, f32[16,2048]{1,0:T(8,128)}, bf16[2048,256]{1,0:T(8,128)(2,1)}, bf16[2048,256]{1,0:T(8,128)(2,1)}, bf16[2048,256]{1,...) custom-call(bf16[2048,2048]{1,0:T(8,128)(2,1)} %get-tuple-element.99.terms, ...), custom_call_target="tpu_custom_call" | custom-call | bytes 314572800 | tf_op jit(solution)/shard_map/last_step/pallas_call | solution.py:1010
  641.5 15.8 %results.1 = (bf16[256,2048]{1,0:T(8,128)(2,1)}, f32[256,2048]{1,0:T(8,128)}, f32[2048,256]{1,0:T(8,128)}, f32[2048,256]{1,0:T(8,128)}, f32[2048,256]{1,0:T(8,12...) custom-call(f32[16,2048]{1,0:T(8,128)} %get-tuple-element.107.total,, ...), custom_call_target="tpu_custom_call" | custom-call | bytes 50331648 | tf_op jit(solution)/shard_map/results/pallas_call | solution.py:1064
